TPU v7x, 256 devices: a whole 4x4x8 slice. The times are simulated.
256 devices in a mesh: pairs: 128 (over y, x, z), side: 2 (over core).
Axes of the slice: x: 4, y: 4, z: 8, core: 2. Of those that a mesh axis runs over, the one named last changes fastest.
Arguments:
- features: bfloat16 [128, 196, 768], P('pairs', None, 'side'), may hold values from -6 to 6
- image_slot: int32 [128], replicated, may hold values from 0 to 127, as said below
- slot_images: int32 [384, 2], P('pairs'), may hold values from 0 to 127, as said below
- slot_count: int32 [128], P('pairs'), may hold values from 1 to 3, as said below
- gain_self: float32 [2, 768], P('side'), may hold values from 0.5 to 1.5
- gain_query: float32 [2, 768], P('side'), may hold values from 0.5 to 1.5
- gain_memory: float32 [2, 768], P('side'), may hold values from 0.5 to 1.5
- gain_mlp: float32 [2, 768], P('side'), may hold values from 0.5 to 1.5
- gain_head: float32 [2, 768], P('side'), may hold values from 0.5 to 1.5
- w_qkv: bfloat16 [2, 768, 2304], P('side'), may hold values from -0.21875 to 0.21875
- w_self_out: bfloat16 [2, 768, 768], P('side'), may hold values from -0.21875 to 0.21875
- w_query: bfloat16 [2, 768, 768], P('side'), may hold values from -0.21875 to 0.21875
- w_memory: bfloat16 [2, 768, 1536], P('side'), may hold values from -0.21875 to 0.21875
- w_cross_out: bfloat16 [2, 768, 768], P('side'), may hold values from -0.21875 to 0.21875
- w_fc1: bfloat16 [2, 3072, 768], P('side', 'pairs'), may hold values from -0.21875 to 0.21875
- w_fc2: bfloat16 [2, 3072, 768], P('side', 'pairs'), may hold values from -0.109375 to 0.109375
- w_head: bfloat16 [2, 768, 1024], P('side'), may hold values from -0.21875 to 0.21875
Outputs:
- merged_points: bfloat16 [128, 196, 768], P('pairs', None, 'side')
Inputs may be any that keep to these rules, and one draw needn't show every extreme that they name: A permutation: image i is storage row image_slot[i] of features, held by device image_slot[i] // 1 of pairs. `slot_images`: slot j belongs to device j // 3 of pairs; its two images are distinct, and each is held by device (j // 3 + k) mod the size of pairs for some 0 <= k < 4; k = 3 occurs. `slot_count`: the counts sum to 256; 3 is reached on a quarter of the devices.
All inputs are finite; a program needn't handle non-finite values.
Results may differ from a plain program's by a relative error of at most 0.015.
Values may be sent and summed in bfloat16 or wider, within the bound.
No kernel may reach another device: no remote copies, remote signals or barrier semaphores. Data moves between devices by JAX's collectives and lax.ppermute only.
A program may use at most 128 MiB of HBM per device.

v0:
```python
import jax
import jax.numpy as jnp
from jax import lax
from jax.sharding import PartitionSpec as P

D = 768
HEADS = 12
HEAD_DIM = 64
TOKI = 196
PIXELS = 256
WINDOW = 4


def passed_along(array, axis, by):
    count = lax.axis_size(axis)
    return lax.ppermute(array, axis, [(i, (i + by) % count) for i in range(count)])


def swapped(block, axis, stride):
    count = lax.axis_size(axis)
    route = []
    for low in range(count):
        high = low | 1 << stride
        if high != low and high < count:
            route += [(low, high), (high, low)]
    return lax.ppermute(block, axis, route)


def layer_norm(values, gain):
    center = values - jnp.mean(values, axis=-1, keepdims=True)
    spread = jnp.mean(center * center, axis=-1, keepdims=True)
    return center * lax.rsqrt(spread + 1e-06) * gain


def attend(queries, key_rows, value_rows, slots):
    q_heads = queries.reshape(slots, TOKI, HEADS, HEAD_DIM)
    k_heads = key_rows.reshape(slots, TOKI, HEADS, HEAD_DIM)
    v_heads = value_rows.reshape(slots, TOKI, HEADS, HEAD_DIM)
    scores = jnp.einsum(
        "sqhd,skhd->shqk", q_heads, k_heads, preferred_element_type=jnp.float32
    ) * HEAD_DIM ** (-0.5)
    expon = jnp.exp(scores)
    weights = (expon / jnp.sum(expon, axis=-1, keepdims=True)).astype(jnp.bfloat16)
    mixed = jnp.einsum("shqk,skhd->sqhd", weights, v_heads, preferred_element_type=jnp.float32)
    return mixed.astype(jnp.bfloat16).reshape(slots * TOKI, D)


def decode(tokens, memory, gains, mats, fc_in, fc_out, slots):
    g_self, g_query, g_memory, g_mlp, g_head = gains
    m_qkv, m_self_out, m_query, m_memory, m_cross_out, m_head = mats
    flat_tokens = tokens.reshape(slots * TOKI, D)
    flat_memory = memory.reshape(slots * TOKI, D)
    hidden = layer_norm(flat_tokens.astype(jnp.float32), g_self).astype(jnp.bfloat16)
    triple = jnp.dot(hidden, m_qkv, preferred_element_type=jnp.float32).astype(jnp.bfloat16)
    attended = attend(triple[:, :D], triple[:, D : 2 * D], triple[:, 2 * D :], slots)
    first = flat_tokens.astype(jnp.float32) + jnp.dot(
        attended, m_self_out, preferred_element_type=jnp.float32
    )
    query_in = layer_norm(first, g_query).astype(jnp.bfloat16)
    memory_in = layer_norm(flat_memory.astype(jnp.float32), g_memory).astype(jnp.bfloat16)
    queries = jnp.dot(query_in, m_query, preferred_element_type=jnp.float32).astype(jnp.bfloat16)
    key_value = jnp.dot(memory_in, m_memory, preferred_element_type=jnp.float32).astype(
        jnp.bfloat16
    )
    crossed = attend(queries, key_value[:, :D], key_value[:, D:], slots)
    second = first + jnp.dot(crossed, m_cross_out, preferred_element_type=jnp.float32)
    mlp_in = layer_norm(second, g_mlp).astype(jnp.bfloat16)
    rows_in = lax.all_gather(fc_in, "pairs", axis=1, tiled=True)[0]
    rows_out = lax.all_gather(fc_out, "pairs", axis=1, tiled=True)[0]
    pre_act = jnp.einsum("td,fd->tf", mlp_in, rows_in, preferred_element_type=jnp.float32)
    activated = jax.nn.gelu(pre_act, approximate=False).astype(jnp.bfloat16)
    mlp_sum = jnp.dot(activated, rows_out, preferred_element_type=jnp.float32)
    third = second + mlp_sum
    final = layer_norm(third, g_head).astype(jnp.bfloat16)
    return jnp.dot(final, m_head, preferred_element_type=jnp.float32)


def map_terms(raw):
    lead = raw.shape[:-1]
    parts = raw.reshape(lead + (2, 4, PIXELS // 2))
    conf = 1.0 + jnp.exp(parts[..., 3, :])
    joined = jnp.concatenate([conf[..., None, :] * parts[..., :3, :], conf[..., None, :]], axis=-2)
    return joined.reshape(lead + (4 * PIXELS,))


def on_device(
    features,
    image_slot,
    slot_images,
    slot_count,
    gain_self,
    gain_query,
    gain_memory,
    gain_mlp,
    gain_head,
    w_qkv,
    w_self_out,
    w_query,
    w_memory,
    w_cross_out,
    w_fc1,
    w_fc2,
    w_head,
):
    devices = lax.axis_size("pairs")
    here = lax.axis_index("pairs")
    which_side = lax.axis_index("side")
    img_local = features.shape[0]
    slots = slot_images.shape[0]
    stored = image_slot[slot_images]
    window_index = (stored // img_local - here) % devices * img_local + stored % img_local
    own_index = jnp.where(which_side == 0, window_index[:, 0], window_index[:, 1])
    live_slot = jnp.arange(slots) < slot_count[0]
    full_rows = lax.all_gather(features, "side", axis=2, tiled=True)
    blocks = [full_rows]
    for offset in range(1, WINDOW):
        blocks.append(passed_along(full_rows, "pairs", -offset))
    window = jnp.concatenate(blocks, axis=0)
    own_tokens = jnp.take(window, own_index, axis=0)
    memory = swapped(own_tokens, "side", 0)
    gains = [gain_self[0], gain_query[0], gain_memory[0], gain_mlp[0], gain_head[0]]
    mats = [w_qkv[0], w_self_out[0], w_query[0], w_memory[0], w_cross_out[0], w_head[0]]
    result = decode(own_tokens, memory, gains, mats, w_fc1, w_fc2, slots)
    terms = map_terms(result).reshape(slots, TOKI, 4 * PIXELS)
    select = (
        (own_index[:, None] == jnp.arange(WINDOW * img_local)[None, :]) & live_slot[:, None]
    ).astype(jnp.float32)
    window_sums = jnp.einsum("sw,stc->wtc", select, terms, precision=lax.Precision.HIGHEST)
    total = window_sums[:img_local]
    for offset in range(1, WINDOW):
        piece = window_sums[offset * img_local : (offset + 1) * img_local]
        total = total + passed_along(piece.astype(jnp.bfloat16), "pairs", offset).astype(
            piece.dtype
        )
    owned = lax.psum_scatter(
        total.reshape(img_local, TOKI, 2, 2 * PIXELS).astype(jnp.bfloat16),
        "side",
        scatter_dimension=2,
        tiled=True,
    ).astype(jnp.float32)
    parts = owned.reshape(img_local, TOKI, 4, PIXELS // 2)
    merged = parts[:, :, :3] / jnp.maximum(parts[:, :, 3:], 1.0)
    return merged.reshape(img_local, TOKI, 3 * (PIXELS // 2)).astype(jnp.bfloat16)


def solution(mesh):
    placed = (
        P("pairs", None, "side"),
        P(),
        P("pairs", None),
        P("pairs"),
        P("side", None),
        P("side", None),
        P("side", None),
        P("side", None),
        P("side", None),
        P("side", None, None),
        P("side", None, None),
        P("side", None, None),
        P("side", None, None),
        P("side", None, None),
        P("side", "pairs", None),
        P("side", "pairs", None),
        P("side", None, None),
    )
    return jax.shard_map(
        on_device, mesh=mesh, in_specs=placed, out_specs=P("pairs", None, "side"), check_vma=False
    )
```

profile of v0, /device:TPU:1, one launch (start us, length us, event | category | flops | bytes accessed | tf_op | source)
XLA Modules:
  0.0 385.7 jit_solution(14244061151769425737)
XLA Ops:
  7.3 6.9 %all_gather.9 = bf16[1,196,768]{2,1,0:T(8,128)(2,1)} all-gather(bf16[1,196,384]{2,1,0:T(8,128)(2,1)} %param.17), channel_id=1, replica_groups=mesh['pairs'=128,'side'=2] {'side'}, dimensions={2}, use_global_device_ids=true | all-gather | bytes 451584 | tf_op jit(solution)/shard_map/all_gather | solution.py:114
  14.2 8.5 %collective-permute-start = (bf16[1,196,768]{2,1,0:T(8,128)(2,1)}, bf16[1,196,768]{2,1,0:T(8,128)(2,1)}, u32[]{:S(2)}, u32[]{:S(2)}) collective-permute-start(bf16[1,196,768]{2,1,0:T(8,128)(2,1)} %all_gather.9), channel_id=1, source_target_pairs={{0,254},{2,0},{4,2},{6,4},{8,6},{10,8},{12,10},{14,12},{16,14},{18... | collective-permute-start | bytes 903176 | tf_op jit(solution)/shard_map/ppermute | solution.py:16
  37.9 11.3 %collective-permute-done.1 = bf16[1,196,768]{2,1,0:T(8,128)(2,1)} collective-permute-done((bf16[1,196,768]{2,1,0:T(8,128)(2,1)}, bf16[1,196,768]{2,1,0:T(8,128)(2,1)}, u32[]{:S(2)}, u32[]{:S(2)}) %collective-permute-start.1) | collective-permute-done | bytes 301088 | tf_op jit(solution)/shard_map/ppermute | solution.py:16
  49.3 14.0 %collective-permute-done.2 = bf16[1,196,768]{2,1,0:T(8,128)(2,1)} collective-permute-done((bf16[1,196,768]{2,1,0:T(8,128)(2,1)}, bf16[1,196,768]{2,1,0:T(8,128)(2,1)}, u32[]{:S(2)}, u32[]{:S(2)}) %collective-permute-start.2) | collective-permute-done | bytes 301088 | tf_op jit(solution)/shard_map/ppermute | solution.py:16
  65.7 2.9 gather_fusion.1
  80.6 3.5 convolution_convert_fusion
  85.5 3.0 reshape.315
  88.5 4.0 %reshape.316 = bf16[3,196,12,64]{3,2,1,0:T(8,128)(2,1)} reshape(bf16[588,768]{1,0:T(8,128)(2,1)} %get-tuple-element.12) | data formatting | bytes 1806336 | tf_op jit(solution)/shard_map/reshape | solution.py:37
  95.4 3.7 fusion.10
  110.4 3.3 reshape.318
  121.4 3.5 convolution_convert_fusion.1
  126.3 4.0 %reshape.319 = bf16[3,196,12,64]{3,2,1,0:T(8,128)(2,1)} reshape(bf16[588,768]{1,0:T(8,128)(2,1)} %get-tuple-element.17) | data formatting | bytes 1806336 | tf_op jit(solution)/shard_map/reshape | solution.py:37
  130.4 4.0 %reshape.317 = bf16[3,196,12,64]{3,2,1,0:T(8,128)(2,1)} reshape(bf16[588,768]{1,0:T(8,128)(2,1)} %get-tuple-element.16) | data formatting | bytes 1806336 | tf_op jit(solution)/shard_map/reshape | solution.py:38
  134.4 3.7 fusion.11
  141.9 4.4 %reshape.287 = bf16[588,768]{0,1:T(8,128)(2,1)} reshape(bf16[3,196,12,64]{1,0,3,2:T(4,128)(2,1)} %copy.99) | data formatting | bytes 1806336 | tf_op jit(solution)/shard_map/reshape | solution.py:45
  150.7 9.1 %fusion.14 = f32[588,3072]{1,0:T(8,128)} fusion(bf16[1,3072,768]{2,1,0:T(8,128)(2,1)} %all-gather.3.cloned.1.call-done, f32[588,768]{1,0:T(8,128)} %copy-done.5, f32[768]{0:T(1024)S(1)} %copy-done.12, f32[588]{0:T(1024)S(1)} %add_rsqrt_fusion.1, f32[588]{0:T(1024)S(1)} %broadcast_multiply_fusion.1), kind=kOutput, calls=%fused_computation.29 | convolution fusion | flops 2776338432 | bytes 13758048 | tf_op jit(solution)/shard_map/td,fd->tf/dot_general | solution.py:70
  159.8 97.9 %all-gather.5.cloned.1.call-done = bf16[1,3072,768]{2,1,0:T(8,128)(2,1)} async-done(((bf16[1,24,768]{2,1,0:T(8,128)(2,1)}), bf16[1,3072,768]{2,1,0:T(8,128)(2,1)}) %all-gather.5.cloned.1.call-update) | async-done | bytes 4718608 | tf_op jit(solution)/shard_map/all_gather | solution.py:69
  257.7 20.9 %fusion.124 = (f32[588]{0:T(1024)S(1)}, f32[588,768]{1,0:T(8,128)S(1)}) fusion(f32[588,768]{1,0:T(8,128)S(1)} %copy-done.6, bf16[1,3072,768]{2,1,0:T(8,128)(2,1)} %all-gather.5.cloned.1.call-done, f32[588,3072]{1,0:T(8,128)} %fusion.14), kind=kOutput, calls=%fused_computation.174 | convolution fusion | flops 2892846592 | bytes 15558960 | tf_op jit(solution)/shard_map/dot_general | solution.py:72
  285.6 4.5 %fusion.125 = (bf16[4,196,1024]{2,0,1:T(4,128)(2,1)S(1)}, f32[4,196,1024]{2,0,1:T(4,128)S(1)}) fusion(f32[3,196,1024]{2,1,0:T(8,128)S(1)} %reshape_reshape.3, s32[3]{0:T(128)S(1)} %copy-done.14, pred[3]{0:T(512)(128)(4,1)S(1)} %copy-done.16), kind=kOutput, calls=%fused_computation.175 | convolution fusion | flops 29704216 | bytes 7225359 | tf_op jit(solution)/shard_map/sw,stc->wtc/dot_general | solution.py:128
  296.9 9.4 %collective-permute-done.4 = bf16[1,196,1024]{2,1,0:T(8,128)(2,1)S(1)} collective-permute-done((bf16[1,196,1024]{2,1,0:T(8,128)(2,1)S(1)}, bf16[1,196,1024]{2,1,0:T(8,128)(2,1)S(1)}, u32[]{:S(2)}, u32[]{:S(2)}) %collective-permute-start.4) | collective-permute-done | bytes 401440 | tf_op jit(solution)/shard_map/ppermute | solution.py:16
  306.4 10.3 %collective-permute-done.5 = bf16[1,196,1024]{2,1,0:T(8,128)(2,1)S(1)} collective-permute-done((bf16[1,196,1024]{2,1,0:T(8,128)(2,1)S(1)}, bf16[1,196,1024]{2,1,0:T(8,128)(2,1)S(1)}, u32[]{:S(2)}, u32[]{:S(2)}) %collective-permute-start.5) | collective-permute-done | bytes 401440 | tf_op jit(solution)/shard_map/ppermute | solution.py:16
  316.7 18.5 %collective-permute-done.6 = bf16[1,196,1024]{2,1,0:T(8,128)(2,1)S(1)} collective-permute-done((bf16[1,196,1024]{2,1,0:T(8,128)(2,1)S(1)}, bf16[1,196,1024]{2,1,0:T(8,128)(2,1)S(1)}, u32[]{:S(2)}, u32[]{:S(2)}) %collective-permute-start.6) | collective-permute-done | bytes 401440 | tf_op jit(solution)/shard_map/ppermute | solution.py:16
  335.2 8.0 %convert_reduce_fusion.2 = bf16[196,1024]{1,0:T(8,128)(2,1)} fusion(bf16[1,196,1024]{2,1,0:T(8,128)(2,1)S(1)} %collective-permute-done.6, bf16[1,196,1024]{2,1,0:T(8,128)(2,1)S(1)} %collective-permute-done.5, bf16[1,196,1024]{2,1,0:T(8,128)(2,1)S(1)} %collective-permute-done.4, f32[4,196,1024]{2,0,1:T(4,128)S(1)} %get-tuple-element.32), kind=kLoop, calls=%fused_computation.100 | loop fusion | flops 1404928 | bytes 2408448 | tf_op jit(solution)/shard_map/convert_element_type | solution.py:136
  347.0 25.5 %reduce-scatter.2.cloned.1.call-done = bf16[1,196,1,512]{3,1,0,2:T(8,128)(2,1)} async-done(((bf16[1,196,2,512]{3,1,0,2:T(8,128)(2,1)}), bf16[1,196,1,512]{3,1,0,2:T(8,128)(2,1)}) %reduce-scatter.2.cloned.1.call-update) | async-done | bytes 200720 | tf_op jit(solution)/shard_map/reduce_scatter | solution.py:135
  (122 shorter events, 86.3 us)
Async XLA Ops:
  6.5 74.0 %copy-start = (bf16[1,768,2304]{2,1,0:T(8,128)(2,1)S(1)}, bf16[1,768,2304]{2,1,0:T(8,128)(2,1)}, u32[]{:S(2)}) copy-start(bf16[1,768,2304]{2,1,0:T(8,128)(2,1)} %param.26) | copy-start | bytes 10616836
  6.5 144.2 %all-gather.3.cloned.1.call-start = ((), (), s32[]{:S(2)}) async-start(), calls=%async_computation.1 | async-start | bytes 4755456 | tf_op jit(solution)/shard_map/all_gather | solution.py:68
  7.3 250.5 %all-gather.5.cloned.1.call-start = ((), (), s32[]{:S(2)}) async-start(), calls=%async_computation.2 | async-start | bytes 4755456 | tf_op jit(solution)/shard_map/all_gather | solution.py:69
  14.2 23.7 %collective-permute-start = (bf16[1,196,768]{2,1,0:T(8,128)(2,1)}, bf16[1,196,768]{2,1,0:T(8,128)(2,1)}, u32[]{:S(2)}, u32[]{:S(2)}) collective-permute-start(bf16[1,196,768]{2,1,0:T(8,128)(2,1)} %all_gather.9), channel_id=1, source_target_pairs={{0,254},{2,0},{4,2},{6,4},{8,6},{10,8},{12,10},{14,12},{16,14},{18... | collective-permute-start | bytes 903176 | tf_op jit(solution)/shard_map/ppermute | solution.py:16
  22.7 26.6 %collective-permute-start.1 = (bf16[1,196,768]{2,1,0:T(8,128)(2,1)}, bf16[1,196,768]{2,1,0:T(8,128)(2,1)}, u32[]{:S(2)}, u32[]{:S(2)}) collective-permute-start(bf16[1,196,768]{2,1,0:T(8,128)(2,1)} %all_gather.9), channel_id=1, source_target_pairs={{0,252},{2,254},{4,0},{6,2},{8,4},{10,6},{12,8},{14,10},{16,12},{1... | collective-permute-start | bytes 903176 | tf_op jit(solution)/shard_map/ppermute | solution.py:16
  23.8 39.4 %collective-permute-start.2 = (bf16[1,196,768]{2,1,0:T(8,128)(2,1)}, bf16[1,196,768]{2,1,0:T(8,128)(2,1)}, u32[]{:S(2)}, u32[]{:S(2)}) collective-permute-start(bf16[1,196,768]{2,1,0:T(8,128)(2,1)} %all_gather.9), channel_id=1, source_target_pairs={{0,250},{2,252},{4,254},{6,0},{8,2},{10,4},{12,6},{14,8},{16,10},{... | collective-permute-start | bytes 903176 | tf_op jit(solution)/shard_map/ppermute | solution.py:16
  24.3 348.2 %reduce-scatter.2.cloned.1.call-start = ((), (), s32[]{:S(2)}) async-start(), calls=%async_computation.3 | async-start | bytes 614400 | tf_op jit(solution)/shard_map/reduce_scatter | solution.py:135
  27.4 9.8 %copy-start.10 = (s32[3,1]{1,0:T(4,128)S(1)}, s32[3,1]{1,0:T(4,128)}, u32[]{:S(2)}) copy-start(s32[3,1]{1,0:T(4,128)} %get-tuple-element.10) | copy-start | bytes 40
  73.2 40.5 %collective-permute-start.3 = (bf16[3,196,768]{2,1,0:T(8,128)(2,1)}, bf16[3,196,768]{2,1,0:T(8,128)(2,1)}, u32[]{:S(2)}, u32[]{:S(2)}) collective-permute-start(bf16[3,196,768]{2,1,0:T(8,128)(2,1)} %get-tuple-element.8), channel_id=1, source_target_pairs={{0,1},{1,0},{2,3},{3,2},{4,5},{5,4},{6,7},{7,6},{8,9},{9,8},{10,11... | collective-permute-start | bytes 2709512 | tf_op jit(solution)/shard_map/ppermute | solution.py:26
  95.4 3.7 copy-start.7
  100.7 3.1 copy-start.2
  106.4 1.9 copy-start.17
  134.4 3.8 copy-start.8
  139.7 6.6 %copy-start.4 = (f32[588,768]{1,0:T(8,128)S(1)}, f32[588,768]{1,0:T(8,128)}, u32[]{:S(2)}) copy-start(f32[588,768]{1,0:T(8,128)} %copy-done.3) | copy-start | bytes 5419012
  146.4 4.3 %copy-start.12 = (f32[768]{0:T(1024)S(1)}, f32[768]{0:T(1024)}, u32[]{:S(2)}) copy-start(f32[768]{0:T(1024)} %reduce.10) | copy-start | bytes 9220
  150.7 107.1 %copy-start.6 = (f32[588,768]{1,0:T(8,128)S(1)}, f32[588,768]{1,0:T(8,128)}, u32[]{:S(2)}) copy-start(f32[588,768]{1,0:T(8,128)} %copy-done.5) | copy-start | bytes 5419012
  159.8 119.2 %copy-start.11 = (f32[768]{0:T(1024)S(1)}, f32[768]{0:T(1024)}, u32[]{:S(2)}) copy-start(f32[768]{0:T(1024)} %reduce.11) | copy-start | bytes 9220
  257.7 21.3 %copy-start.9 = (bf16[1024,768]{1,0:T(8,128)(2,1)S(1)}, bf16[1024,768]{1,0:T(8,128)(2,1)}, u32[]{:S(2)}) copy-start(bf16[1024,768]{1,0:T(8,128)(2,1)} %copy.125) | copy-start | bytes 4718596
  283.1 2.5 copy-start.14
  283.1 2.5 copy-start.16
  292.4 14.0 %collective-permute-start.4 = (bf16[1,196,1024]{2,1,0:T(8,128)(2,1)S(1)}, bf16[1,196,1024]{2,1,0:T(8,128)(2,1)S(1)}, u32[]{:S(2)}, u32[]{:S(2)}) collective-permute-start(bf16[1,196,1024]{2,1,0:T(8,128)(2,1)S(1)} %copy.103), channel_id=1, source_target_pairs={{0,2},{2,4},{4,6},{6,8},{8,10},{10,12},{12,14},{14,16},{16,18},{18... | collective-permute-start | bytes 1204232 | tf_op jit(solution)/shard_map/ppermute | solution.py:16
  293.3 23.4 %collective-permute-start.5 = (bf16[1,196,1024]{2,1,0:T(8,128)(2,1)S(1)}, bf16[1,196,1024]{2,1,0:T(8,128)(2,1)S(1)}, u32[]{:S(2)}, u32[]{:S(2)}) collective-permute-start(bf16[1,196,1024]{2,1,0:T(8,128)(2,1)S(1)} %copy.105), channel_id=1, source_target_pairs={{0,4},{2,6},{4,8},{6,10},{8,12},{10,14},{12,16},{14,18},{16,20},{1... | collective-permute-start | bytes 1204232 | tf_op jit(solution)/shard_map/ppermute | solution.py:16
  295.5 39.8 %collective-permute-start.6 = (bf16[1,196,1024]{2,1,0:T(8,128)(2,1)S(1)}, bf16[1,196,1024]{2,1,0:T(8,128)(2,1)S(1)}, u32[]{:S(2)}, u32[]{:S(2)}) collective-permute-start(bf16[1,196,1024]{2,1,0:T(8,128)(2,1)S(1)} %copy.107), channel_id=1, source_target_pairs={{0,6},{2,8},{4,10},{6,12},{8,14},{10,16},{12,18},{14,20},{16,22},{... | collective-permute-start | bytes 1204232 | tf_op jit(solution)/shard_map/ppermute | solution.py:16
  335.2 43.7 %copy-start.1 = (bf16[1,768,2304]{2,1,0:T(8,128)(2,1)S(1)}, bf16[1,768,2304]{2,1,0:T(8,128)(2,1)}, u32[]{:S(2)}) copy-start(bf16[1,768,2304]{2,1,0:T(8,128)(2,1)} %param.26) | copy-start | bytes 10616836
  (4 other events, 4.3 us)
Sparse Core Ops, SparseCore 0:
  11.0 128.8 all-gather.2
  143.6 114.0 all-gather.4
  347.1 25.3 reduce-scatter.1
where the time goes:
time: 391 us; the launch traced here: 386 us
  waiting for transfers between devices  188 us (48%)
  local copies, waits for them, and re-layouts  65.9 us (17%)
  matrix products  60.7 us (16%)
  other arithmetic  34.6 us (9%)
  starting transfers between devices  15.5 us (4%)
  between operations  14.3 us (4%)
  blocking collectives  6.88 us (2%)
    all_gather x1, waiting for transfers between devices, decode(): rows_out = lax.all_gather(fc_out, 'pairs', axis=1, tiled=True)[0]  97.9 us
    ppermute x6, waiting for transfers between devices, passed_along(): lax.ppermute(array, axis, [(i, (i + by) % count) for i in range(count)])  63.6 us
    reduce_scatter x1, waiting for transfers between devices, on_device(): lax.psum_scatter(total.reshape(img_local, TOKI, 2, 2 * PIXELS).astype(jnp...  25.5 us
    dot_general x1, matrix products, decode(): mlp_sum = jnp.dot(activated, rows_out, preferred_element_type=jnp.float32)  20.9 us
    ppermute x6, starting transfers between devices, passed_along(): lax.ppermute(array, axis, [(i, (i + by) % count) for i in range(count)])  14.4 us
    dot_general x1, matrix products, decode(): jnp.einsum('td,fd->tf', mlp_in, rows_in, preferred_element_type=jnp.float32)  9.06 us
    reshape x2, local copies, waits for them, and re-layouts, attend(): k_heads = key_rows.reshape(slots, TOKI, HEADS, HEAD_DIM)  8.09 us
    convert_element_type x1, other arithmetic, on_device(): total.reshape(img_local, TOKI, 2, 2 * PIXELS).astype(jnp.bfloat16)  7.99 us
  transfers between devices with their start and end apart: 10, of which 7 were waited for; matrix products, arithmetic and copies ran while one was open for 27% of the time, Pallas kernels for 0%

commit v1 on v0

v1 whole, which is shorter than its diff:
```python
import jax
import jax.numpy as jnp
from jax import lax
from jax.experimental import pallas as pl
from jax.experimental.pallas import tpu as pltpu
from jax.sharding import PartitionSpec as P

D = 768
HEAD_DIM = 64
TOKI = 196
ROWS = 208
HALF = 384
WINDOW = 4
SLOTS = 3
ALL = SLOTS * ROWS
FF = 3072
CHUNK = 512
F32 = jnp.float32
BF16 = jnp.bfloat16


def shifted(array, by):
    count = lax.axis_size("pairs")
    return lax.ppermute(array, "pairs", [(i, (i + by) % count) for i in range(count)])


def other_core(array):
    return lax.ppermute(array, "side", [(0, 1), (1, 0)])


def layer_norm(values, gain):
    center = values - jnp.mean(values, axis=-1, keepdims=True)
    spread = jnp.mean(center * center, axis=-1, keepdims=True)
    return center * lax.rsqrt(spread + 1e-06) * gain


def window_place(image_slot, slot_images, place, slot, which):
    stored = image_slot[slot_images[2 * slot + which]]
    return lax.rem(stored - place[0] + 128, 128)


def load_tokens(image_slot, slot_images, place, mine, theirs, swap, slot):
    which = place[1] if not swap else 1 - place[1]
    index = window_place(image_slot, slot_images, place, slot, which)
    first = place[1] == 0
    low = mine[index].astype(F32)
    high = theirs[index].astype(F32)
    return jnp.where(first, low, high), jnp.where(first, high, low)


def padded_rows(image_slot, slot_images, place, mine, theirs, swap, target):
    for slot in range(SLOTS):
        low, high = load_tokens(image_slot, slot_images, place, mine, theirs, swap, slot)
        base = slot * ROWS
        target[base + 192 : base + ROWS, :] = jnp.zeros((ROWS - 192, D), F32)
        target[base : base + TOKI, :HALF] = low
        target[base : base + TOKI, HALF:] = high


def norm_into(source, gain, target):
    for slot in range(SLOTS):
        rows = slice(slot * ROWS, (slot + 1) * ROWS)
        target[rows, :] = layer_norm(source[rows, :], gain[...]).astype(BF16)


def attention(q_ref, q_base, k_ref, k_base, v_ref, v_base, out_ref):
    lane = lax.broadcasted_iota(jnp.int32, (ROWS, 128), 1)
    low_lanes = lane < HEAD_DIM
    key_ok = lax.broadcasted_iota(jnp.int32, (ROWS, ROWS), 1) < TOKI

    def step(t, carry):
        slot = t // 3
        group = t - 3 * slot
        rows = pl.ds(pl.multiple_of(slot * ROWS, ROWS), ROWS)
        for pair in range(2):
            col = group * 256 + pair * 128
            q = q_ref[rows, pl.ds(pl.multiple_of(q_base + col, 128), 128)]
            k = k_ref[rows, pl.ds(pl.multiple_of(k_base + col, 128), 128)]
            v = v_ref[rows, pl.ds(pl.multiple_of(v_base + col, 128), 128)]
            outs = []
            for head in range(2):
                own = low_lanes if head == 0 else jnp.logical_not(low_lanes)
                scores = lax.dot_general(
                    jnp.where(own, q, jnp.zeros_like(q)),
                    k,
                    (((1,), (1,)), ((), ())),
                    preferred_element_type=F32,
                )
                expon = jnp.where(key_ok, jnp.exp(scores), 0.0)
                total = jnp.sum(expon, axis=-1, keepdims=True)
                weights = (expon * (1.0 / total)).astype(BF16)
                outs.append(jnp.dot(weights, v, preferred_element_type=F32))
            out_ref[rows, pl.ds(pl.multiple_of(col, 128), 128)] = jnp.where(
                low_lanes, outs[0], outs[1]
            ).astype(BF16)
        return carry

    lax.fori_loop(0, 3 * SLOTS, step, 0)


def project(source, weight, width, write):
    def step(n, carry):
        cols = pl.ds(pl.multiple_of(n * 256, 256), 256)
        write(n, cols, jnp.dot(source[...], weight[:, cols], preferred_element_type=F32))
        return carry

    lax.fori_loop(0, width // 256, step, 0)


def self_kernel(
    image_slot, slot_images, place, mine, theirs, g_self, g_query, w_qkv, w_out, w_query,
    first_ref, query_ref, hidden, triple, mixed,
):
    padded_rows(image_slot, slot_images, place, mine, theirs, False, first_ref)
    norm_into(first_ref, g_self, hidden)

    def write_triple(n, cols, value):
        triple[:, cols] = (value * jnp.where(n < 3, 0.125, 1.0)).astype(BF16)

    project(hidden, w_qkv, 3 * D, write_triple)
    attention(triple, 0, triple, D, triple, 2 * D, mixed)

    def add_first(n, cols, value):
        first_ref[:, cols] = first_ref[:, cols] + value

    project(mixed, w_out, D, add_first)
    norm_into(first_ref, g_query, hidden)

    def write_query(n, cols, value):
        query_ref[:, cols] = (value * 0.125).astype(BF16)

    project(hidden, w_query, D, write_query)


def cross_kernel(
    image_slot, slot_images, place, mine, theirs, first, query, g_memory, g_mlp, w_memory, w_out,
    second_ref, mlp_ref, rows_ref, hidden, key_value, mixed,
):
    padded_rows(image_slot, slot_images, place, mine, theirs, True, rows_ref)
    norm_into(rows_ref, g_memory, hidden)

    def write_kv(n, cols, value):
        key_value[:, cols] = value.astype(BF16)

    project(hidden, w_memory, 2 * D, write_kv)
    attention(query, 0, key_value, 0, key_value, D, mixed)

    def add_second(n, cols, value):
        second_ref[:, cols] = first[:, cols] + value

    project(mixed, w_out, D, add_second)
    norm_into(second_ref, g_mlp, mlp_ref)


def gelu(value):
    return value * (1.0 + lax.erf(value * 0.7071067811865476)) * 0.5


def mlp_kernel(
    place, second, mlp_in, fc, g_head, w_head, keep_ref, send_ref, pre, total, hidden,
):
    steps = FF // CHUNK

    def before(c):
        rows = pl.ds(pl.multiple_of(c * CHUNK, CHUNK), CHUNK)
        return lax.dot_general(
            mlp_in[...], fc[0, rows, :], (((1,), (1,)), ((), ())), preferred_element_type=F32
        )

    pre[0] = before(0)
    total[...] = second[...]

    def step(c, carry):
        now = lax.rem(c, 2)
        active = gelu(pre[now]).astype(BF16)
        pre[1 - now] = before(jnp.minimum(c + 1, steps - 1))
        rows = pl.ds(pl.multiple_of(c * CHUNK, CHUNK), CHUNK)
        total[...] = total[...] + jnp.dot(active, fc[1, rows, :], preferred_element_type=F32)
        return carry

    lax.fori_loop(0, steps, step, 0)
    norm_into(total, g_head, hidden)
    first = place[1] == 0
    for slot in range(SLOTS):
        rows = slice(slot * ROWS, (slot + 1) * ROWS)
        terms = []
        for half in range(2):
            raw = jnp.dot(
                hidden[rows, :], w_head[:, half * 512 : (half + 1) * 512],
                preferred_element_type=F32,
            )
            conf = 1.0 + jnp.exp(raw[:, 384:])
            terms.append([conf * raw[:, c * 128 : (c + 1) * 128] for c in range(3)] + [conf])
        for c in range(4):
            cols = slice(c * 128, (c + 1) * 128)
            low, high = terms[0][c][:TOKI], terms[1][c][:TOKI]
            keep_ref[slot, :, cols] = jnp.where(first, low, high)
            send_ref[slot, :, cols] = jnp.where(first, high, low).astype(BF16)


def window_kernel(
    image_slot, slot_images, slot_count, place, keep, got, out0, out1, out2, out3
):
    outs = [out0, out1, out2, out3]
    chosen = []
    for slot in range(SLOTS):
        live = slot < slot_count[0]
        for which in range(2):
            index = window_place(image_slot, slot_images, place, slot, which)
            chosen.append((slot, which, jnp.where(live, index, -1)))
    for w in range(WINDOW):
        for c in range(4):
            cols = slice(c * 128, (c + 1) * 128)
            acc = jnp.zeros((TOKI, 128), F32)
            for slot in range(SLOTS):
                own = jnp.where(place[1] == 0, chosen[2 * slot][2], chosen[2 * slot + 1][2])
                far = jnp.where(place[1] == 0, chosen[2 * slot + 1][2], chosen[2 * slot][2])
                acc = acc + jnp.where(own == w, keep[slot, :, cols], 0.0)
                acc = acc + jnp.where(far == w, got[slot, :, cols].astype(F32), 0.0)
            outs[w][:, cols] = acc.astype(outs[w].dtype)


def merge_kernel(base, passed, out):
    weight = jnp.maximum(base[:, 384:] + passed[:, 384:].astype(F32), 1.0)
    for c in range(3):
        cols = slice(c * 128, (c + 1) * 128)
        out[0, :, cols] = ((base[:, cols] + passed[:, cols].astype(F32)) / weight).astype(BF16)


SMEM = pl.BlockSpec(memory_space=pltpu.SMEM)
VMEM = pl.BlockSpec(memory_space=pltpu.VMEM)


def call(kernel, scalars, arrays, outs, scratch, flops, name):
    return pl.pallas_call(
        kernel,
        in_specs=[SMEM] * len(scalars) + [VMEM] * len(arrays),
        out_specs=[VMEM] * len(outs),
        out_shape=[jax.ShapeDtypeStruct(s, d) for s, d in outs],
        scratch_shapes=[pltpu.VMEM(s, d) for s, d in scratch],
        compiler_params=pltpu.CompilerParams(vmem_limit_bytes=48 << 20),
        cost_estimate=pl.CostEstimate(flops=flops, transcendentals=0, bytes_accessed=8 << 20),
        name=name,
    )(*scalars, *arrays)


def self_call(scalars, mine, theirs, g_self, g_query, w_qkv, w_out, w_query):
    return call(
        self_kernel, scalars, [mine, theirs, g_self, g_query, w_qkv, w_out, w_query],
        [((ALL, D), F32), ((ALL, D), BF16)],
        [((ALL, D), BF16), ((ALL, 3 * D), BF16), ((ALL, D), BF16)],
        6 * 10**9, "self_part",
    )


def cross_call(scalars, mine, theirs, first, query, g_memory, g_mlp, w_memory, w_out):
    return call(
        cross_kernel, scalars, [mine, theirs, first, query, g_memory, g_mlp, w_memory, w_out],
        [((ALL, D), F32), ((ALL, D), BF16)],
        [((ALL, D), F32), ((ALL, D), BF16), ((ALL, 2 * D), BF16), ((ALL, D), BF16)],
        5 * 10**9, "cross_part",
    )


def mlp_call(place, second, mlp_in, fc, g_head, w_head):
    return call(
        mlp_kernel, [place], [second, mlp_in, fc, g_head, w_head],
        [((SLOTS, TOKI, 512), F32), ((SLOTS, TOKI, 512), BF16)],
        [((2, ALL, CHUNK), F32), ((ALL, D), F32), ((ALL, D), BF16)],
        7 * 10**9, "mlp_part",
    )


def window_call(scalars, keep, got):
    return call(
        window_kernel, scalars, [keep, got],
        [((TOKI, 512), F32)] + [((TOKI, 512), BF16)] * 3, [], 10**8, "window_part",
    )


def merge_call(base, passed):
    return call(merge_kernel, [], [base, passed], [((1, TOKI, HALF), BF16)], [], 10**8, "merge_part")[0]


def gather_hidden(shard):
    return lax.all_gather(shard, "pairs", axis=1, tiled=True)


def on_device(
    features,
    image_slot,
    slot_images,
    slot_count,
    gain_self,
    gain_query,
    gain_memory,
    gain_mlp,
    gain_head,
    w_qkv,
    w_self_out,
    w_query,
    w_memory,
    w_cross_out,
    w_fc1,
    w_fc2,
    w_head,
):
    place = jnp.stack([lax.axis_index("pairs"), lax.axis_index("side")]).astype(jnp.int32)
    fc = gather_hidden(jnp.concatenate([w_fc1, w_fc2], axis=0))
    blocks = [features]
    for _ in range(1, WINDOW):
        blocks.append(shifted(blocks[-1], -1))
    mine = jnp.concatenate(blocks, axis=0)
    theirs = other_core(mine)
    scalars = [image_slot, slot_images.reshape(-1), place]
    first, query = self_call(
        scalars, mine, theirs, gain_self, gain_query, w_qkv[0], w_self_out[0], w_query[0]
    )
    second, mlp_in = cross_call(
        scalars, mine, theirs, first, query, gain_memory, gain_mlp, w_memory[0], w_cross_out[0]
    )
    keep, send = mlp_call(place, second, mlp_in, fc, gain_head, w_head[0])
    got = other_core(send)
    pieces = window_call([image_slot, slot_images.reshape(-1), slot_count, place], keep, got)
    passed = shifted(pieces[3], 1)
    for w in (2, 1):
        passed = shifted((pieces[w].astype(F32) + passed.astype(F32)).astype(BF16), 1)
    return merge_call(pieces[0], passed)


def solution(mesh):
    placed = (
        P("pairs", None, "side"),
        P(),
        P("pairs", None),
        P("pairs"),
        P("side", None),
        P("side", None),
        P("side", None),
        P("side", None),
        P("side", None),
        P("side", None, None),
        P("side", None, None),
        P("side", None, None),
        P("side", None, None),
        P("side", None, None),
        P("side", "pairs", None),
        P("side", "pairs", None),
        P("side", None, None),
    )
    return jax.shard_map(
        on_device, mesh=mesh, in_specs=placed, out_specs=P("pairs", None, "side"), check_vma=False
    )
```

time: 391 us -> 201 us (0.51); the launches traced: 386 us -> 200 us
  waiting for transfers between devices: 188 us -> 98.7 us
  local copies, waits for them, and re-layouts: 65.9 us -> 3.44 us
  matrix products: 60.7 us -> 0 us
  Pallas kernels: 0 us -> 50.5 us
  other arithmetic: 34.6 us -> 1.62 us
  starting transfers between devices: 15.5 us -> 32 us
  blocking collectives: 6.88 us -> 0 us
    dot_general x13 -> x0, matrix products: 60.7 us -> none  [the longest x1 20.9 us: decode(): mlp_sum = jnp.dot(activated, rows_out, preferred_element_type=jnp.float32)]
    pallas_call x0 -> x5, Pallas kernels: none -> 50.5 us  [call(): pl.pallas_call(kernel, in_specs=[SMEM] * len(scalars) + [VMEM] * len(arra...]
    all_gather x2 -> x1, waiting for transfers between devices: 98 us -> 57.8 us  [gather_hidden(): return lax.all_gather(shard, 'pairs', axis=1, tiled=True)]
    reshape x9 -> x1, local copies, waits for them, and re-layouts: 29.5 us -> 0.08 us  [on_device(): slot_images.reshape(-1)]
    reduce_scatter x1 -> x0, waiting for transfers between devices: 25.5 us -> none  [on_device(): lax.psum_scatter(total.reshape(img_local, TOKI, 2, 2 * PIXELS).astype(jnp...]
    ppermute x7 -> x8, waiting for transfers between devices: 63.6 us -> 40.9 us  [the longest x6 38.1 us: shifted(): lax.ppermute(array, 'pairs', [(i, (i + by) % count) for i in range(count)])]
    ppermute x7 -> x8, starting transfers between devices: 15.4 us -> 32 us  [the longest x6 27.2 us: shifted(): lax.ppermute(array, 'pairs', [(i, (i + by) % count) for i in range(count)])]
    convert_element_type x4 -> x2, other arithmetic: 14.7 us -> 0.11 us  [on_device(): (pieces[w].astype(F32) + passed.astype(F32)).astype(BF16)]
  transfers between devices with their start and end apart: 10 -> 9, of which waited for: 7 -> 9; matrix products, arithmetic and copies ran while one was open for 27% -> 2% of each run, Pallas kernels for 0% -> 17%
where the time goes in v1:
time: 201 us; the launch traced here: 200 us
  waiting for transfers between devices  98.7 us (49%)
  Pallas kernels  50.5 us (25%)
  starting transfers between devices  32 us (16%)
  between operations  14.2 us (7%)
  local copies, waits for them, and re-layouts  3.44 us (2%)
    all_gather x1, waiting for transfers between devices, gather_hidden(): return lax.all_gather(shard, 'pairs', axis=1, tiled=True)  57.8 us
    pallas_call x5, Pallas kernels, call(): pl.pallas_call(kernel, in_specs=[SMEM] * len(scalars) + [VMEM] * len(arra...  50.5 us
    ppermute x6, waiting for transfers between devices, shifted(): lax.ppermute(array, 'pairs', [(i, (i + by) % count) for i in range(count)])  38.1 us
    ppermute x6, starting transfers between devices, shifted(): lax.ppermute(array, 'pairs', [(i, (i + by) % count) for i in range(count)])  27.2 us
    ppermute x2, starting transfers between devices, other_core(): return lax.ppermute(array, 'side', [(0, 1), (1, 0)])  4.77 us
  transfers between devices with their start and end apart: 9, of which 9 were waited for; matrix products, arithmetic and copies ran while one was open for 2% of the time, Pallas kernels for 17%

profile of v1, /device:TPU:1, one launch (start us, length us, event | category | flops | bytes accessed | tf_op | source)
XLA Modules:
  0.0 200.5 jit_solution(2832639122291614677)
XLA Ops:
  6.5 1.4 pad_maximum_fusion
  8.0 11.1 %collective-permute-start = (bf16[1,196,384]{2,1,0:T(8,128)(2,1)}, bf16[1,196,384]{2,1,0:T(8,128)(2,1)S(1)}, u32[]{:S(2)}, u32[]{:S(2)}) collective-permute-start(bf16[1,196,384]{2,1,0:T(8,128)(2,1)} %param.17), channel_id=1, source_target_pairs={{0,254},{2,0},{4,2},{6,4},{8,6},{10,8},{12,10},{14,12},{16,14},{18... | collective-permute-start | bytes 451592 | tf_op jit(solution)/shard_map/ppermute | solution.py:24
  19.2 3.0 %collective-permute-done = bf16[1,196,384]{2,1,0:T(8,128)(2,1)S(1)} collective-permute-done((bf16[1,196,384]{2,1,0:T(8,128)(2,1)}, bf16[1,196,384]{2,1,0:T(8,128)(2,1)S(1)}, u32[]{:S(2)}, u32[]{:S(2)}) %collective-permute-start) | collective-permute-done | bytes 150560 | tf_op jit(solution)/shard_map/ppermute | solution.py:24
  22.1 7.5 %collective-permute-start.1 = (bf16[1,196,384]{2,1,0:T(8,128)(2,1)S(1)}, bf16[1,196,384]{2,1,0:T(8,128)(2,1)S(1)}, u32[]{:S(2)}, u32[]{:S(2)}) collective-permute-start(bf16[1,196,384]{2,1,0:T(8,128)(2,1)S(1)} %collective-permute-done), channel_id=1, source_target_pairs={{0,254},{2,0},{4,2},{6,4},{8,6},{10,8},{12,10},{14,12},{16,14},{18... | collective-permute-start | bytes 451592 | tf_op jit(solution)/shard_map/ppermute | solution.py:24
  29.6 0.9 constant_dynamic-update-slice_fusion.3
  30.6 1.2 collective-permute-done.1
  31.8 7.5 %collective-permute-start.2 = (bf16[1,196,384]{2,1,0:T(8,128)(2,1)S(1)}, bf16[1,196,384]{2,1,0:T(8,128)(2,1)S(1)}, u32[]{:S(2)}, u32[]{:S(2)}) collective-permute-start(bf16[1,196,384]{2,1,0:T(8,128)(2,1)S(1)} %collective-permute-done.1), channel_id=1, source_target_pairs={{0,254},{2,0},{4,2},{6,4},{8,6},{10,8},{12,10},{14,12},{16,14},{18... | collective-permute-start | bytes 451592 | tf_op jit(solution)/shard_map/ppermute | solution.py:24
  39.3 2.2 %collective-permute-done.2 = bf16[1,196,384]{2,1,0:T(8,128)(2,1)S(1)} collective-permute-done((bf16[1,196,384]{2,1,0:T(8,128)(2,1)S(1)}, bf16[1,196,384]{2,1,0:T(8,128)(2,1)S(1)}, u32[]{:S(2)}, u32[]{:S(2)}) %collective-permute-start.2) | collective-permute-done | bytes 150560 | tf_op jit(solution)/shard_map/ppermute | solution.py:24
  41.6 1.1 copy.21
  42.7 3.4 %collective-permute-start.3 = (bf16[4,196,384]{2,0,1:T(4,128)(2,1)}, bf16[4,196,384]{2,0,1:T(4,128)(2,1)}, u32[]{:S(2)}, u32[]{:S(2)}) collective-permute-start(bf16[4,196,384]{2,0,1:T(4,128)(2,1)} %copy.21), channel_id=1, source_target_pairs={{0,1},{1,0},{2,3},{3,2},{4,5},{5,4},{6,7},{7,6},{8,9},{9,8},{10,11... | collective-permute-start | bytes 1806344 | tf_op jit(solution)/shard_map/ppermute | solution.py:28
  46.4 1.7 collective-permute-done.3
  48.1 1.1 copy.23.theirs
  49.3 18.0 %self_part.1 = (f32[624,768]{1,0:T(8,128)}, bf16[624,768]{1,0:T(8,128)(2,1)S(1)}) custom-call(s32[128]{0:T(128)S(1)} %copy-done, s32[6]{0:T(128)S(1)} %reshape.4.slot_images, s32[2]{0:T(128)S(1)} %pad_add_fusion.place, bf16[4,196,384]{2,1,0:T(8,128)(2,1)S(1)} %constant_dynamic-update-slice_fusion.mine, bf16[4,196,384]{2,1,0:T(8,128)(2,1)S(1)} %copy.23.theirs, ...), custom_call_target="tpu_custom_call" | custom-call | flops 6000000000 | bytes 8388608 | tf_op jit(solution)/shard_map/self_part/pallas_call | solution.py:235
  67.4 15.5 %cross_part.1 = (f32[624,768]{1,0:T(8,128)}, bf16[624,768]{1,0:T(8,128)(2,1)S(1)}) custom-call(s32[128]{0:T(128)S(1)} %copy-done, s32[6]{0:T(128)S(1)} %reshape.4.slot_images, s32[2]{0:T(128)S(1)} %pad_add_fusion.place, bf16[4,196,384]{2,1,0:T(8,128)(2,1)S(1)} %constant_dynamic-update-slice_fusion.mine, bf16[4,196,384]{2,1,0:T(8,128)(2,1)S(1)} %copy.23.theirs, ...), custom_call_target="tpu_custom_call" | custom-call | flops 5000000000 | bytes 8388608 | tf_op jit(solution)/shard_map/cross_part/pallas_call | solution.py:235
  82.9 57.8 %all-gather.2.cloned.1.call-done.fc = bf16[2,3072,768]{2,1,0:T(8,128)(2,1)} async-done(((bf16[2,24,768]{2,1,0:T(8,128)(2,1)}), bf16[2,3072,768]{2,1,0:T(8,128)(2,1)}) %all-gather.2.cloned.1.call-update) | async-done | bytes 9437200 | tf_op jit(solution)/shard_map/all_gather | solution.py:286
  140.7 14.9 %mlp_part.1 = (f32[3,196,512]{2,1,0:T(8,128)S(1)}, bf16[3,196,512]{2,1,0:T(8,128)(2,1)S(1)}) custom-call(s32[2]{0:T(128)S(1)} %pad_add_fusion.place, f32[624,768]{1,0:T(8,128)} %get-tuple-element.17.second, bf16[624,768]{1,0:T(8,128)(2,1)S(1)} %get-tuple-element.18.mlp_in, bf16[2,3072,768]{2,1,0:T(8,128)(2,1)} %all-gather.2.cloned.1.call-done.fc, ...), custom_call_target="tpu_custom_call" | custom-call | flops 7000000000 | bytes 8388608 | tf_op jit(solution)/shard_map/mlp_part/pallas_call | solution.py:235
  155.6 1.3 collective-permute-start.4
  157.6 1.0 collective-permute-done.4.got
  158.6 1.4 window_part.1
  160.0 0.9 collective-permute-start.5
  160.9 10.9 %collective-permute-done.5 = bf16[196,512]{1,0:T(8,128)(2,1)S(1)} collective-permute-done((bf16[196,512]{1,0:T(8,128)(2,1)S(1)}, bf16[196,512]{1,0:T(8,128)(2,1)S(1)}, u32[]{:S(2)}, u32[]{:S(2)}) %collective-permute-start.5) | collective-permute-done | bytes 200736 | tf_op jit(solution)/shard_map/ppermute | solution.py:24
  171.9 10.8 %collective-permute-done.6 = bf16[196,512]{1,0:T(8,128)(2,1)S(1)} collective-permute-done((bf16[196,512]{1,0:T(8,128)(2,1)S(1)}, bf16[196,512]{1,0:T(8,128)(2,1)S(1)}, u32[]{:S(2)}, u32[]{:S(2)}) %collective-permute-start.6) | collective-permute-done | bytes 200736 | tf_op jit(solution)/shard_map/ppermute | solution.py:24
  182.9 10.0 %collective-permute-done.7.passed = bf16[196,512]{1,0:T(8,128)(2,1)S(1)} collective-permute-done((bf16[196,512]{1,0:T(8,128)(2,1)S(1)}, bf16[196,512]{1,0:T(8,128)(2,1)S(1)}, u32[]{:S(2)}, u32[]{:S(2)}) %collective-permute-start.7) | collective-permute-done | bytes 200736 | tf_op jit(solution)/shard_map/ppermute | solution.py:24
  192.9 0.7 merge_part.1
  (34 shorter events, 0.7 us)
Async XLA Ops:
  6.5 39.6 %copy-start.10 = (s32[3,2]{0,1:T(2,128)S(1)}, s32[3,2]{0,1:T(2,128)}, u32[]{:S(2)}) copy-start(s32[3,2]{0,1:T(2,128)} %param.19) | copy-start | bytes 76
  6.5 134.2 %all-gather.2.cloned.1.call-start = ((), (), s32[]{:S(2)}) async-start(), calls=%async_computation | async-start | bytes 9510912 | tf_op jit(solution)/shard_map/all_gather | solution.py:286
  8.0 41.3 %copy-start = (s32[128]{0:T(128)S(1)}, s32[128]{0:T(128)}, u32[]{:S(2)}) copy-start(s32[128]{0:T(128)} %image_slot.5) | copy-start | bytes 1540
  8.0 41.3 %copy-start.2 = (bf16[1,768,768]{2,1,0:T(8,128)(2,1)S(1)}, bf16[1,768,768]{2,1,0:T(8,128)(2,1)}, u32[]{:S(2)}) copy-start(bf16[1,768,768]{2,1,0:T(8,128)(2,1)} %param.27) | copy-start | bytes 3538948
  8.0 41.3 %copy-start.3 = (bf16[1,768,768]{2,1,0:T(8,128)(2,1)S(1)}, bf16[1,768,768]{2,1,0:T(8,128)(2,1)}, u32[]{:S(2)}) copy-start(bf16[1,768,768]{2,1,0:T(8,128)(2,1)} %param.28) | copy-start | bytes 3538948
  8.0 41.3 %copy-start.5 = (f32[1,768]{1,0:T(1,128)S(1)}, f32[1,768]{1,0:T(1,128)}, u32[]{:S(2)}) copy-start(f32[1,768]{1,0:T(1,128)} %g_self.1) | copy-start | bytes 9220
  8.0 41.3 %copy-start.6 = (f32[1,768]{1,0:T(1,128)S(1)}, f32[1,768]{1,0:T(1,128)}, u32[]{:S(2)}) copy-start(f32[1,768]{1,0:T(1,128)} %g_query.1) | copy-start | bytes 9220
  8.0 14.1 %collective-permute-start = (bf16[1,196,384]{2,1,0:T(8,128)(2,1)}, bf16[1,196,384]{2,1,0:T(8,128)(2,1)S(1)}, u32[]{:S(2)}, u32[]{:S(2)}) collective-permute-start(bf16[1,196,384]{2,1,0:T(8,128)(2,1)} %param.17), channel_id=1, source_target_pairs={{0,254},{2,0},{4,2},{6,4},{8,6},{10,8},{12,10},{14,12},{16,14},{18... | collective-permute-start | bytes 451592 | tf_op jit(solution)/shard_map/ppermute | solution.py:24
  22.1 9.7 %collective-permute-start.1 = (bf16[1,196,384]{2,1,0:T(8,128)(2,1)S(1)}, bf16[1,196,384]{2,1,0:T(8,128)(2,1)S(1)}, u32[]{:S(2)}, u32[]{:S(2)}) collective-permute-start(bf16[1,196,384]{2,1,0:T(8,128)(2,1)S(1)} %collective-permute-done), channel_id=1, source_target_pairs={{0,254},{2,0},{4,2},{6,4},{8,6},{10,8},{12,10},{14,12},{16,14},{18... | collective-permute-start | bytes 451592 | tf_op jit(solution)/shard_map/ppermute | solution.py:24
  31.8 9.8 %collective-permute-start.2 = (bf16[1,196,384]{2,1,0:T(8,128)(2,1)S(1)}, bf16[1,196,384]{2,1,0:T(8,128)(2,1)S(1)}, u32[]{:S(2)}, u32[]{:S(2)}) collective-permute-start(bf16[1,196,384]{2,1,0:T(8,128)(2,1)S(1)} %collective-permute-done.1), channel_id=1, source_target_pairs={{0,254},{2,0},{4,2},{6,4},{8,6},{10,8},{12,10},{14,12},{16,14},{18... | collective-permute-start | bytes 451592 | tf_op jit(solution)/shard_map/ppermute | solution.py:24
  42.7 5.4 %collective-permute-start.3 = (bf16[4,196,384]{2,0,1:T(4,128)(2,1)}, bf16[4,196,384]{2,0,1:T(4,128)(2,1)}, u32[]{:S(2)}, u32[]{:S(2)}) collective-permute-start(bf16[4,196,384]{2,0,1:T(4,128)(2,1)} %copy.21), channel_id=1, source_target_pairs={{0,1},{1,0},{2,3},{3,2},{4,5},{5,4},{6,7},{7,6},{8,9},{9,8},{10,11... | collective-permute-start | bytes 1806344 | tf_op jit(solution)/shard_map/ppermute | solution.py:28
  49.3 18.1 %copy-start.4 = (bf16[1,768,768]{2,1,0:T(8,128)(2,1)S(1)}, bf16[1,768,768]{2,1,0:T(8,128)(2,1)}, u32[]{:S(2)}) copy-start(bf16[1,768,768]{2,1,0:T(8,128)(2,1)} %param.30) | copy-start | bytes 3538948
  49.3 18.0 %copy-start.7 = (f32[1,768]{1,0:T(1,128)S(1)}, f32[1,768]{1,0:T(1,128)}, u32[]{:S(2)}) copy-start(f32[1,768]{1,0:T(1,128)} %g_memory.1) | copy-start | bytes 9220
  49.3 18.0 %copy-start.8 = (f32[1,768]{1,0:T(1,128)S(1)}, f32[1,768]{1,0:T(1,128)}, u32[]{:S(2)}) copy-start(f32[1,768]{1,0:T(1,128)} %g_mlp.1) | copy-start | bytes 9220
  67.4 73.4 %copy-start.1 = (bf16[1,768,1024]{2,1,0:T(8,128)(2,1)S(1)}, bf16[1,768,1024]{2,1,0:T(8,128)(2,1)}, u32[]{:S(2)}) copy-start(bf16[1,768,1024]{2,1,0:T(8,128)(2,1)} %param.33) | copy-start | bytes 4718596
  67.4 73.3 %copy-start.9 = (f32[1,768]{1,0:T(1,128)S(1)}, f32[1,768]{1,0:T(1,128)}, u32[]{:S(2)}) copy-start(f32[1,768]{1,0:T(1,128)} %g_head.1) | copy-start | bytes 9220
  155.6 3.0 %collective-permute-start.4 = (bf16[3,196,512]{2,1,0:T(8,128)(2,1)S(1)}, bf16[3,196,512]{2,1,0:T(8,128)(2,1)S(1)}, u32[]{:S(2)}, u32[]{:S(2)}) collective-permute-start(bf16[3,196,512]{2,1,0:T(8,128)(2,1)S(1)} %get-tuple-element.20), channel_id=1, source_target_pairs={{0,1},{1,0},{2,3},{3,2},{4,5},{5,4},{6,7},{7,6},{8,9},{9,8},{10,11... | collective-permute-start | bytes 1806344 | tf_op jit(solution)/shard_map/ppermute | solution.py:28
  160.0 11.8 %collective-permute-start.5 = (bf16[196,512]{1,0:T(8,128)(2,1)S(1)}, bf16[196,512]{1,0:T(8,128)(2,1)S(1)}, u32[]{:S(2)}, u32[]{:S(2)}) collective-permute-start(bf16[196,512]{1,0:T(8,128)(2,1)S(1)} %get-tuple-element.24), channel_id=1, source_target_pairs={{0,2},{2,4},{4,6},{6,8},{8,10},{10,12},{12,14},{14,16},{16,18},{18... | collective-permute-start | bytes 602120 | tf_op jit(solution)/shard_map/ppermute | solution.py:24
  171.8 10.9 %collective-permute-start.6 = (bf16[196,512]{1,0:T(8,128)(2,1)S(1)}, bf16[196,512]{1,0:T(8,128)(2,1)S(1)}, u32[]{:S(2)}, u32[]{:S(2)}) collective-permute-start(bf16[196,512]{1,0:T(8,128)(2,1)S(1)} %add_convert_fusion.1), channel_id=1, source_target_pairs={{0,2},{2,4},{4,6},{6,8},{8,10},{10,12},{12,14},{14,16},{16,18},{18... | collective-permute-start | bytes 602120 | tf_op jit(solution)/shard_map/ppermute | solution.py:24
  182.8 10.1 %collective-permute-start.7 = (bf16[196,512]{1,0:T(8,128)(2,1)S(1)}, bf16[196,512]{1,0:T(8,128)(2,1)S(1)}, u32[]{:S(2)}, u32[]{:S(2)}) collective-permute-start(bf16[196,512]{1,0:T(8,128)(2,1)S(1)} %add_convert_fusion), channel_id=1, source_target_pairs={{0,2},{2,4},{4,6},{6,8},{8,10},{10,12},{12,14},{14,16},{16,18},{18... | collective-permute-start | bytes 602120 | tf_op jit(solution)/shard_map/ppermute | solution.py:24
Sparse Core Ops, SparseCore 0:
  11.1 129.5 all-gather.1

commit v2 on v1

--- a/solution.py
+++ b/solution.py
@@ -13,8 +13,7 @@
 WINDOW = 4
 SLOTS = 3
 ALL = SLOTS * ROWS
-FF = 3072
-CHUNK = 512
+CHUNK = 256
 F32 = jnp.float32
 BF16 = jnp.bfloat16
 
@@ -107,21 +106,35 @@
     lax.fori_loop(0, width // 256, step, 0)
 
 
-def self_kernel(
-    image_slot, slot_images, place, mine, theirs, g_self, g_query, w_qkv, w_out, w_query,
-    first_ref, query_ref, hidden, triple, mixed,
+def triple_kernel(
+    image_slot, slot_images, place, mine, theirs, g_self, w_qkv, rows_ref, triple_ref, hidden
 ):
-    padded_rows(image_slot, slot_images, place, mine, theirs, False, first_ref)
-    norm_into(first_ref, g_self, hidden)
+    padded_rows(image_slot, slot_images, place, mine, theirs, False, rows_ref)
+    norm_into(rows_ref, g_self, hidden)
 
     def write_triple(n, cols, value):
-        triple[:, cols] = (value * jnp.where(n < 3, 0.125, 1.0)).astype(BF16)
+        triple_ref[:, cols] = (value * jnp.where(n < 3, 0.125, 1.0)).astype(BF16)
 
     project(hidden, w_qkv, 3 * D, write_triple)
+
+
+def memory_kernel(
+    image_slot, slot_images, place, mine, theirs, g_memory, w_memory, kv_ref, rows, hidden
+):
+    padded_rows(image_slot, slot_images, place, mine, theirs, True, rows)
+    norm_into(rows, g_memory, hidden)
+
+    def write_kv(n, cols, value):
+        kv_ref[:, cols] = value.astype(BF16)
+
+    project(hidden, w_memory, 2 * D, write_kv)
+
+
+def self_kernel(rows, triple, g_query, w_out, w_query, first_ref, query_ref, hidden, mixed):
     attention(triple, 0, triple, D, triple, 2 * D, mixed)
 
     def add_first(n, cols, value):
-        first_ref[:, cols] = first_ref[:, cols] + value
+        first_ref[:, cols] = rows[:, cols] + value
 
     project(mixed, w_out, D, add_first)
     norm_into(first_ref, g_query, hidden)
@@ -132,17 +145,7 @@
     project(hidden, w_query, D, write_query)
 
 
-def cross_kernel(
-    image_slot, slot_images, place, mine, theirs, first, query, g_memory, g_mlp, w_memory, w_out,
-    second_ref, mlp_ref, rows_ref, hidden, key_value, mixed,
-):
-    padded_rows(image_slot, slot_images, place, mine, theirs, True, rows_ref)
-    norm_into(rows_ref, g_memory, hidden)
-
-    def write_kv(n, cols, value):
-        key_value[:, cols] = value.astype(BF16)
-
-    project(hidden, w_memory, 2 * D, write_kv)
+def cross_kernel(first, query, key_value, g_mlp, w_out, second_ref, mlp_ref, mixed):
     attention(query, 0, key_value, 0, key_value, D, mixed)
 
     def add_second(n, cols, value):
@@ -156,10 +159,8 @@
     return value * (1.0 + lax.erf(value * 0.7071067811865476)) * 0.5
 
 
-def mlp_kernel(
-    place, second, mlp_in, fc, g_head, w_head, keep_ref, send_ref, pre, total, hidden,
-):
-    steps = FF // CHUNK
+def hidden_units(mlp_in, fc, pre, total):
+    steps = fc.shape[1] // CHUNK
 
     def before(c):
         rows = pl.ds(pl.multiple_of(c * CHUNK, CHUNK), CHUNK)
@@ -167,18 +168,31 @@
             mlp_in[...], fc[0, rows, :], (((1,), (1,)), ((), ())), preferred_element_type=F32
         )
 
+    def after(c, active):
+        rows = pl.ds(pl.multiple_of(c * CHUNK, CHUNK), CHUNK)
+        total[...] = total[...] + jnp.dot(active, fc[1, rows, :], preferred_element_type=F32)
+
     pre[0] = before(0)
-    total[...] = second[...]
 
     def step(c, carry):
         now = lax.rem(c, 2)
         active = gelu(pre[now]).astype(BF16)
-        pre[1 - now] = before(jnp.minimum(c + 1, steps - 1))
-        rows = pl.ds(pl.multiple_of(c * CHUNK, CHUNK), CHUNK)
-        total[...] = total[...] + jnp.dot(active, fc[1, rows, :], preferred_element_type=F32)
+        pre[1 - now] = before(c + 1)
+        after(c, active)
         return carry
 
-    lax.fori_loop(0, steps, step, 0)
+    lax.fori_loop(0, steps - 1, step, 0)
+    after(steps - 1, gelu(pre[(steps - 1) % 2]).astype(BF16))
+
+
+def early_kernel(second, mlp_in, fc, total, pre):
+    total[...] = second[...]
+    hidden_units(mlp_in, fc, pre, total)
+
+
+def late_kernel(place, early, mlp_in, fc, g_head, w_head, keep_ref, send_ref, pre, total, hidden):
+    total[...] = early[...]
+    hidden_units(mlp_in, fc, pre, total)
     norm_into(total, g_head, hidden)
     first = place[1] == 0
     for slot in range(SLOTS):
@@ -244,30 +258,51 @@
     )(*scalars, *arrays)
 
 
-def self_call(scalars, mine, theirs, g_self, g_query, w_qkv, w_out, w_query):
-    return call(
-        self_kernel, scalars, [mine, theirs, g_self, g_query, w_qkv, w_out, w_query],
-        [((ALL, D), F32), ((ALL, D), BF16)],
-        [((ALL, D), BF16), ((ALL, 3 * D), BF16), ((ALL, D), BF16)],
-        6 * 10**9, "self_part",
-    )
-
-
-def cross_call(scalars, mine, theirs, first, query, g_memory, g_mlp, w_memory, w_out):
-    return call(
-        cross_kernel, scalars, [mine, theirs, first, query, g_memory, g_mlp, w_memory, w_out],
-        [((ALL, D), F32), ((ALL, D), BF16)],
-        [((ALL, D), F32), ((ALL, D), BF16), ((ALL, 2 * D), BF16), ((ALL, D), BF16)],
-        5 * 10**9, "cross_part",
-    )
-
-
-def mlp_call(place, second, mlp_in, fc, g_head, w_head):
-    return call(
-        mlp_kernel, [place], [second, mlp_in, fc, g_head, w_head],
+def triple_call(scalars, mine, theirs, g_self, w_qkv):
+    return call(
+        triple_kernel, scalars, [mine, theirs, g_self, w_qkv],
+        [((ALL, D), F32), ((ALL, 3 * D), BF16)], [((ALL, D), BF16)],
+        4 * 10**9, "triple_part",
+    )
+
+
+def memory_call(scalars, mine, theirs, g_memory, w_memory):
+    return call(
+        memory_kernel, scalars, [mine, theirs, g_memory, w_memory],
+        [((ALL, 2 * D), BF16)], [((ALL, D), F32), ((ALL, D), BF16)],
+        3 * 10**9, "memory_part",
+    )[0]
+
+
+def self_call(rows, triple, g_query, w_out, w_query):
+    return call(
+        self_kernel, [], [rows, triple, g_query, w_out, w_query],
+        [((ALL, D), F32), ((ALL, D), BF16)], [((ALL, D), BF16), ((ALL, D), BF16)],
+        12 * 10**9, "self_part",
+    )
+
+
+def cross_call(first, query, key_value, g_mlp, w_out):
+    return call(
+        cross_kernel, [], [first, query, key_value, g_mlp, w_out],
+        [((ALL, D), F32), ((ALL, D), BF16)], [((ALL, D), BF16)],
+        12 * 10**9, "cross_part",
+    )
+
+
+def early_call(second, mlp_in, fc):
+    return call(
+        early_kernel, [], [second, mlp_in, fc],
+        [((ALL, D), F32)], [((2, ALL, CHUNK), F32)], 10 * 10**9, "early_part",
+    )[0]
+
+
+def late_call(place, early, mlp_in, fc, g_head, w_head):
+    return call(
+        late_kernel, [place], [early, mlp_in, fc, g_head, w_head],
         [((SLOTS, TOKI, 512), F32), ((SLOTS, TOKI, 512), BF16)],
         [((2, ALL, CHUNK), F32), ((ALL, D), F32), ((ALL, D), BF16)],
-        7 * 10**9, "mlp_part",
+        5 * 10**9, "late_part",
     )
 
 
@@ -282,8 +317,36 @@
     return call(merge_kernel, [], [base, passed], [((1, TOKI, HALF), BF16)], [], 10**8, "merge_part")[0]
 
 
-def gather_hidden(shard):
-    return lax.all_gather(shard, "pairs", axis=1, tiled=True)
+def along(array, axis, by):
+    count = lax.axis_size("pairs")
+    stride, size = {"y": (32, 4), "x": (8, 4), "z": (1, 8)}[axis]
+
+    def target(p):
+        here = p // stride % size
+        return p + ((here + by) % size - here) * stride
+
+    return lax.ppermute(array, "pairs", [(p, target(p)) for p in range(count)])
+
+
+def tied(*arrays):
+    return lax.optimization_barrier(arrays)
+
+
+def gather_line(shard):
+    up, down = along(shard, "z", 1), along(shard, "z", -1)
+    near = jnp.concatenate([up, shard, down], axis=1)
+    far = along(near, "z", 3)
+    other = along(near[:, : 2 * shard.shape[1]], "z", -3)
+    return jnp.concatenate([near, far, other], axis=1)
+
+
+def first_hop(block, axis):
+    return along(block, axis, 1), along(block, axis, -1)
+
+
+def second_hop(left, right, axis):
+    half = left.shape[1] // 2
+    return along(left[:, :half], axis, 1), along(right[:, half:], axis, -1)
 
 
 def on_device(
@@ -306,20 +369,33 @@
     w_head,
 ):
     place = jnp.stack([lax.axis_index("pairs"), lax.axis_index("side")]).astype(jnp.int32)
-    fc = gather_hidden(jnp.concatenate([w_fc1, w_fc2], axis=0))
+    shard = jnp.concatenate([w_fc1, w_fc2], axis=0)
     blocks = [features]
     for _ in range(1, WINDOW):
         blocks.append(shifted(blocks[-1], -1))
     mine = jnp.concatenate(blocks, axis=0)
     theirs = other_core(mine)
+    line = gather_line(shard)
+    half = line.shape[1] // 2
+    part_x, part_y = line[:, :half], line[:, half:]
     scalars = [image_slot, slot_images.reshape(-1), place]
-    first, query = self_call(
-        scalars, mine, theirs, gain_self, gain_query, w_qkv[0], w_self_out[0], w_query[0]
-    )
-    second, mlp_in = cross_call(
-        scalars, mine, theirs, first, query, gain_memory, gain_mlp, w_memory[0], w_cross_out[0]
-    )
-    keep, send = mlp_call(place, second, mlp_in, fc, gain_head, w_head[0])
+    near_x, near_y = first_hop(part_x, "x"), first_hop(part_y, "y")
+    rows, triple = triple_call(scalars, mine, theirs, gain_self, w_qkv[0])
+    near_x, near_y, rows, triple, mine, theirs = tied(near_x, near_y, rows, triple, mine, theirs)
+    far_x, far_y = second_hop(*near_x, "x"), second_hop(*near_y, "y")
+    key_value = memory_call(scalars, mine, theirs, gain_memory, w_memory[0])
+    far_x, far_y, key_value, rows, triple = tied(far_x, far_y, key_value, rows, triple)
+    plane_x = jnp.concatenate([part_x, *near_x, *far_x], axis=1)
+    plane_y = jnp.concatenate([part_y, *near_y, *far_y], axis=1)
+    near_x, near_y = first_hop(plane_x, "y"), first_hop(plane_y, "x")
+    first, query = self_call(rows, triple, gain_query, w_self_out[0], w_query[0])
+    second, mlp_in = cross_call(first, query, key_value, gain_mlp, w_cross_out[0])
+    near_x, near_y, second, mlp_in = tied(near_x, near_y, second, mlp_in)
+    far_x, far_y = second_hop(*near_x, "y"), second_hop(*near_y, "x")
+    fc_early = jnp.concatenate([plane_x, *near_x, plane_y, *near_y], axis=1)
+    early = early_call(second, mlp_in, fc_early)
+    fc_late = jnp.concatenate([*far_x, *far_y], axis=1)
+    keep, send = late_call(place, early, mlp_in, fc_late, gain_head, w_head[0])
     got = other_core(send)
     pieces = window_call([image_slot, slot_images.reshape(-1), slot_count, place], keep, got)
     passed = shifted(pieces[3], 1)

time: 201 us -> 195 us (0.970)
  waiting for transfers between devices: 98.7 us -> 52.5 us
  starting transfers between devices: 32 us -> 62.8 us
  local copies, waits for them, and re-layouts: 3.44 us -> 22.7 us
  between operations: 14.2 us -> 1.14 us
  Pallas kernels: 50.5 us -> 52.6 us
    all_gather x1 -> x0, waiting for transfers between devices: 57.8 us -> none  [gather_hidden(): return lax.all_gather(shard, 'pairs', axis=1, tiled=True)]
    ppermute x0 -> x20, starting transfers between devices: none -> 29.7 us  [along(): return lax.ppermute(array, 'pairs', [(p, target(p)) for p in range(count)])]
    unnamed x26 -> x54, local copies, waits for them, and re-layouts: 1.13 us -> 19.5 us
    ppermute x0 -> x20, waiting for transfers between devices: none -> 14.6 us  [along(): return lax.ppermute(array, 'pairs', [(p, target(p)) for p in range(count)])]
    ppermute x2, starting transfers between devices: 4.77 us -> 9.16 us  [other_core(): return lax.ppermute(array, 'side', [(0, 1), (1, 0)])]
    ppermute x6, starting transfers between devices: 27.2 us -> 23.9 us  [shifted(): lax.ppermute(array, 'pairs', [(i, (i + by) % count) for i in range(count)])]
    concatenate x0 -> x3, local copies, waits for them, and re-layouts: none -> 2.52 us  [the longest x1 1.09 us: on_device(): fc_early = jnp.concatenate([plane_x, *near_x, plane_y, *near_y], axis=1)]
    pallas_call x5 -> x8, Pallas kernels: 50.5 us -> 52.6 us  [call(): pl.pallas_call(kernel, in_specs=[SMEM] * len(scalars) + [VMEM] * len(arra...]
  transfers between devices with their start and end apart: 9 -> 28, of which waited for: 9 -> 8; matrix products, arithmetic and copies ran while one was open for 2% -> 9% of each run, Pallas kernels for 17% -> 23%
where the time goes in v2:
time: 195 us; the launch traced here: 194 us
  starting transfers between devices  62.8 us (32%)
  Pallas kernels  52.6 us (27%)
  waiting for transfers between devices  52.5 us (27%)
  local copies, waits for them, and re-layouts  22.7 us (12%)
  other arithmetic  2.69 us (1%)
    pallas_call x8, Pallas kernels, call(): pl.pallas_call(kernel, in_specs=[SMEM] * len(scalars) + [VMEM] * len(arra...  52.6 us
    ppermute x6, waiting for transfers between devices, shifted(): lax.ppermute(array, 'pairs', [(i, (i + by) % count) for i in range(count)])  36.8 us
    ppermute x20, starting transfers between devices, along(): return lax.ppermute(array, 'pairs', [(p, target(p)) for p in range(count)])  29.7 us
    ppermute x6, starting transfers between devices, shifted(): lax.ppermute(array, 'pairs', [(i, (i + by) % count) for i in range(count)])  23.9 us
    unnamed x54, local copies, waits for them, and re-layouts  19.5 us
    ppermute x20, waiting for transfers between devices, along(): return lax.ppermute(array, 'pairs', [(p, target(p)) for p in range(count)])  14.6 us
    ppermute x2, starting transfers between devices, other_core(): return lax.ppermute(array, 'side', [(0, 1), (1, 0)])  9.16 us
  transfers between devices with their start and end apart: 28, of which 8 were waited for; matrix products, arithmetic and copies ran while one was open for 9% of the time, Pallas kernels for 23%

profile of v2, /device:TPU:1, one launch (start us, length us, event | category | flops | bytes accessed | tf_op | source)
XLA Modules:
  0.0 194.4 jit_solution(3861414972801048931)
XLA Ops:
  0.0 11.1 %collective-permute-start.8 = (bf16[1,196,384]{2,1,0:T(8,128)(2,1)}, bf16[1,196,384]{2,1,0:T(8,128)(2,1)S(1)}, u32[]{:S(2)}, u32[]{:S(2)}) collective-permute-start(bf16[1,196,384]{2,1,0:T(8,128)(2,1)} %param.17), channel_id=1, source_target_pairs={{0,254},{2,0},{4,2},{6,4},{8,6},{10,8},{12,10},{14,12},{16,14},{18... | collective-permute-start | bytes 451592 | tf_op jit(solution)/shard_map/ppermute | solution.py:23
  14.0 7.5 %collective-permute-start.9 = (bf16[1,196,384]{2,1,0:T(8,128)(2,1)S(1)}, bf16[1,196,384]{2,1,0:T(8,128)(2,1)S(1)}, u32[]{:S(2)}, u32[]{:S(2)}) collective-permute-start(bf16[1,196,384]{2,1,0:T(8,128)(2,1)S(1)} %collective-permute-done.8), channel_id=1, source_target_pairs={{0,254},{2,0},{4,2},{6,4},{8,6},{10,8},{12,10},{14,12},{16,14},{18... | collective-permute-start | bytes 451592 | tf_op jit(solution)/shard_map/ppermute | solution.py:23
  22.3 2.7 %collective-permute-start.1 = (bf16[2,24,768]{2,1,0:T(8,128)(2,1)S(1)}, bf16[2,24,768]{2,1,0:T(8,128)(2,1)S(1)}, u32[]{:S(2)}, u32[]{:S(2)}) collective-permute-start(bf16[2,24,768]{2,1,0:T(8,128)(2,1)S(1)} %constant_dynamic-update-slice_fusion), channel_id=1, source_target_pairs={{0,14},{2,0},{4,2},{6,4},{8,6},{10,8},{12,10},{14,12},{16,30},{18,... | collective-permute-start | bytes 221192 | tf_op jit(solution)/shard_map/ppermute | solution.py:328
  25.9 5.1 %collective-permute-start.10 = (bf16[1,196,384]{2,1,0:T(8,128)(2,1)S(1)}, bf16[1,196,384]{2,1,0:T(8,128)(2,1)S(1)}, u32[]{:S(2)}, u32[]{:S(2)}) collective-permute-start(bf16[1,196,384]{2,1,0:T(8,128)(2,1)S(1)} %collective-permute-done.9), channel_id=1, source_target_pairs={{0,254},{2,0},{4,2},{6,4},{8,6},{10,8},{12,10},{14,12},{16,14},{18... | collective-permute-start | bytes 451592 | tf_op jit(solution)/shard_map/ppermute | solution.py:23
  33.5 3.8 %collective-permute-start.11 = (bf16[4,196,384]{2,0,1:T(4,128)(2,1)S(1)}, bf16[4,196,384]{2,0,1:T(4,128)(2,1)S(1)}, u32[]{:S(2)}, u32[]{:S(2)}) collective-permute-start(bf16[4,196,384]{2,0,1:T(4,128)(2,1)S(1)} %copy.21), channel_id=1, source_target_pairs={{0,1},{1,0},{2,3},{3,2},{4,5},{5,4},{6,7},{7,6},{8,9},{9,8},{10,11... | collective-permute-start | bytes 1806344 | tf_op jit(solution)/shard_map/ppermute | solution.py:27
  37.4 4.5 %collective-permute-start.5 = (bf16[2,48,768]{2,1,0:T(8,128)(2,1)S(1)}, bf16[2,48,768]{2,1,0:T(8,128)(2,1)S(1)}, u32[]{:S(2)}, u32[]{:S(2)}) collective-permute-start(bf16[2,48,768]{2,1,0:T(8,128)(2,1)S(1)} %pad_maximum_fusion.6), channel_id=1, source_target_pairs={{0,10},{2,12},{4,14},{6,0},{8,2},{10,4},{12,6},{14,8},{16,26},{18,... | collective-permute-start | bytes 442376 | tf_op jit(solution)/shard_map/ppermute | solution.py:328
  42.2 8.9 %collective-permute-done.5 = bf16[2,48,768]{2,1,0:T(8,128)(2,1)S(1)} collective-permute-done((bf16[2,48,768]{2,1,0:T(8,128)(2,1)S(1)}, bf16[2,48,768]{2,1,0:T(8,128)(2,1)S(1)}, u32[]{:S(2)}, u32[]{:S(2)}) %collective-permute-start.5) | collective-permute-done | bytes 147488 | tf_op jit(solution)/shard_map/ppermute | solution.py:328
  51.1 5.7 %collective-permute-done.2 = bf16[2,72,768]{2,1,0:T(8,128)(2,1)S(1)} collective-permute-done((bf16[2,72,768]{2,1,0:T(8,128)(2,1)S(1)}, bf16[2,72,768]{2,1,0:T(8,128)(2,1)S(1)}, u32[]{:S(2)}, u32[]{:S(2)}) %collective-permute-start.2) | collective-permute-done | bytes 221216 | tf_op jit(solution)/shard_map/ppermute | solution.py:328
  57.7 2.7 %collective-permute-start.4 = (bf16[2,96,768]{2,1,0:T(8,128)(2,1)S(1)}, bf16[2,96,768]{2,1,0:T(8,128)(2,1)S(1)}, u32[]{:S(2)}, u32[]{:S(2)}) collective-permute-start(bf16[2,96,768]{2,1,0:T(8,128)(2,1)S(1)} %get-tuple-element.80), channel_id=1, source_target_pairs={{0,48},{2,50},{4,52},{6,54},{8,56},{10,58},{12,60},{14,62},{16,0},... | collective-permute-start | bytes 884744 | tf_op jit(solution)/shard_map/ppermute | solution.py:328
  60.4 2.7 %collective-permute-start.7 = (bf16[2,96,768]{2,1,0:T(8,128)(2,1)S(1)}, bf16[2,96,768]{2,1,0:T(8,128)(2,1)S(1)}, u32[]{:S(2)}, u32[]{:S(2)}) collective-permute-start(bf16[2,96,768]{2,1,0:T(8,128)(2,1)S(1)} %get-tuple-element.74), channel_id=1, source_target_pairs={{0,192},{2,194},{4,196},{6,198},{8,200},{10,202},{12,204},{14,206}... | collective-permute-start | bytes 884744 | tf_op jit(solution)/shard_map/ppermute | solution.py:328
  63.9 6.5 %triple_part.1 = (f32[624,768]{1,0:T(8,128)S(1)}, bf16[624,2304]{1,0:T(8,128)(2,1)S(1)}) custom-call(s32[128]{0:T(128)S(1)} %copy-done, s32[6]{0:T(128)S(1)} %reshape.4.slot_images, s32[2]{0:T(128)S(1)} %pad_add_fusion.place, bf16[4,196,384]{2,1,0:T(8,128)(2,1)S(1)} %constant_dynamic-update-slice_fusion.2.mine, bf16[4,196,384]{2,1,0:T(8,128)(2,1)S(1)} %copy.22.theirs, ...), custom_call_target="tpu_custom_call" | custom-call | flops 4000000000 | bytes 8388608 | tf_op jit(solution)/shard_map/triple_part/pallas_call | solution.py:249
  73.6 2.9 %collective-permute-start.13 = (bf16[2,48,768]{2,1,0:T(8,128)(2,1)S(1)}, bf16[2,48,768]{2,1,0:T(8,128)(2,1)S(1)}, u32[]{:S(2)}, u32[]{:S(2)}) collective-permute-start(bf16[2,48,768]{2,1,0:T(8,128)(2,1)S(1)} %slice.37), channel_id=1, source_target_pairs={{0,48},{2,50},{4,52},{6,54},{8,56},{10,58},{12,60},{14,62},{16,0},... | collective-permute-start | bytes 442376 | tf_op jit(solution)/shard_map/ppermute | solution.py:328
  76.6 2.7 %collective-permute-start.15 = (bf16[2,48,768]{2,1,0:T(8,128)(2,1)S(1)}, bf16[2,48,768]{2,1,0:T(8,128)(2,1)S(1)}, u32[]{:S(2)}, u32[]{:S(2)}) collective-permute-start(bf16[2,48,768]{2,1,0:T(8,128)(2,1)S(1)} %slice.39), channel_id=1, source_target_pairs={{0,192},{2,194},{4,196},{6,198},{8,200},{10,202},{12,204},{14,206}... | collective-permute-start | bytes 442376 | tf_op jit(solution)/shard_map/ppermute | solution.py:328
  80.3 3.7 %memory_part.1.key_value = bf16[624,1536]{1,0:T(8,128)(2,1)S(1)} custom-call(s32[128]{0:T(128)S(1)} %copy-done, s32[6]{0:T(128)S(1)} %reshape.4.slot_images, s32[2]{0:T(128)S(1)} %pad_add_fusion.place, bf16[4,196,384]{2,1,0:T(8,128)(2,1)S(1)} %constant_dynamic-update-slice_fusion.2.mine, bf16[4,196,384]{2,1,0:T(8,128)(2,1)S(1)} %copy.23.theirs, ...), custom_call_target="tpu_custom_call" | custom-call | flops 3000000000 | bytes 8388608 | tf_op jit(solution)/shard_map/memory_part/pallas_call | solution.py:249
  93.9 13.0 %self_part.1 = (f32[624,768]{1,0:T(8,128)S(1)}, bf16[624,768]{1,0:T(8,128)(2,1)S(1)}) custom-call(f32[624,768]{1,0:T(8,128)} %copy-done.13, bf16[624,2304]{1,0:T(8,128)(2,1)} %copy-done.12, f32[1,768]{1,0:T(1,128)S(1)} %copy-done.8, bf16[768,768]{1,0:T(8,128)(2,1)S(1)} %bitcast.10, bf16[768,768]{1,0:T(8,128)(2,1)S(1)} %bitcast.11), custom_call_target="tpu_custom_call" | custom-call | flops 12000000000 | bytes 8388608 | tf_op jit(solution)/shard_map/self_part/pallas_call | solution.py:249
  108.3 11.4 %cross_part.1 = (f32[624,768]{1,0:T(8,128)S(1)}, bf16[624,768]{1,0:T(8,128)(2,1)S(1)}) custom-call(f32[624,768]{1,0:T(8,128)} %copy-done.15, bf16[624,768]{1,0:T(8,128)(2,1)S(1)} %get-tuple-element.55.query, bf16[624,1536]{1,0:T(8,128)(2,1)} %copy-done.11, f32[1,768]{1,0:T(1,128)S(1)} %copy-done.9, bf16[768,768]{1,0:T(8,128)(2,1)S(1)} %bitcast.12), custom_call_target="tpu_custom_call" | custom-call | flops 12000000000 | bytes 8388608 | tf_op jit(solution)/shard_map/cross_part/pallas_call | solution.py:249
  119.9 2.7 %collective-permute-start.21 = (bf16[2,192,768]{2,1,0:T(8,128)(2,1)S(1)}, bf16[2,192,768]{2,1,0:T(8,128)(2,1)S(1)}, u32[]{:S(2)}, u32[]{:S(2)}) collective-permute-start(bf16[2,192,768]{2,1,0:T(8,128)(2,1)S(1)} %slice.41), channel_id=1, source_target_pairs={{0,192},{2,194},{4,196},{6,198},{8,200},{10,202},{12,204},{14,206}... | collective-permute-start | bytes 1769480 | tf_op jit(solution)/shard_map/ppermute | solution.py:328
  122.8 3.0 %collective-permute-start.23 = (bf16[2,192,768]{2,1,0:T(8,128)(2,1)S(1)}, bf16[2,192,768]{2,1,0:T(8,128)(2,1)S(1)}, u32[]{:S(2)}, u32[]{:S(2)}) collective-permute-start(bf16[2,192,768]{2,1,0:T(8,128)(2,1)S(1)} %slice.43), channel_id=1, source_target_pairs={{0,48},{2,50},{4,52},{6,54},{8,56},{10,58},{12,60},{14,62},{16,0},... | collective-permute-start | bytes 1769480 | tf_op jit(solution)/shard_map/ppermute | solution.py:328
  133.8 9.8 %early_part.1.early = f32[624,768]{1,0:T(8,128)S(1)} custom-call(f32[624,768]{1,0:T(8,128)S(1)} %get-tuple-element.59.second, bf16[624,768]{1,0:T(8,128)(2,1)S(1)} %get-tuple-element.60.mlp_in, bf16[2,2304,768]{2,1,0:T(8,128)(2,1)} %constant_dynamic-update-slice_fusion.16.fc), custom_call_target="tpu_custom_call" | custom-call | flops 10000000000 | bytes 8388608 | tf_op jit(solution)/shard_map/early_part/pallas_call | solution.py:249
  146.1 6.2 %late_part.1 = (f32[3,196,512]{2,1,0:T(8,128)S(1)}, bf16[3,196,512]{2,1,0:T(8,128)(2,1)S(1)}) custom-call(s32[2]{0:T(128)S(1)} %pad_add_fusion.place, f32[624,768]{1,0:T(8,128)} %copy-done.14, bf16[624,768]{1,0:T(8,128)(2,1)S(1)} %get-tuple-element.60.mlp_in, bf16[2,768,768]{2,1,0:T(8,128)(2,1)} %pad_maximum_fusion.fc, f32[1,768]{1,0:T(1,128)S(1)} %copy-done.10, ...), custom_call_target="tpu_custom_call" | custom-call | flops 5000000000 | bytes 8388608 | tf_op jit(solution)/shard_map/late_part/pallas_call | solution.py:249
  152.3 5.4 %collective-permute-start.24 = (bf16[3,196,512]{2,1,0:T(8,128)(2,1)S(1)}, bf16[3,196,512]{2,1,0:T(8,128)(2,1)S(1)}, u32[]{:S(2)}, u32[]{:S(2)}) collective-permute-start(bf16[3,196,512]{2,1,0:T(8,128)(2,1)S(1)} %get-tuple-element.66), channel_id=1, source_target_pairs={{0,1},{1,0},{2,3},{3,2},{4,5},{5,4},{6,7},{7,6},{8,9},{9,8},{10,11... | collective-permute-start | bytes 1806344 | tf_op jit(solution)/shard_map/ppermute | solution.py:27
  160.8 11.7 %collective-permute-done.25 = bf16[196,512]{1,0:T(8,128)(2,1)S(1)} collective-permute-done((bf16[196,512]{1,0:T(8,128)(2,1)S(1)}, bf16[196,512]{1,0:T(8,128)(2,1)S(1)}, u32[]{:S(2)}, u32[]{:S(2)}) %collective-permute-start.25) | collective-permute-done | bytes 200736 | tf_op jit(solution)/shard_map/ppermute | solution.py:23
  172.7 10.8 %collective-permute-done.26 = bf16[196,512]{1,0:T(8,128)(2,1)S(1)} collective-permute-done((bf16[196,512]{1,0:T(8,128)(2,1)S(1)}, bf16[196,512]{1,0:T(8,128)(2,1)S(1)}, u32[]{:S(2)}, u32[]{:S(2)}) %collective-permute-start.26) | collective-permute-done | bytes 200736 | tf_op jit(solution)/shard_map/ppermute | solution.py:23
  183.6 10.0 %collective-permute-done.27.passed = bf16[196,512]{1,0:T(8,128)(2,1)S(1)} collective-permute-done((bf16[196,512]{1,0:T(8,128)(2,1)S(1)}, bf16[196,512]{1,0:T(8,128)(2,1)S(1)}, u32[]{:S(2)}, u32[]{:S(2)}) %collective-permute-start.27) | collective-permute-done | bytes 200736 | tf_op jit(solution)/shard_map/ppermute | solution.py:23
  (117 shorter events, 38.9 us)
Async XLA Ops:
  0.0 14.0 %collective-permute-start.8 = (bf16[1,196,384]{2,1,0:T(8,128)(2,1)}, bf16[1,196,384]{2,1,0:T(8,128)(2,1)S(1)}, u32[]{:S(2)}, u32[]{:S(2)}) collective-permute-start(bf16[1,196,384]{2,1,0:T(8,128)(2,1)} %param.17), channel_id=1, source_target_pairs={{0,254},{2,0},{4,2},{6,4},{8,6},{10,8},{12,10},{14,12},{16,14},{18... | collective-permute-start | bytes 451592 | tf_op jit(solution)/shard_map/ppermute | solution.py:23
  14.0 11.9 %collective-permute-start.9 = (bf16[1,196,384]{2,1,0:T(8,128)(2,1)S(1)}, bf16[1,196,384]{2,1,0:T(8,128)(2,1)S(1)}, u32[]{:S(2)}, u32[]{:S(2)}) collective-permute-start(bf16[1,196,384]{2,1,0:T(8,128)(2,1)S(1)} %collective-permute-done.8), channel_id=1, source_target_pairs={{0,254},{2,0},{4,2},{6,4},{8,6},{10,8},{12,10},{14,12},{16,14},{18... | collective-permute-start | bytes 451592 | tf_op jit(solution)/shard_map/ppermute | solution.py:23
  22.3 15.0 %collective-permute-start = (bf16[2,24,768]{2,1,0:T(8,128)(2,1)S(1)}, bf16[2,24,768]{2,1,0:T(8,128)(2,1)S(1)}, u32[]{:S(2)}, u32[]{:S(2)}) collective-permute-start(bf16[2,24,768]{2,1,0:T(8,128)(2,1)S(1)} %constant_dynamic-update-slice_fusion), channel_id=1, source_target_pairs={{0,2},{2,4},{4,6},{6,8},{8,10},{10,12},{12,14},{14,0},{16,18},{18,... | collective-permute-start | bytes 221192 | tf_op jit(solution)/shard_map/ppermute | solution.py:328
  22.3 15.0 %collective-permute-start.1 = (bf16[2,24,768]{2,1,0:T(8,128)(2,1)S(1)}, bf16[2,24,768]{2,1,0:T(8,128)(2,1)S(1)}, u32[]{:S(2)}, u32[]{:S(2)}) collective-permute-start(bf16[2,24,768]{2,1,0:T(8,128)(2,1)S(1)} %constant_dynamic-update-slice_fusion), channel_id=1, source_target_pairs={{0,14},{2,0},{4,2},{6,4},{8,6},{10,8},{12,10},{14,12},{16,30},{18,... | collective-permute-start | bytes 221192 | tf_op jit(solution)/shard_map/ppermute | solution.py:328
  33.5 30.3 %collective-permute-start.11 = (bf16[4,196,384]{2,0,1:T(4,128)(2,1)S(1)}, bf16[4,196,384]{2,0,1:T(4,128)(2,1)S(1)}, u32[]{:S(2)}, u32[]{:S(2)}) collective-permute-start(bf16[4,196,384]{2,0,1:T(4,128)(2,1)S(1)} %copy.21), channel_id=1, source_target_pairs={{0,1},{1,0},{2,3},{3,2},{4,5},{5,4},{6,7},{7,6},{8,9},{9,8},{10,11... | collective-permute-start | bytes 1806344 | tf_op jit(solution)/shard_map/ppermute | solution.py:27
  37.3 19.5 %collective-permute-start.2 = (bf16[2,72,768]{2,1,0:T(8,128)(2,1)S(1)}, bf16[2,72,768]{2,1,0:T(8,128)(2,1)S(1)}, u32[]{:S(2)}, u32[]{:S(2)}) collective-permute-start(bf16[2,72,768]{2,1,0:T(8,128)(2,1)S(1)} %pad_maximum_fusion.5), channel_id=1, source_target_pairs={{0,6},{2,8},{4,10},{6,12},{8,14},{10,0},{12,2},{14,4},{16,22},{18,... | collective-permute-start | bytes 663560 | tf_op jit(solution)/shard_map/ppermute | solution.py:328
  37.4 13.7 %collective-permute-start.5 = (bf16[2,48,768]{2,1,0:T(8,128)(2,1)S(1)}, bf16[2,48,768]{2,1,0:T(8,128)(2,1)S(1)}, u32[]{:S(2)}, u32[]{:S(2)}) collective-permute-start(bf16[2,48,768]{2,1,0:T(8,128)(2,1)S(1)} %pad_maximum_fusion.6), channel_id=1, source_target_pairs={{0,10},{2,12},{4,14},{6,0},{8,2},{10,4},{12,6},{14,8},{16,26},{18,... | collective-permute-start | bytes 442376 | tf_op jit(solution)/shard_map/ppermute | solution.py:328
  57.7 15.6 %collective-permute-start.3 = (bf16[2,96,768]{2,1,0:T(8,128)(2,1)S(1)}, bf16[2,96,768]{2,1,0:T(8,128)(2,1)S(1)}, u32[]{:S(2)}, u32[]{:S(2)}) collective-permute-start(bf16[2,96,768]{2,1,0:T(8,128)(2,1)S(1)} %get-tuple-element.80), channel_id=1, source_target_pairs={{0,16},{2,18},{4,20},{6,22},{8,24},{10,26},{12,28},{14,30},{16,32}... | collective-permute-start | bytes 884744 | tf_op jit(solution)/shard_map/ppermute | solution.py:328
  57.7 15.6 %collective-permute-start.4 = (bf16[2,96,768]{2,1,0:T(8,128)(2,1)S(1)}, bf16[2,96,768]{2,1,0:T(8,128)(2,1)S(1)}, u32[]{:S(2)}, u32[]{:S(2)}) collective-permute-start(bf16[2,96,768]{2,1,0:T(8,128)(2,1)S(1)} %get-tuple-element.80), channel_id=1, source_target_pairs={{0,48},{2,50},{4,52},{6,54},{8,56},{10,58},{12,60},{14,62},{16,0},... | collective-permute-start | bytes 884744 | tf_op jit(solution)/shard_map/ppermute | solution.py:328
  60.4 12.9 %collective-permute-start.6 = (bf16[2,96,768]{2,1,0:T(8,128)(2,1)S(1)}, bf16[2,96,768]{2,1,0:T(8,128)(2,1)S(1)}, u32[]{:S(2)}, u32[]{:S(2)}) collective-permute-start(bf16[2,96,768]{2,1,0:T(8,128)(2,1)S(1)} %get-tuple-element.74), channel_id=1, source_target_pairs={{0,64},{2,66},{4,68},{6,70},{8,72},{10,74},{12,76},{14,78},{16,80}... | collective-permute-start | bytes 884744 | tf_op jit(solution)/shard_map/ppermute | solution.py:328
  60.4 13.0 %collective-permute-start.7 = (bf16[2,96,768]{2,1,0:T(8,128)(2,1)S(1)}, bf16[2,96,768]{2,1,0:T(8,128)(2,1)S(1)}, u32[]{:S(2)}, u32[]{:S(2)}) collective-permute-start(bf16[2,96,768]{2,1,0:T(8,128)(2,1)S(1)} %get-tuple-element.74), channel_id=1, source_target_pairs={{0,192},{2,194},{4,196},{6,198},{8,200},{10,202},{12,204},{14,206}... | collective-permute-start | bytes 884744 | tf_op jit(solution)/shard_map/ppermute | solution.py:328
  73.4 12.2 %collective-permute-start.12 = (bf16[2,48,768]{2,1,0:T(8,128)(2,1)S(1)}, bf16[2,48,768]{2,1,0:T(8,128)(2,1)S(1)}, u32[]{:S(2)}, u32[]{:S(2)}) collective-permute-start(bf16[2,48,768]{2,1,0:T(8,128)(2,1)S(1)} %slice.36), channel_id=1, source_target_pairs={{0,16},{2,18},{4,20},{6,22},{8,24},{10,26},{12,28},{14,30},{16,32}... | collective-permute-start | bytes 442376 | tf_op jit(solution)/shard_map/ppermute | solution.py:328
  73.6 12.1 %collective-permute-start.13 = (bf16[2,48,768]{2,1,0:T(8,128)(2,1)S(1)}, bf16[2,48,768]{2,1,0:T(8,128)(2,1)S(1)}, u32[]{:S(2)}, u32[]{:S(2)}) collective-permute-start(bf16[2,48,768]{2,1,0:T(8,128)(2,1)S(1)} %slice.37), channel_id=1, source_target_pairs={{0,48},{2,50},{4,52},{6,54},{8,56},{10,58},{12,60},{14,62},{16,0},... | collective-permute-start | bytes 442376 | tf_op jit(solution)/shard_map/ppermute | solution.py:328
  87.0 32.6 %collective-permute-start.18 = (bf16[2,384,768]{2,1,0:T(8,128)(2,1)}, bf16[2,384,768]{2,1,0:T(8,128)(2,1)S(1)}, u32[]{:S(2)}, u32[]{:S(2)}) collective-permute-start(bf16[2,384,768]{2,1,0:T(8,128)(2,1)} %constant_dynamic-update-slice_fusion.11), channel_id=1, source_target_pairs={{0,16},{2,18},{4,20},{6,22},{8,24},{10,26},{12,28},{14,30},{16,32}... | collective-permute-start | bytes 3538952 | tf_op jit(solution)/shard_map/ppermute | solution.py:328
  87.0 32.6 %collective-permute-start.19 = (bf16[2,384,768]{2,1,0:T(8,128)(2,1)}, bf16[2,384,768]{2,1,0:T(8,128)(2,1)S(1)}, u32[]{:S(2)}, u32[]{:S(2)}) collective-permute-start(bf16[2,384,768]{2,1,0:T(8,128)(2,1)} %constant_dynamic-update-slice_fusion.11), channel_id=1, source_target_pairs={{0,48},{2,50},{4,52},{6,54},{8,56},{10,58},{12,60},{14,62},{16,0},... | collective-permute-start | bytes 3538952 | tf_op jit(solution)/shard_map/ppermute | solution.py:328
  91.2 28.5 %collective-permute-start.16 = (bf16[2,384,768]{2,1,0:T(8,128)(2,1)}, bf16[2,384,768]{2,1,0:T(8,128)(2,1)S(1)}, u32[]{:S(2)}, u32[]{:S(2)}) collective-permute-start(bf16[2,384,768]{2,1,0:T(8,128)(2,1)} %get-tuple-element.82), channel_id=1, source_target_pairs={{0,64},{2,66},{4,68},{6,70},{8,72},{10,74},{12,76},{14,78},{16,80}... | collective-permute-start | bytes 3538952 | tf_op jit(solution)/shard_map/ppermute | solution.py:328
  91.2 28.5 %collective-permute-start.17 = (bf16[2,384,768]{2,1,0:T(8,128)(2,1)}, bf16[2,384,768]{2,1,0:T(8,128)(2,1)S(1)}, u32[]{:S(2)}, u32[]{:S(2)}) collective-permute-start(bf16[2,384,768]{2,1,0:T(8,128)(2,1)} %get-tuple-element.82), channel_id=1, source_target_pairs={{0,192},{2,194},{4,196},{6,198},{8,200},{10,202},{12,204},{14,206}... | collective-permute-start | bytes 3538952 | tf_op jit(solution)/shard_map/ppermute | solution.py:328
  119.7 23.8 %collective-permute-start.20 = (bf16[2,192,768]{2,1,0:T(8,128)(2,1)S(1)}, bf16[2,192,768]{2,1,0:T(8,128)(2,1)S(1)}, u32[]{:S(2)}, u32[]{:S(2)}) collective-permute-start(bf16[2,192,768]{2,1,0:T(8,128)(2,1)S(1)} %slice.40), channel_id=1, source_target_pairs={{0,64},{2,66},{4,68},{6,70},{8,72},{10,74},{12,76},{14,78},{16,80}... | collective-permute-start | bytes 1769480 | tf_op jit(solution)/shard_map/ppermute | solution.py:328
  119.9 23.7 %collective-permute-start.21 = (bf16[2,192,768]{2,1,0:T(8,128)(2,1)S(1)}, bf16[2,192,768]{2,1,0:T(8,128)(2,1)S(1)}, u32[]{:S(2)}, u32[]{:S(2)}) collective-permute-start(bf16[2,192,768]{2,1,0:T(8,128)(2,1)S(1)} %slice.41), channel_id=1, source_target_pairs={{0,192},{2,194},{4,196},{6,198},{8,200},{10,202},{12,204},{14,206}... | collective-permute-start | bytes 1769480 | tf_op jit(solution)/shard_map/ppermute | solution.py:328
  122.7 21.0 %collective-permute-start.22 = (bf16[2,192,768]{2,1,0:T(8,128)(2,1)S(1)}, bf16[2,192,768]{2,1,0:T(8,128)(2,1)S(1)}, u32[]{:S(2)}, u32[]{:S(2)}) collective-permute-start(bf16[2,192,768]{2,1,0:T(8,128)(2,1)S(1)} %slice.42), channel_id=1, source_target_pairs={{0,16},{2,18},{4,20},{6,22},{8,24},{10,26},{12,28},{14,30},{16,32}... | collective-permute-start | bytes 1769480 | tf_op jit(solution)/shard_map/ppermute | solution.py:328
  122.8 20.8 %collective-permute-start.23 = (bf16[2,192,768]{2,1,0:T(8,128)(2,1)S(1)}, bf16[2,192,768]{2,1,0:T(8,128)(2,1)S(1)}, u32[]{:S(2)}, u32[]{:S(2)}) collective-permute-start(bf16[2,192,768]{2,1,0:T(8,128)(2,1)S(1)} %slice.43), channel_id=1, source_target_pairs={{0,48},{2,50},{4,52},{6,54},{8,56},{10,58},{12,60},{14,62},{16,0},... | collective-permute-start | bytes 1769480 | tf_op jit(solution)/shard_map/ppermute | solution.py:328
  160.7 11.8 %collective-permute-start.25 = (bf16[196,512]{1,0:T(8,128)(2,1)S(1)}, bf16[196,512]{1,0:T(8,128)(2,1)S(1)}, u32[]{:S(2)}, u32[]{:S(2)}) collective-permute-start(bf16[196,512]{1,0:T(8,128)(2,1)S(1)} %get-tuple-element.70), channel_id=1, source_target_pairs={{0,2},{2,4},{4,6},{6,8},{8,10},{10,12},{12,14},{14,16},{16,18},{18... | collective-permute-start | bytes 602120 | tf_op jit(solution)/shard_map/ppermute | solution.py:23
  172.6 10.9 %collective-permute-start.26 = (bf16[196,512]{1,0:T(8,128)(2,1)S(1)}, bf16[196,512]{1,0:T(8,128)(2,1)S(1)}, u32[]{:S(2)}, u32[]{:S(2)}) collective-permute-start(bf16[196,512]{1,0:T(8,128)(2,1)S(1)} %add_convert_fusion.1), channel_id=1, source_target_pairs={{0,2},{2,4},{4,6},{6,8},{8,10},{10,12},{12,14},{14,16},{16,18},{18... | collective-permute-start | bytes 602120 | tf_op jit(solution)/shard_map/ppermute | solution.py:23
  183.5 10.1 %collective-permute-start.27 = (bf16[196,512]{1,0:T(8,128)(2,1)S(1)}, bf16[196,512]{1,0:T(8,128)(2,1)S(1)}, u32[]{:S(2)}, u32[]{:S(2)}) collective-permute-start(bf16[196,512]{1,0:T(8,128)(2,1)S(1)} %add_convert_fusion), channel_id=1, source_target_pairs={{0,2},{2,4},{4,6},{6,8},{8,10},{10,12},{12,14},{14,16},{16,18},{18... | collective-permute-start | bytes 602120 | tf_op jit(solution)/shard_map/ppermute | solution.py:23
  (21 other events, 229.0 us)

commit v3 on v2

--- a/solution.py
+++ b/solution.py
@@ -234,11 +234,14 @@
             outs[w][:, cols] = acc.astype(outs[w].dtype)
 
 
-def merge_kernel(base, passed, out):
-    weight = jnp.maximum(base[:, 384:] + passed[:, 384:].astype(F32), 1.0)
+def merge_kernel(base, nearest, further, out):
+    def total(cols):
+        return base[:, cols] + nearest[:, cols].astype(F32) + further[:, cols].astype(F32)
+
+    weight = jnp.maximum(total(slice(384, 512)), 1.0)
     for c in range(3):
         cols = slice(c * 128, (c + 1) * 128)
-        out[0, :, cols] = ((base[:, cols] + passed[:, cols].astype(F32)) / weight).astype(BF16)
+        out[0, :, cols] = (total(cols) / weight).astype(BF16)
 
 
 SMEM = pl.BlockSpec(memory_space=pltpu.SMEM)
@@ -252,7 +255,7 @@
         out_specs=[VMEM] * len(outs),
         out_shape=[jax.ShapeDtypeStruct(s, d) for s, d in outs],
         scratch_shapes=[pltpu.VMEM(s, d) for s, d in scratch],
-        compiler_params=pltpu.CompilerParams(vmem_limit_bytes=48 << 20),
+        compiler_params=pltpu.CompilerParams(vmem_limit_bytes=20 << 20),
         cost_estimate=pl.CostEstimate(flops=flops, transcendentals=0, bytes_accessed=8 << 20),
         name=name,
     )(*scalars, *arrays)
@@ -313,8 +316,8 @@
     )
 
 
-def merge_call(base, passed):
-    return call(merge_kernel, [], [base, passed], [((1, TOKI, HALF), BF16)], [], 10**8, "merge_part")[0]
+def merge_call(*arrays):
+    return call(merge_kernel, [], arrays, [((1, TOKI, HALF), BF16)], [], 10**8, "merge_part")[0]
 
 
 def along(array, axis, by):
@@ -333,11 +336,8 @@
 
 
 def gather_line(shard):
-    up, down = along(shard, "z", 1), along(shard, "z", -1)
-    near = jnp.concatenate([up, shard, down], axis=1)
-    far = along(near, "z", 3)
-    other = along(near[:, : 2 * shard.shape[1]], "z", -3)
-    return jnp.concatenate([near, far, other], axis=1)
+    others = [along(shard, "z", by) for by in (4, 3, -3, 2, -2, 1, -1)]
+    return jnp.concatenate([shard, *others], axis=1)
 
 
 def first_hop(block, axis):
@@ -370,9 +370,8 @@
 ):
     place = jnp.stack([lax.axis_index("pairs"), lax.axis_index("side")]).astype(jnp.int32)
     shard = jnp.concatenate([w_fc1, w_fc2], axis=0)
-    blocks = [features]
-    for _ in range(1, WINDOW):
-        blocks.append(shifted(blocks[-1], -1))
+    second_next = shifted(features, -2)
+    blocks = [features, shifted(features, -1), second_next, shifted(second_next, -1)]
     mine = jnp.concatenate(blocks, axis=0)
     theirs = other_core(mine)
     line = gather_line(shard)
@@ -398,10 +397,10 @@
     keep, send = late_call(place, early, mlp_in, fc_late, gain_head, w_head[0])
     got = other_core(send)
     pieces = window_call([image_slot, slot_images.reshape(-1), slot_count, place], keep, got)
-    passed = shifted(pieces[3], 1)
-    for w in (2, 1):
-        passed = shifted((pieces[w].astype(F32) + passed.astype(F32)).astype(BF16), 1)
-    return merge_call(pieces[0], passed)
+    third = shifted(pieces[3], 1)
+    nearest = shifted(pieces[1], 1)
+    further = shifted((pieces[2].astype(F32) + third.astype(F32)).astype(BF16), 2)
+    return merge_call(pieces[0], nearest, further)
 
 
 def solution(mesh):

time: 195 us -> 153 us (0.78)
  waiting for transfers between devices: 52.5 us -> 32.8 us
  local copies, waits for them, and re-layouts: 22.7 us -> 9.08 us
  Pallas kernels: 52.6 us -> 41.7 us
  starting transfers between devices: 62.8 us -> 67.1 us
  other arithmetic: 2.69 us -> 0.31 us
    ppermute x20 -> x23, waiting for transfers between devices: 14.6 us -> 0.06 us  [along(): return lax.ppermute(array, 'pairs', [(p, target(p)) for p in range(count)])]
    unnamed x54 -> x58, local copies, waits for them, and re-layouts: 19.5 us -> 8.29 us
    pallas_call x8, Pallas kernels: 52.6 us -> 41.7 us  [call(): pl.pallas_call(kernel, in_specs=[SMEM] * len(scalars) + [VMEM] * len(arra...]
    ppermute x2, starting transfers between devices: 9.16 us -> 14.8 us  [other_core(): return lax.ppermute(array, 'side', [(0, 1), (1, 0)])]
    ppermute x6, waiting for transfers between devices: 36.8 us -> 31.7 us  [shifted(): lax.ppermute(array, 'pairs', [(i, (i + by) % count) for i in range(count)])]
    ppermute x6, starting transfers between devices: 23.9 us -> 21.6 us  [shifted(): lax.ppermute(array, 'pairs', [(i, (i + by) % count) for i in range(count)])]
    ppermute x20 -> x23, starting transfers between devices: 29.7 us -> 30.7 us  [along(): return lax.ppermute(array, 'pairs', [(p, target(p)) for p in range(count)])]
  transfers between devices with their start and end apart: 28 -> 31, of which waited for: 8 -> 7; matrix products, arithmetic and copies ran while one was open for 9% -> 3% of each run, Pallas kernels for 23% -> 23%
where the time goes in v3:
time: 153 us; the launch traced here: 152 us
  starting transfers between devices  67.1 us (44%)
  Pallas kernels  41.7 us (27%)
  waiting for transfers between devices  32.8 us (21%)
  local copies, waits for them, and re-layouts  9.08 us (6%)
    pallas_call x8, Pallas kernels, call(): pl.pallas_call(kernel, in_specs=[SMEM] * len(scalars) + [VMEM] * len(arra...  41.7 us
    ppermute x6, waiting for transfers between devices, shifted(): lax.ppermute(array, 'pairs', [(i, (i + by) % count) for i in range(count)])  31.7 us
    ppermute x23, starting transfers between devices, along(): return lax.ppermute(array, 'pairs', [(p, target(p)) for p in range(count)])  30.7 us
    ppermute x6, starting transfers between devices, shifted(): lax.ppermute(array, 'pairs', [(i, (i + by) % count) for i in range(count)])  21.6 us
    ppermute x2, starting transfers between devices, other_core(): return lax.ppermute(array, 'side', [(0, 1), (1, 0)])  14.8 us
    unnamed x58, local copies, waits for them, and re-layouts  8.29 us
  transfers between devices with their start and end apart: 31, of which 7 were waited for; matrix products, arithmetic and copies ran while one was open for 3% of the time, Pallas kernels for 23%

profile of v3, /device:TPU:1, one launch (start us, length us, event | category | flops | bytes accessed | tf_op | source)
XLA Modules:
  0.0 152.3 jit_solution(327601235184379833)
XLA Ops:
  2.8 3.8 %collective-permute-start.5 = (bf16[2,24,768]{2,1,0:T(8,128)(2,1)S(1)}, bf16[2,24,768]{2,1,0:T(8,128)(2,1)S(1)}, u32[]{:S(2)}, u32[]{:S(2)}) collective-permute-start(bf16[2,24,768]{2,1,0:T(8,128)(2,1)S(1)} %get-tuple-element.95), channel_id=1, source_target_pairs={{0,4},{2,6},{4,8},{6,10},{8,12},{10,14},{12,0},{14,2},{16,20},{18,... | collective-permute-start | bytes 221192 | tf_op jit(solution)/shard_map/ppermute | solution.py:331
  6.6 3.0 %collective-permute-start.6 = (bf16[2,24,768]{2,1,0:T(8,128)(2,1)S(1)}, bf16[2,24,768]{2,1,0:T(8,128)(2,1)S(1)}, u32[]{:S(2)}, u32[]{:S(2)}) collective-permute-start(bf16[2,24,768]{2,1,0:T(8,128)(2,1)S(1)} %get-tuple-element.95), channel_id=1, source_target_pairs={{0,12},{2,14},{4,0},{6,2},{8,4},{10,6},{12,8},{14,10},{16,28},{18,... | collective-permute-start | bytes 221192 | tf_op jit(solution)/shard_map/ppermute | solution.py:331
  12.3 6.3 %collective-permute-start.12 = (bf16[1,196,384]{2,1,0:T(8,128)(2,1)}, bf16[1,196,384]{2,1,0:T(8,128)(2,1)S(1)}, u32[]{:S(2)}, u32[]{:S(2)}) collective-permute-start(bf16[1,196,384]{2,1,0:T(8,128)(2,1)} %param.17), channel_id=1, source_target_pairs={{0,252},{2,254},{4,0},{6,2},{8,4},{10,6},{12,8},{14,10},{16,12},{1... | collective-permute-start | bytes 451592 | tf_op jit(solution)/shard_map/ppermute | solution.py:23
  24.3 7.1 %collective-permute-done.11 = bf16[1,196,384]{2,1,0:T(8,128)(2,1)S(1)} collective-permute-done((bf16[1,196,384]{2,1,0:T(8,128)(2,1)}, bf16[1,196,384]{2,1,0:T(8,128)(2,1)S(1)}, u32[]{:S(2)}, u32[]{:S(2)}) %collective-permute-start.11) | collective-permute-done | bytes 150560 | tf_op jit(solution)/shard_map/ppermute | solution.py:23
  31.4 7.7 %collective-permute-start.13 = (bf16[1,196,384]{2,1,0:T(8,128)(2,1)S(1)}, bf16[1,196,384]{2,1,0:T(8,128)(2,1)S(1)}, u32[]{:S(2)}, u32[]{:S(2)}) collective-permute-start(bf16[1,196,384]{2,1,0:T(8,128)(2,1)S(1)} %collective-permute-done.12), channel_id=1, source_target_pairs={{0,254},{2,0},{4,2},{6,4},{8,6},{10,8},{12,10},{14,12},{16,14},{18... | collective-permute-start | bytes 451592 | tf_op jit(solution)/shard_map/ppermute | solution.py:23
  41.5 3.8 %collective-permute-start.14 = (bf16[4,196,384]{2,0,1:T(4,128)(2,1)S(1)}, bf16[4,196,384]{2,0,1:T(4,128)(2,1)S(1)}, u32[]{:S(2)}, u32[]{:S(2)}) collective-permute-start(bf16[4,196,384]{2,0,1:T(4,128)(2,1)S(1)} %copy.21), channel_id=1, source_target_pairs={{0,1},{1,0},{2,3},{3,2},{4,5},{5,4},{6,7},{7,6},{8,9},{9,8},{10,11... | collective-permute-start | bytes 1806344 | tf_op jit(solution)/shard_map/ppermute | solution.py:27
  47.0 2.7 %collective-permute-start.4 = (bf16[2,96,768]{2,1,0:T(8,128)(2,1)S(1)}, bf16[2,96,768]{2,1,0:T(8,128)(2,1)S(1)}, u32[]{:S(2)}, u32[]{:S(2)}) collective-permute-start(bf16[2,96,768]{2,1,0:T(8,128)(2,1)S(1)} %pad_maximum_fusion.1), channel_id=1, source_target_pairs={{0,48},{2,50},{4,52},{6,54},{8,56},{10,58},{12,60},{14,62},{16,0},... | collective-permute-start | bytes 884744 | tf_op jit(solution)/shard_map/ppermute | solution.py:331
  51.7 5.0 %triple_part.1 = (f32[624,768]{1,0:T(8,128)S(1)}, bf16[624,2304]{1,0:T(8,128)(2,1)S(1)}) custom-call(s32[128]{0:T(128)S(1)} %copy-done, s32[6]{0:T(128)S(1)} %reshape.4.slot_images, s32[2]{0:T(128)S(1)} %pad_add_fusion.place, bf16[4,196,384]{2,1,0:T(8,128)(2,1)S(1)} %constant_dynamic-update-slice_fusion.6.mine, bf16[4,196,384]{2,1,0:T(8,128)(2,1)S(1)} %copy.22.theirs, ...), custom_call_target="tpu_custom_call" | custom-call | flops 4000000000 | bytes 8388608 | tf_op jit(solution)/shard_map/triple_part/pallas_call | solution.py:252
  57.0 2.7 %collective-permute-start.16 = (bf16[2,48,768]{2,1,0:T(8,128)(2,1)S(1)}, bf16[2,48,768]{2,1,0:T(8,128)(2,1)S(1)}, u32[]{:S(2)}, u32[]{:S(2)}) collective-permute-start(bf16[2,48,768]{2,1,0:T(8,128)(2,1)S(1)} %slice.29), channel_id=1, source_target_pairs={{0,48},{2,50},{4,52},{6,54},{8,56},{10,58},{12,60},{14,62},{16,0},... | collective-permute-start | bytes 442376 | tf_op jit(solution)/shard_map/ppermute | solution.py:331
  59.9 2.7 %collective-permute-start.18 = (bf16[2,48,768]{2,1,0:T(8,128)(2,1)S(1)}, bf16[2,48,768]{2,1,0:T(8,128)(2,1)S(1)}, u32[]{:S(2)}, u32[]{:S(2)}) collective-permute-start(bf16[2,48,768]{2,1,0:T(8,128)(2,1)S(1)} %slice.31), channel_id=1, source_target_pairs={{0,192},{2,194},{4,196},{6,198},{8,200},{10,202},{12,204},{14,206}... | collective-permute-start | bytes 442376 | tf_op jit(solution)/shard_map/ppermute | solution.py:331
  62.7 3.7 %memory_part.1.key_value = bf16[624,1536]{1,0:T(8,128)(2,1)S(1)} custom-call(s32[128]{0:T(128)S(1)} %copy-done, s32[6]{0:T(128)S(1)} %reshape.4.slot_images, s32[2]{0:T(128)S(1)} %pad_add_fusion.place, bf16[4,196,384]{2,1,0:T(8,128)(2,1)S(1)} %constant_dynamic-update-slice_fusion.6.mine, bf16[4,196,384]{2,1,0:T(8,128)(2,1)S(1)} %copy.23.theirs, ...), custom_call_target="tpu_custom_call" | custom-call | flops 3000000000 | bytes 8388608 | tf_op jit(solution)/shard_map/memory_part/pallas_call | solution.py:252
  66.7 2.7 %collective-permute-start.22 = (bf16[2,384,768]{2,1,0:T(8,128)(2,1)S(1)}, bf16[2,384,768]{2,1,0:T(8,128)(2,1)S(1)}, u32[]{:S(2)}, u32[]{:S(2)}) collective-permute-start(bf16[2,384,768]{2,1,0:T(8,128)(2,1)S(1)} %constant_dynamic-update-slice_fusion.19), channel_id=1, source_target_pairs={{0,48},{2,50},{4,52},{6,54},{8,56},{10,58},{12,60},{14,62},{16,0},... | collective-permute-start | bytes 3538952 | tf_op jit(solution)/shard_map/ppermute | solution.py:331
  69.5 2.7 %collective-permute-start.20 = (bf16[2,384,768]{2,1,0:T(8,128)(2,1)S(1)}, bf16[2,384,768]{2,1,0:T(8,128)(2,1)S(1)}, u32[]{:S(2)}, u32[]{:S(2)}) collective-permute-start(bf16[2,384,768]{2,1,0:T(8,128)(2,1)S(1)} %get-tuple-element.76), channel_id=1, source_target_pairs={{0,192},{2,194},{4,196},{6,198},{8,200},{10,202},{12,204},{14,206}... | collective-permute-start | bytes 3538952 | tf_op jit(solution)/shard_map/ppermute | solution.py:331
  72.2 10.5 %self_part.1 = (f32[624,768]{1,0:T(8,128)S(1)}, bf16[624,768]{1,0:T(8,128)(2,1)S(1)}) custom-call(f32[624,768]{1,0:T(8,128)S(1)} %get-tuple-element.52.rows, bf16[624,2304]{1,0:T(8,128)(2,1)S(1)} %get-tuple-element.53.triple, f32[1,768]{1,0:T(1,128)S(1)} %copy-done.9, bf16[768,768]{1,0:T(8,128)(2,1)S(1)} %bitcast.13, bf16[768,768]{1,0:T(8,128)(2,1)S(1)} %bitcast.14), custom_call_target="tpu_custom_call" | custom-call | flops 12000000000 | bytes 8388608 | tf_op jit(solution)/shard_map/self_part/pallas_call | solution.py:252
  82.8 9.3 %cross_part.1 = (f32[624,768]{1,0:T(8,128)S(1)}, bf16[624,768]{1,0:T(8,128)(2,1)S(1)}) custom-call(f32[624,768]{1,0:T(8,128)S(1)} %get-tuple-element.54.first, bf16[624,768]{1,0:T(8,128)(2,1)S(1)} %get-tuple-element.55.query, bf16[624,1536]{1,0:T(8,128)(2,1)S(1)} %memory_part.1.key_value, f32[1,768]{1,0:T(1,128)S(1)} %copy-done.10, bf16[768,768]{1,0:T(8,128)(2,1)S(1)} %bitcast.15), custom_call_target="tpu_custom_call" | custom-call | flops 12000000000 | bytes 8388608 | tf_op jit(solution)/shard_map/cross_part/pallas_call | solution.py:252
  92.3 2.7 %collective-permute-start.24 = (bf16[2,192,768]{2,1,0:T(8,128)(2,1)S(1)}, bf16[2,192,768]{2,1,0:T(8,128)(2,1)S(1)}, u32[]{:S(2)}, u32[]{:S(2)}) collective-permute-start(bf16[2,192,768]{2,1,0:T(8,128)(2,1)S(1)} %slice.33), channel_id=1, source_target_pairs={{0,192},{2,194},{4,196},{6,198},{8,200},{10,202},{12,204},{14,206}... | collective-permute-start | bytes 1769480 | tf_op jit(solution)/shard_map/ppermute | solution.py:331
  95.2 2.7 %collective-permute-start.26 = (bf16[2,192,768]{2,1,0:T(8,128)(2,1)S(1)}, bf16[2,192,768]{2,1,0:T(8,128)(2,1)S(1)}, u32[]{:S(2)}, u32[]{:S(2)}) collective-permute-start(bf16[2,192,768]{2,1,0:T(8,128)(2,1)S(1)} %slice.35), channel_id=1, source_target_pairs={{0,48},{2,50},{4,52},{6,54},{8,56},{10,58},{12,60},{14,62},{16,0},... | collective-permute-start | bytes 1769480 | tf_op jit(solution)/shard_map/ppermute | solution.py:331
  98.4 6.6 %early_part.1.early = f32[624,768]{1,0:T(8,128)S(1)} custom-call(f32[624,768]{1,0:T(8,128)S(1)} %get-tuple-element.59.second, bf16[624,768]{1,0:T(8,128)(2,1)S(1)} %get-tuple-element.60.mlp_in, bf16[2,2304,768]{2,1,0:T(8,128)(2,1)S(1)} %constant_dynamic-update-slice_fusion.27.fc), custom_call_target="tpu_custom_call" | custom-call | flops 10000000000 | bytes 8388608 | tf_op jit(solution)/shard_map/early_part/pallas_call | solution.py:252
  106.4 4.5 %late_part.1 = (f32[3,196,512]{2,1,0:T(8,128)S(1)}, bf16[3,196,512]{2,1,0:T(8,128)(2,1)S(1)}) custom-call(s32[2]{0:T(128)S(1)} %pad_add_fusion.place, f32[624,768]{1,0:T(8,128)S(1)} %early_part.1.early, bf16[624,768]{1,0:T(8,128)(2,1)S(1)} %get-tuple-element.60.mlp_in, bf16[2,768,768]{2,1,0:T(8,128)(2,1)S(1)} %pad_maximum_fusion.fc, ...), custom_call_target="tpu_custom_call" | custom-call | flops 5000000000 | bytes 8388608 | tf_op jit(solution)/shard_map/late_part/pallas_call | solution.py:252
  110.9 11.0 %collective-permute-start.27 = (bf16[3,196,512]{2,1,0:T(8,128)(2,1)S(1)}, bf16[3,196,512]{2,1,0:T(8,128)(2,1)S(1)}, u32[]{:S(2)}, u32[]{:S(2)}) collective-permute-start(bf16[3,196,512]{2,1,0:T(8,128)(2,1)S(1)} %get-tuple-element.66), channel_id=1, source_target_pairs={{0,1},{1,0},{2,3},{3,2},{4,5},{5,4},{6,7},{7,6},{8,9},{9,8},{10,11... | collective-permute-start | bytes 1806344 | tf_op jit(solution)/shard_map/ppermute | solution.py:27
  125.0 6.0 %collective-permute-start.28 = (bf16[196,512]{1,0:T(8,128)(2,1)S(1)}, bf16[196,512]{1,0:T(8,128)(2,1)S(1)}, u32[]{:S(2)}, u32[]{:S(2)}) collective-permute-start(bf16[196,512]{1,0:T(8,128)(2,1)S(1)} %get-tuple-element.68), channel_id=1, source_target_pairs={{0,2},{2,4},{4,6},{6,8},{8,10},{10,12},{12,14},{14,16},{16,18},{18... | collective-permute-start | bytes 602120 | tf_op jit(solution)/shard_map/ppermute | solution.py:23
  131.0 6.5 %collective-permute-done.29 = bf16[196,512]{1,0:T(8,128)(2,1)S(1)} collective-permute-done((bf16[196,512]{1,0:T(8,128)(2,1)S(1)}, bf16[196,512]{1,0:T(8,128)(2,1)S(1)}, u32[]{:S(2)}, u32[]{:S(2)}) %collective-permute-start.29) | collective-permute-done | bytes 200736 | tf_op jit(solution)/shard_map/ppermute | solution.py:23
  137.6 4.2 %collective-permute-done.28.nearest = bf16[196,512]{1,0:T(8,128)(2,1)S(1)} collective-permute-done((bf16[196,512]{1,0:T(8,128)(2,1)S(1)}, bf16[196,512]{1,0:T(8,128)(2,1)S(1)}, u32[]{:S(2)}, u32[]{:S(2)}) %collective-permute-start.28) | collective-permute-done | bytes 200736 | tf_op jit(solution)/shard_map/ppermute | solution.py:23
  141.9 9.6 %collective-permute-done.30.further = bf16[196,512]{1,0:T(8,128)(2,1)S(1)} collective-permute-done((bf16[196,512]{1,0:T(8,128)(2,1)S(1)}, bf16[196,512]{1,0:T(8,128)(2,1)S(1)}, u32[]{:S(2)}, u32[]{:S(2)}) %collective-permute-start.30) | collective-permute-done | bytes 200736 | tf_op jit(solution)/shard_map/ppermute | solution.py:23
  (124 shorter events, 23.3 us)
Async XLA Ops:
  2.8 17.7 %collective-permute-start.5 = (bf16[2,24,768]{2,1,0:T(8,128)(2,1)S(1)}, bf16[2,24,768]{2,1,0:T(8,128)(2,1)S(1)}, u32[]{:S(2)}, u32[]{:S(2)}) collective-permute-start(bf16[2,24,768]{2,1,0:T(8,128)(2,1)S(1)} %get-tuple-element.95), channel_id=1, source_target_pairs={{0,4},{2,6},{4,8},{6,10},{8,12},{10,14},{12,0},{14,2},{16,20},{18,... | collective-permute-start | bytes 221192 | tf_op jit(solution)/shard_map/ppermute | solution.py:331
  6.6 15.4 %collective-permute-start.6 = (bf16[2,24,768]{2,1,0:T(8,128)(2,1)S(1)}, bf16[2,24,768]{2,1,0:T(8,128)(2,1)S(1)}, u32[]{:S(2)}, u32[]{:S(2)}) collective-permute-start(bf16[2,24,768]{2,1,0:T(8,128)(2,1)S(1)} %get-tuple-element.95), channel_id=1, source_target_pairs={{0,12},{2,14},{4,0},{6,2},{8,4},{10,6},{12,8},{14,10},{16,28},{18,... | collective-permute-start | bytes 221192 | tf_op jit(solution)/shard_map/ppermute | solution.py:331
  9.6 31.8 %collective-permute-start.7 = (bf16[2,24,768]{2,1,0:T(8,128)(2,1)S(1)}, bf16[2,24,768]{2,1,0:T(8,128)(2,1)S(1)}, u32[]{:S(2)}, u32[]{:S(2)}) collective-permute-start(bf16[2,24,768]{2,1,0:T(8,128)(2,1)S(1)} %get-tuple-element.95), channel_id=1, source_target_pairs={{0,2},{2,4},{4,6},{6,8},{8,10},{10,12},{12,14},{14,0},{16,18},{18,... | collective-permute-start | bytes 221192 | tf_op jit(solution)/shard_map/ppermute | solution.py:331
  10.4 34.9 %collective-permute-start.8 = (bf16[2,24,768]{2,1,0:T(8,128)(2,1)S(1)}, bf16[2,24,768]{2,1,0:T(8,128)(2,1)S(1)}, u32[]{:S(2)}, u32[]{:S(2)}) collective-permute-start(bf16[2,24,768]{2,1,0:T(8,128)(2,1)S(1)} %get-tuple-element.95), channel_id=1, source_target_pairs={{0,14},{2,0},{4,2},{6,4},{8,6},{10,8},{12,10},{14,12},{16,30},{18,... | collective-permute-start | bytes 221192 | tf_op jit(solution)/shard_map/ppermute | solution.py:331
  12.3 12.0 %collective-permute-start.12 = (bf16[1,196,384]{2,1,0:T(8,128)(2,1)}, bf16[1,196,384]{2,1,0:T(8,128)(2,1)S(1)}, u32[]{:S(2)}, u32[]{:S(2)}) collective-permute-start(bf16[1,196,384]{2,1,0:T(8,128)(2,1)} %param.17), channel_id=1, source_target_pairs={{0,252},{2,254},{4,0},{6,2},{8,4},{10,6},{12,8},{14,10},{16,12},{1... | collective-permute-start | bytes 451592 | tf_op jit(solution)/shard_map/ppermute | solution.py:23
  20.5 10.9 %collective-permute-start.11 = (bf16[1,196,384]{2,1,0:T(8,128)(2,1)}, bf16[1,196,384]{2,1,0:T(8,128)(2,1)S(1)}, u32[]{:S(2)}, u32[]{:S(2)}) collective-permute-start(bf16[1,196,384]{2,1,0:T(8,128)(2,1)} %param.17), channel_id=1, source_target_pairs={{0,254},{2,0},{4,2},{6,4},{8,6},{10,8},{12,10},{14,12},{16,14},{18... | collective-permute-start | bytes 451592 | tf_op jit(solution)/shard_map/ppermute | solution.py:23
  22.0 23.5 %collective-permute-start = (bf16[2,24,768]{2,1,0:T(8,128)(2,1)S(1)}, bf16[2,24,768]{2,1,0:T(8,128)(2,1)S(1)}, u32[]{:S(2)}, u32[]{:S(2)}) collective-permute-start(bf16[2,24,768]{2,1,0:T(8,128)(2,1)S(1)} %get-tuple-element.95), channel_id=1, source_target_pairs={{0,8},{2,10},{4,12},{6,14},{8,0},{10,2},{12,4},{14,6},{16,24},{18,... | collective-permute-start | bytes 221192 | tf_op jit(solution)/shard_map/ppermute | solution.py:331
  24.3 22.6 %collective-permute-start.1 = (bf16[2,24,768]{2,1,0:T(8,128)(2,1)S(1)}, bf16[2,24,768]{2,1,0:T(8,128)(2,1)S(1)}, u32[]{:S(2)}, u32[]{:S(2)}) collective-permute-start(bf16[2,24,768]{2,1,0:T(8,128)(2,1)S(1)} %get-tuple-element.95), channel_id=1, source_target_pairs={{0,6},{2,8},{4,10},{6,12},{8,14},{10,0},{12,2},{14,4},{16,22},{18,... | collective-permute-start | bytes 221192 | tf_op jit(solution)/shard_map/ppermute | solution.py:331
  41.5 10.1 %collective-permute-start.14 = (bf16[4,196,384]{2,0,1:T(4,128)(2,1)S(1)}, bf16[4,196,384]{2,0,1:T(4,128)(2,1)S(1)}, u32[]{:S(2)}, u32[]{:S(2)}) collective-permute-start(bf16[4,196,384]{2,0,1:T(4,128)(2,1)S(1)} %copy.21), channel_id=1, source_target_pairs={{0,1},{1,0},{2,3},{3,2},{4,5},{5,4},{6,7},{7,6},{8,9},{9,8},{10,11... | collective-permute-start | bytes 1806344 | tf_op jit(solution)/shard_map/ppermute | solution.py:27
  45.4 11.4 %collective-permute-start.10 = (bf16[2,96,768]{2,1,0:T(8,128)(2,1)S(1)}, bf16[2,96,768]{2,1,0:T(8,128)(2,1)S(1)}, u32[]{:S(2)}, u32[]{:S(2)}) collective-permute-start(bf16[2,96,768]{2,1,0:T(8,128)(2,1)S(1)} %get-tuple-element.86), channel_id=1, source_target_pairs={{0,192},{2,194},{4,196},{6,198},{8,200},{10,202},{12,204},{14,206}... | collective-permute-start | bytes 884744 | tf_op jit(solution)/shard_map/ppermute | solution.py:331
  45.5 11.3 %collective-permute-start.9 = (bf16[2,96,768]{2,1,0:T(8,128)(2,1)S(1)}, bf16[2,96,768]{2,1,0:T(8,128)(2,1)S(1)}, u32[]{:S(2)}, u32[]{:S(2)}) collective-permute-start(bf16[2,96,768]{2,1,0:T(8,128)(2,1)S(1)} %get-tuple-element.86), channel_id=1, source_target_pairs={{0,64},{2,66},{4,68},{6,70},{8,72},{10,74},{12,76},{14,78},{16,80}... | collective-permute-start | bytes 884744 | tf_op jit(solution)/shard_map/ppermute | solution.py:331
  46.9 9.9 %collective-permute-start.3 = (bf16[2,96,768]{2,1,0:T(8,128)(2,1)S(1)}, bf16[2,96,768]{2,1,0:T(8,128)(2,1)S(1)}, u32[]{:S(2)}, u32[]{:S(2)}) collective-permute-start(bf16[2,96,768]{2,1,0:T(8,128)(2,1)S(1)} %pad_maximum_fusion.1), channel_id=1, source_target_pairs={{0,16},{2,18},{4,20},{6,22},{8,24},{10,26},{12,28},{14,30},{16,32}... | collective-permute-start | bytes 884744 | tf_op jit(solution)/shard_map/ppermute | solution.py:331
  66.6 25.4 %collective-permute-start.21 = (bf16[2,384,768]{2,1,0:T(8,128)(2,1)S(1)}, bf16[2,384,768]{2,1,0:T(8,128)(2,1)S(1)}, u32[]{:S(2)}, u32[]{:S(2)}) collective-permute-start(bf16[2,384,768]{2,1,0:T(8,128)(2,1)S(1)} %constant_dynamic-update-slice_fusion.19), channel_id=1, source_target_pairs={{0,16},{2,18},{4,20},{6,22},{8,24},{10,26},{12,28},{14,30},{16,32}... | collective-permute-start | bytes 3538952 | tf_op jit(solution)/shard_map/ppermute | solution.py:331
  66.7 25.3 %collective-permute-start.22 = (bf16[2,384,768]{2,1,0:T(8,128)(2,1)S(1)}, bf16[2,384,768]{2,1,0:T(8,128)(2,1)S(1)}, u32[]{:S(2)}, u32[]{:S(2)}) collective-permute-start(bf16[2,384,768]{2,1,0:T(8,128)(2,1)S(1)} %constant_dynamic-update-slice_fusion.19), channel_id=1, source_target_pairs={{0,48},{2,50},{4,52},{6,54},{8,56},{10,58},{12,60},{14,62},{16,0},... | collective-permute-start | bytes 3538952 | tf_op jit(solution)/shard_map/ppermute | solution.py:331
  69.4 22.6 %collective-permute-start.19 = (bf16[2,384,768]{2,1,0:T(8,128)(2,1)S(1)}, bf16[2,384,768]{2,1,0:T(8,128)(2,1)S(1)}, u32[]{:S(2)}, u32[]{:S(2)}) collective-permute-start(bf16[2,384,768]{2,1,0:T(8,128)(2,1)S(1)} %get-tuple-element.76), channel_id=1, source_target_pairs={{0,64},{2,66},{4,68},{6,70},{8,72},{10,74},{12,76},{14,78},{16,80}... | collective-permute-start | bytes 3538952 | tf_op jit(solution)/shard_map/ppermute | solution.py:331
  69.5 22.5 %collective-permute-start.20 = (bf16[2,384,768]{2,1,0:T(8,128)(2,1)S(1)}, bf16[2,384,768]{2,1,0:T(8,128)(2,1)S(1)}, u32[]{:S(2)}, u32[]{:S(2)}) collective-permute-start(bf16[2,384,768]{2,1,0:T(8,128)(2,1)S(1)} %get-tuple-element.76), channel_id=1, source_target_pairs={{0,192},{2,194},{4,196},{6,198},{8,200},{10,202},{12,204},{14,206}... | collective-permute-start | bytes 3538952 | tf_op jit(solution)/shard_map/ppermute | solution.py:331
  92.1 12.9 %collective-permute-start.23 = (bf16[2,192,768]{2,1,0:T(8,128)(2,1)S(1)}, bf16[2,192,768]{2,1,0:T(8,128)(2,1)S(1)}, u32[]{:S(2)}, u32[]{:S(2)}) collective-permute-start(bf16[2,192,768]{2,1,0:T(8,128)(2,1)S(1)} %slice.32), channel_id=1, source_target_pairs={{0,64},{2,66},{4,68},{6,70},{8,72},{10,74},{12,76},{14,78},{16,80}... | collective-permute-start | bytes 1769480 | tf_op jit(solution)/shard_map/ppermute | solution.py:331
  92.3 12.8 %collective-permute-start.24 = (bf16[2,192,768]{2,1,0:T(8,128)(2,1)S(1)}, bf16[2,192,768]{2,1,0:T(8,128)(2,1)S(1)}, u32[]{:S(2)}, u32[]{:S(2)}) collective-permute-start(bf16[2,192,768]{2,1,0:T(8,128)(2,1)S(1)} %slice.33), channel_id=1, source_target_pairs={{0,192},{2,194},{4,196},{6,198},{8,200},{10,202},{12,204},{14,206}... | collective-permute-start | bytes 1769480 | tf_op jit(solution)/shard_map/ppermute | solution.py:331
  95.0 10.0 %collective-permute-start.25 = (bf16[2,192,768]{2,1,0:T(8,128)(2,1)S(1)}, bf16[2,192,768]{2,1,0:T(8,128)(2,1)S(1)}, u32[]{:S(2)}, u32[]{:S(2)}) collective-permute-start(bf16[2,192,768]{2,1,0:T(8,128)(2,1)S(1)} %slice.34), channel_id=1, source_target_pairs={{0,16},{2,18},{4,20},{6,22},{8,24},{10,26},{12,28},{14,30},{16,32}... | collective-permute-start | bytes 1769480 | tf_op jit(solution)/shard_map/ppermute | solution.py:331
  95.2 9.9 %collective-permute-start.26 = (bf16[2,192,768]{2,1,0:T(8,128)(2,1)S(1)}, bf16[2,192,768]{2,1,0:T(8,128)(2,1)S(1)}, u32[]{:S(2)}, u32[]{:S(2)}) collective-permute-start(bf16[2,192,768]{2,1,0:T(8,128)(2,1)S(1)} %slice.35), channel_id=1, source_target_pairs={{0,48},{2,50},{4,52},{6,54},{8,56},{10,58},{12,60},{14,62},{16,0},... | collective-permute-start | bytes 1769480 | tf_op jit(solution)/shard_map/ppermute | solution.py:331
  110.9 12.7 %collective-permute-start.27 = (bf16[3,196,512]{2,1,0:T(8,128)(2,1)S(1)}, bf16[3,196,512]{2,1,0:T(8,128)(2,1)S(1)}, u32[]{:S(2)}, u32[]{:S(2)}) collective-permute-start(bf16[3,196,512]{2,1,0:T(8,128)(2,1)S(1)} %get-tuple-element.66), channel_id=1, source_target_pairs={{0,1},{1,0},{2,3},{3,2},{4,5},{5,4},{6,7},{7,6},{8,9},{9,8},{10,11... | collective-permute-start | bytes 1806344 | tf_op jit(solution)/shard_map/ppermute | solution.py:27
  124.9 12.6 %collective-permute-start.29 = (bf16[196,512]{1,0:T(8,128)(2,1)S(1)}, bf16[196,512]{1,0:T(8,128)(2,1)S(1)}, u32[]{:S(2)}, u32[]{:S(2)}) collective-permute-start(bf16[196,512]{1,0:T(8,128)(2,1)S(1)} %get-tuple-element.70), channel_id=1, source_target_pairs={{0,2},{2,4},{4,6},{6,8},{8,10},{10,12},{12,14},{14,16},{16,18},{18... | collective-permute-start | bytes 602120 | tf_op jit(solution)/shard_map/ppermute | solution.py:23
  125.0 16.9 %collective-permute-start.28 = (bf16[196,512]{1,0:T(8,128)(2,1)S(1)}, bf16[196,512]{1,0:T(8,128)(2,1)S(1)}, u32[]{:S(2)}, u32[]{:S(2)}) collective-permute-start(bf16[196,512]{1,0:T(8,128)(2,1)S(1)} %get-tuple-element.68), channel_id=1, source_target_pairs={{0,2},{2,4},{4,6},{6,8},{8,10},{10,12},{12,14},{14,16},{16,18},{18... | collective-permute-start | bytes 602120 | tf_op jit(solution)/shard_map/ppermute | solution.py:23
  137.6 14.0 %collective-permute-start.30 = (bf16[196,512]{1,0:T(8,128)(2,1)S(1)}, bf16[196,512]{1,0:T(8,128)(2,1)S(1)}, u32[]{:S(2)}, u32[]{:S(2)}) collective-permute-start(bf16[196,512]{1,0:T(8,128)(2,1)S(1)} %add_convert_fusion), channel_id=1, source_target_pairs={{0,4},{2,6},{4,8},{6,10},{8,12},{10,14},{12,16},{14,18},{16,20},{1... | collective-permute-start | bytes 602120 | tf_op jit(solution)/shard_map/ppermute | solution.py:23
  (21 other events, 170.7 us)

commit v4 on v3

--- a/solution.py
+++ b/solution.py
@@ -10,6 +10,7 @@
 TOKI = 196
 ROWS = 208
 HALF = 384
+TOP = 104
 WINDOW = 4
 SLOTS = 3
 ALL = SLOTS * ROWS
@@ -38,22 +39,19 @@
     return lax.rem(stored - place[0] + 128, 128)
 
 
-def load_tokens(image_slot, slot_images, place, mine, theirs, swap, slot):
+def padded_rows(image_slot, slot_images, place, mine, theirs, swap, target):
     which = place[1] if not swap else 1 - place[1]
-    index = window_place(image_slot, slot_images, place, slot, which)
     first = place[1] == 0
-    low = mine[index].astype(F32)
-    high = theirs[index].astype(F32)
-    return jnp.where(first, low, high), jnp.where(first, high, low)
-
-
-def padded_rows(image_slot, slot_images, place, mine, theirs, swap, target):
     for slot in range(SLOTS):
-        low, high = load_tokens(image_slot, slot_images, place, mine, theirs, swap, slot)
+        index = window_place(image_slot, slot_images, place, slot, which)
+        own, far = mine[index].astype(F32), theirs[index].astype(F32)
         base = slot * ROWS
         target[base + 192 : base + ROWS, :] = jnp.zeros((ROWS - 192, D), F32)
-        target[base : base + TOKI, :HALF] = low
-        target[base : base + TOKI, HALF:] = high
+        for part, count in ((0, TOP), (1, TOKI - TOP)):
+            rows = slice(base + part * TOP, base + part * TOP + count)
+            cols = slice(part * HALF, (part + 1) * HALF)
+            target[rows, :HALF] = jnp.where(first, own[:count, cols], far[:count, cols])
+            target[rows, HALF:] = jnp.where(first, far[:count, cols], own[:count, cols])
 
 
 def norm_into(source, gain, target):
@@ -335,9 +333,20 @@
     return lax.optimization_barrier(arrays)
 
 
-def gather_line(shard):
-    others = [along(shard, "z", by) for by in (4, 3, -3, 2, -2, 1, -1)]
-    return jnp.concatenate([shard, *others], axis=1)
+def packed_shard(features, w_in, w_out):
+    low, high = features[0, :TOP], features[0, TOP:]
+    high = jnp.pad(high, ((0, 2 * TOP - TOKI), (0, 0)))
+    return jnp.concatenate([jnp.concatenate([low, high], axis=1), w_in[0], w_out[0]], axis=0)
+
+
+def hidden_rows(shards):
+    inner = [s[-48:-24] for s in shards]
+    outer = [s[-24:] for s in shards]
+    return jnp.stack([jnp.concatenate(inner, axis=0), jnp.concatenate(outer, axis=0)])
+
+
+def three_hops(block, axis):
+    return [along(block, axis, by) for by in (1, -1, 2)]
 
 
 def first_hop(block, axis):
@@ -369,23 +378,25 @@
     w_head,
 ):
     place = jnp.stack([lax.axis_index("pairs"), lax.axis_index("side")]).astype(jnp.int32)
-    shard = jnp.concatenate([w_fc1, w_fc2], axis=0)
-    second_next = shifted(features, -2)
-    blocks = [features, shifted(features, -1), second_next, shifted(second_next, -1)]
-    mine = jnp.concatenate(blocks, axis=0)
+    (own,) = tied(packed_shard(features, w_fc1, w_fc2))
+    next2 = shifted(own, -2)
+    next1 = shifted(own, -1)
+    last1 = shifted(own[TOP:], 1)
+    last2 = shifted(own[TOP:], 2)
+    next2, next1, last1, last2 = tied(next2, next1, last1, last2)
+    next3 = shifted(next2, -1)
+    last34 = shifted(jnp.concatenate([last1, last2], axis=0), 2)
+    mine = jnp.stack([own[:TOP], next1[:TOP], next2[:TOP], next3[:TOP]])
     theirs = other_core(mine)
-    line = gather_line(shard)
-    half = line.shape[1] // 2
-    part_x, part_y = line[:, :half], line[:, half:]
+    part_x = hidden_rows([own, next1, next2, last1])
+    part_y = hidden_rows([last2, next3, last34[:48], last34[48:]])
     scalars = [image_slot, slot_images.reshape(-1), place]
-    near_x, near_y = first_hop(part_x, "x"), first_hop(part_y, "y")
+    near_x, near_y = three_hops(part_x, "x"), three_hops(part_y, "y")
     rows, triple = triple_call(scalars, mine, theirs, gain_self, w_qkv[0])
-    near_x, near_y, rows, triple, mine, theirs = tied(near_x, near_y, rows, triple, mine, theirs)
-    far_x, far_y = second_hop(*near_x, "x"), second_hop(*near_y, "y")
     key_value = memory_call(scalars, mine, theirs, gain_memory, w_memory[0])
-    far_x, far_y, key_value, rows, triple = tied(far_x, far_y, key_value, rows, triple)
-    plane_x = jnp.concatenate([part_x, *near_x, *far_x], axis=1)
-    plane_y = jnp.concatenate([part_y, *near_y, *far_y], axis=1)
+    near_x, near_y, rows, triple, key_value = tied(near_x, near_y, rows, triple, key_value)
+    plane_x = jnp.concatenate([part_x, *near_x], axis=1)
+    plane_y = jnp.concatenate([part_y, *near_y], axis=1)
     near_x, near_y = first_hop(plane_x, "y"), first_hop(plane_y, "x")
     first, query = self_call(rows, triple, gain_query, w_self_out[0], w_query[0])
     second, mlp_in = cross_call(first, query, key_value, gain_mlp, w_cross_out[0])
@@ -397,9 +408,9 @@
     keep, send = late_call(place, early, mlp_in, fc_late, gain_head, w_head[0])
     got = other_core(send)
     pieces = window_call([image_slot, slot_images.reshape(-1), slot_count, place], keep, got)
-    third = shifted(pieces[3], 1)
-    nearest = shifted(pieces[1], 1)
+    third, nearest = tied(shifted(pieces[3], 1), pieces[1])
     further = shifted((pieces[2].astype(F32) + third.astype(F32)).astype(BF16), 2)
+    nearest = shifted(nearest, 1)
     return merge_call(pieces[0], nearest, further)
 
 

time: 153 us -> 144 us (0.941)
  starting transfers between devices: 67.1 us -> 45.9 us
  waiting for transfers between devices: 32.8 us -> 50.4 us
  local copies, waits for them, and re-layouts: 9.08 us -> 3.44 us
    ppermute x23 -> x14, starting transfers between devices: 30.7 us -> 13 us  [along(): return lax.ppermute(array, 'pairs', [(p, target(p)) for p in range(count)])]
    ppermute x6 -> x9, waiting for transfers between devices: 31.7 us -> 43 us  [shifted(): lax.ppermute(array, 'pairs', [(i, (i + by) % count) for i in range(count)])]
    unnamed x58 -> x34, local copies, waits for them, and re-layouts: 8.29 us -> 1.2 us
    ppermute x23 -> x14, waiting for transfers between devices: 0.06 us -> 6.41 us  [along(): return lax.ppermute(array, 'pairs', [(p, target(p)) for p in range(count)])]
    ppermute x2, starting transfers between devices: 14.8 us -> 11.3 us  [other_core(): return lax.ppermute(array, 'side', [(0, 1), (1, 0)])]
    squeeze x0 -> x2, local copies, waits for them, and re-layouts: none -> 1.79 us  [packed_shard(): low, high = (features[0, :TOP], features[0, TOP:])]
    ppermute x6 -> x9, starting transfers between devices: 21.6 us -> 21.6 us  [shifted(): lax.ppermute(array, 'pairs', [(i, (i + by) % count) for i in range(count)])]
  transfers between devices with their start and end apart: 31 -> 25, of which waited for: 7 -> 12; matrix products, arithmetic and copies ran while one was open for 3% -> 1% of each run, Pallas kernels for 23% -> 24%
where the time goes in v4:
time: 144 us
  waiting for transfers between devices  50.4 us (35%)
  starting transfers between devices  45.9 us (32%)
  Pallas kernels  41.6 us (29%)
  local copies, waits for them, and re-layouts  3.44 us (2%)
  other arithmetic  1.48 us (1%)
    ppermute x9, waiting for transfers between devices, shifted(): lax.ppermute(array, 'pairs', [(i, (i + by) % count) for i in range(count)])  43 us
    pallas_call x8, Pallas kernels, call(): pl.pallas_call(kernel, in_specs=[SMEM] * len(scalars) + [VMEM] * len(arra...  41.6 us
    ppermute x9, starting transfers between devices, shifted(): lax.ppermute(array, 'pairs', [(i, (i + by) % count) for i in range(count)])  21.6 us
    ppermute x14, starting transfers between devices, along(): return lax.ppermute(array, 'pairs', [(p, target(p)) for p in range(count)])  13 us
    ppermute x2, starting transfers between devices, other_core(): return lax.ppermute(array, 'side', [(0, 1), (1, 0)])  11.3 us
    ppermute x14, waiting for transfers between devices, along(): return lax.ppermute(array, 'pairs', [(p, target(p)) for p in range(count)])  6.41 us
  transfers between devices with their start and end apart: 25, of which 12 were waited for; matrix products, arithmetic and copies ran while one was open for 1% of the time, Pallas kernels for 24%

profile of v4, /device:TPU:1, one launch (start us, length us, event | category | flops | bytes accessed | tf_op | source)
XLA Modules:
  0.0 144.1 jit_solution(6270543303814732497)
XLA Ops:
  2.6 3.9 %collective-permute-start.3 = (bf16[48,768]{1,0:T(8,128)(2,1)S(1)}, bf16[48,768]{1,0:T(8,128)(2,1)S(1)}, u32[]{:S(2)}, u32[]{:S(2)}) collective-permute-start(bf16[48,768]{1,0:T(8,128)(2,1)S(1)} %slice.116), channel_id=1, source_target_pairs={{0,4},{2,6},{4,8},{6,10},{8,12},{10,14},{12,16},{14,18},{16,20},{1... | collective-permute-start | bytes 221192 | tf_op jit(solution)/shard_map/ppermute | solution.py:24
  6.5 1.6 %collective-permute-start.2 = (bf16[48,768]{1,0:T(8,128)(2,1)S(1)}, bf16[48,768]{1,0:T(8,128)(2,1)S(1)}, u32[]{:S(2)}, u32[]{:S(2)}) collective-permute-start(bf16[48,768]{1,0:T(8,128)(2,1)S(1)} %slice.116), channel_id=1, source_target_pairs={{0,2},{2,4},{4,6},{6,8},{8,10},{10,12},{12,14},{14,16},{16,18},{18... | collective-permute-start | bytes 221192 | tf_op jit(solution)/shard_map/ppermute | solution.py:24
  8.1 5.8 %collective-permute-start.1 = (bf16[152,768]{1,0:T(8,128)(2,1)S(1)}, bf16[152,768]{1,0:T(8,128)(2,1)S(1)}, u32[]{:S(2)}, u32[]{:S(2)}) collective-permute-start(bf16[152,768]{1,0:T(8,128)(2,1)S(1)} %fusion.5), channel_id=1, source_target_pairs={{0,254},{2,0},{4,2},{6,4},{8,6},{10,8},{12,10},{14,12},{16,14},{18... | collective-permute-start | bytes 700424 | tf_op jit(solution)/shard_map/ppermute | solution.py:24
  13.9 2.2 %collective-permute-start = (bf16[152,768]{1,0:T(8,128)(2,1)S(1)}, bf16[152,768]{1,0:T(8,128)(2,1)S(1)}, u32[]{:S(2)}, u32[]{:S(2)}) collective-permute-start(bf16[152,768]{1,0:T(8,128)(2,1)S(1)} %fusion.5), channel_id=1, source_target_pairs={{0,252},{2,254},{4,0},{6,2},{8,4},{10,6},{12,8},{14,10},{16,12},{1... | collective-permute-start | bytes 700424 | tf_op jit(solution)/shard_map/ppermute | solution.py:24
  17.1 2.1 %collective-permute-done.2 = bf16[48,768]{1,0:T(8,128)(2,1)S(1)} collective-permute-done((bf16[48,768]{1,0:T(8,128)(2,1)S(1)}, bf16[48,768]{1,0:T(8,128)(2,1)S(1)}, u32[]{:S(2)}, u32[]{:S(2)}) %collective-permute-start.2) | collective-permute-done | bytes 73760 | tf_op jit(solution)/shard_map/ppermute | solution.py:24
  20.6 7.6 %collective-permute-done = bf16[152,768]{1,0:T(8,128)(2,1)S(1)} collective-permute-done((bf16[152,768]{1,0:T(8,128)(2,1)S(1)}, bf16[152,768]{1,0:T(8,128)(2,1)S(1)}, u32[]{:S(2)}, u32[]{:S(2)}) %collective-permute-start) | collective-permute-done | bytes 233504 | tf_op jit(solution)/shard_map/ppermute | solution.py:24
  28.3 2.7 %collective-permute-start.7 = (bf16[152,768]{1,0:T(8,128)(2,1)S(1)}, bf16[152,768]{1,0:T(8,128)(2,1)S(1)}, u32[]{:S(2)}, u32[]{:S(2)}) collective-permute-start(bf16[152,768]{1,0:T(8,128)(2,1)S(1)} %collective-permute-done), channel_id=1, source_target_pairs={{0,254},{2,0},{4,2},{6,4},{8,6},{10,8},{12,10},{14,12},{16,14},{18... | collective-permute-start | bytes 700424 | tf_op jit(solution)/shard_map/ppermute | solution.py:24
  31.3 1.5 %collective-permute-start.4 = (bf16[2,96,768]{2,1,0:T(8,128)(2,1)S(1)}, bf16[2,96,768]{2,1,0:T(8,128)(2,1)S(1)}, u32[]{:S(2)}, u32[]{:S(2)}) collective-permute-start(bf16[2,96,768]{2,1,0:T(8,128)(2,1)S(1)} %get-tuple-element.72), channel_id=1, source_target_pairs={{0,16},{2,18},{4,20},{6,22},{8,24},{10,26},{12,28},{14,30},{16,32}... | collective-permute-start | bytes 884744 | tf_op jit(solution)/shard_map/ppermute | solution.py:329
  34.1 4.4 %collective-permute-start.12 = (bf16[4,104,768]{2,1,0:T(8,128)(2,1)S(1)}, bf16[4,104,768]{2,1,0:T(8,128)(2,1)S(1)}, u32[]{:S(2)}, u32[]{:S(2)}) collective-permute-start(bf16[4,104,768]{2,1,0:T(8,128)(2,1)S(1)} %pad_maximum_fusion.3.mine), channel_id=1, source_target_pairs={{0,1},{1,0},{2,3},{3,2},{4,5},{5,4},{6,7},{7,6},{8,9},{9,8},{10,11... | collective-permute-start | bytes 1916936 | tf_op jit(solution)/shard_map/ppermute | solution.py:28
  38.5 5.0 %collective-permute-done.8 = bf16[96,768]{1,0:T(8,128)(2,1)S(1)} collective-permute-done((bf16[96,768]{1,0:T(8,128)(2,1)S(1)}, bf16[96,768]{1,0:T(8,128)(2,1)S(1)}, u32[]{:S(2)}, u32[]{:S(2)}) %collective-permute-start.8) | collective-permute-done | bytes 147488 | tf_op jit(solution)/shard_map/ppermute | solution.py:24
  45.5 5.0 %triple_part.1 = (f32[624,768]{1,0:T(8,128)S(1)}, bf16[624,2304]{1,0:T(8,128)(2,1)S(1)}) custom-call(s32[128]{0:T(128)S(1)} %copy-done, s32[6]{0:T(128)S(1)} %reshape.4.slot_images, s32[2]{0:T(128)S(1)} %pad_add_fusion.place, bf16[4,104,768]{2,1,0:T(8,128)(2,1)S(1)} %pad_maximum_fusion.3.mine, bf16[4,104,768]{2,1,0:T(8,128)(2,1)S(1)} %collective-permute-done.12.theirs, ...), custom_call_target="tpu_custom_call" | custom-call | flops 4000000000 | bytes 8388608 | tf_op jit(solution)/shard_map/triple_part/pallas_call | solution.py:250
  50.5 3.7 %memory_part.1.key_value = bf16[624,1536]{1,0:T(8,128)(2,1)S(1)} custom-call(s32[128]{0:T(128)S(1)} %copy-done, s32[6]{0:T(128)S(1)} %reshape.4.slot_images, s32[2]{0:T(128)S(1)} %pad_add_fusion.place, bf16[4,104,768]{2,1,0:T(8,128)(2,1)S(1)} %pad_maximum_fusion.3.mine, bf16[4,104,768]{2,1,0:T(8,128)(2,1)S(1)} %collective-permute-done.12.theirs, ...), custom_call_target="tpu_custom_call" | custom-call | flops 3000000000 | bytes 8388608 | tf_op jit(solution)/shard_map/memory_part/pallas_call | solution.py:250
  54.8 3.5 %collective-permute-start.16 = (bf16[2,384,768]{2,1,0:T(8,128)(2,1)S(1)}, bf16[2,384,768]{2,1,0:T(8,128)(2,1)S(1)}, u32[]{:S(2)}, u32[]{:S(2)}) collective-permute-start(bf16[2,384,768]{2,1,0:T(8,128)(2,1)S(1)} %pad_maximum_fusion.2), channel_id=1, source_target_pairs={{0,48},{2,50},{4,52},{6,54},{8,56},{10,58},{12,60},{14,62},{16,0},... | collective-permute-start | bytes 3538952 | tf_op jit(solution)/shard_map/ppermute | solution.py:329
  60.1 10.5 %self_part.1 = (f32[624,768]{1,0:T(8,128)S(1)}, bf16[624,768]{1,0:T(8,128)(2,1)S(1)}) custom-call(f32[624,768]{1,0:T(8,128)S(1)} %get-tuple-element.50.rows, bf16[624,2304]{1,0:T(8,128)(2,1)S(1)} %get-tuple-element.51.triple, f32[1,768]{1,0:T(1,128)S(1)} %copy-done.9, bf16[768,768]{1,0:T(8,128)(2,1)S(1)} %bitcast.33, bf16[768,768]{1,0:T(8,128)(2,1)S(1)} %bitcast.34), custom_call_target="tpu_custom_call" | custom-call | flops 12000000000 | bytes 8388608 | tf_op jit(solution)/shard_map/self_part/pallas_call | solution.py:250
  70.7 9.2 %cross_part.1 = (f32[624,768]{1,0:T(8,128)S(1)}, bf16[624,768]{1,0:T(8,128)(2,1)S(1)}) custom-call(f32[624,768]{1,0:T(8,128)S(1)} %get-tuple-element.52.first, bf16[624,768]{1,0:T(8,128)(2,1)S(1)} %get-tuple-element.53.query, bf16[624,1536]{1,0:T(8,128)(2,1)S(1)} %memory_part.1.key_value, f32[1,768]{1,0:T(1,128)S(1)} %copy-done.10, bf16[768,768]{1,0:T(8,128)(2,1)S(1)} %bitcast.35), custom_call_target="tpu_custom_call" | custom-call | flops 12000000000 | bytes 8388608 | tf_op jit(solution)/shard_map/cross_part/pallas_call | solution.py:250
  80.0 3.0 %collective-permute-done.15 = bf16[2,384,768]{2,1,0:T(8,128)(2,1)S(1)} collective-permute-done((bf16[2,384,768]{2,1,0:T(8,128)(2,1)S(1)}, bf16[2,384,768]{2,1,0:T(8,128)(2,1)S(1)}, u32[]{:S(2)}, u32[]{:S(2)}) %collective-permute-start.15) | collective-permute-done | bytes 1179680 | tf_op jit(solution)/shard_map/ppermute | solution.py:329
  83.7 3.0 %collective-permute-start.20 = (bf16[2,192,768]{2,1,0:T(8,128)(2,1)S(1)}, bf16[2,192,768]{2,1,0:T(8,128)(2,1)S(1)}, u32[]{:S(2)}, u32[]{:S(2)}) collective-permute-start(bf16[2,192,768]{2,1,0:T(8,128)(2,1)S(1)} %slice.114), channel_id=1, source_target_pairs={{0,48},{2,50},{4,52},{6,54},{8,56},{10,58},{12,60},{14,62},{16,0},... | collective-permute-start | bytes 1769480 | tf_op jit(solution)/shard_map/ppermute | solution.py:329
  88.2 6.5 %early_part.1.early = f32[624,768]{1,0:T(8,128)S(1)} custom-call(f32[624,768]{1,0:T(8,128)S(1)} %get-tuple-element.57.second, bf16[624,768]{1,0:T(8,128)(2,1)S(1)} %get-tuple-element.58.mlp_in, bf16[2,2304,768]{2,1,0:T(8,128)(2,1)S(1)} %constant_dynamic-update-slice_fusion.fc), custom_call_target="tpu_custom_call" | custom-call | flops 10000000000 | bytes 8388608 | tf_op jit(solution)/shard_map/early_part/pallas_call | solution.py:250
  94.8 2.8 %collective-permute-done.19 = bf16[2,192,768]{2,1,0:T(8,128)(2,1)S(1)} collective-permute-done((bf16[2,192,768]{2,1,0:T(8,128)(2,1)S(1)}, bf16[2,192,768]{2,1,0:T(8,128)(2,1)S(1)}, u32[]{:S(2)}, u32[]{:S(2)}) %collective-permute-start.19) | collective-permute-done | bytes 589856 | tf_op jit(solution)/shard_map/ppermute | solution.py:329
  97.8 4.4 %late_part.1 = (f32[3,196,512]{2,1,0:T(8,128)S(1)}, bf16[3,196,512]{2,1,0:T(8,128)(2,1)S(1)}) custom-call(s32[2]{0:T(128)S(1)} %pad_add_fusion.place, f32[624,768]{1,0:T(8,128)S(1)} %early_part.1.early, bf16[624,768]{1,0:T(8,128)(2,1)S(1)} %get-tuple-element.58.mlp_in, bf16[2,768,768]{2,1,0:T(8,128)(2,1)S(1)} %pad_maximum_fusion.fc, ...), custom_call_target="tpu_custom_call" | custom-call | flops 5000000000 | bytes 8388608 | tf_op jit(solution)/shard_map/late_part/pallas_call | solution.py:250
  102.2 6.9 %collective-permute-start.21 = (bf16[3,196,512]{2,1,0:T(8,128)(2,1)S(1)}, bf16[3,196,512]{2,1,0:T(8,128)(2,1)S(1)}, u32[]{:S(2)}, u32[]{:S(2)}) collective-permute-start(bf16[3,196,512]{2,1,0:T(8,128)(2,1)S(1)} %get-tuple-element.64), channel_id=1, source_target_pairs={{0,1},{1,0},{2,3},{3,2},{4,5},{5,4},{6,7},{7,6},{8,9},{9,8},{10,11... | collective-permute-start | bytes 1806344 | tf_op jit(solution)/shard_map/ppermute | solution.py:28
  112.2 4.6 %collective-permute-start.22 = (bf16[196,512]{1,0:T(8,128)(2,1)S(1)}, bf16[196,512]{1,0:T(8,128)(2,1)S(1)}, u32[]{:S(2)}, u32[]{:S(2)}) collective-permute-start(bf16[196,512]{1,0:T(8,128)(2,1)S(1)} %get-tuple-element.66), channel_id=1, source_target_pairs={{0,2},{2,4},{4,6},{6,8},{8,10},{10,12},{12,14},{14,16},{16,18},{18... | collective-permute-start | bytes 602120 | tf_op jit(solution)/shard_map/ppermute | solution.py:24
  116.7 10.8 %collective-permute-done.22 = bf16[196,512]{1,0:T(8,128)(2,1)S(1)} collective-permute-done((bf16[196,512]{1,0:T(8,128)(2,1)S(1)}, bf16[196,512]{1,0:T(8,128)(2,1)S(1)}, u32[]{:S(2)}, u32[]{:S(2)}) %collective-permute-start.22) | collective-permute-done | bytes 200736 | tf_op jit(solution)/shard_map/ppermute | solution.py:24
  127.8 15.5 %collective-permute-done.24.further = bf16[196,512]{1,0:T(8,128)(2,1)S(1)} collective-permute-done((bf16[196,512]{1,0:T(8,128)(2,1)S(1)}, bf16[196,512]{1,0:T(8,128)(2,1)S(1)}, u32[]{:S(2)}, u32[]{:S(2)}) %collective-permute-start.24) | collective-permute-done | bytes 200736 | tf_op jit(solution)/shard_map/ppermute | solution.py:24
  (100 shorter events, 16.5 us)
Async XLA Ops:
  2.6 14.4 %collective-permute-start.3 = (bf16[48,768]{1,0:T(8,128)(2,1)S(1)}, bf16[48,768]{1,0:T(8,128)(2,1)S(1)}, u32[]{:S(2)}, u32[]{:S(2)}) collective-permute-start(bf16[48,768]{1,0:T(8,128)(2,1)S(1)} %slice.116), channel_id=1, source_target_pairs={{0,4},{2,6},{4,8},{6,10},{8,12},{10,14},{12,16},{14,18},{16,20},{1... | collective-permute-start | bytes 221192 | tf_op jit(solution)/shard_map/ppermute | solution.py:24
  6.5 12.7 %collective-permute-start.2 = (bf16[48,768]{1,0:T(8,128)(2,1)S(1)}, bf16[48,768]{1,0:T(8,128)(2,1)S(1)}, u32[]{:S(2)}, u32[]{:S(2)}) collective-permute-start(bf16[48,768]{1,0:T(8,128)(2,1)S(1)} %slice.116), channel_id=1, source_target_pairs={{0,2},{2,4},{4,6},{6,8},{8,10},{10,12},{12,14},{14,16},{16,18},{18... | collective-permute-start | bytes 221192 | tf_op jit(solution)/shard_map/ppermute | solution.py:24
  8.1 12.5 %collective-permute-start.1 = (bf16[152,768]{1,0:T(8,128)(2,1)S(1)}, bf16[152,768]{1,0:T(8,128)(2,1)S(1)}, u32[]{:S(2)}, u32[]{:S(2)}) collective-permute-start(bf16[152,768]{1,0:T(8,128)(2,1)S(1)} %fusion.5), channel_id=1, source_target_pairs={{0,254},{2,0},{4,2},{6,4},{8,6},{10,8},{12,10},{14,12},{16,14},{18... | collective-permute-start | bytes 700424 | tf_op jit(solution)/shard_map/ppermute | solution.py:24
  13.9 14.3 %collective-permute-start = (bf16[152,768]{1,0:T(8,128)(2,1)S(1)}, bf16[152,768]{1,0:T(8,128)(2,1)S(1)}, u32[]{:S(2)}, u32[]{:S(2)}) collective-permute-start(bf16[152,768]{1,0:T(8,128)(2,1)S(1)} %fusion.5), channel_id=1, source_target_pairs={{0,252},{2,254},{4,0},{6,2},{8,4},{10,6},{12,8},{14,10},{16,12},{1... | collective-permute-start | bytes 700424 | tf_op jit(solution)/shard_map/ppermute | solution.py:24
  31.1 12.9 %collective-permute-start.6 = (bf16[2,96,768]{2,1,0:T(8,128)(2,1)S(1)}, bf16[2,96,768]{2,1,0:T(8,128)(2,1)S(1)}, u32[]{:S(2)}, u32[]{:S(2)}) collective-permute-start(bf16[2,96,768]{2,1,0:T(8,128)(2,1)S(1)} %get-tuple-element.72), channel_id=1, source_target_pairs={{0,32},{2,34},{4,36},{6,38},{8,40},{10,42},{12,44},{14,46},{16,48}... | collective-permute-start | bytes 884744 | tf_op jit(solution)/shard_map/ppermute | solution.py:329
  31.2 23.1 %collective-permute-start.5 = (bf16[2,96,768]{2,1,0:T(8,128)(2,1)S(1)}, bf16[2,96,768]{2,1,0:T(8,128)(2,1)S(1)}, u32[]{:S(2)}, u32[]{:S(2)}) collective-permute-start(bf16[2,96,768]{2,1,0:T(8,128)(2,1)S(1)} %get-tuple-element.72), channel_id=1, source_target_pairs={{0,48},{2,50},{4,52},{6,54},{8,56},{10,58},{12,60},{14,62},{16,0},... | collective-permute-start | bytes 884744 | tf_op jit(solution)/shard_map/ppermute | solution.py:329
  31.3 23.0 %collective-permute-start.4 = (bf16[2,96,768]{2,1,0:T(8,128)(2,1)S(1)}, bf16[2,96,768]{2,1,0:T(8,128)(2,1)S(1)}, u32[]{:S(2)}, u32[]{:S(2)}) collective-permute-start(bf16[2,96,768]{2,1,0:T(8,128)(2,1)S(1)} %get-tuple-element.72), channel_id=1, source_target_pairs={{0,16},{2,18},{4,20},{6,22},{8,24},{10,26},{12,28},{14,30},{16,32}... | collective-permute-start | bytes 884744 | tf_op jit(solution)/shard_map/ppermute | solution.py:329
  32.8 10.8 %collective-permute-start.8 = (bf16[96,768]{1,0:T(8,128)(2,1)S(1)}, bf16[96,768]{1,0:T(8,128)(2,1)S(1)}, u32[]{:S(2)}, u32[]{:S(2)}) collective-permute-start(bf16[96,768]{1,0:T(8,128)(2,1)S(1)} %pad_maximum_fusion.6), channel_id=1, source_target_pairs={{0,4},{2,6},{4,8},{6,10},{8,12},{10,14},{12,16},{14,18},{16,20},{1... | collective-permute-start | bytes 442376 | tf_op jit(solution)/shard_map/ppermute | solution.py:24
  34.1 11.0 %collective-permute-start.12 = (bf16[4,104,768]{2,1,0:T(8,128)(2,1)S(1)}, bf16[4,104,768]{2,1,0:T(8,128)(2,1)S(1)}, u32[]{:S(2)}, u32[]{:S(2)}) collective-permute-start(bf16[4,104,768]{2,1,0:T(8,128)(2,1)S(1)} %pad_maximum_fusion.3.mine), channel_id=1, source_target_pairs={{0,1},{1,0},{2,3},{3,2},{4,5},{5,4},{6,7},{7,6},{8,9},{9,8},{10,11... | collective-permute-start | bytes 1916936 | tf_op jit(solution)/shard_map/ppermute | solution.py:28
  43.6 10.7 %collective-permute-start.11 = (bf16[2,96,768]{2,1,0:T(8,128)(2,1)S(1)}, bf16[2,96,768]{2,1,0:T(8,128)(2,1)S(1)}, u32[]{:S(2)}, u32[]{:S(2)}) collective-permute-start(bf16[2,96,768]{2,1,0:T(8,128)(2,1)S(1)} %pad_maximum_fusion.5), channel_id=1, source_target_pairs={{0,128},{2,130},{4,132},{6,134},{8,136},{10,138},{12,140},{14,142}... | collective-permute-start | bytes 884744 | tf_op jit(solution)/shard_map/ppermute | solution.py:329
  44.0 10.3 %collective-permute-start.10 = (bf16[2,96,768]{2,1,0:T(8,128)(2,1)S(1)}, bf16[2,96,768]{2,1,0:T(8,128)(2,1)S(1)}, u32[]{:S(2)}, u32[]{:S(2)}) collective-permute-start(bf16[2,96,768]{2,1,0:T(8,128)(2,1)S(1)} %pad_maximum_fusion.5), channel_id=1, source_target_pairs={{0,192},{2,194},{4,196},{6,198},{8,200},{10,202},{12,204},{14,206}... | collective-permute-start | bytes 884744 | tf_op jit(solution)/shard_map/ppermute | solution.py:329
  45.0 9.7 %collective-permute-start.9 = (bf16[2,96,768]{2,1,0:T(8,128)(2,1)S(1)}, bf16[2,96,768]{2,1,0:T(8,128)(2,1)S(1)}, u32[]{:S(2)}, u32[]{:S(2)}) collective-permute-start(bf16[2,96,768]{2,1,0:T(8,128)(2,1)S(1)} %pad_maximum_fusion.5), channel_id=1, source_target_pairs={{0,64},{2,66},{4,68},{6,70},{8,72},{10,74},{12,76},{14,78},{16,80}... | collective-permute-start | bytes 884744 | tf_op jit(solution)/shard_map/ppermute | solution.py:329
  54.8 25.2 %collective-permute-start.16 = (bf16[2,384,768]{2,1,0:T(8,128)(2,1)S(1)}, bf16[2,384,768]{2,1,0:T(8,128)(2,1)S(1)}, u32[]{:S(2)}, u32[]{:S(2)}) collective-permute-start(bf16[2,384,768]{2,1,0:T(8,128)(2,1)S(1)} %pad_maximum_fusion.2), channel_id=1, source_target_pairs={{0,48},{2,50},{4,52},{6,54},{8,56},{10,58},{12,60},{14,62},{16,0},... | collective-permute-start | bytes 3538952 | tf_op jit(solution)/shard_map/ppermute | solution.py:329
  58.3 24.7 %collective-permute-start.15 = (bf16[2,384,768]{2,1,0:T(8,128)(2,1)S(1)}, bf16[2,384,768]{2,1,0:T(8,128)(2,1)S(1)}, u32[]{:S(2)}, u32[]{:S(2)}) collective-permute-start(bf16[2,384,768]{2,1,0:T(8,128)(2,1)S(1)} %pad_maximum_fusion.2), channel_id=1, source_target_pairs={{0,16},{2,18},{4,20},{6,22},{8,24},{10,26},{12,28},{14,30},{16,32}... | collective-permute-start | bytes 3538952 | tf_op jit(solution)/shard_map/ppermute | solution.py:329
  58.4 24.6 %collective-permute-start.14 = (bf16[2,384,768]{2,1,0:T(8,128)(2,1)S(1)}, bf16[2,384,768]{2,1,0:T(8,128)(2,1)S(1)}, u32[]{:S(2)}, u32[]{:S(2)}) collective-permute-start(bf16[2,384,768]{2,1,0:T(8,128)(2,1)S(1)} %pad_maximum_fusion.1), channel_id=1, source_target_pairs={{0,192},{2,194},{4,196},{6,198},{8,200},{10,202},{12,204},{14,206}... | collective-permute-start | bytes 3538952 | tf_op jit(solution)/shard_map/ppermute | solution.py:329
  58.6 24.5 %collective-permute-start.13 = (bf16[2,384,768]{2,1,0:T(8,128)(2,1)S(1)}, bf16[2,384,768]{2,1,0:T(8,128)(2,1)S(1)}, u32[]{:S(2)}, u32[]{:S(2)}) collective-permute-start(bf16[2,384,768]{2,1,0:T(8,128)(2,1)S(1)} %pad_maximum_fusion.1), channel_id=1, source_target_pairs={{0,64},{2,66},{4,68},{6,70},{8,72},{10,74},{12,76},{14,78},{16,80}... | collective-permute-start | bytes 3538952 | tf_op jit(solution)/shard_map/ppermute | solution.py:329
  83.7 11.1 %collective-permute-start.20 = (bf16[2,192,768]{2,1,0:T(8,128)(2,1)S(1)}, bf16[2,192,768]{2,1,0:T(8,128)(2,1)S(1)}, u32[]{:S(2)}, u32[]{:S(2)}) collective-permute-start(bf16[2,192,768]{2,1,0:T(8,128)(2,1)S(1)} %slice.114), channel_id=1, source_target_pairs={{0,48},{2,50},{4,52},{6,54},{8,56},{10,58},{12,60},{14,62},{16,0},... | collective-permute-start | bytes 1769480 | tf_op jit(solution)/shard_map/ppermute | solution.py:329
  86.7 10.9 %collective-permute-start.19 = (bf16[2,192,768]{2,1,0:T(8,128)(2,1)S(1)}, bf16[2,192,768]{2,1,0:T(8,128)(2,1)S(1)}, u32[]{:S(2)}, u32[]{:S(2)}) collective-permute-start(bf16[2,192,768]{2,1,0:T(8,128)(2,1)S(1)} %slice.113), channel_id=1, source_target_pairs={{0,16},{2,18},{4,20},{6,22},{8,24},{10,26},{12,28},{14,30},{16,32}... | collective-permute-start | bytes 1769480 | tf_op jit(solution)/shard_map/ppermute | solution.py:329
  86.7 10.9 %collective-permute-start.18 = (bf16[2,192,768]{2,1,0:T(8,128)(2,1)S(1)}, bf16[2,192,768]{2,1,0:T(8,128)(2,1)S(1)}, u32[]{:S(2)}, u32[]{:S(2)}) collective-permute-start(bf16[2,192,768]{2,1,0:T(8,128)(2,1)S(1)} %slice.112), channel_id=1, source_target_pairs={{0,192},{2,194},{4,196},{6,198},{8,200},{10,202},{12,204},{14,206}... | collective-permute-start | bytes 1769480 | tf_op jit(solution)/shard_map/ppermute | solution.py:329
  86.8 10.8 %collective-permute-start.17 = (bf16[2,192,768]{2,1,0:T(8,128)(2,1)S(1)}, bf16[2,192,768]{2,1,0:T(8,128)(2,1)S(1)}, u32[]{:S(2)}, u32[]{:S(2)}) collective-permute-start(bf16[2,192,768]{2,1,0:T(8,128)(2,1)S(1)} %slice.111), channel_id=1, source_target_pairs={{0,64},{2,66},{4,68},{6,70},{8,72},{10,74},{12,76},{14,78},{16,80}... | collective-permute-start | bytes 1769480 | tf_op jit(solution)/shard_map/ppermute | solution.py:329
  102.2 8.6 %collective-permute-start.21 = (bf16[3,196,512]{2,1,0:T(8,128)(2,1)S(1)}, bf16[3,196,512]{2,1,0:T(8,128)(2,1)S(1)}, u32[]{:S(2)}, u32[]{:S(2)}) collective-permute-start(bf16[3,196,512]{2,1,0:T(8,128)(2,1)S(1)} %get-tuple-element.64), channel_id=1, source_target_pairs={{0,1},{1,0},{2,3},{3,2},{4,5},{5,4},{6,7},{7,6},{8,9},{9,8},{10,11... | collective-permute-start | bytes 1806344 | tf_op jit(solution)/shard_map/ppermute | solution.py:28
  112.2 15.4 %collective-permute-start.22 = (bf16[196,512]{1,0:T(8,128)(2,1)S(1)}, bf16[196,512]{1,0:T(8,128)(2,1)S(1)}, u32[]{:S(2)}, u32[]{:S(2)}) collective-permute-start(bf16[196,512]{1,0:T(8,128)(2,1)S(1)} %get-tuple-element.66), channel_id=1, source_target_pairs={{0,2},{2,4},{4,6},{6,8},{8,10},{10,12},{12,14},{14,16},{16,18},{18... | collective-permute-start | bytes 602120 | tf_op jit(solution)/shard_map/ppermute | solution.py:24
  127.6 15.7 %collective-permute-start.24 = (bf16[196,512]{1,0:T(8,128)(2,1)S(1)}, bf16[196,512]{1,0:T(8,128)(2,1)S(1)}, u32[]{:S(2)}, u32[]{:S(2)}) collective-permute-start(bf16[196,512]{1,0:T(8,128)(2,1)S(1)} %add_convert_fusion), channel_id=1, source_target_pairs={{0,4},{2,6},{4,8},{6,10},{8,12},{10,14},{12,16},{14,18},{16,20},{1... | collective-permute-start | bytes 602120 | tf_op jit(solution)/shard_map/ppermute | solution.py:24
  127.7 15.6 %collective-permute-start.23 = (bf16[196,512]{1,0:T(8,128)(2,1)S(1)}, bf16[196,512]{1,0:T(8,128)(2,1)S(1)}, u32[]{:S(2)}, u32[]{:S(2)}) collective-permute-start(bf16[196,512]{1,0:T(8,128)(2,1)S(1)} %get-tuple-element.68), channel_id=1, source_target_pairs={{0,2},{2,4},{4,6},{6,8},{8,10},{10,12},{12,14},{14,16},{16,18},{18... | collective-permute-start | bytes 602120 | tf_op jit(solution)/shard_map/ppermute | solution.py:24
  (13 other events, 102.0 us)

commit v5 on v4

--- a/solution.py
+++ b/solution.py
@@ -242,6 +242,28 @@
         out[0, :, cols] = (total(cols) / weight).astype(BF16)
 
 
+def pack_kernel(
+    features, w_in, w_out, packed, shard, features_here, w_in_here, w_out_here, sems
+):
+    copies = [
+        pltpu.make_async_copy(src, dst, sems.at[i])
+        for i, (src, dst) in enumerate(
+            ((features, features_here), (w_in, w_in_here), (w_out, w_out_here))
+        )
+    ]
+    for copy in copies:
+        copy.start()
+    for copy in copies:
+        copy.wait()
+    count = TOKI - TOP
+    packed[88:TOP, HALF:] = jnp.zeros((TOP - 88, HALF), BF16)
+    packed[:TOP, :HALF] = features_here[0, :TOP]
+    packed[:count, HALF:] = features_here[0, TOP:]
+    for target, base in ((packed, TOP), (shard, 0)):
+        target[base : base + 24] = w_in_here[0]
+        target[base + 24 : base + 48] = w_out_here[0]
+
+
 SMEM = pl.BlockSpec(memory_space=pltpu.SMEM)
 VMEM = pl.BlockSpec(memory_space=pltpu.VMEM)
 
@@ -314,6 +336,23 @@
     )
 
 
+def pack_call(features, w_in, w_out):
+    outs = [((TOP + 48, D), BF16), ((48, D), BF16)]
+    return pl.pallas_call(
+        pack_kernel,
+        in_specs=[pl.BlockSpec(memory_space=pltpu.MemorySpace.HBM)] * 3,
+        out_specs=[VMEM] * 2,
+        out_shape=[jax.ShapeDtypeStruct(s, d) for s, d in outs],
+        scratch_shapes=[
+            pltpu.VMEM((1, TOKI, HALF), BF16),
+            pltpu.VMEM((1, 24, D), BF16),
+            pltpu.VMEM((1, 24, D), BF16),
+            pltpu.SemaphoreType.DMA((3,)),
+        ],
+        name="pack_part",
+    )(features, w_in, w_out)
+
+
 def merge_call(*arrays):
     return call(merge_kernel, [], arrays, [((1, TOKI, HALF), BF16)], [], 10**8, "merge_part")[0]
 
@@ -331,12 +370,6 @@
 
 def tied(*arrays):
     return lax.optimization_barrier(arrays)
-
-
-def packed_shard(features, w_in, w_out):
-    low, high = features[0, :TOP], features[0, TOP:]
-    high = jnp.pad(high, ((0, 2 * TOP - TOKI), (0, 0)))
-    return jnp.concatenate([jnp.concatenate([low, high], axis=1), w_in[0], w_out[0]], axis=0)
 
 
 def hidden_rows(shards):
@@ -378,21 +411,20 @@
     w_head,
 ):
     place = jnp.stack([lax.axis_index("pairs"), lax.axis_index("side")]).astype(jnp.int32)
-    (own,) = tied(packed_shard(features, w_fc1, w_fc2))
-    next2 = shifted(own, -2)
-    next1 = shifted(own, -1)
-    last1 = shifted(own[TOP:], 1)
-    last2 = shifted(own[TOP:], 2)
-    next2, next1, last1, last2 = tied(next2, next1, last1, last2)
-    next3 = shifted(next2, -1)
+    packed, shard = pack_call(features, w_fc1, w_fc2)
+    next3, next2, next1 = [shifted(packed, -by) for by in (3, 2, 1)]
+    last1, last2 = shifted(shard, 1), shifted(shard, 2)
     last34 = shifted(jnp.concatenate([last1, last2], axis=0), 2)
-    mine = jnp.stack([own[:TOP], next1[:TOP], next2[:TOP], next3[:TOP]])
+    next1, next2, next3, last34 = tied(next1, next2, next3, last34)
+    part_x = hidden_rows([shard, next1, next2, last1])
+    part_y = hidden_rows([last2, next3, last34[:48], last34[48:]])
+    mine = jnp.stack([packed[:TOP], next1[:TOP], next2[:TOP], next3[:TOP]])
     theirs = other_core(mine)
-    part_x = hidden_rows([own, next1, next2, last1])
-    part_y = hidden_rows([last2, next3, last34[:48], last34[48:]])
     scalars = [image_slot, slot_images.reshape(-1), place]
-    near_x, near_y = three_hops(part_x, "x"), three_hops(part_y, "y")
+    near_x, near_y = three_hops(part_x, "x"), list(first_hop(part_y, "y"))
     rows, triple = triple_call(scalars, mine, theirs, gain_self, w_qkv[0])
+    triple, later = tied(triple, part_y)
+    near_y.append(along(later, "y", 2))
     key_value = memory_call(scalars, mine, theirs, gain_memory, w_memory[0])
     near_x, near_y, rows, triple, key_value = tied(near_x, near_y, rows, triple, key_value)
     plane_x = jnp.concatenate([part_x, *near_x], axis=1)

time: 144 us -> 153 us (1.062)
  waiting for transfers between devices: 50.4 us -> 67 us
  starting transfers between devices: 45.9 us -> 37.1 us
  Pallas kernels: 41.6 us -> 43.3 us
    ppermute x9, waiting for transfers between devices: 43 us -> 51.8 us  [shifted(): lax.ppermute(array, 'pairs', [(i, (i + by) % count) for i in range(count)])]
    ppermute x14, waiting for transfers between devices: 6.41 us -> 14.2 us  [along(): return lax.ppermute(array, 'pairs', [(p, target(p)) for p in range(count)])]
    ppermute x2, starting transfers between devices: 11.3 us -> 6.05 us  [other_core(): return lax.ppermute(array, 'side', [(0, 1), (1, 0)])]
    ppermute x9, starting transfers between devices: 21.6 us -> 18.1 us  [shifted(): lax.ppermute(array, 'pairs', [(i, (i + by) % count) for i in range(count)])]
    squeeze x2 -> x0, local copies, waits for them, and re-layouts: 1.79 us -> none  [packed_shard(): low, high = (features[0, :TOP], features[0, TOP:])]
    pallas_call x0 -> x1, Pallas kernels: none -> 1.67 us  [pack_call(): pl.pallas_call(pack_kernel, in_specs=[pl.BlockSpec(memory_space=pltpu.Mem...]
  transfers between devices with their start and end apart: 25 -> 25, of which waited for: 12 -> 16; matrix products, arithmetic and copies ran while one was open for 1% -> 2% of each run, Pallas kernels for 24% -> 23%
where the time goes in v5:
time: 153 us
  waiting for transfers between devices  67 us (44%)
  Pallas kernels  43.3 us (28%)
  starting transfers between devices  37.1 us (24%)
  local copies, waits for them, and re-layouts  3.34 us (2%)
    ppermute x9, waiting for transfers between devices, shifted(): lax.ppermute(array, 'pairs', [(i, (i + by) % count) for i in range(count)])  51.8 us
    pallas_call x8, Pallas kernels, call(): pl.pallas_call(kernel, in_specs=[SMEM] * len(scalars) + [VMEM] * len(arra...  41.6 us
    ppermute x9, starting transfers between devices, shifted(): lax.ppermute(array, 'pairs', [(i, (i + by) % count) for i in range(count)])  18.1 us
    ppermute x14, waiting for transfers between devices, along(): return lax.ppermute(array, 'pairs', [(p, target(p)) for p in range(count)])  14.2 us
    ppermute x14, starting transfers between devices, along(): return lax.ppermute(array, 'pairs', [(p, target(p)) for p in range(count)])  13 us
    ppermute x2, starting transfers between devices, other_core(): return lax.ppermute(array, 'side', [(0, 1), (1, 0)])  6.05 us
  transfers between devices with their start and end apart: 25, of which 16 were waited for; matrix products, arithmetic and copies ran while one was open for 2% of the time, Pallas kernels for 23%

profile of v5, /device:TPU:1, one launch (start us, length us, event | category | flops | bytes accessed | tf_op | source)
XLA Modules:
  0.0 152.5 jit_solution(8066441697215019723)
XLA Ops:
  0.0 1.7 %pack_part.1 = (bf16[152,768]{1,0:T(8,128)(2,1)}, bf16[48,768]{1,0:T(8,128)(2,1)}) custom-call(bf16[1,196,384]{2,1,0:T(8,128)(2,1)} %features.1, bf16[1,24,768]{2,1,0:T(8,128)(2,1)} %w_in.1, bf16[1,24,768]{2,1,0:T(8,128)(2,1)} %w_out.1), custom_call_target="tpu_custom_call" | custom-call | tf_op jit(solution)/shard_map/pack_part/pallas_call | solution.py:341
  1.7 3.9 %collective-permute-start.4 = (bf16[48,768]{1,0:T(8,128)(2,1)}, bf16[48,768]{1,0:T(8,128)(2,1)S(1)}, u32[]{:S(2)}, u32[]{:S(2)}) collective-permute-start(bf16[48,768]{1,0:T(8,128)(2,1)} %get-tuple-element.42), channel_id=1, source_target_pairs={{0,4},{2,6},{4,8},{6,10},{8,12},{10,14},{12,16},{14,18},{16,20},{1... | collective-permute-start | bytes 221192 | tf_op jit(solution)/shard_map/ppermute | solution.py:24
  7.2 7.7 %collective-permute-start.2 = (bf16[152,768]{1,0:T(8,128)(2,1)}, bf16[152,768]{1,0:T(8,128)(2,1)S(1)}, u32[]{:S(2)}, u32[]{:S(2)}) collective-permute-start(bf16[152,768]{1,0:T(8,128)(2,1)} %get-tuple-element.43), channel_id=1, source_target_pairs={{0,250},{2,252},{4,254},{6,0},{8,2},{10,4},{12,6},{14,8},{16,10},{... | collective-permute-start | bytes 700424 | tf_op jit(solution)/shard_map/ppermute | solution.py:24
  14.9 3.1 %collective-permute-start.1 = (bf16[152,768]{1,0:T(8,128)(2,1)}, bf16[152,768]{1,0:T(8,128)(2,1)S(1)}, u32[]{:S(2)}, u32[]{:S(2)}) collective-permute-start(bf16[152,768]{1,0:T(8,128)(2,1)} %get-tuple-element.43), channel_id=1, source_target_pairs={{0,252},{2,254},{4,0},{6,2},{8,4},{10,6},{12,8},{14,10},{16,12},{1... | collective-permute-start | bytes 700424 | tf_op jit(solution)/shard_map/ppermute | solution.py:24
  21.5 11.7 %collective-permute-done.5 = bf16[96,768]{1,0:T(8,128)(2,1)S(1)} collective-permute-done((bf16[96,768]{1,0:T(8,128)(2,1)S(1)}, bf16[96,768]{1,0:T(8,128)(2,1)S(1)}, u32[]{:S(2)}, u32[]{:S(2)}) %collective-permute-start.5) | collective-permute-done | bytes 147488 | tf_op jit(solution)/shard_map/ppermute | solution.py:24
  34.0 6.5 %collective-permute-done.1 = bf16[152,768]{1,0:T(8,128)(2,1)S(1)} collective-permute-done((bf16[152,768]{1,0:T(8,128)(2,1)}, bf16[152,768]{1,0:T(8,128)(2,1)S(1)}, u32[]{:S(2)}, u32[]{:S(2)}) %collective-permute-start.1) | collective-permute-done | bytes 233504 | tf_op jit(solution)/shard_map/ppermute | solution.py:24
  40.5 5.0 %collective-permute-done = bf16[152,768]{1,0:T(8,128)(2,1)S(1)} collective-permute-done((bf16[152,768]{1,0:T(8,128)(2,1)}, bf16[152,768]{1,0:T(8,128)(2,1)S(1)}, u32[]{:S(2)}, u32[]{:S(2)}) %collective-permute-start) | collective-permute-done | bytes 233504 | tf_op jit(solution)/shard_map/ppermute | solution.py:24
  50.1 5.0 %triple_part.1 = (f32[624,768]{1,0:T(8,128)S(1)}, bf16[624,2304]{1,0:T(8,128)(2,1)S(1)}) custom-call(s32[128]{0:T(128)S(1)} %copy-done, s32[6]{0:T(128)S(1)} %reshape.4.slot_images, s32[2]{0:T(128)S(1)} %pad_add_fusion.place, bf16[4,104,768]{2,1,0:T(8,128)(2,1)S(1)} %pad_maximum_fusion.3.mine, bf16[4,104,768]{2,1,0:T(8,128)(2,1)S(1)} %collective-permute-done.11.theirs, ...), custom_call_target="tpu_custom_call" | custom-call | flops 4000000000 | bytes 8388608 | tf_op jit(solution)/shard_map/triple_part/pallas_call | solution.py:272
  55.2 1.7 %collective-permute-start.12 = (bf16[2,96,768]{2,1,0:T(8,128)(2,1)S(1)}, bf16[2,96,768]{2,1,0:T(8,128)(2,1)S(1)}, u32[]{:S(2)}, u32[]{:S(2)}) collective-permute-start(bf16[2,96,768]{2,1,0:T(8,128)(2,1)S(1)} %pad_maximum_fusion.5), channel_id=1, source_target_pairs={{0,128},{2,130},{4,132},{6,134},{8,136},{10,138},{12,140},{14,142}... | collective-permute-start | bytes 884744 | tf_op jit(solution)/shard_map/ppermute | solution.py:368
  56.9 3.7 %memory_part.1.key_value = bf16[624,1536]{1,0:T(8,128)(2,1)S(1)} custom-call(s32[128]{0:T(128)S(1)} %copy-done, s32[6]{0:T(128)S(1)} %reshape.4.slot_images, s32[2]{0:T(128)S(1)} %pad_add_fusion.place, bf16[4,104,768]{2,1,0:T(8,128)(2,1)S(1)} %pad_maximum_fusion.3.mine, bf16[4,104,768]{2,1,0:T(8,128)(2,1)S(1)} %collective-permute-done.11.theirs, ...), custom_call_target="tpu_custom_call" | custom-call | flops 3000000000 | bytes 8388608 | tf_op jit(solution)/shard_map/memory_part/pallas_call | solution.py:272
  60.6 1.8 %collective-permute-done.7 = bf16[2,96,768]{2,1,0:T(8,128)(2,1)S(1)} collective-permute-done((bf16[2,96,768]{2,1,0:T(8,128)(2,1)S(1)}, bf16[2,96,768]{2,1,0:T(8,128)(2,1)S(1)}, u32[]{:S(2)}, u32[]{:S(2)}) %collective-permute-start.7) | collective-permute-done | bytes 294944 | tf_op jit(solution)/shard_map/ppermute | solution.py:368
  62.4 2.5 %collective-permute-done.6 = bf16[2,96,768]{2,1,0:T(8,128)(2,1)S(1)} collective-permute-done((bf16[2,96,768]{2,1,0:T(8,128)(2,1)S(1)}, bf16[2,96,768]{2,1,0:T(8,128)(2,1)S(1)}, u32[]{:S(2)}, u32[]{:S(2)}) %collective-permute-start.6) | collective-permute-done | bytes 294944 | tf_op jit(solution)/shard_map/ppermute | solution.py:368
  66.9 2.2 %collective-permute-start.14 = (bf16[2,384,768]{2,1,0:T(8,128)(2,1)S(1)}, bf16[2,384,768]{2,1,0:T(8,128)(2,1)S(1)}, u32[]{:S(2)}, u32[]{:S(2)}) collective-permute-start(bf16[2,384,768]{2,1,0:T(8,128)(2,1)S(1)} %pad_maximum_fusion.1), channel_id=1, source_target_pairs={{0,192},{2,194},{4,196},{6,198},{8,200},{10,202},{12,204},{14,206}... | collective-permute-start | bytes 3538952 | tf_op jit(solution)/shard_map/ppermute | solution.py:368
  69.2 10.5 %self_part.1 = (f32[624,768]{1,0:T(8,128)S(1)}, bf16[624,768]{1,0:T(8,128)(2,1)S(1)}) custom-call(f32[624,768]{1,0:T(8,128)S(1)} %get-tuple-element.58.rows, bf16[624,2304]{1,0:T(8,128)(2,1)S(1)} %get-tuple-element.59.triple, f32[1,768]{1,0:T(1,128)S(1)} %copy-done.9, bf16[768,768]{1,0:T(8,128)(2,1)S(1)} %bitcast.27, bf16[768,768]{1,0:T(8,128)(2,1)S(1)} %bitcast.28), custom_call_target="tpu_custom_call" | custom-call | flops 12000000000 | bytes 8388608 | tf_op jit(solution)/shard_map/self_part/pallas_call | solution.py:272
  79.8 9.2 %cross_part.1 = (f32[624,768]{1,0:T(8,128)S(1)}, bf16[624,768]{1,0:T(8,128)(2,1)S(1)}) custom-call(f32[624,768]{1,0:T(8,128)S(1)} %get-tuple-element.60.first, bf16[624,768]{1,0:T(8,128)(2,1)S(1)} %get-tuple-element.61.query, bf16[624,1536]{1,0:T(8,128)(2,1)S(1)} %memory_part.1.key_value, f32[1,768]{1,0:T(1,128)S(1)} %copy-done.10, bf16[768,768]{1,0:T(8,128)(2,1)S(1)} %bitcast.29), custom_call_target="tpu_custom_call" | custom-call | flops 12000000000 | bytes 8388608 | tf_op jit(solution)/shard_map/cross_part/pallas_call | solution.py:272
  89.0 2.6 %collective-permute-done.16 = bf16[2,384,768]{2,1,0:T(8,128)(2,1)S(1)} collective-permute-done((bf16[2,384,768]{2,1,0:T(8,128)(2,1)S(1)}, bf16[2,384,768]{2,1,0:T(8,128)(2,1)S(1)}, u32[]{:S(2)}, u32[]{:S(2)}) %collective-permute-start.16) | collective-permute-done | bytes 1179680 | tf_op jit(solution)/shard_map/ppermute | solution.py:368
  92.9 2.0 %collective-permute-done.13 = bf16[2,384,768]{2,1,0:T(8,128)(2,1)S(1)} collective-permute-done((bf16[2,384,768]{2,1,0:T(8,128)(2,1)S(1)}, bf16[2,384,768]{2,1,0:T(8,128)(2,1)S(1)}, u32[]{:S(2)}, u32[]{:S(2)}) %collective-permute-start.13) | collective-permute-done | bytes 1179680 | tf_op jit(solution)/shard_map/ppermute | solution.py:368
  95.5 2.5 %collective-permute-start.20 = (bf16[2,192,768]{2,1,0:T(8,128)(2,1)S(1)}, bf16[2,192,768]{2,1,0:T(8,128)(2,1)S(1)}, u32[]{:S(2)}, u32[]{:S(2)}) collective-permute-start(bf16[2,192,768]{2,1,0:T(8,128)(2,1)S(1)} %slice.101), channel_id=1, source_target_pairs={{0,48},{2,50},{4,52},{6,54},{8,56},{10,58},{12,60},{14,62},{16,0},... | collective-permute-start | bytes 1769480 | tf_op jit(solution)/shard_map/ppermute | solution.py:368
  99.4 6.5 %early_part.1.early = f32[624,768]{1,0:T(8,128)S(1)} custom-call(f32[624,768]{1,0:T(8,128)S(1)} %get-tuple-element.65.second, bf16[624,768]{1,0:T(8,128)(2,1)S(1)} %get-tuple-element.66.mlp_in, bf16[2,2304,768]{2,1,0:T(8,128)(2,1)S(1)} %constant_dynamic-update-slice_fusion.fc), custom_call_target="tpu_custom_call" | custom-call | flops 10000000000 | bytes 8388608 | tf_op jit(solution)/shard_map/early_part/pallas_call | solution.py:272
  106.6 3.0 %collective-permute-done.19 = bf16[2,192,768]{2,1,0:T(8,128)(2,1)S(1)} collective-permute-done((bf16[2,192,768]{2,1,0:T(8,128)(2,1)S(1)}, bf16[2,192,768]{2,1,0:T(8,128)(2,1)S(1)}, u32[]{:S(2)}, u32[]{:S(2)}) %collective-permute-start.19) | collective-permute-done | bytes 589856 | tf_op jit(solution)/shard_map/ppermute | solution.py:368
  110.1 4.4 %late_part.1 = (f32[3,196,512]{2,1,0:T(8,128)S(1)}, bf16[3,196,512]{2,1,0:T(8,128)(2,1)S(1)}) custom-call(s32[2]{0:T(128)S(1)} %pad_add_fusion.place, f32[624,768]{1,0:T(8,128)S(1)} %early_part.1.early, bf16[624,768]{1,0:T(8,128)(2,1)S(1)} %get-tuple-element.66.mlp_in, bf16[2,768,768]{2,1,0:T(8,128)(2,1)S(1)} %pad_maximum_fusion.fc, ...), custom_call_target="tpu_custom_call" | custom-call | flops 5000000000 | bytes 8388608 | tf_op jit(solution)/shard_map/late_part/pallas_call | solution.py:272
  114.5 5.4 %collective-permute-start.21 = (bf16[3,196,512]{2,1,0:T(8,128)(2,1)S(1)}, bf16[3,196,512]{2,1,0:T(8,128)(2,1)S(1)}, u32[]{:S(2)}, u32[]{:S(2)}) collective-permute-start(bf16[3,196,512]{2,1,0:T(8,128)(2,1)S(1)} %get-tuple-element.72), channel_id=1, source_target_pairs={{0,1},{1,0},{2,3},{3,2},{4,5},{5,4},{6,7},{7,6},{8,9},{9,8},{10,11... | collective-permute-start | bytes 1806344 | tf_op jit(solution)/shard_map/ppermute | solution.py:28
  123.7 12.6 %collective-permute-done.22 = bf16[196,512]{1,0:T(8,128)(2,1)S(1)} collective-permute-done((bf16[196,512]{1,0:T(8,128)(2,1)S(1)}, bf16[196,512]{1,0:T(8,128)(2,1)S(1)}, u32[]{:S(2)}, u32[]{:S(2)}) %collective-permute-start.22) | collective-permute-done | bytes 200736 | tf_op jit(solution)/shard_map/ppermute | solution.py:24
  136.5 15.2 %collective-permute-done.24.further = bf16[196,512]{1,0:T(8,128)(2,1)S(1)} collective-permute-done((bf16[196,512]{1,0:T(8,128)(2,1)S(1)}, bf16[196,512]{1,0:T(8,128)(2,1)S(1)}, u32[]{:S(2)}, u32[]{:S(2)}) %collective-permute-start.24) | collective-permute-done | bytes 200736 | tf_op jit(solution)/shard_map/ppermute | solution.py:24
  (97 shorter events, 20.8 us)
Async XLA Ops:
  1.7 19.7 %collective-permute-start.4 = (bf16[48,768]{1,0:T(8,128)(2,1)}, bf16[48,768]{1,0:T(8,128)(2,1)S(1)}, u32[]{:S(2)}, u32[]{:S(2)}) collective-permute-start(bf16[48,768]{1,0:T(8,128)(2,1)} %get-tuple-element.42), channel_id=1, source_target_pairs={{0,4},{2,6},{4,8},{6,10},{8,12},{10,14},{12,16},{14,18},{16,20},{1... | collective-permute-start | bytes 221192 | tf_op jit(solution)/shard_map/ppermute | solution.py:24
  5.6 15.8 %collective-permute-start.3 = (bf16[48,768]{1,0:T(8,128)(2,1)}, bf16[48,768]{1,0:T(8,128)(2,1)S(1)}, u32[]{:S(2)}, u32[]{:S(2)}) collective-permute-start(bf16[48,768]{1,0:T(8,128)(2,1)} %get-tuple-element.42), channel_id=1, source_target_pairs={{0,2},{2,4},{4,6},{6,8},{8,10},{10,12},{12,14},{14,16},{16,18},{18... | collective-permute-start | bytes 221192 | tf_op jit(solution)/shard_map/ppermute | solution.py:24
  7.2 26.8 %collective-permute-start.2 = (bf16[152,768]{1,0:T(8,128)(2,1)}, bf16[152,768]{1,0:T(8,128)(2,1)S(1)}, u32[]{:S(2)}, u32[]{:S(2)}) collective-permute-start(bf16[152,768]{1,0:T(8,128)(2,1)} %get-tuple-element.43), channel_id=1, source_target_pairs={{0,250},{2,252},{4,254},{6,0},{8,2},{10,4},{12,6},{14,8},{16,10},{... | collective-permute-start | bytes 700424 | tf_op jit(solution)/shard_map/ppermute | solution.py:24
  14.9 25.7 %collective-permute-start.1 = (bf16[152,768]{1,0:T(8,128)(2,1)}, bf16[152,768]{1,0:T(8,128)(2,1)S(1)}, u32[]{:S(2)}, u32[]{:S(2)}) collective-permute-start(bf16[152,768]{1,0:T(8,128)(2,1)} %get-tuple-element.43), channel_id=1, source_target_pairs={{0,252},{2,254},{4,0},{6,2},{8,4},{10,6},{12,8},{14,10},{16,12},{1... | collective-permute-start | bytes 700424 | tf_op jit(solution)/shard_map/ppermute | solution.py:24
  18.0 27.5 %collective-permute-start = (bf16[152,768]{1,0:T(8,128)(2,1)}, bf16[152,768]{1,0:T(8,128)(2,1)S(1)}, u32[]{:S(2)}, u32[]{:S(2)}) collective-permute-start(bf16[152,768]{1,0:T(8,128)(2,1)} %get-tuple-element.43), channel_id=1, source_target_pairs={{0,254},{2,0},{4,2},{6,4},{8,6},{10,8},{12,10},{14,12},{16,14},{18... | collective-permute-start | bytes 700424 | tf_op jit(solution)/shard_map/ppermute | solution.py:24
  21.4 11.8 %collective-permute-start.5 = (bf16[96,768]{1,0:T(8,128)(2,1)S(1)}, bf16[96,768]{1,0:T(8,128)(2,1)S(1)}, u32[]{:S(2)}, u32[]{:S(2)}) collective-permute-start(bf16[96,768]{1,0:T(8,128)(2,1)S(1)} %pad_maximum_fusion.6), channel_id=1, source_target_pairs={{0,4},{2,6},{4,8},{6,10},{8,12},{10,14},{12,16},{14,18},{16,20},{1... | collective-permute-start | bytes 442376 | tf_op jit(solution)/shard_map/ppermute | solution.py:24
  46.5 8.7 %collective-permute-start.10 = (bf16[2,96,768]{2,1,0:T(8,128)(2,1)S(1)}, bf16[2,96,768]{2,1,0:T(8,128)(2,1)S(1)}, u32[]{:S(2)}, u32[]{:S(2)}) collective-permute-start(bf16[2,96,768]{2,1,0:T(8,128)(2,1)S(1)} %pad_maximum_fusion.5), channel_id=1, source_target_pairs={{0,192},{2,194},{4,196},{6,198},{8,200},{10,202},{12,204},{14,206}... | collective-permute-start | bytes 884744 | tf_op jit(solution)/shard_map/ppermute | solution.py:368
  47.1 13.5 %collective-permute-start.9 = (bf16[2,96,768]{2,1,0:T(8,128)(2,1)S(1)}, bf16[2,96,768]{2,1,0:T(8,128)(2,1)S(1)}, u32[]{:S(2)}, u32[]{:S(2)}) collective-permute-start(bf16[2,96,768]{2,1,0:T(8,128)(2,1)S(1)} %pad_maximum_fusion.5), channel_id=1, source_target_pairs={{0,64},{2,66},{4,68},{6,70},{8,72},{10,74},{12,76},{14,78},{16,80}... | collective-permute-start | bytes 884744 | tf_op jit(solution)/shard_map/ppermute | solution.py:368
  48.1 12.5 %collective-permute-start.8 = (bf16[2,96,768]{2,1,0:T(8,128)(2,1)S(1)}, bf16[2,96,768]{2,1,0:T(8,128)(2,1)S(1)}, u32[]{:S(2)}, u32[]{:S(2)}) collective-permute-start(bf16[2,96,768]{2,1,0:T(8,128)(2,1)S(1)} %get-tuple-element.80), channel_id=1, source_target_pairs={{0,32},{2,34},{4,36},{6,38},{8,40},{10,42},{12,44},{14,46},{16,48}... | collective-permute-start | bytes 884744 | tf_op jit(solution)/shard_map/ppermute | solution.py:368
  48.6 13.8 %collective-permute-start.7 = (bf16[2,96,768]{2,1,0:T(8,128)(2,1)S(1)}, bf16[2,96,768]{2,1,0:T(8,128)(2,1)S(1)}, u32[]{:S(2)}, u32[]{:S(2)}) collective-permute-start(bf16[2,96,768]{2,1,0:T(8,128)(2,1)S(1)} %get-tuple-element.80), channel_id=1, source_target_pairs={{0,48},{2,50},{4,52},{6,54},{8,56},{10,58},{12,60},{14,62},{16,0},... | collective-permute-start | bytes 884744 | tf_op jit(solution)/shard_map/ppermute | solution.py:368
  49.5 15.5 %collective-permute-start.6 = (bf16[2,96,768]{2,1,0:T(8,128)(2,1)S(1)}, bf16[2,96,768]{2,1,0:T(8,128)(2,1)S(1)}, u32[]{:S(2)}, u32[]{:S(2)}) collective-permute-start(bf16[2,96,768]{2,1,0:T(8,128)(2,1)S(1)} %get-tuple-element.80), channel_id=1, source_target_pairs={{0,16},{2,18},{4,20},{6,22},{8,24},{10,26},{12,28},{14,30},{16,32}... | collective-permute-start | bytes 884744 | tf_op jit(solution)/shard_map/ppermute | solution.py:368
  55.2 9.8 %collective-permute-start.12 = (bf16[2,96,768]{2,1,0:T(8,128)(2,1)S(1)}, bf16[2,96,768]{2,1,0:T(8,128)(2,1)S(1)}, u32[]{:S(2)}, u32[]{:S(2)}) collective-permute-start(bf16[2,96,768]{2,1,0:T(8,128)(2,1)S(1)} %pad_maximum_fusion.5), channel_id=1, source_target_pairs={{0,128},{2,130},{4,132},{6,134},{8,136},{10,138},{12,140},{14,142}... | collective-permute-start | bytes 884744 | tf_op jit(solution)/shard_map/ppermute | solution.py:368
  65.1 26.6 %collective-permute-start.16 = (bf16[2,384,768]{2,1,0:T(8,128)(2,1)S(1)}, bf16[2,384,768]{2,1,0:T(8,128)(2,1)S(1)}, u32[]{:S(2)}, u32[]{:S(2)}) collective-permute-start(bf16[2,384,768]{2,1,0:T(8,128)(2,1)S(1)} %pad_maximum_fusion.2), channel_id=1, source_target_pairs={{0,48},{2,50},{4,52},{6,54},{8,56},{10,58},{12,60},{14,62},{16,0},... | collective-permute-start | bytes 3538952 | tf_op jit(solution)/shard_map/ppermute | solution.py:368
  66.5 26.3 %collective-permute-start.15 = (bf16[2,384,768]{2,1,0:T(8,128)(2,1)S(1)}, bf16[2,384,768]{2,1,0:T(8,128)(2,1)S(1)}, u32[]{:S(2)}, u32[]{:S(2)}) collective-permute-start(bf16[2,384,768]{2,1,0:T(8,128)(2,1)S(1)} %pad_maximum_fusion.2), channel_id=1, source_target_pairs={{0,16},{2,18},{4,20},{6,22},{8,24},{10,26},{12,28},{14,30},{16,32}... | collective-permute-start | bytes 3538952 | tf_op jit(solution)/shard_map/ppermute | solution.py:368
  66.9 26.0 %collective-permute-start.14 = (bf16[2,384,768]{2,1,0:T(8,128)(2,1)S(1)}, bf16[2,384,768]{2,1,0:T(8,128)(2,1)S(1)}, u32[]{:S(2)}, u32[]{:S(2)}) collective-permute-start(bf16[2,384,768]{2,1,0:T(8,128)(2,1)S(1)} %pad_maximum_fusion.1), channel_id=1, source_target_pairs={{0,192},{2,194},{4,196},{6,198},{8,200},{10,202},{12,204},{14,206}... | collective-permute-start | bytes 3538952 | tf_op jit(solution)/shard_map/ppermute | solution.py:368
  69.1 25.8 %collective-permute-start.13 = (bf16[2,384,768]{2,1,0:T(8,128)(2,1)S(1)}, bf16[2,384,768]{2,1,0:T(8,128)(2,1)S(1)}, u32[]{:S(2)}, u32[]{:S(2)}) collective-permute-start(bf16[2,384,768]{2,1,0:T(8,128)(2,1)S(1)} %pad_maximum_fusion.1), channel_id=1, source_target_pairs={{0,64},{2,66},{4,68},{6,70},{8,72},{10,74},{12,76},{14,78},{16,80}... | collective-permute-start | bytes 3538952 | tf_op jit(solution)/shard_map/ppermute | solution.py:368
  95.5 11.1 %collective-permute-start.20 = (bf16[2,192,768]{2,1,0:T(8,128)(2,1)S(1)}, bf16[2,192,768]{2,1,0:T(8,128)(2,1)S(1)}, u32[]{:S(2)}, u32[]{:S(2)}) collective-permute-start(bf16[2,192,768]{2,1,0:T(8,128)(2,1)S(1)} %slice.101), channel_id=1, source_target_pairs={{0,48},{2,50},{4,52},{6,54},{8,56},{10,58},{12,60},{14,62},{16,0},... | collective-permute-start | bytes 1769480 | tf_op jit(solution)/shard_map/ppermute | solution.py:368
  98.0 11.6 %collective-permute-start.19 = (bf16[2,192,768]{2,1,0:T(8,128)(2,1)S(1)}, bf16[2,192,768]{2,1,0:T(8,128)(2,1)S(1)}, u32[]{:S(2)}, u32[]{:S(2)}) collective-permute-start(bf16[2,192,768]{2,1,0:T(8,128)(2,1)S(1)} %slice.100), channel_id=1, source_target_pairs={{0,16},{2,18},{4,20},{6,22},{8,24},{10,26},{12,28},{14,30},{16,32}... | collective-permute-start | bytes 1769480 | tf_op jit(solution)/shard_map/ppermute | solution.py:368
  98.0 11.6 %collective-permute-start.18 = (bf16[2,192,768]{2,1,0:T(8,128)(2,1)S(1)}, bf16[2,192,768]{2,1,0:T(8,128)(2,1)S(1)}, u32[]{:S(2)}, u32[]{:S(2)}) collective-permute-start(bf16[2,192,768]{2,1,0:T(8,128)(2,1)S(1)} %slice.99), channel_id=1, source_target_pairs={{0,192},{2,194},{4,196},{6,198},{8,200},{10,202},{12,204},{14,206}... | collective-permute-start | bytes 1769480 | tf_op jit(solution)/shard_map/ppermute | solution.py:368
  98.3 11.6 %collective-permute-start.17 = (bf16[2,192,768]{2,1,0:T(8,128)(2,1)S(1)}, bf16[2,192,768]{2,1,0:T(8,128)(2,1)S(1)}, u32[]{:S(2)}, u32[]{:S(2)}) collective-permute-start(bf16[2,192,768]{2,1,0:T(8,128)(2,1)S(1)} %slice.98), channel_id=1, source_target_pairs={{0,64},{2,66},{4,68},{6,70},{8,72},{10,74},{12,76},{14,78},{16,80}... | collective-permute-start | bytes 1769480 | tf_op jit(solution)/shard_map/ppermute | solution.py:368
  114.5 7.1 %collective-permute-start.21 = (bf16[3,196,512]{2,1,0:T(8,128)(2,1)S(1)}, bf16[3,196,512]{2,1,0:T(8,128)(2,1)S(1)}, u32[]{:S(2)}, u32[]{:S(2)}) collective-permute-start(bf16[3,196,512]{2,1,0:T(8,128)(2,1)S(1)} %get-tuple-element.72), channel_id=1, source_target_pairs={{0,1},{1,0},{2,3},{3,2},{4,5},{5,4},{6,7},{7,6},{8,9},{9,8},{10,11... | collective-permute-start | bytes 1806344 | tf_op jit(solution)/shard_map/ppermute | solution.py:28
  123.0 13.3 %collective-permute-start.22 = (bf16[196,512]{1,0:T(8,128)(2,1)S(1)}, bf16[196,512]{1,0:T(8,128)(2,1)S(1)}, u32[]{:S(2)}, u32[]{:S(2)}) collective-permute-start(bf16[196,512]{1,0:T(8,128)(2,1)S(1)} %get-tuple-element.74), channel_id=1, source_target_pairs={{0,2},{2,4},{4,6},{6,8},{8,10},{10,12},{12,14},{14,16},{16,18},{18... | collective-permute-start | bytes 602120 | tf_op jit(solution)/shard_map/ppermute | solution.py:24
  136.4 15.4 %collective-permute-start.24 = (bf16[196,512]{1,0:T(8,128)(2,1)S(1)}, bf16[196,512]{1,0:T(8,128)(2,1)S(1)}, u32[]{:S(2)}, u32[]{:S(2)}) collective-permute-start(bf16[196,512]{1,0:T(8,128)(2,1)S(1)} %add_convert_fusion), channel_id=1, source_target_pairs={{0,4},{2,6},{4,8},{6,10},{8,12},{10,14},{12,16},{14,18},{16,20},{1... | collective-permute-start | bytes 602120 | tf_op jit(solution)/shard_map/ppermute | solution.py:24
  136.5 15.3 %collective-permute-start.23 = (bf16[196,512]{1,0:T(8,128)(2,1)S(1)}, bf16[196,512]{1,0:T(8,128)(2,1)S(1)}, u32[]{:S(2)}, u32[]{:S(2)}) collective-permute-start(bf16[196,512]{1,0:T(8,128)(2,1)S(1)} %get-tuple-element.76), channel_id=1, source_target_pairs={{0,2},{2,4},{4,6},{6,8},{8,10},{10,12},{12,14},{14,16},{16,18},{18... | collective-permute-start | bytes 602120 | tf_op jit(solution)/shard_map/ppermute | solution.py:24
  (13 other events, 72.2 us)

commit v6 on v5

--- a/solution.py
+++ b/solution.py
@@ -243,7 +243,7 @@
 
 
 def pack_kernel(
-    features, w_in, w_out, packed, shard, features_here, w_in_here, w_out_here, sems
+    features, w_in, w_out, tokens, shard, features_here, w_in_here, w_out_here, sems
 ):
     copies = [
         pltpu.make_async_copy(src, dst, sems.at[i])
@@ -256,12 +256,11 @@
     for copy in copies:
         copy.wait()
     count = TOKI - TOP
-    packed[88:TOP, HALF:] = jnp.zeros((TOP - 88, HALF), BF16)
-    packed[:TOP, :HALF] = features_here[0, :TOP]
-    packed[:count, HALF:] = features_here[0, TOP:]
-    for target, base in ((packed, TOP), (shard, 0)):
-        target[base : base + 24] = w_in_here[0]
-        target[base + 24 : base + 48] = w_out_here[0]
+    tokens[88:TOP, HALF:] = jnp.zeros((TOP - 88, HALF), BF16)
+    tokens[:TOP, :HALF] = features_here[0, :TOP]
+    tokens[:count, HALF:] = features_here[0, TOP:]
+    shard[:24] = w_in_here[0]
+    shard[24:] = w_out_here[0]
 
 
 SMEM = pl.BlockSpec(memory_space=pltpu.SMEM)
@@ -337,7 +336,7 @@
 
 
 def pack_call(features, w_in, w_out):
-    outs = [((TOP + 48, D), BF16), ((48, D), BF16)]
+    outs = [((TOP, D), BF16), ((48, D), BF16)]
     return pl.pallas_call(
         pack_kernel,
         in_specs=[pl.BlockSpec(memory_space=pltpu.MemorySpace.HBM)] * 3,
@@ -376,10 +375,6 @@
     inner = [s[-48:-24] for s in shards]
     outer = [s[-24:] for s in shards]
     return jnp.stack([jnp.concatenate(inner, axis=0), jnp.concatenate(outer, axis=0)])
-
-
-def three_hops(block, axis):
-    return [along(block, axis, by) for by in (1, -1, 2)]
 
 
 def first_hop(block, axis):
@@ -411,20 +406,25 @@
     w_head,
 ):
     place = jnp.stack([lax.axis_index("pairs"), lax.axis_index("side")]).astype(jnp.int32)
-    packed, shard = pack_call(features, w_fc1, w_fc2)
-    next3, next2, next1 = [shifted(packed, -by) for by in (3, 2, 1)]
-    last1, last2 = shifted(shard, 1), shifted(shard, 2)
+    tokens, shard = pack_call(features, w_fc1, w_fc2)
+    last1, last2, below1, below2 = [shifted(shard, by) for by in (1, 2, -1, -2)]
+    next2 = shifted(tokens, -2)
+    last1, last2, below1, below2, tokens = tied(last1, last2, below1, below2, tokens)
     last34 = shifted(jnp.concatenate([last1, last2], axis=0), 2)
-    next1, next2, next3, last34 = tied(next1, next2, next3, last34)
-    part_x = hidden_rows([shard, next1, next2, last1])
-    part_y = hidden_rows([last2, next3, last34[:48], last34[48:]])
-    mine = jnp.stack([packed[:TOP], next1[:TOP], next2[:TOP], next3[:TOP]])
+    below3 = shifted(below2, -1)
+    next1 = shifted(tokens, -1)
+    part_x = hidden_rows([shard, last1, below1, below2])
+    last34, below3, next1, next2, part_x = tied(last34, below3, next1, next2, part_x)
+    next3 = shifted(next2, -1)
+    part_y = hidden_rows([last2, below3, last34[:48], last34[48:]])
+    near_x, near_y = first_hop(part_x, "x"), first_hop(part_y, "y")
+    next3, near_x, near_y, part_x, part_y = tied(next3, near_x, near_y, part_x, part_y)
+    near_x = [*near_x, along(part_x, "x", 2)]
+    near_y = [*near_y, along(part_y, "y", 2)]
+    mine = jnp.stack([tokens, next1, next2, next3])
     theirs = other_core(mine)
     scalars = [image_slot, slot_images.reshape(-1), place]
-    near_x, near_y = three_hops(part_x, "x"), list(first_hop(part_y, "y"))
     rows, triple = triple_call(scalars, mine, theirs, gain_self, w_qkv[0])
-    triple, later = tied(triple, part_y)
-    near_y.append(along(later, "y", 2))
     key_value = memory_call(scalars, mine, theirs, gain_memory, w_memory[0])
     near_x, near_y, rows, triple, key_value = tied(near_x, near_y, rows, triple, key_value)
     plane_x = jnp.concatenate([part_x, *near_x], axis=1)

time: 153 us -> 160 us (1.046)
  starting transfers between devices: 37.1 us -> 57.6 us
  waiting for transfers between devices: 67 us -> 52.7 us
    ppermute x9 -> x12, starting transfers between devices: 18.1 us -> 39 us  [shifted(): lax.ppermute(array, 'pairs', [(i, (i + by) % count) for i in range(count)])]
    ppermute x9 -> x12, waiting for transfers between devices: 51.8 us -> 38.3 us  [shifted(): lax.ppermute(array, 'pairs', [(i, (i + by) % count) for i in range(count)])]
    ppermute x14, starting transfers between devices: 13 us -> 9.38 us  [along(): return lax.ppermute(array, 'pairs', [(p, target(p)) for p in range(count)])]
    ppermute x2, starting transfers between devices: 6.05 us -> 9.31 us  [other_core(): return lax.ppermute(array, 'side', [(0, 1), (1, 0)])]
    ppermute x14, waiting for transfers between devices: 14.2 us -> 12.3 us  [along(): return lax.ppermute(array, 'pairs', [(p, target(p)) for p in range(count)])]
  transfers between devices with their start and end apart: 25 -> 28, of which waited for: 16 -> 15; matrix products, arithmetic and copies ran while one was open for 2% -> 1% of each run, Pallas kernels for 23% -> 22%
where the time goes in v6:
time: 160 us; the launch traced here: 159 us
  starting transfers between devices  57.6 us (36%)
  waiting for transfers between devices  52.7 us (33%)
  Pallas kernels  43.4 us (27%)
  local copies, waits for them, and re-layouts  3.9 us (2%)
    pallas_call x8, Pallas kernels, call(): pl.pallas_call(kernel, in_specs=[SMEM] * len(scalars) + [VMEM] * len(arra...  41.7 us
    ppermute x12, starting transfers between devices, shifted(): lax.ppermute(array, 'pairs', [(i, (i + by) % count) for i in range(count)])  39 us
    ppermute x12, waiting for transfers between devices, shifted(): lax.ppermute(array, 'pairs', [(i, (i + by) % count) for i in range(count)])  38.3 us
    ppermute x14, waiting for transfers between devices, along(): return lax.ppermute(array, 'pairs', [(p, target(p)) for p in range(count)])  12.3 us
    ppermute x14, starting transfers between devices, along(): return lax.ppermute(array, 'pairs', [(p, target(p)) for p in range(count)])  9.38 us
    ppermute x2, starting transfers between devices, other_core(): return lax.ppermute(array, 'side', [(0, 1), (1, 0)])  9.31 us
  transfers between devices with their start and end apart: 28, of which 15 were waited for; matrix products, arithmetic and copies ran while one was open for 1% of the time, Pallas kernels for 22%

profile of v6, /device:TPU:1, one launch (start us, length us, event | category | flops | bytes accessed | tf_op | source)
XLA Modules:
  0.0 159.3 jit_solution(1809705583807454157)
XLA Ops:
  0.0 1.6 %pack_part.1 = (bf16[104,768]{1,0:T(8,128)(2,1)}, bf16[48,768]{1,0:T(8,128)(2,1)}) custom-call(bf16[1,196,384]{2,1,0:T(8,128)(2,1)} %features.1, bf16[1,24,768]{2,1,0:T(8,128)(2,1)} %w_in.1, bf16[1,24,768]{2,1,0:T(8,128)(2,1)} %w_out.1), custom_call_target="tpu_custom_call" | custom-call | tf_op jit(solution)/shard_map/pack_part/pallas_call | solution.py:340
  1.7 11.6 %collective-permute-start.3 = (bf16[48,768]{1,0:T(8,128)(2,1)}, bf16[48,768]{1,0:T(8,128)(2,1)S(1)}, u32[]{:S(2)}, u32[]{:S(2)}) collective-permute-start(bf16[48,768]{1,0:T(8,128)(2,1)} %get-tuple-element.53), channel_id=1, source_target_pairs={{0,252},{2,254},{4,0},{6,2},{8,4},{10,6},{12,8},{14,10},{16,12},{1... | collective-permute-start | bytes 221192 | tf_op jit(solution)/shard_map/ppermute | solution.py:24
  15.2 7.3 %collective-permute-start.7 = (bf16[104,768]{1,0:T(8,128)(2,1)}, bf16[104,768]{1,0:T(8,128)(2,1)S(1)}, u32[]{:S(2)}, u32[]{:S(2)}) collective-permute-start(bf16[104,768]{1,0:T(8,128)(2,1)} %get-tuple-element.58), channel_id=1, source_target_pairs={{0,252},{2,254},{4,0},{6,2},{8,4},{10,6},{12,8},{14,10},{16,12},{1... | collective-permute-start | bytes 479240 | tf_op jit(solution)/shard_map/ppermute | solution.py:24
  23.8 2.4 %collective-permute-done = bf16[48,768]{1,0:T(8,128)(2,1)S(1)} collective-permute-done((bf16[48,768]{1,0:T(8,128)(2,1)}, bf16[48,768]{1,0:T(8,128)(2,1)S(1)}, u32[]{:S(2)}, u32[]{:S(2)}) %collective-permute-start) | collective-permute-done | bytes 73760 | tf_op jit(solution)/shard_map/ppermute | solution.py:24
  26.6 7.9 %collective-permute-start.6 = (bf16[104,768]{1,0:T(8,128)(2,1)}, bf16[104,768]{1,0:T(8,128)(2,1)S(1)}, u32[]{:S(2)}, u32[]{:S(2)}) collective-permute-start(bf16[104,768]{1,0:T(8,128)(2,1)} %get-tuple-element.58), channel_id=1, source_target_pairs={{0,254},{2,0},{4,2},{6,4},{8,6},{10,8},{12,10},{14,12},{16,14},{18... | collective-permute-start | bytes 479240 | tf_op jit(solution)/shard_map/ppermute | solution.py:24
  34.6 2.2 %collective-permute-done.4 = bf16[96,768]{1,0:T(8,128)(2,1)S(1)} collective-permute-done((bf16[96,768]{1,0:T(8,128)(2,1)S(1)}, bf16[96,768]{1,0:T(8,128)(2,1)S(1)}, u32[]{:S(2)}, u32[]{:S(2)}) %collective-permute-start.4) | collective-permute-done | bytes 147488 | tf_op jit(solution)/shard_map/ppermute | solution.py:24
  38.7 1.5 collective-permute-start.9
  40.2 9.7 %collective-permute-start.8 = (bf16[104,768]{1,0:T(8,128)(2,1)S(1)}, bf16[104,768]{1,0:T(8,128)(2,1)S(1)}, u32[]{:S(2)}, u32[]{:S(2)}) collective-permute-start(bf16[104,768]{1,0:T(8,128)(2,1)S(1)} %collective-permute-done.7), channel_id=1, source_target_pairs={{0,254},{2,0},{4,2},{6,4},{8,6},{10,8},{12,10},{14,12},{16,14},{18... | collective-permute-start | bytes 479240 | tf_op jit(solution)/shard_map/ppermute | solution.py:24
  49.8 2.2 %collective-permute-done.8 = bf16[104,768]{1,0:T(8,128)(2,1)S(1)} collective-permute-done((bf16[104,768]{1,0:T(8,128)(2,1)S(1)}, bf16[104,768]{1,0:T(8,128)(2,1)S(1)}, u32[]{:S(2)}, u32[]{:S(2)}) %collective-permute-start.8) | collective-permute-done | bytes 159776 | tf_op jit(solution)/shard_map/ppermute | solution.py:24
  52.2 5.4 %collective-permute-start.15 = (bf16[4,104,768]{2,1,0:T(8,128)(2,1)S(1)}, bf16[4,104,768]{2,1,0:T(8,128)(2,1)S(1)}, u32[]{:S(2)}, u32[]{:S(2)}) collective-permute-start(bf16[4,104,768]{2,1,0:T(8,128)(2,1)S(1)} %pad_maximum_fusion.1.mine), channel_id=1, source_target_pairs={{0,1},{1,0},{2,3},{3,2},{4,5},{5,4},{6,7},{7,6},{8,9},{9,8},{10,11... | collective-permute-start | bytes 1916936 | tf_op jit(solution)/shard_map/ppermute | solution.py:28
  59.3 2.0 %copy-done.1 = bf16[1,768,2304]{2,1,0:T(8,128)(2,1)S(1)} copy-done((bf16[1,768,2304]{2,1,0:T(8,128)(2,1)S(1)}, bf16[1,768,2304]{2,1,0:T(8,128)(2,1)}, u32[]{:S(2)}) %copy-start.1) | copy-done | bytes 3538968
  61.3 5.0 %triple_part.1 = (f32[624,768]{1,0:T(8,128)S(1)}, bf16[624,2304]{1,0:T(8,128)(2,1)S(1)}) custom-call(s32[128]{0:T(128)S(1)} %copy-done, s32[6]{0:T(128)S(1)} %reshape.4.slot_images, s32[2]{0:T(128)S(1)} %pad_add_fusion.place, bf16[4,104,768]{2,1,0:T(8,128)(2,1)S(1)} %pad_maximum_fusion.1.mine, bf16[4,104,768]{2,1,0:T(8,128)(2,1)S(1)} %collective-permute-done.15.theirs, ...), custom_call_target="tpu_custom_call" | custom-call | flops 4000000000 | bytes 8388608 | tf_op jit(solution)/shard_map/triple_part/pallas_call | solution.py:271
  66.3 3.7 %memory_part.1.key_value = bf16[624,1536]{1,0:T(8,128)(2,1)S(1)} custom-call(s32[128]{0:T(128)S(1)} %copy-done, s32[6]{0:T(128)S(1)} %reshape.4.slot_images, s32[2]{0:T(128)S(1)} %pad_add_fusion.place, bf16[4,104,768]{2,1,0:T(8,128)(2,1)S(1)} %pad_maximum_fusion.1.mine, bf16[4,104,768]{2,1,0:T(8,128)(2,1)S(1)} %collective-permute-done.15.theirs, ...), custom_call_target="tpu_custom_call" | custom-call | flops 3000000000 | bytes 8388608 | tf_op jit(solution)/shard_map/memory_part/pallas_call | solution.py:271
  70.3 1.5 collective-permute-start.18
  73.5 10.5 %self_part.1 = (f32[624,768]{1,0:T(8,128)S(1)}, bf16[624,768]{1,0:T(8,128)(2,1)S(1)}) custom-call(f32[624,768]{1,0:T(8,128)S(1)} %get-tuple-element.80.rows, bf16[624,2304]{1,0:T(8,128)(2,1)S(1)} %get-tuple-element.81.triple, f32[1,768]{1,0:T(1,128)S(1)} %copy-done.9, bf16[768,768]{1,0:T(8,128)(2,1)S(1)} %bitcast.23, bf16[768,768]{1,0:T(8,128)(2,1)S(1)} %bitcast.24), custom_call_target="tpu_custom_call" | custom-call | flops 12000000000 | bytes 8388608 | tf_op jit(solution)/shard_map/self_part/pallas_call | solution.py:271
  84.0 9.3 %cross_part.1 = (f32[624,768]{1,0:T(8,128)S(1)}, bf16[624,768]{1,0:T(8,128)(2,1)S(1)}) custom-call(f32[624,768]{1,0:T(8,128)S(1)} %get-tuple-element.82.first, bf16[624,768]{1,0:T(8,128)(2,1)S(1)} %get-tuple-element.83.query, bf16[624,1536]{1,0:T(8,128)(2,1)S(1)} %memory_part.1.key_value, f32[1,768]{1,0:T(1,128)S(1)} %copy-done.10, bf16[768,768]{1,0:T(8,128)(2,1)S(1)} %bitcast.25), custom_call_target="tpu_custom_call" | custom-call | flops 12000000000 | bytes 8388608 | tf_op jit(solution)/shard_map/cross_part/pallas_call | solution.py:271
  93.3 4.2 %collective-permute-done.19 = bf16[2,384,768]{2,1,0:T(8,128)(2,1)S(1)} collective-permute-done((bf16[2,384,768]{2,1,0:T(8,128)(2,1)S(1)}, bf16[2,384,768]{2,1,0:T(8,128)(2,1)S(1)}, u32[]{:S(2)}, u32[]{:S(2)}) %collective-permute-start.19) | collective-permute-done | bytes 1179680 | tf_op jit(solution)/shard_map/ppermute | solution.py:367
  103.5 6.6 %early_part.1.early = f32[624,768]{1,0:T(8,128)S(1)} custom-call(f32[624,768]{1,0:T(8,128)S(1)} %get-tuple-element.87.second, bf16[624,768]{1,0:T(8,128)(2,1)S(1)} %get-tuple-element.88.mlp_in, bf16[2,2304,768]{2,1,0:T(8,128)(2,1)S(1)} %constant_dynamic-update-slice_fusion.8.fc), custom_call_target="tpu_custom_call" | custom-call | flops 10000000000 | bytes 8388608 | tf_op jit(solution)/shard_map/early_part/pallas_call | solution.py:271
  110.1 3.4 %collective-permute-done.23 = bf16[2,192,768]{2,1,0:T(8,128)(2,1)S(1)} collective-permute-done((bf16[2,192,768]{2,1,0:T(8,128)(2,1)S(1)}, bf16[2,192,768]{2,1,0:T(8,128)(2,1)S(1)}, u32[]{:S(2)}, u32[]{:S(2)}) %collective-permute-start.23) | collective-permute-done | bytes 589856 | tf_op jit(solution)/shard_map/ppermute | solution.py:367
  113.5 1.8 %collective-permute-done.22 = bf16[2,192,768]{2,1,0:T(8,128)(2,1)S(1)} collective-permute-done((bf16[2,192,768]{2,1,0:T(8,128)(2,1)S(1)}, bf16[2,192,768]{2,1,0:T(8,128)(2,1)S(1)}, u32[]{:S(2)}, u32[]{:S(2)}) %collective-permute-start.22) | collective-permute-done | bytes 589856 | tf_op jit(solution)/shard_map/ppermute | solution.py:367
  116.1 4.5 %late_part.1 = (f32[3,196,512]{2,1,0:T(8,128)S(1)}, bf16[3,196,512]{2,1,0:T(8,128)(2,1)S(1)}) custom-call(s32[2]{0:T(128)S(1)} %pad_add_fusion.place, f32[624,768]{1,0:T(8,128)S(1)} %early_part.1.early, bf16[624,768]{1,0:T(8,128)(2,1)S(1)} %get-tuple-element.88.mlp_in, bf16[2,768,768]{2,1,0:T(8,128)(2,1)S(1)} %pad_maximum_fusion.fc, ...), custom_call_target="tpu_custom_call" | custom-call | flops 5000000000 | bytes 8388608 | tf_op jit(solution)/shard_map/late_part/pallas_call | solution.py:271
  120.5 3.9 %collective-permute-start.24 = (bf16[3,196,512]{2,1,0:T(8,128)(2,1)S(1)}, bf16[3,196,512]{2,1,0:T(8,128)(2,1)S(1)}, u32[]{:S(2)}, u32[]{:S(2)}) collective-permute-start(bf16[3,196,512]{2,1,0:T(8,128)(2,1)S(1)} %get-tuple-element.94), channel_id=1, source_target_pairs={{0,1},{1,0},{2,3},{3,2},{4,5},{5,4},{6,7},{7,6},{8,9},{9,8},{10,11... | collective-permute-start | bytes 1806344 | tf_op jit(solution)/shard_map/ppermute | solution.py:28
  127.6 14.4 %collective-permute-done.25 = bf16[196,512]{1,0:T(8,128)(2,1)S(1)} collective-permute-done((bf16[196,512]{1,0:T(8,128)(2,1)S(1)}, bf16[196,512]{1,0:T(8,128)(2,1)S(1)}, u32[]{:S(2)}, u32[]{:S(2)}) %collective-permute-start.25) | collective-permute-done | bytes 200736 | tf_op jit(solution)/shard_map/ppermute | solution.py:24
  142.2 16.3 %collective-permute-done.27.further = bf16[196,512]{1,0:T(8,128)(2,1)S(1)} collective-permute-done((bf16[196,512]{1,0:T(8,128)(2,1)S(1)}, bf16[196,512]{1,0:T(8,128)(2,1)S(1)}, u32[]{:S(2)}, u32[]{:S(2)}) %collective-permute-start.27) | collective-permute-done | bytes 200736 | tf_op jit(solution)/shard_map/ppermute | solution.py:24
  (107 shorter events, 19.2 us)
Async XLA Ops:
  1.7 21.6 %collective-permute-start.3 = (bf16[48,768]{1,0:T(8,128)(2,1)}, bf16[48,768]{1,0:T(8,128)(2,1)S(1)}, u32[]{:S(2)}, u32[]{:S(2)}) collective-permute-start(bf16[48,768]{1,0:T(8,128)(2,1)} %get-tuple-element.53), channel_id=1, source_target_pairs={{0,252},{2,254},{4,0},{6,2},{8,4},{10,6},{12,8},{14,10},{16,12},{1... | collective-permute-start | bytes 221192 | tf_op jit(solution)/shard_map/ppermute | solution.py:24
  13.2 10.1 %collective-permute-start.2 = (bf16[48,768]{1,0:T(8,128)(2,1)}, bf16[48,768]{1,0:T(8,128)(2,1)S(1)}, u32[]{:S(2)}, u32[]{:S(2)}) collective-permute-start(bf16[48,768]{1,0:T(8,128)(2,1)} %get-tuple-element.53), channel_id=1, source_target_pairs={{0,254},{2,0},{4,2},{6,4},{8,6},{10,8},{12,10},{14,12},{16,14},{18... | collective-permute-start | bytes 221192 | tf_op jit(solution)/shard_map/ppermute | solution.py:24
  15.2 11.1 %collective-permute-start = (bf16[48,768]{1,0:T(8,128)(2,1)}, bf16[48,768]{1,0:T(8,128)(2,1)S(1)}, u32[]{:S(2)}, u32[]{:S(2)}) collective-permute-start(bf16[48,768]{1,0:T(8,128)(2,1)} %get-tuple-element.53), channel_id=1, source_target_pairs={{0,2},{2,4},{4,6},{6,8},{8,10},{10,12},{12,14},{14,16},{16,18},{18... | collective-permute-start | bytes 221192 | tf_op jit(solution)/shard_map/ppermute | solution.py:24
  15.2 19.5 %collective-permute-start.7 = (bf16[104,768]{1,0:T(8,128)(2,1)}, bf16[104,768]{1,0:T(8,128)(2,1)S(1)}, u32[]{:S(2)}, u32[]{:S(2)}) collective-permute-start(bf16[104,768]{1,0:T(8,128)(2,1)} %get-tuple-element.58), channel_id=1, source_target_pairs={{0,252},{2,254},{4,0},{6,2},{8,4},{10,6},{12,8},{14,10},{16,12},{1... | collective-permute-start | bytes 479240 | tf_op jit(solution)/shard_map/ppermute | solution.py:24
  26.4 10.5 %collective-permute-start.4 = (bf16[96,768]{1,0:T(8,128)(2,1)S(1)}, bf16[96,768]{1,0:T(8,128)(2,1)S(1)}, u32[]{:S(2)}, u32[]{:S(2)}) collective-permute-start(bf16[96,768]{1,0:T(8,128)(2,1)S(1)} %pad_maximum_fusion.4), channel_id=1, source_target_pairs={{0,4},{2,6},{4,8},{6,10},{8,12},{10,14},{12,16},{14,18},{16,20},{1... | collective-permute-start | bytes 442376 | tf_op jit(solution)/shard_map/ppermute | solution.py:24
  26.6 10.4 %collective-permute-start.6 = (bf16[104,768]{1,0:T(8,128)(2,1)}, bf16[104,768]{1,0:T(8,128)(2,1)S(1)}, u32[]{:S(2)}, u32[]{:S(2)}) collective-permute-start(bf16[104,768]{1,0:T(8,128)(2,1)} %get-tuple-element.58), channel_id=1, source_target_pairs={{0,254},{2,0},{4,2},{6,4},{8,6},{10,8},{12,10},{14,12},{16,14},{18... | collective-permute-start | bytes 479240 | tf_op jit(solution)/shard_map/ppermute | solution.py:24
  37.2 14.9 %collective-permute-start.12 = (bf16[2,96,768]{2,1,0:T(8,128)(2,1)S(1)}, bf16[2,96,768]{2,1,0:T(8,128)(2,1)S(1)}, u32[]{:S(2)}, u32[]{:S(2)}) collective-permute-start(bf16[2,96,768]{2,1,0:T(8,128)(2,1)S(1)} %pad_maximum_fusion.3), channel_id=1, source_target_pairs={{0,192},{2,194},{4,196},{6,198},{8,200},{10,202},{12,204},{14,206}... | collective-permute-start | bytes 884744 | tf_op jit(solution)/shard_map/ppermute | solution.py:367
  37.3 14.8 %collective-permute-start.11 = (bf16[2,96,768]{2,1,0:T(8,128)(2,1)S(1)}, bf16[2,96,768]{2,1,0:T(8,128)(2,1)S(1)}, u32[]{:S(2)}, u32[]{:S(2)}) collective-permute-start(bf16[2,96,768]{2,1,0:T(8,128)(2,1)S(1)} %pad_maximum_fusion.3), channel_id=1, source_target_pairs={{0,64},{2,66},{4,68},{6,70},{8,72},{10,74},{12,76},{14,78},{16,80}... | collective-permute-start | bytes 884744 | tf_op jit(solution)/shard_map/ppermute | solution.py:367
  38.7 13.3 %collective-permute-start.10 = (bf16[2,96,768]{2,1,0:T(8,128)(2,1)S(1)}, bf16[2,96,768]{2,1,0:T(8,128)(2,1)S(1)}, u32[]{:S(2)}, u32[]{:S(2)}) collective-permute-start(bf16[2,96,768]{2,1,0:T(8,128)(2,1)S(1)} %pad_maximum_fusion.2), channel_id=1, source_target_pairs={{0,48},{2,50},{4,52},{6,54},{8,56},{10,58},{12,60},{14,62},{16,0},... | collective-permute-start | bytes 884744 | tf_op jit(solution)/shard_map/ppermute | solution.py:367
  38.7 13.3 %collective-permute-start.9 = (bf16[2,96,768]{2,1,0:T(8,128)(2,1)S(1)}, bf16[2,96,768]{2,1,0:T(8,128)(2,1)S(1)}, u32[]{:S(2)}, u32[]{:S(2)}) collective-permute-start(bf16[2,96,768]{2,1,0:T(8,128)(2,1)S(1)} %pad_maximum_fusion.2), channel_id=1, source_target_pairs={{0,16},{2,18},{4,20},{6,22},{8,24},{10,26},{12,28},{14,30},{16,32}... | collective-permute-start | bytes 884744 | tf_op jit(solution)/shard_map/ppermute | solution.py:367
  40.2 11.9 %collective-permute-start.8 = (bf16[104,768]{1,0:T(8,128)(2,1)S(1)}, bf16[104,768]{1,0:T(8,128)(2,1)S(1)}, u32[]{:S(2)}, u32[]{:S(2)}) collective-permute-start(bf16[104,768]{1,0:T(8,128)(2,1)S(1)} %collective-permute-done.7), channel_id=1, source_target_pairs={{0,254},{2,0},{4,2},{6,4},{8,6},{10,8},{12,10},{14,12},{16,14},{18... | collective-permute-start | bytes 479240 | tf_op jit(solution)/shard_map/ppermute | solution.py:24
  57.9 12.2 %collective-permute-start.13 = (bf16[2,96,768]{2,1,0:T(8,128)(2,1)S(1)}, bf16[2,96,768]{2,1,0:T(8,128)(2,1)S(1)}, u32[]{:S(2)}, u32[]{:S(2)}) collective-permute-start(bf16[2,96,768]{2,1,0:T(8,128)(2,1)S(1)} %pad_maximum_fusion.2), channel_id=1, source_target_pairs={{0,32},{2,34},{4,36},{6,38},{8,40},{10,42},{12,44},{14,46},{16,48}... | collective-permute-start | bytes 884744 | tf_op jit(solution)/shard_map/ppermute | solution.py:367
  57.9 12.2 %collective-permute-start.14 = (bf16[2,96,768]{2,1,0:T(8,128)(2,1)S(1)}, bf16[2,96,768]{2,1,0:T(8,128)(2,1)S(1)}, u32[]{:S(2)}, u32[]{:S(2)}) collective-permute-start(bf16[2,96,768]{2,1,0:T(8,128)(2,1)S(1)} %pad_maximum_fusion.3), channel_id=1, source_target_pairs={{0,128},{2,130},{4,132},{6,134},{8,136},{10,138},{12,140},{14,142}... | collective-permute-start | bytes 884744 | tf_op jit(solution)/shard_map/ppermute | solution.py:367
  70.2 27.3 %collective-permute-start.19 = (bf16[2,384,768]{2,1,0:T(8,128)(2,1)S(1)}, bf16[2,384,768]{2,1,0:T(8,128)(2,1)S(1)}, u32[]{:S(2)}, u32[]{:S(2)}) collective-permute-start(bf16[2,384,768]{2,1,0:T(8,128)(2,1)S(1)} %constant_dynamic-update-slice_fusion.4), channel_id=1, source_target_pairs={{0,48},{2,50},{4,52},{6,54},{8,56},{10,58},{12,60},{14,62},{16,0},... | collective-permute-start | bytes 3538952 | tf_op jit(solution)/shard_map/ppermute | solution.py:367
  70.3 28.5 %collective-permute-start.18 = (bf16[2,384,768]{2,1,0:T(8,128)(2,1)S(1)}, bf16[2,384,768]{2,1,0:T(8,128)(2,1)S(1)}, u32[]{:S(2)}, u32[]{:S(2)}) collective-permute-start(bf16[2,384,768]{2,1,0:T(8,128)(2,1)S(1)} %constant_dynamic-update-slice_fusion.4), channel_id=1, source_target_pairs={{0,16},{2,18},{4,20},{6,22},{8,24},{10,26},{12,28},{14,30},{16,32}... | collective-permute-start | bytes 3538952 | tf_op jit(solution)/shard_map/ppermute | solution.py:367
  71.9 26.9 %collective-permute-start.17 = (bf16[2,384,768]{2,1,0:T(8,128)(2,1)S(1)}, bf16[2,384,768]{2,1,0:T(8,128)(2,1)S(1)}, u32[]{:S(2)}, u32[]{:S(2)}) collective-permute-start(bf16[2,384,768]{2,1,0:T(8,128)(2,1)S(1)} %get-tuple-element.102), channel_id=1, source_target_pairs={{0,192},{2,194},{4,196},{6,198},{8,200},{10,202},{12,204},{14,206}... | collective-permute-start | bytes 3538952 | tf_op jit(solution)/shard_map/ppermute | solution.py:367
  72.0 27.8 %collective-permute-start.16 = (bf16[2,384,768]{2,1,0:T(8,128)(2,1)S(1)}, bf16[2,384,768]{2,1,0:T(8,128)(2,1)S(1)}, u32[]{:S(2)}, u32[]{:S(2)}) collective-permute-start(bf16[2,384,768]{2,1,0:T(8,128)(2,1)S(1)} %get-tuple-element.102), channel_id=1, source_target_pairs={{0,64},{2,66},{4,68},{6,70},{8,72},{10,74},{12,76},{14,78},{16,80}... | collective-permute-start | bytes 3538952 | tf_op jit(solution)/shard_map/ppermute | solution.py:367
  100.5 13.1 %collective-permute-start.23 = (bf16[2,192,768]{2,1,0:T(8,128)(2,1)S(1)}, bf16[2,192,768]{2,1,0:T(8,128)(2,1)S(1)}, u32[]{:S(2)}, u32[]{:S(2)}) collective-permute-start(bf16[2,192,768]{2,1,0:T(8,128)(2,1)S(1)} %slice.85), channel_id=1, source_target_pairs={{0,48},{2,50},{4,52},{6,54},{8,56},{10,58},{12,60},{14,62},{16,0},... | collective-permute-start | bytes 1769480 | tf_op jit(solution)/shard_map/ppermute | solution.py:367
  101.6 13.7 %collective-permute-start.22 = (bf16[2,192,768]{2,1,0:T(8,128)(2,1)S(1)}, bf16[2,192,768]{2,1,0:T(8,128)(2,1)S(1)}, u32[]{:S(2)}, u32[]{:S(2)}) collective-permute-start(bf16[2,192,768]{2,1,0:T(8,128)(2,1)S(1)} %slice.84), channel_id=1, source_target_pairs={{0,16},{2,18},{4,20},{6,22},{8,24},{10,26},{12,28},{14,30},{16,32}... | collective-permute-start | bytes 1769480 | tf_op jit(solution)/shard_map/ppermute | solution.py:367
  102.0 13.3 %collective-permute-start.21 = (bf16[2,192,768]{2,1,0:T(8,128)(2,1)S(1)}, bf16[2,192,768]{2,1,0:T(8,128)(2,1)S(1)}, u32[]{:S(2)}, u32[]{:S(2)}) collective-permute-start(bf16[2,192,768]{2,1,0:T(8,128)(2,1)S(1)} %slice.83), channel_id=1, source_target_pairs={{0,192},{2,194},{4,196},{6,198},{8,200},{10,202},{12,204},{14,206}... | collective-permute-start | bytes 1769480 | tf_op jit(solution)/shard_map/ppermute | solution.py:367
  102.7 13.2 %collective-permute-start.20 = (bf16[2,192,768]{2,1,0:T(8,128)(2,1)S(1)}, bf16[2,192,768]{2,1,0:T(8,128)(2,1)S(1)}, u32[]{:S(2)}, u32[]{:S(2)}) collective-permute-start(bf16[2,192,768]{2,1,0:T(8,128)(2,1)S(1)} %slice.82), channel_id=1, source_target_pairs={{0,64},{2,66},{4,68},{6,70},{8,72},{10,74},{12,76},{14,78},{16,80}... | collective-permute-start | bytes 1769480 | tf_op jit(solution)/shard_map/ppermute | solution.py:367
  127.5 14.5 %collective-permute-start.25 = (bf16[196,512]{1,0:T(8,128)(2,1)S(1)}, bf16[196,512]{1,0:T(8,128)(2,1)S(1)}, u32[]{:S(2)}, u32[]{:S(2)}) collective-permute-start(bf16[196,512]{1,0:T(8,128)(2,1)S(1)} %get-tuple-element.96), channel_id=1, source_target_pairs={{0,2},{2,4},{4,6},{6,8},{8,10},{10,12},{12,14},{14,16},{16,18},{18... | collective-permute-start | bytes 602120 | tf_op jit(solution)/shard_map/ppermute | solution.py:24
  142.0 16.5 %collective-permute-start.27 = (bf16[196,512]{1,0:T(8,128)(2,1)S(1)}, bf16[196,512]{1,0:T(8,128)(2,1)S(1)}, u32[]{:S(2)}, u32[]{:S(2)}) collective-permute-start(bf16[196,512]{1,0:T(8,128)(2,1)S(1)} %add_convert_fusion), channel_id=1, source_target_pairs={{0,4},{2,6},{4,8},{6,10},{8,12},{10,14},{12,16},{14,18},{16,20},{1... | collective-permute-start | bytes 602120 | tf_op jit(solution)/shard_map/ppermute | solution.py:24
  142.1 16.4 %collective-permute-start.26 = (bf16[196,512]{1,0:T(8,128)(2,1)S(1)}, bf16[196,512]{1,0:T(8,128)(2,1)S(1)}, u32[]{:S(2)}, u32[]{:S(2)}) collective-permute-start(bf16[196,512]{1,0:T(8,128)(2,1)S(1)} %get-tuple-element.98), channel_id=1, source_target_pairs={{0,2},{2,4},{4,6},{6,8},{8,10},{10,12},{12,14},{14,16},{16,18},{18... | collective-permute-start | bytes 602120 | tf_op jit(solution)/shard_map/ppermute | solution.py:24
  (18 other events, 217.3 us)

commit v7 on v5

--- a/solution.py
+++ b/solution.py
@@ -1,3 +1,5 @@
+import functools
+
 import jax
 import jax.numpy as jnp
 from jax import lax
@@ -210,26 +212,24 @@
             send_ref[slot, :, cols] = jnp.where(first, high, low).astype(BF16)
 
 
-def window_kernel(
-    image_slot, slot_images, slot_count, place, keep, got, out0, out1, out2, out3
-):
-    outs = [out0, out1, out2, out3]
+def window_kernel(windows, image_slot, slot_images, slot_count, place, keep, got, *outs):
     chosen = []
     for slot in range(SLOTS):
         live = slot < slot_count[0]
         for which in range(2):
             index = window_place(image_slot, slot_images, place, slot, which)
-            chosen.append((slot, which, jnp.where(live, index, -1)))
-    for w in range(WINDOW):
+            chosen.append(jnp.where(live, index, -1))
+    first = place[1] == 0
+    for w, out in zip(windows, outs):
         for c in range(4):
             cols = slice(c * 128, (c + 1) * 128)
             acc = jnp.zeros((TOKI, 128), F32)
             for slot in range(SLOTS):
-                own = jnp.where(place[1] == 0, chosen[2 * slot][2], chosen[2 * slot + 1][2])
-                far = jnp.where(place[1] == 0, chosen[2 * slot + 1][2], chosen[2 * slot][2])
+                own = jnp.where(first, chosen[2 * slot], chosen[2 * slot + 1])
+                far = jnp.where(first, chosen[2 * slot + 1], chosen[2 * slot])
                 acc = acc + jnp.where(own == w, keep[slot, :, cols], 0.0)
                 acc = acc + jnp.where(far == w, got[slot, :, cols].astype(F32), 0.0)
-            outs[w][:, cols] = acc.astype(outs[w].dtype)
+            out[:, cols] = acc.astype(out.dtype)
 
 
 def merge_kernel(base, nearest, further, out):
@@ -329,10 +329,11 @@
     )
 
 
-def window_call(scalars, keep, got):
-    return call(
-        window_kernel, scalars, [keep, got],
-        [((TOKI, 512), F32)] + [((TOKI, 512), BF16)] * 3, [], 10**8, "window_part",
+def window_call(windows, scalars, keep, got):
+    return call(
+        functools.partial(window_kernel, windows), scalars, [keep, got],
+        [((TOKI, 512), BF16 if w else F32) for w in windows], [], 10**8,
+        "furthest_part" if windows == (3,) else "window_part",
     )
 
 
@@ -412,10 +413,10 @@
 ):
     place = jnp.stack([lax.axis_index("pairs"), lax.axis_index("side")]).astype(jnp.int32)
     packed, shard = pack_call(features, w_fc1, w_fc2)
-    next3, next2, next1 = [shifted(packed, -by) for by in (3, 2, 1)]
+    next2, next1 = shifted(packed, -2), shifted(packed, -1)
     last1, last2 = shifted(shard, 1), shifted(shard, 2)
     last34 = shifted(jnp.concatenate([last1, last2], axis=0), 2)
-    next1, next2, next3, last34 = tied(next1, next2, next3, last34)
+    next3, last34 = tied(shifted(next2, -1), last34)
     part_x = hidden_rows([shard, next1, next2, last1])
     part_y = hidden_rows([last2, next3, last34[:48], last34[48:]])
     mine = jnp.stack([packed[:TOP], next1[:TOP], next2[:TOP], next3[:TOP]])
@@ -439,11 +440,13 @@
     fc_late = jnp.concatenate([*far_x, *far_y], axis=1)
     keep, send = late_call(place, early, mlp_in, fc_late, gain_head, w_head[0])
     got = other_core(send)
-    pieces = window_call([image_slot, slot_images.reshape(-1), slot_count, place], keep, got)
-    third, nearest = tied(shifted(pieces[3], 1), pieces[1])
-    further = shifted((pieces[2].astype(F32) + third.astype(F32)).astype(BF16), 2)
-    nearest = shifted(nearest, 1)
-    return merge_call(pieces[0], nearest, further)
+    scalars = [image_slot, slot_images.reshape(-1), slot_count, place]
+    (furthest,) = window_call((3,), scalars, keep, got)
+    third = shifted(furthest, 1)
+    base, piece1, piece2 = window_call((0, 1, 2), scalars, keep, got)
+    nearest = shifted(piece1, 1)
+    further = shifted((piece2.astype(F32) + third.astype(F32)).astype(BF16), 2)
+    return merge_call(base, nearest, further)
 
 
 def solution(mesh):

time: 153 us -> 143 us (0.935)
  waiting for transfers between devices: 67 us -> 52.1 us
  starting transfers between devices: 37.1 us -> 41.8 us
    ppermute x9, waiting for transfers between devices: 51.8 us -> 36.1 us  [shifted(): lax.ppermute(array, 'pairs', [(i, (i + by) % count) for i in range(count)])]
    ppermute x9, starting transfers between devices: 18.1 us -> 21.3 us  [shifted(): lax.ppermute(array, 'pairs', [(i, (i + by) % count) for i in range(count)])]
    ppermute x2, starting transfers between devices: 6.05 us -> 8 us  [other_core(): return lax.ppermute(array, 'side', [(0, 1), (1, 0)])]
    pallas_call x8 -> x9, Pallas kernels: 41.6 us -> 42.2 us  [call(): pl.pallas_call(kernel, in_specs=[SMEM] * len(scalars) + [VMEM] * len(arra...]
  transfers between devices with their start and end apart: 25 -> 25, of which waited for: 16 -> 17; matrix products, arithmetic and copies ran while one was open for 2% -> 2% of each run, Pallas kernels for 23% -> 25%
where the time goes in v7:
time: 143 us
  waiting for transfers between devices  52.1 us (36%)
  Pallas kernels  43.8 us (31%)
  starting transfers between devices  41.8 us (29%)
  local copies, waits for them, and re-layouts  3.33 us (2%)
    pallas_call x9, Pallas kernels, call(): pl.pallas_call(kernel, in_specs=[SMEM] * len(scalars) + [VMEM] * len(arra...  42.2 us
    ppermute x9, waiting for transfers between devices, shifted(): lax.ppermute(array, 'pairs', [(i, (i + by) % count) for i in range(count)])  36.1 us
    ppermute x9, starting transfers between devices, shifted(): lax.ppermute(array, 'pairs', [(i, (i + by) % count) for i in range(count)])  21.3 us
    ppermute x14, waiting for transfers between devices, along(): return lax.ppermute(array, 'pairs', [(p, target(p)) for p in range(count)])  15 us
    ppermute x14, starting transfers between devices, along(): return lax.ppermute(array, 'pairs', [(p, target(p)) for p in range(count)])  12.6 us
    ppermute x2, starting transfers between devices, other_core(): return lax.ppermute(array, 'side', [(0, 1), (1, 0)])  8 us
  transfers between devices with their start and end apart: 25, of which 17 were waited for; matrix products, arithmetic and copies ran while one was open for 2% of the time, Pallas kernels for 25%

profile of v7, /device:TPU:1, one launch (start us, length us, event | category | flops | bytes accessed | tf_op | source)
XLA Modules:
  0.0 142.9 jit_solution(7906000017107924106)
XLA Ops:
  1.7 3.9 %collective-permute-start.6 = (bf16[48,768]{1,0:T(8,128)(2,1)}, bf16[48,768]{1,0:T(8,128)(2,1)S(1)}, u32[]{:S(2)}, u32[]{:S(2)}) collective-permute-start(bf16[48,768]{1,0:T(8,128)(2,1)} %get-tuple-element.37), channel_id=1, source_target_pairs={{0,4},{2,6},{4,8},{6,10},{8,12},{10,14},{12,16},{14,18},{16,20},{1... | collective-permute-start | bytes 221192 | tf_op jit(solution)/shard_map/ppermute | solution.py:26
  7.2 6.9 %collective-permute-start.1 = (bf16[152,768]{1,0:T(8,128)(2,1)}, bf16[152,768]{1,0:T(8,128)(2,1)S(1)}, u32[]{:S(2)}, u32[]{:S(2)}) collective-permute-start(bf16[152,768]{1,0:T(8,128)(2,1)} %get-tuple-element.38), channel_id=1, source_target_pairs={{0,252},{2,254},{4,0},{6,2},{8,4},{10,6},{12,8},{14,10},{16,12},{1... | collective-permute-start | bytes 700424 | tf_op jit(solution)/shard_map/ppermute | solution.py:26
  18.6 5.8 %collective-permute-done.1 = bf16[152,768]{1,0:T(8,128)(2,1)S(1)} collective-permute-done((bf16[152,768]{1,0:T(8,128)(2,1)}, bf16[152,768]{1,0:T(8,128)(2,1)S(1)}, u32[]{:S(2)}, u32[]{:S(2)}) %collective-permute-start.1) | collective-permute-done | bytes 233504 | tf_op jit(solution)/shard_map/ppermute | solution.py:26
  24.4 5.1 %collective-permute-start.7 = (bf16[152,768]{1,0:T(8,128)(2,1)S(1)}, bf16[152,768]{1,0:T(8,128)(2,1)S(1)}, u32[]{:S(2)}, u32[]{:S(2)}) collective-permute-start(bf16[152,768]{1,0:T(8,128)(2,1)S(1)} %collective-permute-done.1), channel_id=1, source_target_pairs={{0,254},{2,0},{4,2},{6,4},{8,6},{10,8},{12,10},{14,12},{16,14},{18... | collective-permute-start | bytes 700424 | tf_op jit(solution)/shard_map/ppermute | solution.py:26
  29.8 3.1 %collective-permute-done.7 = bf16[152,768]{1,0:T(8,128)(2,1)S(1)} collective-permute-done((bf16[152,768]{1,0:T(8,128)(2,1)S(1)}, bf16[152,768]{1,0:T(8,128)(2,1)S(1)}, u32[]{:S(2)}, u32[]{:S(2)}) %collective-permute-start.7) | collective-permute-done | bytes 233504 | tf_op jit(solution)/shard_map/ppermute | solution.py:26
  33.0 2.6 %collective-permute-start.11 = (bf16[4,104,768]{2,1,0:T(8,128)(2,1)S(1)}, bf16[4,104,768]{2,1,0:T(8,128)(2,1)S(1)}, u32[]{:S(2)}, u32[]{:S(2)}) collective-permute-start(bf16[4,104,768]{2,1,0:T(8,128)(2,1)S(1)} %pad_maximum_fusion.3.mine), channel_id=1, source_target_pairs={{0,1},{1,0},{2,3},{3,2},{4,5},{5,4},{6,7},{7,6},{8,9},{9,8},{10,11... | collective-permute-start | bytes 1916936 | tf_op jit(solution)/shard_map/ppermute | solution.py:30
  37.4 2.3 %collective-permute-start.10 = (bf16[2,96,768]{2,1,0:T(8,128)(2,1)S(1)}, bf16[2,96,768]{2,1,0:T(8,128)(2,1)S(1)}, u32[]{:S(2)}, u32[]{:S(2)}) collective-permute-start(bf16[2,96,768]{2,1,0:T(8,128)(2,1)S(1)} %pad_maximum_fusion.5), channel_id=1, source_target_pairs={{0,192},{2,194},{4,196},{6,198},{8,200},{10,202},{12,204},{14,206}... | collective-permute-start | bytes 884744 | tf_op jit(solution)/shard_map/ppermute | solution.py:369
  39.7 5.0 %triple_part.1 = (f32[624,768]{1,0:T(8,128)S(1)}, bf16[624,2304]{1,0:T(8,128)(2,1)S(1)}) custom-call(s32[128]{0:T(128)S(1)} %copy-done, s32[6]{0:T(128)S(1)} %reshape.4.slot_images, s32[2]{0:T(128)S(1)} %pad_add_fusion.place, bf16[4,104,768]{2,1,0:T(8,128)(2,1)S(1)} %pad_maximum_fusion.3.mine, bf16[4,104,768]{2,1,0:T(8,128)(2,1)S(1)} %collective-permute-done.11.theirs, ...), custom_call_target="tpu_custom_call" | custom-call | flops 4000000000 | bytes 8388608 | tf_op jit(solution)/shard_map/triple_part/pallas_call | solution.py:272
  46.9 3.7 %memory_part.1.key_value = bf16[624,1536]{1,0:T(8,128)(2,1)S(1)} custom-call(s32[128]{0:T(128)S(1)} %copy-done, s32[6]{0:T(128)S(1)} %reshape.4.slot_images, s32[2]{0:T(128)S(1)} %pad_add_fusion.place, bf16[4,104,768]{2,1,0:T(8,128)(2,1)S(1)} %pad_maximum_fusion.3.mine, bf16[4,104,768]{2,1,0:T(8,128)(2,1)S(1)} %collective-permute-done.11.theirs, ...), custom_call_target="tpu_custom_call" | custom-call | flops 3000000000 | bytes 8388608 | tf_op jit(solution)/shard_map/memory_part/pallas_call | solution.py:272
  50.7 1.9 %collective-permute-done.3 = bf16[2,96,768]{2,1,0:T(8,128)(2,1)S(1)} collective-permute-done((bf16[2,96,768]{2,1,0:T(8,128)(2,1)S(1)}, bf16[2,96,768]{2,1,0:T(8,128)(2,1)S(1)}, u32[]{:S(2)}, u32[]{:S(2)}) %collective-permute-start.3) | collective-permute-done | bytes 294944 | tf_op jit(solution)/shard_map/ppermute | solution.py:369
  52.6 2.2 %collective-permute-done.12 = bf16[2,96,768]{2,1,0:T(8,128)(2,1)S(1)} collective-permute-done((bf16[2,96,768]{2,1,0:T(8,128)(2,1)S(1)}, bf16[2,96,768]{2,1,0:T(8,128)(2,1)S(1)}, u32[]{:S(2)}, u32[]{:S(2)}) %collective-permute-start.12) | collective-permute-done | bytes 294944 | tf_op jit(solution)/shard_map/ppermute | solution.py:369
  56.7 2.0 %collective-permute-start.14 = (bf16[2,384,768]{2,1,0:T(8,128)(2,1)S(1)}, bf16[2,384,768]{2,1,0:T(8,128)(2,1)S(1)}, u32[]{:S(2)}, u32[]{:S(2)}) collective-permute-start(bf16[2,384,768]{2,1,0:T(8,128)(2,1)S(1)} %pad_maximum_fusion.1), channel_id=1, source_target_pairs={{0,192},{2,194},{4,196},{6,198},{8,200},{10,202},{12,204},{14,206}... | collective-permute-start | bytes 3538952 | tf_op jit(solution)/shard_map/ppermute | solution.py:369
  58.8 10.5 %self_part.1 = (f32[624,768]{1,0:T(8,128)S(1)}, bf16[624,768]{1,0:T(8,128)(2,1)S(1)}) custom-call(f32[624,768]{1,0:T(8,128)S(1)} %get-tuple-element.51.rows, bf16[624,2304]{1,0:T(8,128)(2,1)S(1)} %get-tuple-element.52.triple, f32[1,768]{1,0:T(1,128)S(1)} %copy-done.9, bf16[768,768]{1,0:T(8,128)(2,1)S(1)} %bitcast.27, bf16[768,768]{1,0:T(8,128)(2,1)S(1)} %bitcast.28), custom_call_target="tpu_custom_call" | custom-call | flops 12000000000 | bytes 8388608 | tf_op jit(solution)/shard_map/self_part/pallas_call | solution.py:272
  69.4 9.2 %cross_part.1 = (f32[624,768]{1,0:T(8,128)S(1)}, bf16[624,768]{1,0:T(8,128)(2,1)S(1)}) custom-call(f32[624,768]{1,0:T(8,128)S(1)} %get-tuple-element.53.first, bf16[624,768]{1,0:T(8,128)(2,1)S(1)} %get-tuple-element.54.query, bf16[624,1536]{1,0:T(8,128)(2,1)S(1)} %memory_part.1.key_value, f32[1,768]{1,0:T(1,128)S(1)} %copy-done.10, bf16[768,768]{1,0:T(8,128)(2,1)S(1)} %bitcast.29), custom_call_target="tpu_custom_call" | custom-call | flops 12000000000 | bytes 8388608 | tf_op jit(solution)/shard_map/cross_part/pallas_call | solution.py:272
  81.8 2.7 %collective-permute-done.13 = bf16[2,384,768]{2,1,0:T(8,128)(2,1)S(1)} collective-permute-done((bf16[2,384,768]{2,1,0:T(8,128)(2,1)S(1)}, bf16[2,384,768]{2,1,0:T(8,128)(2,1)S(1)}, u32[]{:S(2)}, u32[]{:S(2)}) %collective-permute-start.13) | collective-permute-done | bytes 1179680 | tf_op jit(solution)/shard_map/ppermute | solution.py:369
  85.1 2.5 %collective-permute-start.20 = (bf16[2,192,768]{2,1,0:T(8,128)(2,1)S(1)}, bf16[2,192,768]{2,1,0:T(8,128)(2,1)S(1)}, u32[]{:S(2)}, u32[]{:S(2)}) collective-permute-start(bf16[2,192,768]{2,1,0:T(8,128)(2,1)S(1)} %slice.101), channel_id=1, source_target_pairs={{0,48},{2,50},{4,52},{6,54},{8,56},{10,58},{12,60},{14,62},{16,0},... | collective-permute-start | bytes 1769480 | tf_op jit(solution)/shard_map/ppermute | solution.py:369
  89.1 6.5 %early_part.1.early = f32[624,768]{1,0:T(8,128)S(1)} custom-call(f32[624,768]{1,0:T(8,128)S(1)} %get-tuple-element.58.second, bf16[624,768]{1,0:T(8,128)(2,1)S(1)} %get-tuple-element.59.mlp_in, bf16[2,2304,768]{2,1,0:T(8,128)(2,1)S(1)} %constant_dynamic-update-slice_fusion.fc), custom_call_target="tpu_custom_call" | custom-call | flops 10000000000 | bytes 8388608 | tf_op jit(solution)/shard_map/early_part/pallas_call | solution.py:272
  96.2 3.0 %collective-permute-done.19 = bf16[2,192,768]{2,1,0:T(8,128)(2,1)S(1)} collective-permute-done((bf16[2,192,768]{2,1,0:T(8,128)(2,1)S(1)}, bf16[2,192,768]{2,1,0:T(8,128)(2,1)S(1)}, u32[]{:S(2)}, u32[]{:S(2)}) %collective-permute-start.19) | collective-permute-done | bytes 589856 | tf_op jit(solution)/shard_map/ppermute | solution.py:369
  99.7 4.4 %late_part.1 = (f32[3,196,512]{2,1,0:T(8,128)S(1)}, bf16[3,196,512]{2,1,0:T(8,128)(2,1)S(1)}) custom-call(s32[2]{0:T(128)S(1)} %pad_add_fusion.place, f32[624,768]{1,0:T(8,128)S(1)} %early_part.1.early, bf16[624,768]{1,0:T(8,128)(2,1)S(1)} %get-tuple-element.59.mlp_in, bf16[2,768,768]{2,1,0:T(8,128)(2,1)S(1)} %pad_maximum_fusion.fc, ...), custom_call_target="tpu_custom_call" | custom-call | flops 5000000000 | bytes 8388608 | tf_op jit(solution)/shard_map/late_part/pallas_call | solution.py:272
  104.1 5.4 %collective-permute-start.21 = (bf16[3,196,512]{2,1,0:T(8,128)(2,1)S(1)}, bf16[3,196,512]{2,1,0:T(8,128)(2,1)S(1)}, u32[]{:S(2)}, u32[]{:S(2)}) collective-permute-start(bf16[3,196,512]{2,1,0:T(8,128)(2,1)S(1)} %get-tuple-element.65), channel_id=1, source_target_pairs={{0,1},{1,0},{2,3},{3,2},{4,5},{5,4},{6,7},{7,6},{8,9},{9,8},{10,11... | collective-permute-start | bytes 1806344 | tf_op jit(solution)/shard_map/ppermute | solution.py:30
  113.7 2.0 %collective-permute-start.22 = (bf16[196,512]{1,0:T(8,128)(2,1)S(1)}, bf16[196,512]{1,0:T(8,128)(2,1)S(1)}, u32[]{:S(2)}, u32[]{:S(2)}) collective-permute-start(bf16[196,512]{1,0:T(8,128)(2,1)S(1)} %get-tuple-element.67), channel_id=1, source_target_pairs={{0,2},{2,4},{4,6},{6,8},{8,10},{10,12},{12,14},{14,16},{16,18},{18... | collective-permute-start | bytes 602120 | tf_op jit(solution)/shard_map/ppermute | solution.py:26
  115.6 9.4 %collective-permute-done.23 = bf16[196,512]{1,0:T(8,128)(2,1)S(1)} collective-permute-done((bf16[196,512]{1,0:T(8,128)(2,1)S(1)}, bf16[196,512]{1,0:T(8,128)(2,1)S(1)}, u32[]{:S(2)}, u32[]{:S(2)}) %collective-permute-start.23) | collective-permute-done | bytes 200736 | tf_op jit(solution)/shard_map/ppermute | solution.py:26
  125.2 4.2 %collective-permute-done.22.nearest = bf16[196,512]{1,0:T(8,128)(2,1)S(1)} collective-permute-done((bf16[196,512]{1,0:T(8,128)(2,1)S(1)}, bf16[196,512]{1,0:T(8,128)(2,1)S(1)}, u32[]{:S(2)}, u32[]{:S(2)}) %collective-permute-start.22) | collective-permute-done | bytes 200736 | tf_op jit(solution)/shard_map/ppermute | solution.py:26
  129.4 12.8 %collective-permute-done.24.further = bf16[196,512]{1,0:T(8,128)(2,1)S(1)} collective-permute-done((bf16[196,512]{1,0:T(8,128)(2,1)S(1)}, bf16[196,512]{1,0:T(8,128)(2,1)S(1)}, u32[]{:S(2)}, u32[]{:S(2)}) %collective-permute-start.24) | collective-permute-done | bytes 200736 | tf_op jit(solution)/shard_map/ppermute | solution.py:26
  (99 shorter events, 24.6 us)
Async XLA Ops:
  1.7 16.1 %collective-permute-start.6 = (bf16[48,768]{1,0:T(8,128)(2,1)}, bf16[48,768]{1,0:T(8,128)(2,1)S(1)}, u32[]{:S(2)}, u32[]{:S(2)}) collective-permute-start(bf16[48,768]{1,0:T(8,128)(2,1)} %get-tuple-element.37), channel_id=1, source_target_pairs={{0,4},{2,6},{4,8},{6,10},{8,12},{10,14},{12,16},{14,18},{16,20},{1... | collective-permute-start | bytes 221192 | tf_op jit(solution)/shard_map/ppermute | solution.py:26
  5.6 12.9 %collective-permute-start.2 = (bf16[48,768]{1,0:T(8,128)(2,1)}, bf16[48,768]{1,0:T(8,128)(2,1)S(1)}, u32[]{:S(2)}, u32[]{:S(2)}) collective-permute-start(bf16[48,768]{1,0:T(8,128)(2,1)} %get-tuple-element.37), channel_id=1, source_target_pairs={{0,2},{2,4},{4,6},{6,8},{8,10},{10,12},{12,14},{14,16},{16,18},{18... | collective-permute-start | bytes 221192 | tf_op jit(solution)/shard_map/ppermute | solution.py:26
  7.2 17.2 %collective-permute-start.1 = (bf16[152,768]{1,0:T(8,128)(2,1)}, bf16[152,768]{1,0:T(8,128)(2,1)S(1)}, u32[]{:S(2)}, u32[]{:S(2)}) collective-permute-start(bf16[152,768]{1,0:T(8,128)(2,1)} %get-tuple-element.38), channel_id=1, source_target_pairs={{0,252},{2,254},{4,0},{6,2},{8,4},{10,6},{12,8},{14,10},{16,12},{1... | collective-permute-start | bytes 700424 | tf_op jit(solution)/shard_map/ppermute | solution.py:26
  14.1 15.5 %collective-permute-start = (bf16[152,768]{1,0:T(8,128)(2,1)}, bf16[152,768]{1,0:T(8,128)(2,1)S(1)}, u32[]{:S(2)}, u32[]{:S(2)}) collective-permute-start(bf16[152,768]{1,0:T(8,128)(2,1)} %get-tuple-element.38), channel_id=1, source_target_pairs={{0,254},{2,0},{4,2},{6,4},{8,6},{10,8},{12,10},{14,12},{16,14},{18... | collective-permute-start | bytes 700424 | tf_op jit(solution)/shard_map/ppermute | solution.py:26
  18.5 11.3 %collective-permute-start.8 = (bf16[96,768]{1,0:T(8,128)(2,1)S(1)}, bf16[96,768]{1,0:T(8,128)(2,1)S(1)}, u32[]{:S(2)}, u32[]{:S(2)}) collective-permute-start(bf16[96,768]{1,0:T(8,128)(2,1)S(1)} %pad_maximum_fusion.6), channel_id=1, source_target_pairs={{0,4},{2,6},{4,8},{6,10},{8,12},{10,14},{12,16},{14,18},{16,20},{1... | collective-permute-start | bytes 442376 | tf_op jit(solution)/shard_map/ppermute | solution.py:26
  24.4 8.5 %collective-permute-start.7 = (bf16[152,768]{1,0:T(8,128)(2,1)S(1)}, bf16[152,768]{1,0:T(8,128)(2,1)S(1)}, u32[]{:S(2)}, u32[]{:S(2)}) collective-permute-start(bf16[152,768]{1,0:T(8,128)(2,1)S(1)} %collective-permute-done.1), channel_id=1, source_target_pairs={{0,254},{2,0},{4,2},{6,4},{8,6},{10,8},{12,10},{14,12},{16,14},{18... | collective-permute-start | bytes 700424 | tf_op jit(solution)/shard_map/ppermute | solution.py:26
  35.7 10.3 %collective-permute-start.5 = (bf16[2,96,768]{2,1,0:T(8,128)(2,1)S(1)}, bf16[2,96,768]{2,1,0:T(8,128)(2,1)S(1)}, u32[]{:S(2)}, u32[]{:S(2)}) collective-permute-start(bf16[2,96,768]{2,1,0:T(8,128)(2,1)S(1)} %get-tuple-element.70), channel_id=1, source_target_pairs={{0,32},{2,34},{4,36},{6,38},{8,40},{10,42},{12,44},{14,46},{16,48}... | collective-permute-start | bytes 884744 | tf_op jit(solution)/shard_map/ppermute | solution.py:369
  35.8 14.9 %collective-permute-start.4 = (bf16[2,96,768]{2,1,0:T(8,128)(2,1)S(1)}, bf16[2,96,768]{2,1,0:T(8,128)(2,1)S(1)}, u32[]{:S(2)}, u32[]{:S(2)}) collective-permute-start(bf16[2,96,768]{2,1,0:T(8,128)(2,1)S(1)} %get-tuple-element.70), channel_id=1, source_target_pairs={{0,48},{2,50},{4,52},{6,54},{8,56},{10,58},{12,60},{14,62},{16,0},... | collective-permute-start | bytes 884744 | tf_op jit(solution)/shard_map/ppermute | solution.py:369
  36.2 16.4 %collective-permute-start.3 = (bf16[2,96,768]{2,1,0:T(8,128)(2,1)S(1)}, bf16[2,96,768]{2,1,0:T(8,128)(2,1)S(1)}, u32[]{:S(2)}, u32[]{:S(2)}) collective-permute-start(bf16[2,96,768]{2,1,0:T(8,128)(2,1)S(1)} %get-tuple-element.70), channel_id=1, source_target_pairs={{0,16},{2,18},{4,20},{6,22},{8,24},{10,26},{12,28},{14,30},{16,32}... | collective-permute-start | bytes 884744 | tf_op jit(solution)/shard_map/ppermute | solution.py:369
  37.4 15.1 %collective-permute-start.10 = (bf16[2,96,768]{2,1,0:T(8,128)(2,1)S(1)}, bf16[2,96,768]{2,1,0:T(8,128)(2,1)S(1)}, u32[]{:S(2)}, u32[]{:S(2)}) collective-permute-start(bf16[2,96,768]{2,1,0:T(8,128)(2,1)S(1)} %pad_maximum_fusion.5), channel_id=1, source_target_pairs={{0,192},{2,194},{4,196},{6,198},{8,200},{10,202},{12,204},{14,206}... | collective-permute-start | bytes 884744 | tf_op jit(solution)/shard_map/ppermute | solution.py:369
  39.7 12.9 %collective-permute-start.9 = (bf16[2,96,768]{2,1,0:T(8,128)(2,1)S(1)}, bf16[2,96,768]{2,1,0:T(8,128)(2,1)S(1)}, u32[]{:S(2)}, u32[]{:S(2)}) collective-permute-start(bf16[2,96,768]{2,1,0:T(8,128)(2,1)S(1)} %pad_maximum_fusion.5), channel_id=1, source_target_pairs={{0,64},{2,66},{4,68},{6,70},{8,72},{10,74},{12,76},{14,78},{16,80}... | collective-permute-start | bytes 884744 | tf_op jit(solution)/shard_map/ppermute | solution.py:369
  46.0 8.8 %collective-permute-start.12 = (bf16[2,96,768]{2,1,0:T(8,128)(2,1)S(1)}, bf16[2,96,768]{2,1,0:T(8,128)(2,1)S(1)}, u32[]{:S(2)}, u32[]{:S(2)}) collective-permute-start(bf16[2,96,768]{2,1,0:T(8,128)(2,1)S(1)} %pad_maximum_fusion.5), channel_id=1, source_target_pairs={{0,128},{2,130},{4,132},{6,134},{8,136},{10,138},{12,140},{14,142}... | collective-permute-start | bytes 884744 | tf_op jit(solution)/shard_map/ppermute | solution.py:369
  54.9 25.6 %collective-permute-start.16 = (bf16[2,384,768]{2,1,0:T(8,128)(2,1)S(1)}, bf16[2,384,768]{2,1,0:T(8,128)(2,1)S(1)}, u32[]{:S(2)}, u32[]{:S(2)}) collective-permute-start(bf16[2,384,768]{2,1,0:T(8,128)(2,1)S(1)} %pad_maximum_fusion.2), channel_id=1, source_target_pairs={{0,48},{2,50},{4,52},{6,54},{8,56},{10,58},{12,60},{14,62},{16,0},... | collective-permute-start | bytes 3538952 | tf_op jit(solution)/shard_map/ppermute | solution.py:369
  56.2 25.5 %collective-permute-start.15 = (bf16[2,384,768]{2,1,0:T(8,128)(2,1)S(1)}, bf16[2,384,768]{2,1,0:T(8,128)(2,1)S(1)}, u32[]{:S(2)}, u32[]{:S(2)}) collective-permute-start(bf16[2,384,768]{2,1,0:T(8,128)(2,1)S(1)} %pad_maximum_fusion.2), channel_id=1, source_target_pairs={{0,16},{2,18},{4,20},{6,22},{8,24},{10,26},{12,28},{14,30},{16,32}... | collective-permute-start | bytes 3538952 | tf_op jit(solution)/shard_map/ppermute | solution.py:369
  56.7 25.1 %collective-permute-start.14 = (bf16[2,384,768]{2,1,0:T(8,128)(2,1)S(1)}, bf16[2,384,768]{2,1,0:T(8,128)(2,1)S(1)}, u32[]{:S(2)}, u32[]{:S(2)}) collective-permute-start(bf16[2,384,768]{2,1,0:T(8,128)(2,1)S(1)} %pad_maximum_fusion.1), channel_id=1, source_target_pairs={{0,192},{2,194},{4,196},{6,198},{8,200},{10,202},{12,204},{14,206}... | collective-permute-start | bytes 3538952 | tf_op jit(solution)/shard_map/ppermute | solution.py:369
  58.7 25.8 %collective-permute-start.13 = (bf16[2,384,768]{2,1,0:T(8,128)(2,1)S(1)}, bf16[2,384,768]{2,1,0:T(8,128)(2,1)S(1)}, u32[]{:S(2)}, u32[]{:S(2)}) collective-permute-start(bf16[2,384,768]{2,1,0:T(8,128)(2,1)S(1)} %pad_maximum_fusion.1), channel_id=1, source_target_pairs={{0,64},{2,66},{4,68},{6,70},{8,72},{10,74},{12,76},{14,78},{16,80}... | collective-permute-start | bytes 3538952 | tf_op jit(solution)/shard_map/ppermute | solution.py:369
  85.1 11.1 %collective-permute-start.20 = (bf16[2,192,768]{2,1,0:T(8,128)(2,1)S(1)}, bf16[2,192,768]{2,1,0:T(8,128)(2,1)S(1)}, u32[]{:S(2)}, u32[]{:S(2)}) collective-permute-start(bf16[2,192,768]{2,1,0:T(8,128)(2,1)S(1)} %slice.101), channel_id=1, source_target_pairs={{0,48},{2,50},{4,52},{6,54},{8,56},{10,58},{12,60},{14,62},{16,0},... | collective-permute-start | bytes 1769480 | tf_op jit(solution)/shard_map/ppermute | solution.py:369
  87.6 11.6 %collective-permute-start.19 = (bf16[2,192,768]{2,1,0:T(8,128)(2,1)S(1)}, bf16[2,192,768]{2,1,0:T(8,128)(2,1)S(1)}, u32[]{:S(2)}, u32[]{:S(2)}) collective-permute-start(bf16[2,192,768]{2,1,0:T(8,128)(2,1)S(1)} %slice.100), channel_id=1, source_target_pairs={{0,16},{2,18},{4,20},{6,22},{8,24},{10,26},{12,28},{14,30},{16,32}... | collective-permute-start | bytes 1769480 | tf_op jit(solution)/shard_map/ppermute | solution.py:369
  87.6 11.6 %collective-permute-start.18 = (bf16[2,192,768]{2,1,0:T(8,128)(2,1)S(1)}, bf16[2,192,768]{2,1,0:T(8,128)(2,1)S(1)}, u32[]{:S(2)}, u32[]{:S(2)}) collective-permute-start(bf16[2,192,768]{2,1,0:T(8,128)(2,1)S(1)} %slice.99), channel_id=1, source_target_pairs={{0,192},{2,194},{4,196},{6,198},{8,200},{10,202},{12,204},{14,206}... | collective-permute-start | bytes 1769480 | tf_op jit(solution)/shard_map/ppermute | solution.py:369
  87.9 11.6 %collective-permute-start.17 = (bf16[2,192,768]{2,1,0:T(8,128)(2,1)S(1)}, bf16[2,192,768]{2,1,0:T(8,128)(2,1)S(1)}, u32[]{:S(2)}, u32[]{:S(2)}) collective-permute-start(bf16[2,192,768]{2,1,0:T(8,128)(2,1)S(1)} %slice.98), channel_id=1, source_target_pairs={{0,64},{2,66},{4,68},{6,70},{8,72},{10,74},{12,76},{14,78},{16,80}... | collective-permute-start | bytes 1769480 | tf_op jit(solution)/shard_map/ppermute | solution.py:369
  104.1 7.1 %collective-permute-start.21 = (bf16[3,196,512]{2,1,0:T(8,128)(2,1)S(1)}, bf16[3,196,512]{2,1,0:T(8,128)(2,1)S(1)}, u32[]{:S(2)}, u32[]{:S(2)}) collective-permute-start(bf16[3,196,512]{2,1,0:T(8,128)(2,1)S(1)} %get-tuple-element.65), channel_id=1, source_target_pairs={{0,1},{1,0},{2,3},{3,2},{4,5},{5,4},{6,7},{7,6},{8,9},{9,8},{10,11... | collective-permute-start | bytes 1806344 | tf_op jit(solution)/shard_map/ppermute | solution.py:30
  112.0 13.0 %collective-permute-start.23 = (bf16[196,512]{1,0:T(8,128)(2,1)S(1)}, bf16[196,512]{1,0:T(8,128)(2,1)S(1)}, u32[]{:S(2)}, u32[]{:S(2)}) collective-permute-start(bf16[196,512]{1,0:T(8,128)(2,1)S(1)} %furthest_part.1), channel_id=1, source_target_pairs={{0,2},{2,4},{4,6},{6,8},{8,10},{10,12},{12,14},{14,16},{16,18},{18... | collective-permute-start | bytes 602120 | tf_op jit(solution)/shard_map/ppermute | solution.py:26
  113.7 15.7 %collective-permute-start.22 = (bf16[196,512]{1,0:T(8,128)(2,1)S(1)}, bf16[196,512]{1,0:T(8,128)(2,1)S(1)}, u32[]{:S(2)}, u32[]{:S(2)}) collective-permute-start(bf16[196,512]{1,0:T(8,128)(2,1)S(1)} %get-tuple-element.67), channel_id=1, source_target_pairs={{0,2},{2,4},{4,6},{6,8},{8,10},{10,12},{12,14},{14,16},{16,18},{18... | collective-permute-start | bytes 602120 | tf_op jit(solution)/shard_map/ppermute | solution.py:26
  125.1 17.1 %collective-permute-start.24 = (bf16[196,512]{1,0:T(8,128)(2,1)S(1)}, bf16[196,512]{1,0:T(8,128)(2,1)S(1)}, u32[]{:S(2)}, u32[]{:S(2)}) collective-permute-start(bf16[196,512]{1,0:T(8,128)(2,1)S(1)} %add_convert_fusion), channel_id=1, source_target_pairs={{0,4},{2,6},{4,8},{6,10},{8,12},{10,14},{12,16},{14,18},{16,20},{1... | collective-permute-start | bytes 602120 | tf_op jit(solution)/shard_map/ppermute | solution.py:26
  (13 other events, 92.4 us)

commit v8 on v7

--- a/solution.py
+++ b/solution.py
@@ -417,15 +417,13 @@
     last1, last2 = shifted(shard, 1), shifted(shard, 2)
     last34 = shifted(jnp.concatenate([last1, last2], axis=0), 2)
     next3, last34 = tied(shifted(next2, -1), last34)
-    part_x = hidden_rows([shard, next1, next2, last1])
-    part_y = hidden_rows([last2, next3, last34[:48], last34[48:]])
+    part_x = hidden_rows([shard, last1, last2, next1])
+    part_y = hidden_rows([next2, next3, last34[:48], last34[48:]])
     mine = jnp.stack([packed[:TOP], next1[:TOP], next2[:TOP], next3[:TOP]])
     theirs = other_core(mine)
     scalars = [image_slot, slot_images.reshape(-1), place]
-    near_x, near_y = three_hops(part_x, "x"), list(first_hop(part_y, "y"))
+    near_x, near_y = three_hops(part_x, "x"), three_hops(part_y, "y")
     rows, triple = triple_call(scalars, mine, theirs, gain_self, w_qkv[0])
-    triple, later = tied(triple, part_y)
-    near_y.append(along(later, "y", 2))
     key_value = memory_call(scalars, mine, theirs, gain_memory, w_memory[0])
     near_x, near_y, rows, triple, key_value = tied(near_x, near_y, rows, triple, key_value)
     plane_x = jnp.concatenate([part_x, *near_x], axis=1)

time: 143 us -> 155 us (1.084)
  waiting for transfers between devices: 52.1 us -> 67.7 us
  starting transfers between devices: 41.8 us -> 37.8 us
    ppermute x9, waiting for transfers between devices: 36.1 us -> 47.6 us  [shifted(): lax.ppermute(array, 'pairs', [(i, (i + by) % count) for i in range(count)])]
    ppermute x14, starting transfers between devices: 12.6 us -> 8.25 us  [along(): return lax.ppermute(array, 'pairs', [(p, target(p)) for p in range(count)])]
    ppermute x14, waiting for transfers between devices: 15 us -> 17.7 us  [along(): return lax.ppermute(array, 'pairs', [(p, target(p)) for p in range(count)])]
  transfers between devices with their start and end apart: 25 -> 25, of which waited for: 17 -> 15; matrix products, arithmetic and copies ran while one was open for 2% -> 2% of each run, Pallas kernels for 25% -> 23%
where the time goes in v8:
time: 155 us
  waiting for transfers between devices  67.7 us (44%)
  Pallas kernels  43.8 us (28%)
  starting transfers between devices  37.8 us (24%)
  local copies, waits for them, and re-layouts  3.32 us (2%)
    ppermute x9, waiting for transfers between devices, shifted(): lax.ppermute(array, 'pairs', [(i, (i + by) % count) for i in range(count)])  47.6 us
    pallas_call x9, Pallas kernels, call(): pl.pallas_call(kernel, in_specs=[SMEM] * len(scalars) + [VMEM] * len(arra...  42.2 us
    ppermute x9, starting transfers between devices, shifted(): lax.ppermute(array, 'pairs', [(i, (i + by) % count) for i in range(count)])  22.6 us
    ppermute x14, waiting for transfers between devices, along(): return lax.ppermute(array, 'pairs', [(p, target(p)) for p in range(count)])  17.7 us
    ppermute x14, starting transfers between devices, along(): return lax.ppermute(array, 'pairs', [(p, target(p)) for p in range(count)])  8.25 us
    ppermute x2, starting transfers between devices, other_core(): return lax.ppermute(array, 'side', [(0, 1), (1, 0)])  6.96 us
  transfers between devices with their start and end apart: 25, of which 15 were waited for; matrix products, arithmetic and copies ran while one was open for 2% of the time, Pallas kernels for 23%

profile of v8, /device:TPU:1, one launch (start us, length us, event | category | flops | bytes accessed | tf_op | source)
XLA Modules:
  0.0 154.5 jit_solution(10477229539143508107)
XLA Ops:
  0.0 1.7 %pack_part.1 = (bf16[152,768]{1,0:T(8,128)(2,1)}, bf16[48,768]{1,0:T(8,128)(2,1)}) custom-call(bf16[1,196,384]{2,1,0:T(8,128)(2,1)} %features.1, bf16[1,24,768]{2,1,0:T(8,128)(2,1)} %w_in.1, bf16[1,24,768]{2,1,0:T(8,128)(2,1)} %w_out.1), custom_call_target="tpu_custom_call" | custom-call | tf_op jit(solution)/shard_map/pack_part/pallas_call | solution.py:342
  1.7 3.9 %collective-permute-start.1 = (bf16[48,768]{1,0:T(8,128)(2,1)}, bf16[48,768]{1,0:T(8,128)(2,1)S(1)}, u32[]{:S(2)}, u32[]{:S(2)}) collective-permute-start(bf16[48,768]{1,0:T(8,128)(2,1)} %get-tuple-element.35), channel_id=1, source_target_pairs={{0,4},{2,6},{4,8},{6,10},{8,12},{10,14},{12,16},{14,18},{16,20},{1... | collective-permute-start | bytes 221192 | tf_op jit(solution)/shard_map/ppermute | solution.py:26
  5.6 1.6 %collective-permute-start = (bf16[48,768]{1,0:T(8,128)(2,1)}, bf16[48,768]{1,0:T(8,128)(2,1)S(1)}, u32[]{:S(2)}, u32[]{:S(2)}) collective-permute-start(bf16[48,768]{1,0:T(8,128)(2,1)} %get-tuple-element.35), channel_id=1, source_target_pairs={{0,2},{2,4},{4,6},{6,8},{8,10},{10,12},{12,14},{14,16},{16,18},{18... | collective-permute-start | bytes 221192 | tf_op jit(solution)/shard_map/ppermute | solution.py:26
  7.2 6.9 %collective-permute-start.6 = (bf16[152,768]{1,0:T(8,128)(2,1)}, bf16[152,768]{1,0:T(8,128)(2,1)S(1)}, u32[]{:S(2)}, u32[]{:S(2)}) collective-permute-start(bf16[152,768]{1,0:T(8,128)(2,1)} %get-tuple-element.36), channel_id=1, source_target_pairs={{0,252},{2,254},{4,0},{6,2},{8,4},{10,6},{12,8},{14,10},{16,12},{1... | collective-permute-start | bytes 700424 | tf_op jit(solution)/shard_map/ppermute | solution.py:26
  18.6 11.0 %collective-permute-done.2 = bf16[152,768]{1,0:T(8,128)(2,1)S(1)} collective-permute-done((bf16[152,768]{1,0:T(8,128)(2,1)}, bf16[152,768]{1,0:T(8,128)(2,1)S(1)}, u32[]{:S(2)}, u32[]{:S(2)}) %collective-permute-start.2) | collective-permute-done | bytes 233504 | tf_op jit(solution)/shard_map/ppermute | solution.py:26
  31.3 8.7 %collective-permute-start.7 = (bf16[152,768]{1,0:T(8,128)(2,1)S(1)}, bf16[152,768]{1,0:T(8,128)(2,1)S(1)}, u32[]{:S(2)}, u32[]{:S(2)}) collective-permute-start(bf16[152,768]{1,0:T(8,128)(2,1)S(1)} %collective-permute-done.6), channel_id=1, source_target_pairs={{0,254},{2,0},{4,2},{6,4},{8,6},{10,8},{12,10},{14,12},{16,14},{18... | collective-permute-start | bytes 700424 | tf_op jit(solution)/shard_map/ppermute | solution.py:26
  40.1 4.7 %collective-permute-done.7 = bf16[152,768]{1,0:T(8,128)(2,1)S(1)} collective-permute-done((bf16[152,768]{1,0:T(8,128)(2,1)S(1)}, bf16[152,768]{1,0:T(8,128)(2,1)S(1)}, u32[]{:S(2)}, u32[]{:S(2)}) %collective-permute-start.7) | collective-permute-done | bytes 233504 | tf_op jit(solution)/shard_map/ppermute | solution.py:26
  45.0 3.4 %collective-permute-start.12 = (bf16[4,104,768]{2,1,0:T(8,128)(2,1)S(1)}, bf16[4,104,768]{2,1,0:T(8,128)(2,1)S(1)}, u32[]{:S(2)}, u32[]{:S(2)}) collective-permute-start(bf16[4,104,768]{2,1,0:T(8,128)(2,1)S(1)} %pad_maximum_fusion.3.mine), channel_id=1, source_target_pairs={{0,1},{1,0},{2,3},{3,2},{4,5},{5,4},{6,7},{7,6},{8,9},{9,8},{10,11... | collective-permute-start | bytes 1916936 | tf_op jit(solution)/shard_map/ppermute | solution.py:30
  50.1 5.0 %triple_part.1 = (f32[624,768]{1,0:T(8,128)S(1)}, bf16[624,2304]{1,0:T(8,128)(2,1)S(1)}) custom-call(s32[128]{0:T(128)S(1)} %copy-done, s32[6]{0:T(128)S(1)} %reshape.4.slot_images, s32[2]{0:T(128)S(1)} %pad_add_fusion.place, bf16[4,104,768]{2,1,0:T(8,128)(2,1)S(1)} %pad_maximum_fusion.3.mine, bf16[4,104,768]{2,1,0:T(8,128)(2,1)S(1)} %collective-permute-done.12.theirs, ...), custom_call_target="tpu_custom_call" | custom-call | flops 4000000000 | bytes 8388608 | tf_op jit(solution)/shard_map/triple_part/pallas_call | solution.py:272
  55.1 3.7 %memory_part.1.key_value = bf16[624,1536]{1,0:T(8,128)(2,1)S(1)} custom-call(s32[128]{0:T(128)S(1)} %copy-done, s32[6]{0:T(128)S(1)} %reshape.4.slot_images, s32[2]{0:T(128)S(1)} %pad_add_fusion.place, bf16[4,104,768]{2,1,0:T(8,128)(2,1)S(1)} %pad_maximum_fusion.3.mine, bf16[4,104,768]{2,1,0:T(8,128)(2,1)S(1)} %collective-permute-done.12.theirs, ...), custom_call_target="tpu_custom_call" | custom-call | flops 3000000000 | bytes 8388608 | tf_op jit(solution)/shard_map/memory_part/pallas_call | solution.py:272
  59.8 5.5 %collective-permute-done.9 = bf16[2,96,768]{2,1,0:T(8,128)(2,1)S(1)} collective-permute-done((bf16[2,96,768]{2,1,0:T(8,128)(2,1)S(1)}, bf16[2,96,768]{2,1,0:T(8,128)(2,1)S(1)}, u32[]{:S(2)}, u32[]{:S(2)}) %collective-permute-start.9) | collective-permute-done | bytes 294944 | tf_op jit(solution)/shard_map/ppermute | solution.py:369
  67.3 1.5 collective-permute-start.13
  68.9 10.5 %self_part.1 = (f32[624,768]{1,0:T(8,128)S(1)}, bf16[624,768]{1,0:T(8,128)(2,1)S(1)}) custom-call(f32[624,768]{1,0:T(8,128)S(1)} %get-tuple-element.47.rows, bf16[624,2304]{1,0:T(8,128)(2,1)S(1)} %get-tuple-element.48.triple, f32[1,768]{1,0:T(1,128)S(1)} %copy-done.9, bf16[768,768]{1,0:T(8,128)(2,1)S(1)} %bitcast.27, bf16[768,768]{1,0:T(8,128)(2,1)S(1)} %bitcast.28), custom_call_target="tpu_custom_call" | custom-call | flops 12000000000 | bytes 8388608 | tf_op jit(solution)/shard_map/self_part/pallas_call | solution.py:272
  79.4 9.2 %cross_part.1 = (f32[624,768]{1,0:T(8,128)S(1)}, bf16[624,768]{1,0:T(8,128)(2,1)S(1)}) custom-call(f32[624,768]{1,0:T(8,128)S(1)} %get-tuple-element.49.first, bf16[624,768]{1,0:T(8,128)(2,1)S(1)} %get-tuple-element.50.query, bf16[624,1536]{1,0:T(8,128)(2,1)S(1)} %memory_part.1.key_value, f32[1,768]{1,0:T(1,128)S(1)} %copy-done.10, bf16[768,768]{1,0:T(8,128)(2,1)S(1)} %bitcast.29), custom_call_target="tpu_custom_call" | custom-call | flops 12000000000 | bytes 8388608 | tf_op jit(solution)/shard_map/cross_part/pallas_call | solution.py:272
  88.7 4.0 %collective-permute-done.16 = bf16[2,384,768]{2,1,0:T(8,128)(2,1)S(1)} collective-permute-done((bf16[2,384,768]{2,1,0:T(8,128)(2,1)S(1)}, bf16[2,384,768]{2,1,0:T(8,128)(2,1)S(1)}, u32[]{:S(2)}, u32[]{:S(2)}) %collective-permute-start.16) | collective-permute-done | bytes 1179680 | tf_op jit(solution)/shard_map/ppermute | solution.py:369
  95.2 1.7 %collective-permute-start.20 = (bf16[2,192,768]{2,1,0:T(8,128)(2,1)S(1)}, bf16[2,192,768]{2,1,0:T(8,128)(2,1)S(1)}, u32[]{:S(2)}, u32[]{:S(2)}) collective-permute-start(bf16[2,192,768]{2,1,0:T(8,128)(2,1)S(1)} %slice.101), channel_id=1, source_target_pairs={{0,48},{2,50},{4,52},{6,54},{8,56},{10,58},{12,60},{14,62},{16,0},... | collective-permute-start | bytes 1769480 | tf_op jit(solution)/shard_map/ppermute | solution.py:369
  98.3 6.6 %early_part.1.early = f32[624,768]{1,0:T(8,128)S(1)} custom-call(f32[624,768]{1,0:T(8,128)S(1)} %get-tuple-element.54.second, bf16[624,768]{1,0:T(8,128)(2,1)S(1)} %get-tuple-element.55.mlp_in, bf16[2,2304,768]{2,1,0:T(8,128)(2,1)S(1)} %constant_dynamic-update-slice_fusion.fc), custom_call_target="tpu_custom_call" | custom-call | flops 10000000000 | bytes 8388608 | tf_op jit(solution)/shard_map/early_part/pallas_call | solution.py:272
  104.9 2.7 %collective-permute-done.20 = bf16[2,192,768]{2,1,0:T(8,128)(2,1)S(1)} collective-permute-done((bf16[2,192,768]{2,1,0:T(8,128)(2,1)S(1)}, bf16[2,192,768]{2,1,0:T(8,128)(2,1)S(1)}, u32[]{:S(2)}, u32[]{:S(2)}) %collective-permute-start.20) | collective-permute-done | bytes 589856 | tf_op jit(solution)/shard_map/ppermute | solution.py:369
  107.6 2.8 %collective-permute-done.19 = bf16[2,192,768]{2,1,0:T(8,128)(2,1)S(1)} collective-permute-done((bf16[2,192,768]{2,1,0:T(8,128)(2,1)S(1)}, bf16[2,192,768]{2,1,0:T(8,128)(2,1)S(1)}, u32[]{:S(2)}, u32[]{:S(2)}) %collective-permute-start.19) | collective-permute-done | bytes 589856 | tf_op jit(solution)/shard_map/ppermute | solution.py:369
  110.6 4.4 %late_part.1 = (f32[3,196,512]{2,1,0:T(8,128)S(1)}, bf16[3,196,512]{2,1,0:T(8,128)(2,1)S(1)}) custom-call(s32[2]{0:T(128)S(1)} %pad_add_fusion.place, f32[624,768]{1,0:T(8,128)S(1)} %early_part.1.early, bf16[624,768]{1,0:T(8,128)(2,1)S(1)} %get-tuple-element.55.mlp_in, bf16[2,768,768]{2,1,0:T(8,128)(2,1)S(1)} %pad_maximum_fusion.fc, ...), custom_call_target="tpu_custom_call" | custom-call | flops 5000000000 | bytes 8388608 | tf_op jit(solution)/shard_map/late_part/pallas_call | solution.py:272
  115.0 3.6 %collective-permute-start.21 = (bf16[3,196,512]{2,1,0:T(8,128)(2,1)S(1)}, bf16[3,196,512]{2,1,0:T(8,128)(2,1)S(1)}, u32[]{:S(2)}, u32[]{:S(2)}) collective-permute-start(bf16[3,196,512]{2,1,0:T(8,128)(2,1)S(1)} %get-tuple-element.61), channel_id=1, source_target_pairs={{0,1},{1,0},{2,3},{3,2},{4,5},{5,4},{6,7},{7,6},{8,9},{9,8},{10,11... | collective-permute-start | bytes 1806344 | tf_op jit(solution)/shard_map/ppermute | solution.py:30
  122.4 14.1 %collective-permute-done.23 = bf16[196,512]{1,0:T(8,128)(2,1)S(1)} collective-permute-done((bf16[196,512]{1,0:T(8,128)(2,1)S(1)}, bf16[196,512]{1,0:T(8,128)(2,1)S(1)}, u32[]{:S(2)}, u32[]{:S(2)}) %collective-permute-start.23) | collective-permute-done | bytes 200736 | tf_op jit(solution)/shard_map/ppermute | solution.py:26
  136.7 4.2 %collective-permute-done.22.nearest = bf16[196,512]{1,0:T(8,128)(2,1)S(1)} collective-permute-done((bf16[196,512]{1,0:T(8,128)(2,1)S(1)}, bf16[196,512]{1,0:T(8,128)(2,1)S(1)}, u32[]{:S(2)}, u32[]{:S(2)}) %collective-permute-start.22) | collective-permute-done | bytes 200736 | tf_op jit(solution)/shard_map/ppermute | solution.py:26
  140.9 12.8 %collective-permute-done.24.further = bf16[196,512]{1,0:T(8,128)(2,1)S(1)} collective-permute-done((bf16[196,512]{1,0:T(8,128)(2,1)S(1)}, bf16[196,512]{1,0:T(8,128)(2,1)S(1)}, u32[]{:S(2)}, u32[]{:S(2)}) %collective-permute-start.24) | collective-permute-done | bytes 200736 | tf_op jit(solution)/shard_map/ppermute | solution.py:26
  (99 shorter events, 19.0 us)
Async XLA Ops:
  1.7 16.1 %collective-permute-start.1 = (bf16[48,768]{1,0:T(8,128)(2,1)}, bf16[48,768]{1,0:T(8,128)(2,1)S(1)}, u32[]{:S(2)}, u32[]{:S(2)}) collective-permute-start(bf16[48,768]{1,0:T(8,128)(2,1)} %get-tuple-element.35), channel_id=1, source_target_pairs={{0,4},{2,6},{4,8},{6,10},{8,12},{10,14},{12,16},{14,18},{16,20},{1... | collective-permute-start | bytes 221192 | tf_op jit(solution)/shard_map/ppermute | solution.py:26
  5.6 12.9 %collective-permute-start = (bf16[48,768]{1,0:T(8,128)(2,1)}, bf16[48,768]{1,0:T(8,128)(2,1)S(1)}, u32[]{:S(2)}, u32[]{:S(2)}) collective-permute-start(bf16[48,768]{1,0:T(8,128)(2,1)} %get-tuple-element.35), channel_id=1, source_target_pairs={{0,2},{2,4},{4,6},{6,8},{8,10},{10,12},{12,14},{14,16},{16,18},{18... | collective-permute-start | bytes 221192 | tf_op jit(solution)/shard_map/ppermute | solution.py:26
  7.2 24.1 %collective-permute-start.6 = (bf16[152,768]{1,0:T(8,128)(2,1)}, bf16[152,768]{1,0:T(8,128)(2,1)S(1)}, u32[]{:S(2)}, u32[]{:S(2)}) collective-permute-start(bf16[152,768]{1,0:T(8,128)(2,1)} %get-tuple-element.36), channel_id=1, source_target_pairs={{0,252},{2,254},{4,0},{6,2},{8,4},{10,6},{12,8},{14,10},{16,12},{1... | collective-permute-start | bytes 700424 | tf_op jit(solution)/shard_map/ppermute | solution.py:26
  14.1 15.5 %collective-permute-start.2 = (bf16[152,768]{1,0:T(8,128)(2,1)}, bf16[152,768]{1,0:T(8,128)(2,1)S(1)}, u32[]{:S(2)}, u32[]{:S(2)}) collective-permute-start(bf16[152,768]{1,0:T(8,128)(2,1)} %get-tuple-element.36), channel_id=1, source_target_pairs={{0,254},{2,0},{4,2},{6,4},{8,6},{10,8},{12,10},{14,12},{16,14},{18... | collective-permute-start | bytes 700424 | tf_op jit(solution)/shard_map/ppermute | solution.py:26
  18.5 21.6 %collective-permute-start.8 = (bf16[96,768]{1,0:T(8,128)(2,1)S(1)}, bf16[96,768]{1,0:T(8,128)(2,1)S(1)}, u32[]{:S(2)}, u32[]{:S(2)}) collective-permute-start(bf16[96,768]{1,0:T(8,128)(2,1)S(1)} %pad_maximum_fusion.6), channel_id=1, source_target_pairs={{0,4},{2,6},{4,8},{6,10},{8,12},{10,14},{12,16},{14,18},{16,20},{1... | collective-permute-start | bytes 442376 | tf_op jit(solution)/shard_map/ppermute | solution.py:26
  29.7 18.8 %collective-permute-start.5 = (bf16[2,96,768]{2,1,0:T(8,128)(2,1)S(1)}, bf16[2,96,768]{2,1,0:T(8,128)(2,1)S(1)}, u32[]{:S(2)}, u32[]{:S(2)}) collective-permute-start(bf16[2,96,768]{2,1,0:T(8,128)(2,1)S(1)} %get-tuple-element.66), channel_id=1, source_target_pairs={{0,32},{2,34},{4,36},{6,38},{8,40},{10,42},{12,44},{14,46},{16,48}... | collective-permute-start | bytes 884744 | tf_op jit(solution)/shard_map/ppermute | solution.py:369
  29.8 29.1 %collective-permute-start.4 = (bf16[2,96,768]{2,1,0:T(8,128)(2,1)S(1)}, bf16[2,96,768]{2,1,0:T(8,128)(2,1)S(1)}, u32[]{:S(2)}, u32[]{:S(2)}) collective-permute-start(bf16[2,96,768]{2,1,0:T(8,128)(2,1)S(1)} %get-tuple-element.66), channel_id=1, source_target_pairs={{0,48},{2,50},{4,52},{6,54},{8,56},{10,58},{12,60},{14,62},{16,0},... | collective-permute-start | bytes 884744 | tf_op jit(solution)/shard_map/ppermute | solution.py:369
  30.4 28.5 %collective-permute-start.3 = (bf16[2,96,768]{2,1,0:T(8,128)(2,1)S(1)}, bf16[2,96,768]{2,1,0:T(8,128)(2,1)S(1)}, u32[]{:S(2)}, u32[]{:S(2)}) collective-permute-start(bf16[2,96,768]{2,1,0:T(8,128)(2,1)S(1)} %get-tuple-element.66), channel_id=1, source_target_pairs={{0,16},{2,18},{4,20},{6,22},{8,24},{10,26},{12,28},{14,30},{16,32}... | collective-permute-start | bytes 884744 | tf_op jit(solution)/shard_map/ppermute | solution.py:369
  31.3 13.5 %collective-permute-start.7 = (bf16[152,768]{1,0:T(8,128)(2,1)S(1)}, bf16[152,768]{1,0:T(8,128)(2,1)S(1)}, u32[]{:S(2)}, u32[]{:S(2)}) collective-permute-start(bf16[152,768]{1,0:T(8,128)(2,1)S(1)} %collective-permute-done.6), channel_id=1, source_target_pairs={{0,254},{2,0},{4,2},{6,4},{8,6},{10,8},{12,10},{14,12},{16,14},{18... | collective-permute-start | bytes 700424 | tf_op jit(solution)/shard_map/ppermute | solution.py:26
  48.4 10.5 %collective-permute-start.11 = (bf16[2,96,768]{2,1,0:T(8,128)(2,1)S(1)}, bf16[2,96,768]{2,1,0:T(8,128)(2,1)S(1)}, u32[]{:S(2)}, u32[]{:S(2)}) collective-permute-start(bf16[2,96,768]{2,1,0:T(8,128)(2,1)S(1)} %pad_maximum_fusion.5), channel_id=1, source_target_pairs={{0,128},{2,130},{4,132},{6,134},{8,136},{10,138},{12,140},{14,142}... | collective-permute-start | bytes 884744 | tf_op jit(solution)/shard_map/ppermute | solution.py:369
  48.5 11.3 %collective-permute-start.10 = (bf16[2,96,768]{2,1,0:T(8,128)(2,1)S(1)}, bf16[2,96,768]{2,1,0:T(8,128)(2,1)S(1)}, u32[]{:S(2)}, u32[]{:S(2)}) collective-permute-start(bf16[2,96,768]{2,1,0:T(8,128)(2,1)S(1)} %pad_maximum_fusion.5), channel_id=1, source_target_pairs={{0,192},{2,194},{4,196},{6,198},{8,200},{10,202},{12,204},{14,206}... | collective-permute-start | bytes 884744 | tf_op jit(solution)/shard_map/ppermute | solution.py:369
  50.0 15.3 %collective-permute-start.9 = (bf16[2,96,768]{2,1,0:T(8,128)(2,1)S(1)}, bf16[2,96,768]{2,1,0:T(8,128)(2,1)S(1)}, u32[]{:S(2)}, u32[]{:S(2)}) collective-permute-start(bf16[2,96,768]{2,1,0:T(8,128)(2,1)S(1)} %pad_maximum_fusion.5), channel_id=1, source_target_pairs={{0,64},{2,66},{4,68},{6,70},{8,72},{10,74},{12,76},{14,78},{16,80}... | collective-permute-start | bytes 884744 | tf_op jit(solution)/shard_map/ppermute | solution.py:369
  65.4 27.3 %collective-permute-start.16 = (bf16[2,384,768]{2,1,0:T(8,128)(2,1)S(1)}, bf16[2,384,768]{2,1,0:T(8,128)(2,1)S(1)}, u32[]{:S(2)}, u32[]{:S(2)}) collective-permute-start(bf16[2,384,768]{2,1,0:T(8,128)(2,1)S(1)} %pad_maximum_fusion.2), channel_id=1, source_target_pairs={{0,48},{2,50},{4,52},{6,54},{8,56},{10,58},{12,60},{14,62},{16,0},... | collective-permute-start | bytes 3538952 | tf_op jit(solution)/shard_map/ppermute | solution.py:369
  65.7 28.3 %collective-permute-start.15 = (bf16[2,384,768]{2,1,0:T(8,128)(2,1)S(1)}, bf16[2,384,768]{2,1,0:T(8,128)(2,1)S(1)}, u32[]{:S(2)}, u32[]{:S(2)}) collective-permute-start(bf16[2,384,768]{2,1,0:T(8,128)(2,1)S(1)} %pad_maximum_fusion.2), channel_id=1, source_target_pairs={{0,16},{2,18},{4,20},{6,22},{8,24},{10,26},{12,28},{14,30},{16,32}... | collective-permute-start | bytes 3538952 | tf_op jit(solution)/shard_map/ppermute | solution.py:369
  67.2 26.8 %collective-permute-start.14 = (bf16[2,384,768]{2,1,0:T(8,128)(2,1)S(1)}, bf16[2,384,768]{2,1,0:T(8,128)(2,1)S(1)}, u32[]{:S(2)}, u32[]{:S(2)}) collective-permute-start(bf16[2,384,768]{2,1,0:T(8,128)(2,1)S(1)} %pad_maximum_fusion.1), channel_id=1, source_target_pairs={{0,192},{2,194},{4,196},{6,198},{8,200},{10,202},{12,204},{14,206}... | collective-permute-start | bytes 3538952 | tf_op jit(solution)/shard_map/ppermute | solution.py:369
  67.3 27.2 %collective-permute-start.13 = (bf16[2,384,768]{2,1,0:T(8,128)(2,1)S(1)}, bf16[2,384,768]{2,1,0:T(8,128)(2,1)S(1)}, u32[]{:S(2)}, u32[]{:S(2)}) collective-permute-start(bf16[2,384,768]{2,1,0:T(8,128)(2,1)S(1)} %pad_maximum_fusion.1), channel_id=1, source_target_pairs={{0,64},{2,66},{4,68},{6,70},{8,72},{10,74},{12,76},{14,78},{16,80}... | collective-permute-start | bytes 3538952 | tf_op jit(solution)/shard_map/ppermute | solution.py:369
  95.2 12.4 %collective-permute-start.20 = (bf16[2,192,768]{2,1,0:T(8,128)(2,1)S(1)}, bf16[2,192,768]{2,1,0:T(8,128)(2,1)S(1)}, u32[]{:S(2)}, u32[]{:S(2)}) collective-permute-start(bf16[2,192,768]{2,1,0:T(8,128)(2,1)S(1)} %slice.101), channel_id=1, source_target_pairs={{0,48},{2,50},{4,52},{6,54},{8,56},{10,58},{12,60},{14,62},{16,0},... | collective-permute-start | bytes 1769480 | tf_op jit(solution)/shard_map/ppermute | solution.py:369
  96.8 13.6 %collective-permute-start.19 = (bf16[2,192,768]{2,1,0:T(8,128)(2,1)S(1)}, bf16[2,192,768]{2,1,0:T(8,128)(2,1)S(1)}, u32[]{:S(2)}, u32[]{:S(2)}) collective-permute-start(bf16[2,192,768]{2,1,0:T(8,128)(2,1)S(1)} %slice.100), channel_id=1, source_target_pairs={{0,16},{2,18},{4,20},{6,22},{8,24},{10,26},{12,28},{14,30},{16,32}... | collective-permute-start | bytes 1769480 | tf_op jit(solution)/shard_map/ppermute | solution.py:369
  96.8 13.6 %collective-permute-start.18 = (bf16[2,192,768]{2,1,0:T(8,128)(2,1)S(1)}, bf16[2,192,768]{2,1,0:T(8,128)(2,1)S(1)}, u32[]{:S(2)}, u32[]{:S(2)}) collective-permute-start(bf16[2,192,768]{2,1,0:T(8,128)(2,1)S(1)} %slice.99), channel_id=1, source_target_pairs={{0,192},{2,194},{4,196},{6,198},{8,200},{10,202},{12,204},{14,206}... | collective-permute-start | bytes 1769480 | tf_op jit(solution)/shard_map/ppermute | solution.py:369
  96.9 13.4 %collective-permute-start.17 = (bf16[2,192,768]{2,1,0:T(8,128)(2,1)S(1)}, bf16[2,192,768]{2,1,0:T(8,128)(2,1)S(1)}, u32[]{:S(2)}, u32[]{:S(2)}) collective-permute-start(bf16[2,192,768]{2,1,0:T(8,128)(2,1)S(1)} %slice.98), channel_id=1, source_target_pairs={{0,64},{2,66},{4,68},{6,70},{8,72},{10,74},{12,76},{14,78},{16,80}... | collective-permute-start | bytes 1769480 | tf_op jit(solution)/shard_map/ppermute | solution.py:369
  115.0 5.3 %collective-permute-start.21 = (bf16[3,196,512]{2,1,0:T(8,128)(2,1)S(1)}, bf16[3,196,512]{2,1,0:T(8,128)(2,1)S(1)}, u32[]{:S(2)}, u32[]{:S(2)}) collective-permute-start(bf16[3,196,512]{2,1,0:T(8,128)(2,1)S(1)} %get-tuple-element.61), channel_id=1, source_target_pairs={{0,1},{1,0},{2,3},{3,2},{4,5},{5,4},{6,7},{7,6},{8,9},{9,8},{10,11... | collective-permute-start | bytes 1806344 | tf_op jit(solution)/shard_map/ppermute | solution.py:30
  121.0 15.5 %collective-permute-start.23 = (bf16[196,512]{1,0:T(8,128)(2,1)S(1)}, bf16[196,512]{1,0:T(8,128)(2,1)S(1)}, u32[]{:S(2)}, u32[]{:S(2)}) collective-permute-start(bf16[196,512]{1,0:T(8,128)(2,1)S(1)} %furthest_part.1), channel_id=1, source_target_pairs={{0,2},{2,4},{4,6},{6,8},{8,10},{10,12},{12,14},{14,16},{16,18},{18... | collective-permute-start | bytes 602120 | tf_op jit(solution)/shard_map/ppermute | solution.py:26
  122.3 18.6 %collective-permute-start.22 = (bf16[196,512]{1,0:T(8,128)(2,1)S(1)}, bf16[196,512]{1,0:T(8,128)(2,1)S(1)}, u32[]{:S(2)}, u32[]{:S(2)}) collective-permute-start(bf16[196,512]{1,0:T(8,128)(2,1)S(1)} %get-tuple-element.63), channel_id=1, source_target_pairs={{0,2},{2,4},{4,6},{6,8},{8,10},{10,12},{12,14},{14,16},{16,18},{18... | collective-permute-start | bytes 602120 | tf_op jit(solution)/shard_map/ppermute | solution.py:26
  136.6 17.2 %collective-permute-start.24 = (bf16[196,512]{1,0:T(8,128)(2,1)S(1)}, bf16[196,512]{1,0:T(8,128)(2,1)S(1)}, u32[]{:S(2)}, u32[]{:S(2)}) collective-permute-start(bf16[196,512]{1,0:T(8,128)(2,1)S(1)} %add_convert_fusion), channel_id=1, source_target_pairs={{0,4},{2,6},{4,8},{6,10},{8,12},{10,14},{12,16},{14,18},{16,20},{1... | collective-permute-start | bytes 602120 | tf_op jit(solution)/shard_map/ppermute | solution.py:26
  (13 other events, 119.4 us)

commit v9 on v8

--- a/solution.py
+++ b/solution.py
@@ -413,12 +413,13 @@
 ):
     place = jnp.stack([lax.axis_index("pairs"), lax.axis_index("side")]).astype(jnp.int32)
     packed, shard = pack_call(features, w_fc1, w_fc2)
-    next2, next1 = shifted(packed, -2), shifted(packed, -1)
-    last1, last2 = shifted(shard, 1), shifted(shard, 2)
+    next2 = shifted(packed, -2)
+    last1, last2, later = tied(shifted(shard, 1), shifted(shard, 2), packed)
+    next1 = shifted(later, -1)
     last34 = shifted(jnp.concatenate([last1, last2], axis=0), 2)
-    next3, last34 = tied(shifted(next2, -1), last34)
-    part_x = hidden_rows([shard, last1, last2, next1])
-    part_y = hidden_rows([next2, next3, last34[:48], last34[48:]])
+    next3, last34, next1 = tied(shifted(next2, -1), last34, next1)
+    part_x = hidden_rows([shard, last1, last2, next2])
+    part_y = hidden_rows([next1, next3, last34[:48], last34[48:]])
     mine = jnp.stack([packed[:TOP], next1[:TOP], next2[:TOP], next3[:TOP]])
     theirs = other_core(mine)
     scalars = [image_slot, slot_images.reshape(-1), place]

time: 155 us -> 143 us (0.923)
  waiting for transfers between devices: 67.7 us -> 51.7 us
  starting transfers between devices: 37.8 us -> 42.4 us
    ppermute x9, waiting for transfers between devices: 47.6 us -> 31.8 us  [shifted(): lax.ppermute(array, 'pairs', [(i, (i + by) % count) for i in range(count)])]
    ppermute x9, starting transfers between devices: 22.6 us -> 25.6 us  [shifted(): lax.ppermute(array, 'pairs', [(i, (i + by) % count) for i in range(count)])]
  transfers between devices with their start and end apart: 25 -> 25, of which waited for: 15 -> 15; matrix products, arithmetic and copies ran while one was open for 2% -> 2% of each run, Pallas kernels for 23% -> 25%
where the time goes in v9:
time: 143 us
  waiting for transfers between devices  51.7 us (36%)
  Pallas kernels  43.8 us (31%)
  starting transfers between devices  42.4 us (30%)
  local copies, waits for them, and re-layouts  3.34 us (2%)
    pallas_call x9, Pallas kernels, call(): pl.pallas_call(kernel, in_specs=[SMEM] * len(scalars) + [VMEM] * len(arra...  42.1 us
    ppermute x9, waiting for transfers between devices, shifted(): lax.ppermute(array, 'pairs', [(i, (i + by) % count) for i in range(count)])  31.8 us
    ppermute x9, starting transfers between devices, shifted(): lax.ppermute(array, 'pairs', [(i, (i + by) % count) for i in range(count)])  25.6 us
    ppermute x14, waiting for transfers between devices, along(): return lax.ppermute(array, 'pairs', [(p, target(p)) for p in range(count)])  17.5 us
    ppermute x14, starting transfers between devices, along(): return lax.ppermute(array, 'pairs', [(p, target(p)) for p in range(count)])  8.8 us
    ppermute x2, starting transfers between devices, other_core(): return lax.ppermute(array, 'side', [(0, 1), (1, 0)])  8.02 us
  transfers between devices with their start and end apart: 25, of which 15 were waited for; matrix products, arithmetic and copies ran while one was open for 2% of the time, Pallas kernels for 25%

profile of v9, /device:TPU:1, one launch (start us, length us, event | category | flops | bytes accessed | tf_op | source)
XLA Modules:
  0.0 143.1 jit_solution(11351156615553031725)
XLA Ops:
  0.0 1.7 %pack_part.1 = (bf16[152,768]{1,0:T(8,128)(2,1)}, bf16[48,768]{1,0:T(8,128)(2,1)}) custom-call(bf16[1,196,384]{2,1,0:T(8,128)(2,1)} %features.1, bf16[1,24,768]{2,1,0:T(8,128)(2,1)} %w_in.1, bf16[1,24,768]{2,1,0:T(8,128)(2,1)} %w_out.1), custom_call_target="tpu_custom_call" | custom-call | tf_op jit(solution)/shard_map/pack_part/pallas_call | solution.py:342
  1.7 3.9 %collective-permute-start.1 = (bf16[48,768]{1,0:T(8,128)(2,1)}, bf16[48,768]{1,0:T(8,128)(2,1)S(1)}, u32[]{:S(2)}, u32[]{:S(2)}) collective-permute-start(bf16[48,768]{1,0:T(8,128)(2,1)} %get-tuple-element.39), channel_id=1, source_target_pairs={{0,4},{2,6},{4,8},{6,10},{8,12},{10,14},{12,16},{14,18},{16,20},{1... | collective-permute-start | bytes 221192 | tf_op jit(solution)/shard_map/ppermute | solution.py:26
  7.2 6.9 %collective-permute-start.2 = (bf16[152,768]{1,0:T(8,128)(2,1)}, bf16[152,768]{1,0:T(8,128)(2,1)S(1)}, u32[]{:S(2)}, u32[]{:S(2)}) collective-permute-start(bf16[152,768]{1,0:T(8,128)(2,1)} %get-tuple-element.43), channel_id=1, source_target_pairs={{0,252},{2,254},{4,0},{6,2},{8,4},{10,6},{12,8},{14,10},{16,12},{1... | collective-permute-start | bytes 700424 | tf_op jit(solution)/shard_map/ppermute | solution.py:26
  16.7 1.8 %collective-permute-done = bf16[48,768]{1,0:T(8,128)(2,1)S(1)} collective-permute-done((bf16[48,768]{1,0:T(8,128)(2,1)}, bf16[48,768]{1,0:T(8,128)(2,1)S(1)}, u32[]{:S(2)}, u32[]{:S(2)}) %collective-permute-start) | collective-permute-done | bytes 73760 | tf_op jit(solution)/shard_map/ppermute | solution.py:26
  18.6 5.9 %collective-permute-start.8 = (bf16[152,768]{1,0:T(8,128)(2,1)}, bf16[152,768]{1,0:T(8,128)(2,1)S(1)}, u32[]{:S(2)}, u32[]{:S(2)}) collective-permute-start(bf16[152,768]{1,0:T(8,128)(2,1)} %get-tuple-element.43), channel_id=1, source_target_pairs={{0,254},{2,0},{4,2},{6,4},{8,6},{10,8},{12,10},{14,12},{16,14},{18... | collective-permute-start | bytes 700424 | tf_op jit(solution)/shard_map/ppermute | solution.py:26
  24.6 4.6 %collective-permute-start.6 = (bf16[152,768]{1,0:T(8,128)(2,1)S(1)}, bf16[152,768]{1,0:T(8,128)(2,1)S(1)}, u32[]{:S(2)}, u32[]{:S(2)}) collective-permute-start(bf16[152,768]{1,0:T(8,128)(2,1)S(1)} %collective-permute-done.2), channel_id=1, source_target_pairs={{0,254},{2,0},{4,2},{6,4},{8,6},{10,8},{12,10},{14,12},{16,14},{18... | collective-permute-start | bytes 700424 | tf_op jit(solution)/shard_map/ppermute | solution.py:26
  31.0 1.8 %collective-permute-done.6 = bf16[152,768]{1,0:T(8,128)(2,1)S(1)} collective-permute-done((bf16[152,768]{1,0:T(8,128)(2,1)S(1)}, bf16[152,768]{1,0:T(8,128)(2,1)S(1)}, u32[]{:S(2)}, u32[]{:S(2)}) %collective-permute-start.6) | collective-permute-done | bytes 233504 | tf_op jit(solution)/shard_map/ppermute | solution.py:26
  33.0 4.3 %collective-permute-start.12 = (bf16[4,104,768]{2,1,0:T(8,128)(2,1)S(1)}, bf16[4,104,768]{2,1,0:T(8,128)(2,1)S(1)}, u32[]{:S(2)}, u32[]{:S(2)}) collective-permute-start(bf16[4,104,768]{2,1,0:T(8,128)(2,1)S(1)} %pad_maximum_fusion.3.mine), channel_id=1, source_target_pairs={{0,1},{1,0},{2,3},{3,2},{4,5},{5,4},{6,7},{7,6},{8,9},{9,8},{10,11... | collective-permute-start | bytes 1916936 | tf_op jit(solution)/shard_map/ppermute | solution.py:30
  39.1 5.0 %triple_part.1 = (f32[624,768]{1,0:T(8,128)S(1)}, bf16[624,2304]{1,0:T(8,128)(2,1)S(1)}) custom-call(s32[128]{0:T(128)S(1)} %copy-done, s32[6]{0:T(128)S(1)} %reshape.4.slot_images, s32[2]{0:T(128)S(1)} %pad_add_fusion.place, bf16[4,104,768]{2,1,0:T(8,128)(2,1)S(1)} %pad_maximum_fusion.3.mine, bf16[4,104,768]{2,1,0:T(8,128)(2,1)S(1)} %collective-permute-done.12.theirs, ...), custom_call_target="tpu_custom_call" | custom-call | flops 4000000000 | bytes 8388608 | tf_op jit(solution)/shard_map/triple_part/pallas_call | solution.py:272
  44.1 3.7 %memory_part.1.key_value = bf16[624,1536]{1,0:T(8,128)(2,1)S(1)} custom-call(s32[128]{0:T(128)S(1)} %copy-done, s32[6]{0:T(128)S(1)} %reshape.4.slot_images, s32[2]{0:T(128)S(1)} %pad_add_fusion.place, bf16[4,104,768]{2,1,0:T(8,128)(2,1)S(1)} %pad_maximum_fusion.3.mine, bf16[4,104,768]{2,1,0:T(8,128)(2,1)S(1)} %collective-permute-done.12.theirs, ...), custom_call_target="tpu_custom_call" | custom-call | flops 3000000000 | bytes 8388608 | tf_op jit(solution)/shard_map/memory_part/pallas_call | solution.py:272
  48.6 5.6 %collective-permute-done.9 = bf16[2,96,768]{2,1,0:T(8,128)(2,1)S(1)} collective-permute-done((bf16[2,96,768]{2,1,0:T(8,128)(2,1)S(1)}, bf16[2,96,768]{2,1,0:T(8,128)(2,1)S(1)}, u32[]{:S(2)}, u32[]{:S(2)}) %collective-permute-start.9) | collective-permute-done | bytes 294944 | tf_op jit(solution)/shard_map/ppermute | solution.py:369
  57.8 10.5 %self_part.1 = (f32[624,768]{1,0:T(8,128)S(1)}, bf16[624,768]{1,0:T(8,128)(2,1)S(1)}) custom-call(f32[624,768]{1,0:T(8,128)S(1)} %get-tuple-element.55.rows, bf16[624,2304]{1,0:T(8,128)(2,1)S(1)} %get-tuple-element.56.triple, f32[1,768]{1,0:T(1,128)S(1)} %copy-done.9, bf16[768,768]{1,0:T(8,128)(2,1)S(1)} %bitcast.27, bf16[768,768]{1,0:T(8,128)(2,1)S(1)} %bitcast.28), custom_call_target="tpu_custom_call" | custom-call | flops 12000000000 | bytes 8388608 | tf_op jit(solution)/shard_map/self_part/pallas_call | solution.py:272
  68.4 9.2 %cross_part.1 = (f32[624,768]{1,0:T(8,128)S(1)}, bf16[624,768]{1,0:T(8,128)(2,1)S(1)}) custom-call(f32[624,768]{1,0:T(8,128)S(1)} %get-tuple-element.57.first, bf16[624,768]{1,0:T(8,128)(2,1)S(1)} %get-tuple-element.58.query, bf16[624,1536]{1,0:T(8,128)(2,1)S(1)} %memory_part.1.key_value, f32[1,768]{1,0:T(1,128)S(1)} %copy-done.10, bf16[768,768]{1,0:T(8,128)(2,1)S(1)} %bitcast.29), custom_call_target="tpu_custom_call" | custom-call | flops 12000000000 | bytes 8388608 | tf_op jit(solution)/shard_map/cross_part/pallas_call | solution.py:272
  77.6 4.0 %collective-permute-done.16 = bf16[2,384,768]{2,1,0:T(8,128)(2,1)S(1)} collective-permute-done((bf16[2,384,768]{2,1,0:T(8,128)(2,1)S(1)}, bf16[2,384,768]{2,1,0:T(8,128)(2,1)S(1)}, u32[]{:S(2)}, u32[]{:S(2)}) %collective-permute-start.16) | collective-permute-done | bytes 1179680 | tf_op jit(solution)/shard_map/ppermute | solution.py:369
  83.8 2.1 %collective-permute-start.20 = (bf16[2,192,768]{2,1,0:T(8,128)(2,1)S(1)}, bf16[2,192,768]{2,1,0:T(8,128)(2,1)S(1)}, u32[]{:S(2)}, u32[]{:S(2)}) collective-permute-start(bf16[2,192,768]{2,1,0:T(8,128)(2,1)S(1)} %slice.101), channel_id=1, source_target_pairs={{0,48},{2,50},{4,52},{6,54},{8,56},{10,58},{12,60},{14,62},{16,0},... | collective-permute-start | bytes 1769480 | tf_op jit(solution)/shard_map/ppermute | solution.py:369
  87.4 6.5 %early_part.1.early = f32[624,768]{1,0:T(8,128)S(1)} custom-call(f32[624,768]{1,0:T(8,128)S(1)} %get-tuple-element.62.second, bf16[624,768]{1,0:T(8,128)(2,1)S(1)} %get-tuple-element.63.mlp_in, bf16[2,2304,768]{2,1,0:T(8,128)(2,1)S(1)} %constant_dynamic-update-slice_fusion.fc), custom_call_target="tpu_custom_call" | custom-call | flops 10000000000 | bytes 8388608 | tf_op jit(solution)/shard_map/early_part/pallas_call | solution.py:272
  94.0 2.3 %collective-permute-done.20 = bf16[2,192,768]{2,1,0:T(8,128)(2,1)S(1)} collective-permute-done((bf16[2,192,768]{2,1,0:T(8,128)(2,1)S(1)}, bf16[2,192,768]{2,1,0:T(8,128)(2,1)S(1)}, u32[]{:S(2)}, u32[]{:S(2)}) %collective-permute-start.20) | collective-permute-done | bytes 589856 | tf_op jit(solution)/shard_map/ppermute | solution.py:369
  96.3 3.1 %collective-permute-done.19 = bf16[2,192,768]{2,1,0:T(8,128)(2,1)S(1)} collective-permute-done((bf16[2,192,768]{2,1,0:T(8,128)(2,1)S(1)}, bf16[2,192,768]{2,1,0:T(8,128)(2,1)S(1)}, u32[]{:S(2)}, u32[]{:S(2)}) %collective-permute-start.19) | collective-permute-done | bytes 589856 | tf_op jit(solution)/shard_map/ppermute | solution.py:369
  99.8 4.4 %late_part.1 = (f32[3,196,512]{2,1,0:T(8,128)S(1)}, bf16[3,196,512]{2,1,0:T(8,128)(2,1)S(1)}) custom-call(s32[2]{0:T(128)S(1)} %pad_add_fusion.place, f32[624,768]{1,0:T(8,128)S(1)} %early_part.1.early, bf16[624,768]{1,0:T(8,128)(2,1)S(1)} %get-tuple-element.63.mlp_in, bf16[2,768,768]{2,1,0:T(8,128)(2,1)S(1)} %pad_maximum_fusion.fc, ...), custom_call_target="tpu_custom_call" | custom-call | flops 5000000000 | bytes 8388608 | tf_op jit(solution)/shard_map/late_part/pallas_call | solution.py:272
  104.2 3.7 %collective-permute-start.21 = (bf16[3,196,512]{2,1,0:T(8,128)(2,1)S(1)}, bf16[3,196,512]{2,1,0:T(8,128)(2,1)S(1)}, u32[]{:S(2)}, u32[]{:S(2)}) collective-permute-start(bf16[3,196,512]{2,1,0:T(8,128)(2,1)S(1)} %get-tuple-element.69), channel_id=1, source_target_pairs={{0,1},{1,0},{2,3},{3,2},{4,5},{5,4},{6,7},{7,6},{8,9},{9,8},{10,11... | collective-permute-start | bytes 1806344 | tf_op jit(solution)/shard_map/ppermute | solution.py:30
  112.1 1.9 %collective-permute-start.22 = (bf16[196,512]{1,0:T(8,128)(2,1)S(1)}, bf16[196,512]{1,0:T(8,128)(2,1)S(1)}, u32[]{:S(2)}, u32[]{:S(2)}) collective-permute-start(bf16[196,512]{1,0:T(8,128)(2,1)S(1)} %get-tuple-element.71), channel_id=1, source_target_pairs={{0,2},{2,4},{4,6},{6,8},{8,10},{10,12},{12,14},{14,16},{16,18},{18... | collective-permute-start | bytes 602120 | tf_op jit(solution)/shard_map/ppermute | solution.py:26
  114.0 12.5 %collective-permute-done.23 = bf16[196,512]{1,0:T(8,128)(2,1)S(1)} collective-permute-done((bf16[196,512]{1,0:T(8,128)(2,1)S(1)}, bf16[196,512]{1,0:T(8,128)(2,1)S(1)}, u32[]{:S(2)}, u32[]{:S(2)}) %collective-permute-start.23) | collective-permute-done | bytes 200736 | tf_op jit(solution)/shard_map/ppermute | solution.py:26
  126.6 4.2 %collective-permute-done.22.nearest = bf16[196,512]{1,0:T(8,128)(2,1)S(1)} collective-permute-done((bf16[196,512]{1,0:T(8,128)(2,1)S(1)}, bf16[196,512]{1,0:T(8,128)(2,1)S(1)}, u32[]{:S(2)}, u32[]{:S(2)}) %collective-permute-start.22) | collective-permute-done | bytes 200736 | tf_op jit(solution)/shard_map/ppermute | solution.py:26
  130.9 11.5 %collective-permute-done.24.further = bf16[196,512]{1,0:T(8,128)(2,1)S(1)} collective-permute-done((bf16[196,512]{1,0:T(8,128)(2,1)S(1)}, bf16[196,512]{1,0:T(8,128)(2,1)S(1)}, u32[]{:S(2)}, u32[]{:S(2)}) %collective-permute-start.24) | collective-permute-done | bytes 200736 | tf_op jit(solution)/shard_map/ppermute | solution.py:26
  (98 shorter events, 20.7 us)
Async XLA Ops:
  1.7 15.1 %collective-permute-start.1 = (bf16[48,768]{1,0:T(8,128)(2,1)}, bf16[48,768]{1,0:T(8,128)(2,1)S(1)}, u32[]{:S(2)}, u32[]{:S(2)}) collective-permute-start(bf16[48,768]{1,0:T(8,128)(2,1)} %get-tuple-element.39), channel_id=1, source_target_pairs={{0,4},{2,6},{4,8},{6,10},{8,12},{10,14},{12,16},{14,18},{16,20},{1... | collective-permute-start | bytes 221192 | tf_op jit(solution)/shard_map/ppermute | solution.py:26
  5.6 12.9 %collective-permute-start = (bf16[48,768]{1,0:T(8,128)(2,1)}, bf16[48,768]{1,0:T(8,128)(2,1)S(1)}, u32[]{:S(2)}, u32[]{:S(2)}) collective-permute-start(bf16[48,768]{1,0:T(8,128)(2,1)} %get-tuple-element.39), channel_id=1, source_target_pairs={{0,2},{2,4},{4,6},{6,8},{8,10},{10,12},{12,14},{14,16},{16,18},{18... | collective-permute-start | bytes 221192 | tf_op jit(solution)/shard_map/ppermute | solution.py:26
  7.2 17.2 %collective-permute-start.2 = (bf16[152,768]{1,0:T(8,128)(2,1)}, bf16[152,768]{1,0:T(8,128)(2,1)S(1)}, u32[]{:S(2)}, u32[]{:S(2)}) collective-permute-start(bf16[152,768]{1,0:T(8,128)(2,1)} %get-tuple-element.43), channel_id=1, source_target_pairs={{0,252},{2,254},{4,0},{6,2},{8,4},{10,6},{12,8},{14,10},{16,12},{1... | collective-permute-start | bytes 700424 | tf_op jit(solution)/shard_map/ppermute | solution.py:26
  18.5 11.0 %collective-permute-start.7 = (bf16[96,768]{1,0:T(8,128)(2,1)S(1)}, bf16[96,768]{1,0:T(8,128)(2,1)S(1)}, u32[]{:S(2)}, u32[]{:S(2)}) collective-permute-start(bf16[96,768]{1,0:T(8,128)(2,1)S(1)} %pad_maximum_fusion.6), channel_id=1, source_target_pairs={{0,4},{2,6},{4,8},{6,10},{8,12},{10,14},{12,16},{14,18},{16,20},{1... | collective-permute-start | bytes 442376 | tf_op jit(solution)/shard_map/ppermute | solution.py:26
  18.6 12.4 %collective-permute-start.8 = (bf16[152,768]{1,0:T(8,128)(2,1)}, bf16[152,768]{1,0:T(8,128)(2,1)S(1)}, u32[]{:S(2)}, u32[]{:S(2)}) collective-permute-start(bf16[152,768]{1,0:T(8,128)(2,1)} %get-tuple-element.43), channel_id=1, source_target_pairs={{0,254},{2,0},{4,2},{6,4},{8,6},{10,8},{12,10},{14,12},{16,14},{18... | collective-permute-start | bytes 700424 | tf_op jit(solution)/shard_map/ppermute | solution.py:26
  24.6 8.3 %collective-permute-start.6 = (bf16[152,768]{1,0:T(8,128)(2,1)S(1)}, bf16[152,768]{1,0:T(8,128)(2,1)S(1)}, u32[]{:S(2)}, u32[]{:S(2)}) collective-permute-start(bf16[152,768]{1,0:T(8,128)(2,1)S(1)} %collective-permute-done.2), channel_id=1, source_target_pairs={{0,254},{2,0},{4,2},{6,4},{8,6},{10,8},{12,10},{14,12},{16,14},{18... | collective-permute-start | bytes 700424 | tf_op jit(solution)/shard_map/ppermute | solution.py:26
  29.2 8.3 %collective-permute-start.5 = (bf16[2,96,768]{2,1,0:T(8,128)(2,1)S(1)}, bf16[2,96,768]{2,1,0:T(8,128)(2,1)S(1)}, u32[]{:S(2)}, u32[]{:S(2)}) collective-permute-start(bf16[2,96,768]{2,1,0:T(8,128)(2,1)S(1)} %get-tuple-element.74), channel_id=1, source_target_pairs={{0,32},{2,34},{4,36},{6,38},{8,40},{10,42},{12,44},{14,46},{16,48}... | collective-permute-start | bytes 884744 | tf_op jit(solution)/shard_map/ppermute | solution.py:369
  29.3 18.5 %collective-permute-start.4 = (bf16[2,96,768]{2,1,0:T(8,128)(2,1)S(1)}, bf16[2,96,768]{2,1,0:T(8,128)(2,1)S(1)}, u32[]{:S(2)}, u32[]{:S(2)}) collective-permute-start(bf16[2,96,768]{2,1,0:T(8,128)(2,1)S(1)} %get-tuple-element.74), channel_id=1, source_target_pairs={{0,48},{2,50},{4,52},{6,54},{8,56},{10,58},{12,60},{14,62},{16,0},... | collective-permute-start | bytes 884744 | tf_op jit(solution)/shard_map/ppermute | solution.py:369
  29.5 18.4 %collective-permute-start.3 = (bf16[2,96,768]{2,1,0:T(8,128)(2,1)S(1)}, bf16[2,96,768]{2,1,0:T(8,128)(2,1)S(1)}, u32[]{:S(2)}, u32[]{:S(2)}) collective-permute-start(bf16[2,96,768]{2,1,0:T(8,128)(2,1)S(1)} %get-tuple-element.74), channel_id=1, source_target_pairs={{0,16},{2,18},{4,20},{6,22},{8,24},{10,26},{12,28},{14,30},{16,32}... | collective-permute-start | bytes 884744 | tf_op jit(solution)/shard_map/ppermute | solution.py:369
  33.0 6.0 %collective-permute-start.12 = (bf16[4,104,768]{2,1,0:T(8,128)(2,1)S(1)}, bf16[4,104,768]{2,1,0:T(8,128)(2,1)S(1)}, u32[]{:S(2)}, u32[]{:S(2)}) collective-permute-start(bf16[4,104,768]{2,1,0:T(8,128)(2,1)S(1)} %pad_maximum_fusion.3.mine), channel_id=1, source_target_pairs={{0,1},{1,0},{2,3},{3,2},{4,5},{5,4},{6,7},{7,6},{8,9},{9,8},{10,11... | collective-permute-start | bytes 1916936 | tf_op jit(solution)/shard_map/ppermute | solution.py:30
  37.4 10.5 %collective-permute-start.11 = (bf16[2,96,768]{2,1,0:T(8,128)(2,1)S(1)}, bf16[2,96,768]{2,1,0:T(8,128)(2,1)S(1)}, u32[]{:S(2)}, u32[]{:S(2)}) collective-permute-start(bf16[2,96,768]{2,1,0:T(8,128)(2,1)S(1)} %pad_maximum_fusion.5), channel_id=1, source_target_pairs={{0,128},{2,130},{4,132},{6,134},{8,136},{10,138},{12,140},{14,142}... | collective-permute-start | bytes 884744 | tf_op jit(solution)/shard_map/ppermute | solution.py:369
  37.5 11.1 %collective-permute-start.10 = (bf16[2,96,768]{2,1,0:T(8,128)(2,1)S(1)}, bf16[2,96,768]{2,1,0:T(8,128)(2,1)S(1)}, u32[]{:S(2)}, u32[]{:S(2)}) collective-permute-start(bf16[2,96,768]{2,1,0:T(8,128)(2,1)S(1)} %pad_maximum_fusion.5), channel_id=1, source_target_pairs={{0,192},{2,194},{4,196},{6,198},{8,200},{10,202},{12,204},{14,206}... | collective-permute-start | bytes 884744 | tf_op jit(solution)/shard_map/ppermute | solution.py:369
  39.0 15.2 %collective-permute-start.9 = (bf16[2,96,768]{2,1,0:T(8,128)(2,1)S(1)}, bf16[2,96,768]{2,1,0:T(8,128)(2,1)S(1)}, u32[]{:S(2)}, u32[]{:S(2)}) collective-permute-start(bf16[2,96,768]{2,1,0:T(8,128)(2,1)S(1)} %pad_maximum_fusion.5), channel_id=1, source_target_pairs={{0,64},{2,66},{4,68},{6,70},{8,72},{10,74},{12,76},{14,78},{16,80}... | collective-permute-start | bytes 884744 | tf_op jit(solution)/shard_map/ppermute | solution.py:369
  54.3 27.3 %collective-permute-start.16 = (bf16[2,384,768]{2,1,0:T(8,128)(2,1)S(1)}, bf16[2,384,768]{2,1,0:T(8,128)(2,1)S(1)}, u32[]{:S(2)}, u32[]{:S(2)}) collective-permute-start(bf16[2,384,768]{2,1,0:T(8,128)(2,1)S(1)} %pad_maximum_fusion.2), channel_id=1, source_target_pairs={{0,48},{2,50},{4,52},{6,54},{8,56},{10,58},{12,60},{14,62},{16,0},... | collective-permute-start | bytes 3538952 | tf_op jit(solution)/shard_map/ppermute | solution.py:369
  54.6 28.3 %collective-permute-start.15 = (bf16[2,384,768]{2,1,0:T(8,128)(2,1)S(1)}, bf16[2,384,768]{2,1,0:T(8,128)(2,1)S(1)}, u32[]{:S(2)}, u32[]{:S(2)}) collective-permute-start(bf16[2,384,768]{2,1,0:T(8,128)(2,1)S(1)} %pad_maximum_fusion.2), channel_id=1, source_target_pairs={{0,16},{2,18},{4,20},{6,22},{8,24},{10,26},{12,28},{14,30},{16,32}... | collective-permute-start | bytes 3538952 | tf_op jit(solution)/shard_map/ppermute | solution.py:369
  56.1 26.8 %collective-permute-start.14 = (bf16[2,384,768]{2,1,0:T(8,128)(2,1)S(1)}, bf16[2,384,768]{2,1,0:T(8,128)(2,1)S(1)}, u32[]{:S(2)}, u32[]{:S(2)}) collective-permute-start(bf16[2,384,768]{2,1,0:T(8,128)(2,1)S(1)} %pad_maximum_fusion.1), channel_id=1, source_target_pairs={{0,192},{2,194},{4,196},{6,198},{8,200},{10,202},{12,204},{14,206}... | collective-permute-start | bytes 3538952 | tf_op jit(solution)/shard_map/ppermute | solution.py:369
  56.3 26.9 %collective-permute-start.13 = (bf16[2,384,768]{2,1,0:T(8,128)(2,1)S(1)}, bf16[2,384,768]{2,1,0:T(8,128)(2,1)S(1)}, u32[]{:S(2)}, u32[]{:S(2)}) collective-permute-start(bf16[2,384,768]{2,1,0:T(8,128)(2,1)S(1)} %pad_maximum_fusion.1), channel_id=1, source_target_pairs={{0,64},{2,66},{4,68},{6,70},{8,72},{10,74},{12,76},{14,78},{16,80}... | collective-permute-start | bytes 3538952 | tf_op jit(solution)/shard_map/ppermute | solution.py:369
  83.8 12.5 %collective-permute-start.20 = (bf16[2,192,768]{2,1,0:T(8,128)(2,1)S(1)}, bf16[2,192,768]{2,1,0:T(8,128)(2,1)S(1)}, u32[]{:S(2)}, u32[]{:S(2)}) collective-permute-start(bf16[2,192,768]{2,1,0:T(8,128)(2,1)S(1)} %slice.101), channel_id=1, source_target_pairs={{0,48},{2,50},{4,52},{6,54},{8,56},{10,58},{12,60},{14,62},{16,0},... | collective-permute-start | bytes 1769480 | tf_op jit(solution)/shard_map/ppermute | solution.py:369
  86.0 13.5 %collective-permute-start.19 = (bf16[2,192,768]{2,1,0:T(8,128)(2,1)S(1)}, bf16[2,192,768]{2,1,0:T(8,128)(2,1)S(1)}, u32[]{:S(2)}, u32[]{:S(2)}) collective-permute-start(bf16[2,192,768]{2,1,0:T(8,128)(2,1)S(1)} %slice.100), channel_id=1, source_target_pairs={{0,16},{2,18},{4,20},{6,22},{8,24},{10,26},{12,28},{14,30},{16,32}... | collective-permute-start | bytes 1769480 | tf_op jit(solution)/shard_map/ppermute | solution.py:369
  86.0 13.5 %collective-permute-start.18 = (bf16[2,192,768]{2,1,0:T(8,128)(2,1)S(1)}, bf16[2,192,768]{2,1,0:T(8,128)(2,1)S(1)}, u32[]{:S(2)}, u32[]{:S(2)}) collective-permute-start(bf16[2,192,768]{2,1,0:T(8,128)(2,1)S(1)} %slice.99), channel_id=1, source_target_pairs={{0,192},{2,194},{4,196},{6,198},{8,200},{10,202},{12,204},{14,206}... | collective-permute-start | bytes 1769480 | tf_op jit(solution)/shard_map/ppermute | solution.py:369
  86.2 13.4 %collective-permute-start.17 = (bf16[2,192,768]{2,1,0:T(8,128)(2,1)S(1)}, bf16[2,192,768]{2,1,0:T(8,128)(2,1)S(1)}, u32[]{:S(2)}, u32[]{:S(2)}) collective-permute-start(bf16[2,192,768]{2,1,0:T(8,128)(2,1)S(1)} %slice.98), channel_id=1, source_target_pairs={{0,64},{2,66},{4,68},{6,70},{8,72},{10,74},{12,76},{14,78},{16,80}... | collective-permute-start | bytes 1769480 | tf_op jit(solution)/shard_map/ppermute | solution.py:369
  110.3 16.2 %collective-permute-start.23 = (bf16[196,512]{1,0:T(8,128)(2,1)S(1)}, bf16[196,512]{1,0:T(8,128)(2,1)S(1)}, u32[]{:S(2)}, u32[]{:S(2)}) collective-permute-start(bf16[196,512]{1,0:T(8,128)(2,1)S(1)} %furthest_part.1), channel_id=1, source_target_pairs={{0,2},{2,4},{4,6},{6,8},{8,10},{10,12},{12,14},{14,16},{16,18},{18... | collective-permute-start | bytes 602120 | tf_op jit(solution)/shard_map/ppermute | solution.py:26
  112.1 18.8 %collective-permute-start.22 = (bf16[196,512]{1,0:T(8,128)(2,1)S(1)}, bf16[196,512]{1,0:T(8,128)(2,1)S(1)}, u32[]{:S(2)}, u32[]{:S(2)}) collective-permute-start(bf16[196,512]{1,0:T(8,128)(2,1)S(1)} %get-tuple-element.71), channel_id=1, source_target_pairs={{0,2},{2,4},{4,6},{6,8},{8,10},{10,12},{12,14},{14,16},{16,18},{18... | collective-permute-start | bytes 602120 | tf_op jit(solution)/shard_map/ppermute | solution.py:26
  126.6 15.8 %collective-permute-start.24 = (bf16[196,512]{1,0:T(8,128)(2,1)S(1)}, bf16[196,512]{1,0:T(8,128)(2,1)S(1)}, u32[]{:S(2)}, u32[]{:S(2)}) collective-permute-start(bf16[196,512]{1,0:T(8,128)(2,1)S(1)} %add_convert_fusion), channel_id=1, source_target_pairs={{0,4},{2,6},{4,8},{6,10},{8,12},{10,14},{12,16},{14,18},{16,20},{1... | collective-permute-start | bytes 602120 | tf_op jit(solution)/shard_map/ppermute | solution.py:26
  (13 other events, 102.1 us)

commit v10 on v9

--- a/solution.py
+++ b/solution.py
@@ -414,7 +414,8 @@
     place = jnp.stack([lax.axis_index("pairs"), lax.axis_index("side")]).astype(jnp.int32)
     packed, shard = pack_call(features, w_fc1, w_fc2)
     next2 = shifted(packed, -2)
-    last1, last2, later = tied(shifted(shard, 1), shifted(shard, 2), packed)
+    last1, later = tied(shifted(shard, 1), packed)
+    last2 = shifted(shard, 2)
     next1 = shifted(later, -1)
     last34 = shifted(jnp.concatenate([last1, last2], axis=0), 2)
     next3, last34, next1 = tied(shifted(next2, -1), last34, next1)
@@ -432,8 +433,10 @@
     near_x, near_y = first_hop(plane_x, "y"), first_hop(plane_y, "x")
     first, query = self_call(rows, triple, gain_query, w_self_out[0], w_query[0])
     second, mlp_in = cross_call(first, query, key_value, gain_mlp, w_cross_out[0])
-    near_x, near_y, second, mlp_in = tied(near_x, near_y, second, mlp_in)
-    far_x, far_y = second_hop(*near_x, "y"), second_hop(*near_y, "x")
+    near_y, second, mlp_in = tied(near_y, second, mlp_in)
+    far_y = second_hop(*near_y, "x")
+    near_x, second, mlp_in = tied(near_x, second, mlp_in)
+    far_x = second_hop(*near_x, "y")
     fc_early = jnp.concatenate([plane_x, *near_x, plane_y, *near_y], axis=1)
     early = early_call(second, mlp_in, fc_early)
     fc_late = jnp.concatenate([*far_x, *far_y], axis=1)

time: 143 us -> 139 us (0.972)
  waiting for transfers between devices: 51.7 us -> 36.4 us
  starting transfers between devices: 42.4 us -> 53.4 us
    ppermute x14, starting transfers between devices: 8.8 us -> 19.7 us  [along(): return lax.ppermute(array, 'pairs', [(p, target(p)) for p in range(count)])]
    ppermute x14, waiting for transfers between devices: 17.5 us -> 7.26 us  [along(): return lax.ppermute(array, 'pairs', [(p, target(p)) for p in range(count)])]
    ppermute x9, waiting for transfers between devices: 31.8 us -> 28.1 us  [shifted(): lax.ppermute(array, 'pairs', [(i, (i + by) % count) for i in range(count)])]
  transfers between devices with their start and end apart: 25 -> 25, of which waited for: 15 -> 12; matrix products, arithmetic and copies ran while one was open for 2% -> 2% of each run, Pallas kernels for 25% -> 26%
where the time goes in v10:
time: 139 us
  starting transfers between devices  53.4 us (38%)
  Pallas kernels  43.8 us (32%)
  waiting for transfers between devices  36.4 us (26%)
  local copies, waits for them, and re-layouts  3.33 us (2%)
    pallas_call x9, Pallas kernels, call(): pl.pallas_call(kernel, in_specs=[SMEM] * len(scalars) + [VMEM] * len(arra...  42.2 us
    ppermute x9, waiting for transfers between devices, shifted(): lax.ppermute(array, 'pairs', [(i, (i + by) % count) for i in range(count)])  28.1 us
    ppermute x9, starting transfers between devices, shifted(): lax.ppermute(array, 'pairs', [(i, (i + by) % count) for i in range(count)])  24.5 us
    ppermute x14, starting transfers between devices, along(): return lax.ppermute(array, 'pairs', [(p, target(p)) for p in range(count)])  19.7 us
    ppermute x2, starting transfers between devices, other_core(): return lax.ppermute(array, 'side', [(0, 1), (1, 0)])  9.16 us
    ppermute x14, waiting for transfers between devices, along(): return lax.ppermute(array, 'pairs', [(p, target(p)) for p in range(count)])  7.26 us
  transfers between devices with their start and end apart: 25, of which 12 were waited for; matrix products, arithmetic and copies ran while one was open for 2% of the time, Pallas kernels for 26%

profile of v10, /device:TPU:1, one launch (start us, length us, event | category | flops | bytes accessed | tf_op | source)
XLA Modules:
  0.0 138.8 jit_solution(345674205056564897)
XLA Ops:
  1.7 3.9 %collective-permute-start.1 = (bf16[48,768]{1,0:T(8,128)(2,1)}, bf16[48,768]{1,0:T(8,128)(2,1)S(1)}, u32[]{:S(2)}, u32[]{:S(2)}) collective-permute-start(bf16[48,768]{1,0:T(8,128)(2,1)} %get-tuple-element.40), channel_id=1, source_target_pairs={{0,4},{2,6},{4,8},{6,10},{8,12},{10,14},{12,16},{14,18},{16,20},{1... | collective-permute-start | bytes 221192 | tf_op jit(solution)/shard_map/ppermute | solution.py:26
  7.2 6.9 %collective-permute-start.2 = (bf16[152,768]{1,0:T(8,128)(2,1)}, bf16[152,768]{1,0:T(8,128)(2,1)S(1)}, u32[]{:S(2)}, u32[]{:S(2)}) collective-permute-start(bf16[152,768]{1,0:T(8,128)(2,1)} %get-tuple-element.43), channel_id=1, source_target_pairs={{0,252},{2,254},{4,0},{6,2},{8,4},{10,6},{12,8},{14,10},{16,12},{1... | collective-permute-start | bytes 700424 | tf_op jit(solution)/shard_map/ppermute | solution.py:26
  16.7 1.8 %collective-permute-done = bf16[48,768]{1,0:T(8,128)(2,1)S(1)} collective-permute-done((bf16[48,768]{1,0:T(8,128)(2,1)}, bf16[48,768]{1,0:T(8,128)(2,1)S(1)}, u32[]{:S(2)}, u32[]{:S(2)}) %collective-permute-start) | collective-permute-done | bytes 73760 | tf_op jit(solution)/shard_map/ppermute | solution.py:26
  18.6 5.8 %collective-permute-start.8 = (bf16[152,768]{1,0:T(8,128)(2,1)}, bf16[152,768]{1,0:T(8,128)(2,1)S(1)}, u32[]{:S(2)}, u32[]{:S(2)}) collective-permute-start(bf16[152,768]{1,0:T(8,128)(2,1)} %get-tuple-element.43), channel_id=1, source_target_pairs={{0,254},{2,0},{4,2},{6,4},{8,6},{10,8},{12,10},{14,12},{16,14},{18... | collective-permute-start | bytes 700424 | tf_op jit(solution)/shard_map/ppermute | solution.py:26
  24.5 4.6 %collective-permute-start.6 = (bf16[152,768]{1,0:T(8,128)(2,1)S(1)}, bf16[152,768]{1,0:T(8,128)(2,1)S(1)}, u32[]{:S(2)}, u32[]{:S(2)}) collective-permute-start(bf16[152,768]{1,0:T(8,128)(2,1)S(1)} %collective-permute-done.2), channel_id=1, source_target_pairs={{0,254},{2,0},{4,2},{6,4},{8,6},{10,8},{12,10},{14,12},{16,14},{18... | collective-permute-start | bytes 700424 | tf_op jit(solution)/shard_map/ppermute | solution.py:26
  29.2 2.7 %collective-permute-start.4 = (bf16[2,96,768]{2,1,0:T(8,128)(2,1)S(1)}, bf16[2,96,768]{2,1,0:T(8,128)(2,1)S(1)}, u32[]{:S(2)}, u32[]{:S(2)}) collective-permute-start(bf16[2,96,768]{2,1,0:T(8,128)(2,1)S(1)} %get-tuple-element.76), channel_id=1, source_target_pairs={{0,48},{2,50},{4,52},{6,54},{8,56},{10,58},{12,60},{14,62},{16,0},... | collective-permute-start | bytes 884744 | tf_op jit(solution)/shard_map/ppermute | solution.py:369
  32.9 3.0 %collective-permute-start.12 = (bf16[4,104,768]{2,1,0:T(8,128)(2,1)S(1)}, bf16[4,104,768]{2,1,0:T(8,128)(2,1)S(1)}, u32[]{:S(2)}, u32[]{:S(2)}) collective-permute-start(bf16[4,104,768]{2,1,0:T(8,128)(2,1)S(1)} %pad_maximum_fusion.3.mine), channel_id=1, source_target_pairs={{0,1},{1,0},{2,3},{3,2},{4,5},{5,4},{6,7},{7,6},{8,9},{9,8},{10,11... | collective-permute-start | bytes 1916936 | tf_op jit(solution)/shard_map/ppermute | solution.py:30
  36.1 2.7 %collective-permute-start.10 = (bf16[2,96,768]{2,1,0:T(8,128)(2,1)S(1)}, bf16[2,96,768]{2,1,0:T(8,128)(2,1)S(1)}, u32[]{:S(2)}, u32[]{:S(2)}) collective-permute-start(bf16[2,96,768]{2,1,0:T(8,128)(2,1)S(1)} %pad_maximum_fusion.5), channel_id=1, source_target_pairs={{0,192},{2,194},{4,196},{6,198},{8,200},{10,202},{12,204},{14,206}... | collective-permute-start | bytes 884744 | tf_op jit(solution)/shard_map/ppermute | solution.py:369
  38.8 5.0 %triple_part.1 = (f32[624,768]{1,0:T(8,128)S(1)}, bf16[624,2304]{1,0:T(8,128)(2,1)S(1)}) custom-call(s32[128]{0:T(128)S(1)} %copy-done, s32[6]{0:T(128)S(1)} %reshape.4.slot_images, s32[2]{0:T(128)S(1)} %pad_add_fusion.place, bf16[4,104,768]{2,1,0:T(8,128)(2,1)S(1)} %pad_maximum_fusion.3.mine, bf16[4,104,768]{2,1,0:T(8,128)(2,1)S(1)} %collective-permute-done.12.theirs, ...), custom_call_target="tpu_custom_call" | custom-call | flops 4000000000 | bytes 8388608 | tf_op jit(solution)/shard_map/triple_part/pallas_call | solution.py:272
  43.8 3.7 %memory_part.1.key_value = bf16[624,1536]{1,0:T(8,128)(2,1)S(1)} custom-call(s32[128]{0:T(128)S(1)} %copy-done, s32[6]{0:T(128)S(1)} %reshape.4.slot_images, s32[2]{0:T(128)S(1)} %pad_add_fusion.place, bf16[4,104,768]{2,1,0:T(8,128)(2,1)S(1)} %pad_maximum_fusion.3.mine, bf16[4,104,768]{2,1,0:T(8,128)(2,1)S(1)} %collective-permute-done.12.theirs, ...), custom_call_target="tpu_custom_call" | custom-call | flops 3000000000 | bytes 8388608 | tf_op jit(solution)/shard_map/memory_part/pallas_call | solution.py:272
  49.4 2.7 %collective-permute-start.14 = (bf16[2,384,768]{2,1,0:T(8,128)(2,1)S(1)}, bf16[2,384,768]{2,1,0:T(8,128)(2,1)S(1)}, u32[]{:S(2)}, u32[]{:S(2)}) collective-permute-start(bf16[2,384,768]{2,1,0:T(8,128)(2,1)S(1)} %pad_maximum_fusion.1), channel_id=1, source_target_pairs={{0,192},{2,194},{4,196},{6,198},{8,200},{10,202},{12,204},{14,206}... | collective-permute-start | bytes 3538952 | tf_op jit(solution)/shard_map/ppermute | solution.py:369
  52.2 3.6 %collective-permute-start.15 = (bf16[2,384,768]{2,1,0:T(8,128)(2,1)S(1)}, bf16[2,384,768]{2,1,0:T(8,128)(2,1)S(1)}, u32[]{:S(2)}, u32[]{:S(2)}) collective-permute-start(bf16[2,384,768]{2,1,0:T(8,128)(2,1)S(1)} %pad_maximum_fusion.2), channel_id=1, source_target_pairs={{0,16},{2,18},{4,20},{6,22},{8,24},{10,26},{12,28},{14,30},{16,32}... | collective-permute-start | bytes 3538952 | tf_op jit(solution)/shard_map/ppermute | solution.py:369
  55.9 10.5 %self_part.1 = (f32[624,768]{1,0:T(8,128)S(1)}, bf16[624,768]{1,0:T(8,128)(2,1)S(1)}) custom-call(f32[624,768]{1,0:T(8,128)S(1)} %get-tuple-element.55.rows, bf16[624,2304]{1,0:T(8,128)(2,1)S(1)} %get-tuple-element.56.triple, f32[1,768]{1,0:T(1,128)S(1)} %copy-done.9, bf16[768,768]{1,0:T(8,128)(2,1)S(1)} %bitcast.27, bf16[768,768]{1,0:T(8,128)(2,1)S(1)} %bitcast.28), custom_call_target="tpu_custom_call" | custom-call | flops 12000000000 | bytes 8388608 | tf_op jit(solution)/shard_map/self_part/pallas_call | solution.py:272
  66.5 9.2 %cross_part.1 = (f32[624,768]{1,0:T(8,128)S(1)}, bf16[624,768]{1,0:T(8,128)(2,1)S(1)}) custom-call(f32[624,768]{1,0:T(8,128)S(1)} %get-tuple-element.57.first, bf16[624,768]{1,0:T(8,128)(2,1)S(1)} %get-tuple-element.58.query, bf16[624,1536]{1,0:T(8,128)(2,1)S(1)} %memory_part.1.key_value, f32[1,768]{1,0:T(1,128)S(1)} %copy-done.10, bf16[768,768]{1,0:T(8,128)(2,1)S(1)} %bitcast.29), custom_call_target="tpu_custom_call" | custom-call | flops 12000000000 | bytes 8388608 | tf_op jit(solution)/shard_map/cross_part/pallas_call | solution.py:272
  75.7 2.2 %collective-permute-done.16 = bf16[2,384,768]{2,1,0:T(8,128)(2,1)S(1)} collective-permute-done((bf16[2,384,768]{2,1,0:T(8,128)(2,1)S(1)}, bf16[2,384,768]{2,1,0:T(8,128)(2,1)S(1)}, u32[]{:S(2)}, u32[]{:S(2)}) %collective-permute-start.16) | collective-permute-done | bytes 1179680 | tf_op jit(solution)/shard_map/ppermute | solution.py:369
  78.6 3.9 %collective-permute-start.20 = (bf16[2,192,768]{2,1,0:T(8,128)(2,1)S(1)}, bf16[2,192,768]{2,1,0:T(8,128)(2,1)S(1)}, u32[]{:S(2)}, u32[]{:S(2)}) collective-permute-start(bf16[2,192,768]{2,1,0:T(8,128)(2,1)S(1)} %slice.101), channel_id=1, source_target_pairs={{0,48},{2,50},{4,52},{6,54},{8,56},{10,58},{12,60},{14,62},{16,0},... | collective-permute-start | bytes 1769480 | tf_op jit(solution)/shard_map/ppermute | solution.py:369
  82.6 2.2 %collective-permute-start.19 = (bf16[2,192,768]{2,1,0:T(8,128)(2,1)S(1)}, bf16[2,192,768]{2,1,0:T(8,128)(2,1)S(1)}, u32[]{:S(2)}, u32[]{:S(2)}) collective-permute-start(bf16[2,192,768]{2,1,0:T(8,128)(2,1)S(1)} %slice.100), channel_id=1, source_target_pairs={{0,16},{2,18},{4,20},{6,22},{8,24},{10,26},{12,28},{14,30},{16,32}... | collective-permute-start | bytes 1769480 | tf_op jit(solution)/shard_map/ppermute | solution.py:369
  86.3 6.5 %early_part.1.early = f32[624,768]{1,0:T(8,128)S(1)} custom-call(f32[624,768]{1,0:T(8,128)S(1)} %get-tuple-element.64.second, bf16[624,768]{1,0:T(8,128)(2,1)S(1)} %get-tuple-element.65.mlp_in, bf16[2,2304,768]{2,1,0:T(8,128)(2,1)S(1)} %constant_dynamic-update-slice_fusion.fc), custom_call_target="tpu_custom_call" | custom-call | flops 10000000000 | bytes 8388608 | tf_op jit(solution)/shard_map/early_part/pallas_call | solution.py:272
  92.8 1.8 %collective-permute-done.20 = bf16[2,192,768]{2,1,0:T(8,128)(2,1)S(1)} collective-permute-done((bf16[2,192,768]{2,1,0:T(8,128)(2,1)S(1)}, bf16[2,192,768]{2,1,0:T(8,128)(2,1)S(1)}, u32[]{:S(2)}, u32[]{:S(2)}) %collective-permute-start.20) | collective-permute-done | bytes 589856 | tf_op jit(solution)/shard_map/ppermute | solution.py:369
  96.5 4.4 %late_part.1 = (f32[3,196,512]{2,1,0:T(8,128)S(1)}, bf16[3,196,512]{2,1,0:T(8,128)(2,1)S(1)}) custom-call(s32[2]{0:T(128)S(1)} %pad_add_fusion.place, f32[624,768]{1,0:T(8,128)S(1)} %early_part.1.early, bf16[624,768]{1,0:T(8,128)(2,1)S(1)} %get-tuple-element.65.mlp_in, bf16[2,768,768]{2,1,0:T(8,128)(2,1)S(1)} %pad_maximum_fusion.fc, ...), custom_call_target="tpu_custom_call" | custom-call | flops 5000000000 | bytes 8388608 | tf_op jit(solution)/shard_map/late_part/pallas_call | solution.py:272
  101.0 6.2 %collective-permute-start.21 = (bf16[3,196,512]{2,1,0:T(8,128)(2,1)S(1)}, bf16[3,196,512]{2,1,0:T(8,128)(2,1)S(1)}, u32[]{:S(2)}, u32[]{:S(2)}) collective-permute-start(bf16[3,196,512]{2,1,0:T(8,128)(2,1)S(1)} %get-tuple-element.71), channel_id=1, source_target_pairs={{0,1},{1,0},{2,3},{3,2},{4,5},{5,4},{6,7},{7,6},{8,9},{9,8},{10,11... | collective-permute-start | bytes 1806344 | tf_op jit(solution)/shard_map/ppermute | solution.py:30
  112.2 9.3 %collective-permute-done.23 = bf16[196,512]{1,0:T(8,128)(2,1)S(1)} collective-permute-done((bf16[196,512]{1,0:T(8,128)(2,1)S(1)}, bf16[196,512]{1,0:T(8,128)(2,1)S(1)}, u32[]{:S(2)}, u32[]{:S(2)}) %collective-permute-start.23) | collective-permute-done | bytes 200736 | tf_op jit(solution)/shard_map/ppermute | solution.py:26
  121.6 4.2 %collective-permute-done.22.nearest = bf16[196,512]{1,0:T(8,128)(2,1)S(1)} collective-permute-done((bf16[196,512]{1,0:T(8,128)(2,1)S(1)}, bf16[196,512]{1,0:T(8,128)(2,1)S(1)}, u32[]{:S(2)}, u32[]{:S(2)}) %collective-permute-start.22) | collective-permute-done | bytes 200736 | tf_op jit(solution)/shard_map/ppermute | solution.py:26
  125.9 12.1 %collective-permute-done.24.further = bf16[196,512]{1,0:T(8,128)(2,1)S(1)} collective-permute-done((bf16[196,512]{1,0:T(8,128)(2,1)S(1)}, bf16[196,512]{1,0:T(8,128)(2,1)S(1)}, u32[]{:S(2)}, u32[]{:S(2)}) %collective-permute-start.24) | collective-permute-done | bytes 200736 | tf_op jit(solution)/shard_map/ppermute | solution.py:26
  (98 shorter events, 18.6 us)
Async XLA Ops:
  1.7 16.8 %collective-permute-start.1 = (bf16[48,768]{1,0:T(8,128)(2,1)}, bf16[48,768]{1,0:T(8,128)(2,1)S(1)}, u32[]{:S(2)}, u32[]{:S(2)}) collective-permute-start(bf16[48,768]{1,0:T(8,128)(2,1)} %get-tuple-element.40), channel_id=1, source_target_pairs={{0,4},{2,6},{4,8},{6,10},{8,12},{10,14},{12,16},{14,18},{16,20},{1... | collective-permute-start | bytes 221192 | tf_op jit(solution)/shard_map/ppermute | solution.py:26
  5.6 12.9 %collective-permute-start = (bf16[48,768]{1,0:T(8,128)(2,1)}, bf16[48,768]{1,0:T(8,128)(2,1)S(1)}, u32[]{:S(2)}, u32[]{:S(2)}) collective-permute-start(bf16[48,768]{1,0:T(8,128)(2,1)} %get-tuple-element.40), channel_id=1, source_target_pairs={{0,2},{2,4},{4,6},{6,8},{8,10},{10,12},{12,14},{14,16},{16,18},{18... | collective-permute-start | bytes 221192 | tf_op jit(solution)/shard_map/ppermute | solution.py:26
  7.2 17.2 %collective-permute-start.2 = (bf16[152,768]{1,0:T(8,128)(2,1)}, bf16[152,768]{1,0:T(8,128)(2,1)S(1)}, u32[]{:S(2)}, u32[]{:S(2)}) collective-permute-start(bf16[152,768]{1,0:T(8,128)(2,1)} %get-tuple-element.43), channel_id=1, source_target_pairs={{0,252},{2,254},{4,0},{6,2},{8,4},{10,6},{12,8},{14,10},{16,12},{1... | collective-permute-start | bytes 700424 | tf_op jit(solution)/shard_map/ppermute | solution.py:26
  18.5 13.4 %collective-permute-start.7 = (bf16[96,768]{1,0:T(8,128)(2,1)S(1)}, bf16[96,768]{1,0:T(8,128)(2,1)S(1)}, u32[]{:S(2)}, u32[]{:S(2)}) collective-permute-start(bf16[96,768]{1,0:T(8,128)(2,1)S(1)} %pad_maximum_fusion.6), channel_id=1, source_target_pairs={{0,4},{2,6},{4,8},{6,10},{8,12},{10,14},{12,16},{14,18},{16,20},{1... | collective-permute-start | bytes 442376 | tf_op jit(solution)/shard_map/ppermute | solution.py:26
  18.6 13.4 %collective-permute-start.8 = (bf16[152,768]{1,0:T(8,128)(2,1)}, bf16[152,768]{1,0:T(8,128)(2,1)S(1)}, u32[]{:S(2)}, u32[]{:S(2)}) collective-permute-start(bf16[152,768]{1,0:T(8,128)(2,1)} %get-tuple-element.43), channel_id=1, source_target_pairs={{0,254},{2,0},{4,2},{6,4},{8,6},{10,8},{12,10},{14,12},{16,14},{18... | collective-permute-start | bytes 700424 | tf_op jit(solution)/shard_map/ppermute | solution.py:26
  24.5 8.2 %collective-permute-start.6 = (bf16[152,768]{1,0:T(8,128)(2,1)S(1)}, bf16[152,768]{1,0:T(8,128)(2,1)S(1)}, u32[]{:S(2)}, u32[]{:S(2)}) collective-permute-start(bf16[152,768]{1,0:T(8,128)(2,1)S(1)} %collective-permute-done.2), channel_id=1, source_target_pairs={{0,254},{2,0},{4,2},{6,4},{8,6},{10,8},{12,10},{14,12},{16,14},{18... | collective-permute-start | bytes 700424 | tf_op jit(solution)/shard_map/ppermute | solution.py:26
  29.1 6.9 %collective-permute-start.3 = (bf16[2,96,768]{2,1,0:T(8,128)(2,1)S(1)}, bf16[2,96,768]{2,1,0:T(8,128)(2,1)S(1)}, u32[]{:S(2)}, u32[]{:S(2)}) collective-permute-start(bf16[2,96,768]{2,1,0:T(8,128)(2,1)S(1)} %get-tuple-element.76), channel_id=1, source_target_pairs={{0,16},{2,18},{4,20},{6,22},{8,24},{10,26},{12,28},{14,30},{16,32}... | collective-permute-start | bytes 884744 | tf_op jit(solution)/shard_map/ppermute | solution.py:369
  29.2 18.3 %collective-permute-start.4 = (bf16[2,96,768]{2,1,0:T(8,128)(2,1)S(1)}, bf16[2,96,768]{2,1,0:T(8,128)(2,1)S(1)}, u32[]{:S(2)}, u32[]{:S(2)}) collective-permute-start(bf16[2,96,768]{2,1,0:T(8,128)(2,1)S(1)} %get-tuple-element.76), channel_id=1, source_target_pairs={{0,48},{2,50},{4,52},{6,54},{8,56},{10,58},{12,60},{14,62},{16,0},... | collective-permute-start | bytes 884744 | tf_op jit(solution)/shard_map/ppermute | solution.py:369
  31.9 15.6 %collective-permute-start.5 = (bf16[2,96,768]{2,1,0:T(8,128)(2,1)S(1)}, bf16[2,96,768]{2,1,0:T(8,128)(2,1)S(1)}, u32[]{:S(2)}, u32[]{:S(2)}) collective-permute-start(bf16[2,96,768]{2,1,0:T(8,128)(2,1)S(1)} %get-tuple-element.76), channel_id=1, source_target_pairs={{0,32},{2,34},{4,36},{6,38},{8,40},{10,42},{12,44},{14,46},{16,48}... | collective-permute-start | bytes 884744 | tf_op jit(solution)/shard_map/ppermute | solution.py:369
  36.0 13.1 %collective-permute-start.9 = (bf16[2,96,768]{2,1,0:T(8,128)(2,1)S(1)}, bf16[2,96,768]{2,1,0:T(8,128)(2,1)S(1)}, u32[]{:S(2)}, u32[]{:S(2)}) collective-permute-start(bf16[2,96,768]{2,1,0:T(8,128)(2,1)S(1)} %pad_maximum_fusion.5), channel_id=1, source_target_pairs={{0,64},{2,66},{4,68},{6,70},{8,72},{10,74},{12,76},{14,78},{16,80}... | collective-permute-start | bytes 884744 | tf_op jit(solution)/shard_map/ppermute | solution.py:369
  36.1 13.0 %collective-permute-start.10 = (bf16[2,96,768]{2,1,0:T(8,128)(2,1)S(1)}, bf16[2,96,768]{2,1,0:T(8,128)(2,1)S(1)}, u32[]{:S(2)}, u32[]{:S(2)}) collective-permute-start(bf16[2,96,768]{2,1,0:T(8,128)(2,1)S(1)} %pad_maximum_fusion.5), channel_id=1, source_target_pairs={{0,192},{2,194},{4,196},{6,198},{8,200},{10,202},{12,204},{14,206}... | collective-permute-start | bytes 884744 | tf_op jit(solution)/shard_map/ppermute | solution.py:369
  38.7 10.3 %collective-permute-start.11 = (bf16[2,96,768]{2,1,0:T(8,128)(2,1)S(1)}, bf16[2,96,768]{2,1,0:T(8,128)(2,1)S(1)}, u32[]{:S(2)}, u32[]{:S(2)}) collective-permute-start(bf16[2,96,768]{2,1,0:T(8,128)(2,1)S(1)} %pad_maximum_fusion.5), channel_id=1, source_target_pairs={{0,128},{2,130},{4,132},{6,134},{8,136},{10,138},{12,140},{14,142}... | collective-permute-start | bytes 884744 | tf_op jit(solution)/shard_map/ppermute | solution.py:369
  49.1 28.8 %collective-permute-start.13 = (bf16[2,384,768]{2,1,0:T(8,128)(2,1)S(1)}, bf16[2,384,768]{2,1,0:T(8,128)(2,1)S(1)}, u32[]{:S(2)}, u32[]{:S(2)}) collective-permute-start(bf16[2,384,768]{2,1,0:T(8,128)(2,1)S(1)} %pad_maximum_fusion.1), channel_id=1, source_target_pairs={{0,64},{2,66},{4,68},{6,70},{8,72},{10,74},{12,76},{14,78},{16,80}... | collective-permute-start | bytes 3538952 | tf_op jit(solution)/shard_map/ppermute | solution.py:369
  49.4 28.6 %collective-permute-start.14 = (bf16[2,384,768]{2,1,0:T(8,128)(2,1)S(1)}, bf16[2,384,768]{2,1,0:T(8,128)(2,1)S(1)}, u32[]{:S(2)}, u32[]{:S(2)}) collective-permute-start(bf16[2,384,768]{2,1,0:T(8,128)(2,1)S(1)} %pad_maximum_fusion.1), channel_id=1, source_target_pairs={{0,192},{2,194},{4,196},{6,198},{8,200},{10,202},{12,204},{14,206}... | collective-permute-start | bytes 3538952 | tf_op jit(solution)/shard_map/ppermute | solution.py:369
  52.2 23.6 %collective-permute-start.15 = (bf16[2,384,768]{2,1,0:T(8,128)(2,1)S(1)}, bf16[2,384,768]{2,1,0:T(8,128)(2,1)S(1)}, u32[]{:S(2)}, u32[]{:S(2)}) collective-permute-start(bf16[2,384,768]{2,1,0:T(8,128)(2,1)S(1)} %pad_maximum_fusion.2), channel_id=1, source_target_pairs={{0,16},{2,18},{4,20},{6,22},{8,24},{10,26},{12,28},{14,30},{16,32}... | collective-permute-start | bytes 3538952 | tf_op jit(solution)/shard_map/ppermute | solution.py:369
  55.8 22.2 %collective-permute-start.16 = (bf16[2,384,768]{2,1,0:T(8,128)(2,1)S(1)}, bf16[2,384,768]{2,1,0:T(8,128)(2,1)S(1)}, u32[]{:S(2)}, u32[]{:S(2)}) collective-permute-start(bf16[2,384,768]{2,1,0:T(8,128)(2,1)S(1)} %pad_maximum_fusion.2), channel_id=1, source_target_pairs={{0,48},{2,50},{4,52},{6,54},{8,56},{10,58},{12,60},{14,62},{16,0},... | collective-permute-start | bytes 3538952 | tf_op jit(solution)/shard_map/ppermute | solution.py:369
  78.6 16.0 %collective-permute-start.20 = (bf16[2,192,768]{2,1,0:T(8,128)(2,1)S(1)}, bf16[2,192,768]{2,1,0:T(8,128)(2,1)S(1)}, u32[]{:S(2)}, u32[]{:S(2)}) collective-permute-start(bf16[2,192,768]{2,1,0:T(8,128)(2,1)S(1)} %slice.101), channel_id=1, source_target_pairs={{0,48},{2,50},{4,52},{6,54},{8,56},{10,58},{12,60},{14,62},{16,0},... | collective-permute-start | bytes 1769480 | tf_op jit(solution)/shard_map/ppermute | solution.py:369
  82.6 12.5 %collective-permute-start.19 = (bf16[2,192,768]{2,1,0:T(8,128)(2,1)S(1)}, bf16[2,192,768]{2,1,0:T(8,128)(2,1)S(1)}, u32[]{:S(2)}, u32[]{:S(2)}) collective-permute-start(bf16[2,192,768]{2,1,0:T(8,128)(2,1)S(1)} %slice.100), channel_id=1, source_target_pairs={{0,16},{2,18},{4,20},{6,22},{8,24},{10,26},{12,28},{14,30},{16,32}... | collective-permute-start | bytes 1769480 | tf_op jit(solution)/shard_map/ppermute | solution.py:369
  84.8 10.9 %collective-permute-start.18 = (bf16[2,192,768]{2,1,0:T(8,128)(2,1)S(1)}, bf16[2,192,768]{2,1,0:T(8,128)(2,1)S(1)}, u32[]{:S(2)}, u32[]{:S(2)}) collective-permute-start(bf16[2,192,768]{2,1,0:T(8,128)(2,1)S(1)} %slice.99), channel_id=1, source_target_pairs={{0,192},{2,194},{4,196},{6,198},{8,200},{10,202},{12,204},{14,206}... | collective-permute-start | bytes 1769480 | tf_op jit(solution)/shard_map/ppermute | solution.py:369
  85.5 10.9 %collective-permute-start.17 = (bf16[2,192,768]{2,1,0:T(8,128)(2,1)S(1)}, bf16[2,192,768]{2,1,0:T(8,128)(2,1)S(1)}, u32[]{:S(2)}, u32[]{:S(2)}) collective-permute-start(bf16[2,192,768]{2,1,0:T(8,128)(2,1)S(1)} %slice.98), channel_id=1, source_target_pairs={{0,64},{2,66},{4,68},{6,70},{8,72},{10,74},{12,76},{14,78},{16,80}... | collective-permute-start | bytes 1769480 | tf_op jit(solution)/shard_map/ppermute | solution.py:369
  101.0 7.8 %collective-permute-start.21 = (bf16[3,196,512]{2,1,0:T(8,128)(2,1)S(1)}, bf16[3,196,512]{2,1,0:T(8,128)(2,1)S(1)}, u32[]{:S(2)}, u32[]{:S(2)}) collective-permute-start(bf16[3,196,512]{2,1,0:T(8,128)(2,1)S(1)} %get-tuple-element.71), channel_id=1, source_target_pairs={{0,1},{1,0},{2,3},{3,2},{4,5},{5,4},{6,7},{7,6},{8,9},{9,8},{10,11... | collective-permute-start | bytes 1806344 | tf_op jit(solution)/shard_map/ppermute | solution.py:30
  109.6 11.9 %collective-permute-start.23 = (bf16[196,512]{1,0:T(8,128)(2,1)S(1)}, bf16[196,512]{1,0:T(8,128)(2,1)S(1)}, u32[]{:S(2)}, u32[]{:S(2)}) collective-permute-start(bf16[196,512]{1,0:T(8,128)(2,1)S(1)} %furthest_part.1), channel_id=1, source_target_pairs={{0,2},{2,4},{4,6},{6,8},{8,10},{10,12},{12,14},{14,16},{16,18},{18... | collective-permute-start | bytes 602120 | tf_op jit(solution)/shard_map/ppermute | solution.py:26
  110.8 15.1 %collective-permute-start.22 = (bf16[196,512]{1,0:T(8,128)(2,1)S(1)}, bf16[196,512]{1,0:T(8,128)(2,1)S(1)}, u32[]{:S(2)}, u32[]{:S(2)}) collective-permute-start(bf16[196,512]{1,0:T(8,128)(2,1)S(1)} %get-tuple-element.73), channel_id=1, source_target_pairs={{0,2},{2,4},{4,6},{6,8},{8,10},{10,12},{12,14},{14,16},{16,18},{18... | collective-permute-start | bytes 602120 | tf_op jit(solution)/shard_map/ppermute | solution.py:26
  121.6 16.5 %collective-permute-start.24 = (bf16[196,512]{1,0:T(8,128)(2,1)S(1)}, bf16[196,512]{1,0:T(8,128)(2,1)S(1)}, u32[]{:S(2)}, u32[]{:S(2)}) collective-permute-start(bf16[196,512]{1,0:T(8,128)(2,1)S(1)} %add_convert_fusion), channel_id=1, source_target_pairs={{0,4},{2,6},{4,8},{6,10},{8,12},{10,14},{12,16},{14,18},{16,20},{1... | collective-permute-start | bytes 602120 | tf_op jit(solution)/shard_map/ppermute | solution.py:26
  (13 other events, 93.6 us)

commit v11 on v10

--- a/solution.py
+++ b/solution.py
@@ -37,7 +37,7 @@
 
 
 def window_place(image_slot, slot_images, place, slot, which):
-    stored = image_slot[slot_images[2 * slot + which]]
+    stored = image_slot[slot_images[SLOTS * which + slot]]
     return lax.rem(stored - place[0] + 128, 128)
 
 
@@ -423,7 +423,7 @@
     part_y = hidden_rows([next1, next3, last34[:48], last34[48:]])
     mine = jnp.stack([packed[:TOP], next1[:TOP], next2[:TOP], next3[:TOP]])
     theirs = other_core(mine)
-    scalars = [image_slot, slot_images.reshape(-1), place]
+    scalars = [image_slot, slot_images.T.reshape(-1), place]
     near_x, near_y = three_hops(part_x, "x"), three_hops(part_y, "y")
     rows, triple = triple_call(scalars, mine, theirs, gain_self, w_qkv[0])
     key_value = memory_call(scalars, mine, theirs, gain_memory, w_memory[0])
@@ -442,12 +442,13 @@
     fc_late = jnp.concatenate([*far_x, *far_y], axis=1)
     keep, send = late_call(place, early, mlp_in, fc_late, gain_head, w_head[0])
     got = other_core(send)
-    scalars = [image_slot, slot_images.reshape(-1), slot_count, place]
+    scalars = [image_slot, slot_images.T.reshape(-1), slot_count, place]
     (furthest,) = window_call((3,), scalars, keep, got)
     third = shifted(furthest, 1)
     base, piece1, piece2 = window_call((0, 1, 2), scalars, keep, got)
+    third, piece1 = tied(third, piece1)
+    further = shifted((piece2.astype(F32) + third.astype(F32)).astype(BF16), 2)
     nearest = shifted(piece1, 1)
-    further = shifted((piece2.astype(F32) + third.astype(F32)).astype(BF16), 2)
     return merge_call(base, nearest, further)
 
 

time: 139 us -> 142 us (1.022)
  the two profiles are of different devices: /device:TPU:1 before, /device:TPU:32 now
where the time goes in v11:
time: 142 us
  waiting for transfers between devices  52.6 us (37%)
  Pallas kernels  43.8 us (31%)
  starting transfers between devices  40.5 us (29%)
  local copies, waits for them, and re-layouts  3.25 us (2%)
    pallas_call x9, Pallas kernels, call(): pl.pallas_call(kernel, in_specs=[SMEM] * len(scalars) + [VMEM] * len(arra...  42.1 us
    ppermute x9, waiting for transfers between devices, shifted(): lax.ppermute(array, 'pairs', [(i, (i + by) % count) for i in range(count)])  33.7 us
    ppermute x9, starting transfers between devices, shifted(): lax.ppermute(array, 'pairs', [(i, (i + by) % count) for i in range(count)])  24.1 us
    ppermute x14, waiting for transfers between devices, along(): return lax.ppermute(array, 'pairs', [(p, target(p)) for p in range(count)])  17.6 us
    ppermute x14, starting transfers between devices, along(): return lax.ppermute(array, 'pairs', [(p, target(p)) for p in range(count)])  16.3 us
  transfers between devices with their start and end apart: 25, of which 14 were waited for; matrix products, arithmetic and copies ran while one was open for 2% of the time, Pallas kernels for 25%

profile of v11, /device:TPU:32, one launch (start us, length us, event | category | flops | bytes accessed | tf_op | source)
XLA Modules:
  0.0 142.0 jit_solution(3072827646757634863)
XLA Ops:
  1.7 3.3 %collective-permute-start.1 = (bf16[48,768]{1,0:T(8,128)(2,1)}, bf16[48,768]{1,0:T(8,128)(2,1)S(1)}, u32[]{:S(2)}, u32[]{:S(2)}) collective-permute-start(bf16[48,768]{1,0:T(8,128)(2,1)} %get-tuple-element.42), channel_id=1, source_target_pairs={{0,4},{2,6},{4,8},{6,10},{8,12},{10,14},{12,16},{14,18},{16,20},{1... | collective-permute-start | bytes 221192 | tf_op jit(solution)/shard_map/ppermute | solution.py:26
  5.0 3.1 %collective-permute-start = (bf16[48,768]{1,0:T(8,128)(2,1)}, bf16[48,768]{1,0:T(8,128)(2,1)S(1)}, u32[]{:S(2)}, u32[]{:S(2)}) collective-permute-start(bf16[48,768]{1,0:T(8,128)(2,1)} %get-tuple-element.42), channel_id=1, source_target_pairs={{0,2},{2,4},{4,6},{6,8},{8,10},{10,12},{12,14},{14,16},{16,18},{18... | collective-permute-start | bytes 221192 | tf_op jit(solution)/shard_map/ppermute | solution.py:26
  8.2 3.9 %collective-permute-start.2 = (bf16[152,768]{1,0:T(8,128)(2,1)}, bf16[152,768]{1,0:T(8,128)(2,1)S(1)}, u32[]{:S(2)}, u32[]{:S(2)}) collective-permute-start(bf16[152,768]{1,0:T(8,128)(2,1)} %get-tuple-element.45), channel_id=1, source_target_pairs={{0,252},{2,254},{4,0},{6,2},{8,4},{10,6},{12,8},{14,10},{16,12},{1... | collective-permute-start | bytes 700424 | tf_op jit(solution)/shard_map/ppermute | solution.py:26
  18.2 3.0 %collective-permute-done.2 = bf16[152,768]{1,0:T(8,128)(2,1)S(1)} collective-permute-done((bf16[152,768]{1,0:T(8,128)(2,1)}, bf16[152,768]{1,0:T(8,128)(2,1)S(1)}, u32[]{:S(2)}, u32[]{:S(2)}) %collective-permute-start.2) | collective-permute-done | bytes 233504 | tf_op jit(solution)/shard_map/ppermute | solution.py:26
  21.2 4.3 %collective-permute-start.6 = (bf16[152,768]{1,0:T(8,128)(2,1)S(1)}, bf16[152,768]{1,0:T(8,128)(2,1)S(1)}, u32[]{:S(2)}, u32[]{:S(2)}) collective-permute-start(bf16[152,768]{1,0:T(8,128)(2,1)S(1)} %collective-permute-done.2), channel_id=1, source_target_pairs={{0,254},{2,0},{4,2},{6,4},{8,6},{10,8},{12,10},{14,12},{16,14},{18... | collective-permute-start | bytes 700424 | tf_op jit(solution)/shard_map/ppermute | solution.py:26
  25.7 3.2 %collective-permute-start.4 = (bf16[2,96,768]{2,1,0:T(8,128)(2,1)S(1)}, bf16[2,96,768]{2,1,0:T(8,128)(2,1)S(1)}, u32[]{:S(2)}, u32[]{:S(2)}) collective-permute-start(bf16[2,96,768]{2,1,0:T(8,128)(2,1)S(1)} %get-tuple-element.80), channel_id=1, source_target_pairs={{0,48},{2,50},{4,52},{6,54},{8,56},{10,58},{12,60},{14,62},{16,0},... | collective-permute-start | bytes 884744 | tf_op jit(solution)/shard_map/ppermute | solution.py:369
  28.9 2.3 %collective-permute-done.7 = bf16[96,768]{1,0:T(8,128)(2,1)S(1)} collective-permute-done((bf16[96,768]{1,0:T(8,128)(2,1)S(1)}, bf16[96,768]{1,0:T(8,128)(2,1)S(1)}, u32[]{:S(2)}, u32[]{:S(2)}) %collective-permute-start.7) | collective-permute-done | bytes 147488 | tf_op jit(solution)/shard_map/ppermute | solution.py:26
  31.6 8.4 %collective-permute-done.3 = bf16[2,96,768]{2,1,0:T(8,128)(2,1)S(1)} collective-permute-done((bf16[2,96,768]{2,1,0:T(8,128)(2,1)S(1)}, bf16[2,96,768]{2,1,0:T(8,128)(2,1)S(1)}, u32[]{:S(2)}, u32[]{:S(2)}) %collective-permute-start.3) | collective-permute-done | bytes 294944 | tf_op jit(solution)/shard_map/ppermute | solution.py:369
  42.1 5.0 %triple_part.1 = (f32[624,768]{1,0:T(8,128)S(1)}, bf16[624,2304]{1,0:T(8,128)(2,1)S(1)}) custom-call(s32[128]{0:T(128)S(1)} %copy-done, s32[6]{0:T(128)S(1)} %reshape.4.slot_images, s32[2]{0:T(128)S(1)} %pad_add_fusion.place, bf16[4,104,768]{2,1,0:T(8,128)(2,1)S(1)} %pad_maximum_fusion.3.mine, bf16[4,104,768]{2,1,0:T(8,128)(2,1)S(1)} %collective-permute-done.12.theirs, ...), custom_call_target="tpu_custom_call" | custom-call | flops 4000000000 | bytes 8388608 | tf_op jit(solution)/shard_map/triple_part/pallas_call | solution.py:272
  47.1 3.7 %memory_part.1.key_value = bf16[624,1536]{1,0:T(8,128)(2,1)S(1)} custom-call(s32[128]{0:T(128)S(1)} %copy-done, s32[6]{0:T(128)S(1)} %reshape.4.slot_images, s32[2]{0:T(128)S(1)} %pad_add_fusion.place, bf16[4,104,768]{2,1,0:T(8,128)(2,1)S(1)} %pad_maximum_fusion.3.mine, bf16[4,104,768]{2,1,0:T(8,128)(2,1)S(1)} %collective-permute-done.12.theirs, ...), custom_call_target="tpu_custom_call" | custom-call | flops 3000000000 | bytes 8388608 | tf_op jit(solution)/shard_map/memory_part/pallas_call | solution.py:272
  52.1 2.7 %collective-permute-start.14 = (bf16[2,384,768]{2,1,0:T(8,128)(2,1)S(1)}, bf16[2,384,768]{2,1,0:T(8,128)(2,1)S(1)}, u32[]{:S(2)}, u32[]{:S(2)}) collective-permute-start(bf16[2,384,768]{2,1,0:T(8,128)(2,1)S(1)} %pad_maximum_fusion.1), channel_id=1, source_target_pairs={{0,192},{2,194},{4,196},{6,198},{8,200},{10,202},{12,204},{14,206}... | collective-permute-start | bytes 3538952 | tf_op jit(solution)/shard_map/ppermute | solution.py:369
  54.9 3.2 %collective-permute-start.16 = (bf16[2,384,768]{2,1,0:T(8,128)(2,1)S(1)}, bf16[2,384,768]{2,1,0:T(8,128)(2,1)S(1)}, u32[]{:S(2)}, u32[]{:S(2)}) collective-permute-start(bf16[2,384,768]{2,1,0:T(8,128)(2,1)S(1)} %pad_maximum_fusion.2), channel_id=1, source_target_pairs={{0,48},{2,50},{4,52},{6,54},{8,56},{10,58},{12,60},{14,62},{16,0},... | collective-permute-start | bytes 3538952 | tf_op jit(solution)/shard_map/ppermute | solution.py:369
  58.2 10.5 %self_part.1 = (f32[624,768]{1,0:T(8,128)S(1)}, bf16[624,768]{1,0:T(8,128)(2,1)S(1)}) custom-call(f32[624,768]{1,0:T(8,128)S(1)} %get-tuple-element.57.rows, bf16[624,2304]{1,0:T(8,128)(2,1)S(1)} %get-tuple-element.58.triple, f32[1,768]{1,0:T(1,128)S(1)} %copy-done.9, bf16[768,768]{1,0:T(8,128)(2,1)S(1)} %bitcast.28, bf16[768,768]{1,0:T(8,128)(2,1)S(1)} %bitcast.29), custom_call_target="tpu_custom_call" | custom-call | flops 12000000000 | bytes 8388608 | tf_op jit(solution)/shard_map/self_part/pallas_call | solution.py:272
  68.8 9.2 %cross_part.1 = (f32[624,768]{1,0:T(8,128)S(1)}, bf16[624,768]{1,0:T(8,128)(2,1)S(1)}) custom-call(f32[624,768]{1,0:T(8,128)S(1)} %get-tuple-element.59.first, bf16[624,768]{1,0:T(8,128)(2,1)S(1)} %get-tuple-element.60.query, bf16[624,1536]{1,0:T(8,128)(2,1)S(1)} %memory_part.1.key_value, f32[1,768]{1,0:T(1,128)S(1)} %copy-done.10, bf16[768,768]{1,0:T(8,128)(2,1)S(1)} %bitcast.30), custom_call_target="tpu_custom_call" | custom-call | flops 12000000000 | bytes 8388608 | tf_op jit(solution)/shard_map/cross_part/pallas_call | solution.py:272
  78.4 2.4 %collective-permute-done.16 = bf16[2,384,768]{2,1,0:T(8,128)(2,1)S(1)} collective-permute-done((bf16[2,384,768]{2,1,0:T(8,128)(2,1)S(1)}, bf16[2,384,768]{2,1,0:T(8,128)(2,1)S(1)}, u32[]{:S(2)}, u32[]{:S(2)}) %collective-permute-start.16) | collective-permute-done | bytes 1179680 | tf_op jit(solution)/shard_map/ppermute | solution.py:369
  85.6 6.5 %early_part.1.early = f32[624,768]{1,0:T(8,128)S(1)} custom-call(f32[624,768]{1,0:T(8,128)S(1)} %get-tuple-element.66.second, bf16[624,768]{1,0:T(8,128)(2,1)S(1)} %get-tuple-element.67.mlp_in, bf16[2,2304,768]{2,1,0:T(8,128)(2,1)S(1)} %constant_dynamic-update-slice_fusion.fc), custom_call_target="tpu_custom_call" | custom-call | flops 10000000000 | bytes 8388608 | tf_op jit(solution)/shard_map/early_part/pallas_call | solution.py:272
  92.2 2.6 %collective-permute-done.20 = bf16[2,192,768]{2,1,0:T(8,128)(2,1)S(1)} collective-permute-done((bf16[2,192,768]{2,1,0:T(8,128)(2,1)S(1)}, bf16[2,192,768]{2,1,0:T(8,128)(2,1)S(1)}, u32[]{:S(2)}, u32[]{:S(2)}) %collective-permute-start.20) | collective-permute-done | bytes 589856 | tf_op jit(solution)/shard_map/ppermute | solution.py:369
  94.7 2.0 %collective-permute-done.19 = bf16[2,192,768]{2,1,0:T(8,128)(2,1)S(1)} collective-permute-done((bf16[2,192,768]{2,1,0:T(8,128)(2,1)S(1)}, bf16[2,192,768]{2,1,0:T(8,128)(2,1)S(1)}, u32[]{:S(2)}, u32[]{:S(2)}) %collective-permute-start.19) | collective-permute-done | bytes 589856 | tf_op jit(solution)/shard_map/ppermute | solution.py:369
  98.5 4.4 %late_part.1 = (f32[3,196,512]{2,1,0:T(8,128)S(1)}, bf16[3,196,512]{2,1,0:T(8,128)(2,1)S(1)}) custom-call(s32[2]{0:T(128)S(1)} %pad_add_fusion.place, f32[624,768]{1,0:T(8,128)S(1)} %early_part.1.early, bf16[624,768]{1,0:T(8,128)(2,1)S(1)} %get-tuple-element.67.mlp_in, bf16[2,768,768]{2,1,0:T(8,128)(2,1)S(1)} %pad_maximum_fusion.fc, ...), custom_call_target="tpu_custom_call" | custom-call | flops 5000000000 | bytes 8388608 | tf_op jit(solution)/shard_map/late_part/pallas_call | solution.py:272
  105.8 2.7 %collective-permute-start.22 = (bf16[196,512]{1,0:T(8,128)(2,1)S(1)}, bf16[196,512]{1,0:T(8,128)(2,1)S(1)}, u32[]{:S(2)}, u32[]{:S(2)}) collective-permute-start(bf16[196,512]{1,0:T(8,128)(2,1)S(1)} %furthest_part.1), channel_id=1, source_target_pairs={{0,2},{2,4},{4,6},{6,8},{8,10},{10,12},{12,14},{14,16},{16,18},{18... | collective-permute-start | bytes 602120 | tf_op jit(solution)/shard_map/ppermute | solution.py:26
  109.7 4.3 %collective-permute-done.22 = bf16[196,512]{1,0:T(8,128)(2,1)S(1)} collective-permute-done((bf16[196,512]{1,0:T(8,128)(2,1)S(1)}, bf16[196,512]{1,0:T(8,128)(2,1)S(1)}, u32[]{:S(2)}, u32[]{:S(2)}) %collective-permute-start.22) | collective-permute-done | bytes 200736 | tf_op jit(solution)/shard_map/ppermute | solution.py:26
  115.7 3.3 %collective-permute-start.24 = (bf16[196,512]{1,0:T(8,128)(2,1)S(1)}, bf16[196,512]{1,0:T(8,128)(2,1)S(1)}, u32[]{:S(2)}, u32[]{:S(2)}) collective-permute-start(bf16[196,512]{1,0:T(8,128)(2,1)S(1)} %add_convert_fusion), channel_id=1, source_target_pairs={{0,4},{2,6},{4,8},{6,10},{8,12},{10,14},{12,16},{14,18},{16,20},{1... | collective-permute-start | bytes 602120 | tf_op jit(solution)/shard_map/ppermute | solution.py:26
  119.0 8.3 %collective-permute-done.23.nearest = bf16[196,512]{1,0:T(8,128)(2,1)S(1)} collective-permute-done((bf16[196,512]{1,0:T(8,128)(2,1)S(1)}, bf16[196,512]{1,0:T(8,128)(2,1)S(1)}, u32[]{:S(2)}, u32[]{:S(2)}) %collective-permute-start.23) | collective-permute-done | bytes 200736 | tf_op jit(solution)/shard_map/ppermute | solution.py:26
  127.3 14.0 %collective-permute-done.24.further = bf16[196,512]{1,0:T(8,128)(2,1)S(1)} collective-permute-done((bf16[196,512]{1,0:T(8,128)(2,1)S(1)}, bf16[196,512]{1,0:T(8,128)(2,1)S(1)}, u32[]{:S(2)}, u32[]{:S(2)}) %collective-permute-start.24) | collective-permute-done | bytes 200736 | tf_op jit(solution)/shard_map/ppermute | solution.py:26
  (97 shorter events, 24.4 us)
Async XLA Ops:
  1.7 14.7 %collective-permute-start.1 = (bf16[48,768]{1,0:T(8,128)(2,1)}, bf16[48,768]{1,0:T(8,128)(2,1)S(1)}, u32[]{:S(2)}, u32[]{:S(2)}) collective-permute-start(bf16[48,768]{1,0:T(8,128)(2,1)} %get-tuple-element.42), channel_id=1, source_target_pairs={{0,4},{2,6},{4,8},{6,10},{8,12},{10,14},{12,16},{14,18},{16,20},{1... | collective-permute-start | bytes 221192 | tf_op jit(solution)/shard_map/ppermute | solution.py:26
  5.0 9.6 %collective-permute-start = (bf16[48,768]{1,0:T(8,128)(2,1)}, bf16[48,768]{1,0:T(8,128)(2,1)S(1)}, u32[]{:S(2)}, u32[]{:S(2)}) collective-permute-start(bf16[48,768]{1,0:T(8,128)(2,1)} %get-tuple-element.42), channel_id=1, source_target_pairs={{0,2},{2,4},{4,6},{6,8},{8,10},{10,12},{12,14},{14,16},{16,18},{18... | collective-permute-start | bytes 221192 | tf_op jit(solution)/shard_map/ppermute | solution.py:26
  8.2 13.0 %collective-permute-start.2 = (bf16[152,768]{1,0:T(8,128)(2,1)}, bf16[152,768]{1,0:T(8,128)(2,1)S(1)}, u32[]{:S(2)}, u32[]{:S(2)}) collective-permute-start(bf16[152,768]{1,0:T(8,128)(2,1)} %get-tuple-element.45), channel_id=1, source_target_pairs={{0,252},{2,254},{4,0},{6,2},{8,4},{10,6},{12,8},{14,10},{16,12},{1... | collective-permute-start | bytes 700424 | tf_op jit(solution)/shard_map/ppermute | solution.py:26
  16.4 14.8 %collective-permute-start.7 = (bf16[96,768]{1,0:T(8,128)(2,1)S(1)}, bf16[96,768]{1,0:T(8,128)(2,1)S(1)}, u32[]{:S(2)}, u32[]{:S(2)}) collective-permute-start(bf16[96,768]{1,0:T(8,128)(2,1)S(1)} %pad_maximum_fusion.6), channel_id=1, source_target_pairs={{0,4},{2,6},{4,8},{6,10},{8,12},{10,14},{12,16},{14,18},{16,20},{1... | collective-permute-start | bytes 442376 | tf_op jit(solution)/shard_map/ppermute | solution.py:26
  16.5 14.7 %collective-permute-start.8 = (bf16[152,768]{1,0:T(8,128)(2,1)}, bf16[152,768]{1,0:T(8,128)(2,1)S(1)}, u32[]{:S(2)}, u32[]{:S(2)}) collective-permute-start(bf16[152,768]{1,0:T(8,128)(2,1)} %get-tuple-element.45), channel_id=1, source_target_pairs={{0,254},{2,0},{4,2},{6,4},{8,6},{10,8},{12,10},{14,12},{16,14},{18... | collective-permute-start | bytes 700424 | tf_op jit(solution)/shard_map/ppermute | solution.py:26
  21.2 10.0 %collective-permute-start.6 = (bf16[152,768]{1,0:T(8,128)(2,1)S(1)}, bf16[152,768]{1,0:T(8,128)(2,1)S(1)}, u32[]{:S(2)}, u32[]{:S(2)}) collective-permute-start(bf16[152,768]{1,0:T(8,128)(2,1)S(1)} %collective-permute-done.2), channel_id=1, source_target_pairs={{0,254},{2,0},{4,2},{6,4},{8,6},{10,8},{12,10},{14,12},{16,14},{18... | collective-permute-start | bytes 700424 | tf_op jit(solution)/shard_map/ppermute | solution.py:26
  25.6 14.5 %collective-permute-start.3 = (bf16[2,96,768]{2,1,0:T(8,128)(2,1)S(1)}, bf16[2,96,768]{2,1,0:T(8,128)(2,1)S(1)}, u32[]{:S(2)}, u32[]{:S(2)}) collective-permute-start(bf16[2,96,768]{2,1,0:T(8,128)(2,1)S(1)} %get-tuple-element.80), channel_id=1, source_target_pairs={{0,16},{2,18},{4,20},{6,22},{8,24},{10,26},{12,28},{14,30},{16,32}... | collective-permute-start | bytes 884744 | tf_op jit(solution)/shard_map/ppermute | solution.py:369
  25.7 25.1 %collective-permute-start.4 = (bf16[2,96,768]{2,1,0:T(8,128)(2,1)S(1)}, bf16[2,96,768]{2,1,0:T(8,128)(2,1)S(1)}, u32[]{:S(2)}, u32[]{:S(2)}) collective-permute-start(bf16[2,96,768]{2,1,0:T(8,128)(2,1)S(1)} %get-tuple-element.80), channel_id=1, source_target_pairs={{0,48},{2,50},{4,52},{6,54},{8,56},{10,58},{12,60},{14,62},{16,0},... | collective-permute-start | bytes 884744 | tf_op jit(solution)/shard_map/ppermute | solution.py:369
  31.2 19.7 %collective-permute-start.5 = (bf16[2,96,768]{2,1,0:T(8,128)(2,1)S(1)}, bf16[2,96,768]{2,1,0:T(8,128)(2,1)S(1)}, u32[]{:S(2)}, u32[]{:S(2)}) collective-permute-start(bf16[2,96,768]{2,1,0:T(8,128)(2,1)S(1)} %get-tuple-element.80), channel_id=1, source_target_pairs={{0,32},{2,34},{4,36},{6,38},{8,40},{10,42},{12,44},{14,46},{16,48}... | collective-permute-start | bytes 884744 | tf_op jit(solution)/shard_map/ppermute | solution.py:369
  31.3 10.7 %collective-permute-start.12 = (bf16[4,104,768]{2,1,0:T(8,128)(2,1)S(1)}, bf16[4,104,768]{2,1,0:T(8,128)(2,1)S(1)}, u32[]{:S(2)}, u32[]{:S(2)}) collective-permute-start(bf16[4,104,768]{2,1,0:T(8,128)(2,1)S(1)} %pad_maximum_fusion.3.mine), channel_id=1, source_target_pairs={{0,1},{1,0},{2,3},{3,2},{4,5},{5,4},{6,7},{7,6},{8,9},{9,8},{10,11... | collective-permute-start | bytes 1916936 | tf_op jit(solution)/shard_map/ppermute | solution.py:30
  31.5 19.3 %collective-permute-start.9 = (bf16[2,96,768]{2,1,0:T(8,128)(2,1)S(1)}, bf16[2,96,768]{2,1,0:T(8,128)(2,1)S(1)}, u32[]{:S(2)}, u32[]{:S(2)}) collective-permute-start(bf16[2,96,768]{2,1,0:T(8,128)(2,1)S(1)} %pad_maximum_fusion.5), channel_id=1, source_target_pairs={{0,64},{2,66},{4,68},{6,70},{8,72},{10,74},{12,76},{14,78},{16,80}... | collective-permute-start | bytes 884744 | tf_op jit(solution)/shard_map/ppermute | solution.py:369
  40.1 10.8 %collective-permute-start.10 = (bf16[2,96,768]{2,1,0:T(8,128)(2,1)S(1)}, bf16[2,96,768]{2,1,0:T(8,128)(2,1)S(1)}, u32[]{:S(2)}, u32[]{:S(2)}) collective-permute-start(bf16[2,96,768]{2,1,0:T(8,128)(2,1)S(1)} %pad_maximum_fusion.5), channel_id=1, source_target_pairs={{0,192},{2,194},{4,196},{6,198},{8,200},{10,202},{12,204},{14,206}... | collective-permute-start | bytes 884744 | tf_op jit(solution)/shard_map/ppermute | solution.py:369
  42.0 9.1 %collective-permute-start.11 = (bf16[2,96,768]{2,1,0:T(8,128)(2,1)S(1)}, bf16[2,96,768]{2,1,0:T(8,128)(2,1)S(1)}, u32[]{:S(2)}, u32[]{:S(2)}) collective-permute-start(bf16[2,96,768]{2,1,0:T(8,128)(2,1)S(1)} %pad_maximum_fusion.5), channel_id=1, source_target_pairs={{0,128},{2,130},{4,132},{6,134},{8,136},{10,138},{12,140},{14,142}... | collective-permute-start | bytes 884744 | tf_op jit(solution)/shard_map/ppermute | solution.py:369
  51.2 29.6 %collective-permute-start.13 = (bf16[2,384,768]{2,1,0:T(8,128)(2,1)S(1)}, bf16[2,384,768]{2,1,0:T(8,128)(2,1)S(1)}, u32[]{:S(2)}, u32[]{:S(2)}) collective-permute-start(bf16[2,384,768]{2,1,0:T(8,128)(2,1)S(1)} %pad_maximum_fusion.1), channel_id=1, source_target_pairs={{0,64},{2,66},{4,68},{6,70},{8,72},{10,74},{12,76},{14,78},{16,80}... | collective-permute-start | bytes 3538952 | tf_op jit(solution)/shard_map/ppermute | solution.py:369
  52.1 28.7 %collective-permute-start.14 = (bf16[2,384,768]{2,1,0:T(8,128)(2,1)S(1)}, bf16[2,384,768]{2,1,0:T(8,128)(2,1)S(1)}, u32[]{:S(2)}, u32[]{:S(2)}) collective-permute-start(bf16[2,384,768]{2,1,0:T(8,128)(2,1)S(1)} %pad_maximum_fusion.1), channel_id=1, source_target_pairs={{0,192},{2,194},{4,196},{6,198},{8,200},{10,202},{12,204},{14,206}... | collective-permute-start | bytes 3538952 | tf_op jit(solution)/shard_map/ppermute | solution.py:369
  54.8 23.6 %collective-permute-start.15 = (bf16[2,384,768]{2,1,0:T(8,128)(2,1)S(1)}, bf16[2,384,768]{2,1,0:T(8,128)(2,1)S(1)}, u32[]{:S(2)}, u32[]{:S(2)}) collective-permute-start(bf16[2,384,768]{2,1,0:T(8,128)(2,1)S(1)} %pad_maximum_fusion.2), channel_id=1, source_target_pairs={{0,16},{2,18},{4,20},{6,22},{8,24},{10,26},{12,28},{14,30},{16,32}... | collective-permute-start | bytes 3538952 | tf_op jit(solution)/shard_map/ppermute | solution.py:369
  54.9 25.9 %collective-permute-start.16 = (bf16[2,384,768]{2,1,0:T(8,128)(2,1)S(1)}, bf16[2,384,768]{2,1,0:T(8,128)(2,1)S(1)}, u32[]{:S(2)}, u32[]{:S(2)}) collective-permute-start(bf16[2,384,768]{2,1,0:T(8,128)(2,1)S(1)} %pad_maximum_fusion.2), channel_id=1, source_target_pairs={{0,48},{2,50},{4,52},{6,54},{8,56},{10,58},{12,60},{14,62},{16,0},... | collective-permute-start | bytes 3538952 | tf_op jit(solution)/shard_map/ppermute | solution.py:369
  81.5 13.3 %collective-permute-start.20 = (bf16[2,192,768]{2,1,0:T(8,128)(2,1)S(1)}, bf16[2,192,768]{2,1,0:T(8,128)(2,1)S(1)}, u32[]{:S(2)}, u32[]{:S(2)}) collective-permute-start(bf16[2,192,768]{2,1,0:T(8,128)(2,1)S(1)} %slice.101), channel_id=1, source_target_pairs={{0,48},{2,50},{4,52},{6,54},{8,56},{10,58},{12,60},{14,62},{16,0},... | collective-permute-start | bytes 1769480 | tf_op jit(solution)/shard_map/ppermute | solution.py:369
  82.4 14.3 %collective-permute-start.19 = (bf16[2,192,768]{2,1,0:T(8,128)(2,1)S(1)}, bf16[2,192,768]{2,1,0:T(8,128)(2,1)S(1)}, u32[]{:S(2)}, u32[]{:S(2)}) collective-permute-start(bf16[2,192,768]{2,1,0:T(8,128)(2,1)S(1)} %slice.100), channel_id=1, source_target_pairs={{0,16},{2,18},{4,20},{6,22},{8,24},{10,26},{12,28},{14,30},{16,32}... | collective-permute-start | bytes 1769480 | tf_op jit(solution)/shard_map/ppermute | solution.py:369
  83.6 13.2 %collective-permute-start.18 = (bf16[2,192,768]{2,1,0:T(8,128)(2,1)S(1)}, bf16[2,192,768]{2,1,0:T(8,128)(2,1)S(1)}, u32[]{:S(2)}, u32[]{:S(2)}) collective-permute-start(bf16[2,192,768]{2,1,0:T(8,128)(2,1)S(1)} %slice.99), channel_id=1, source_target_pairs={{0,192},{2,194},{4,196},{6,198},{8,200},{10,202},{12,204},{14,206}... | collective-permute-start | bytes 1769480 | tf_op jit(solution)/shard_map/ppermute | solution.py:369
  85.0 13.3 %collective-permute-start.17 = (bf16[2,192,768]{2,1,0:T(8,128)(2,1)S(1)}, bf16[2,192,768]{2,1,0:T(8,128)(2,1)S(1)}, u32[]{:S(2)}, u32[]{:S(2)}) collective-permute-start(bf16[2,192,768]{2,1,0:T(8,128)(2,1)S(1)} %slice.98), channel_id=1, source_target_pairs={{0,64},{2,66},{4,68},{6,70},{8,72},{10,74},{12,76},{14,78},{16,80}... | collective-permute-start | bytes 1769480 | tf_op jit(solution)/shard_map/ppermute | solution.py:369
  105.8 8.2 %collective-permute-start.22 = (bf16[196,512]{1,0:T(8,128)(2,1)S(1)}, bf16[196,512]{1,0:T(8,128)(2,1)S(1)}, u32[]{:S(2)}, u32[]{:S(2)}) collective-permute-start(bf16[196,512]{1,0:T(8,128)(2,1)S(1)} %furthest_part.1), channel_id=1, source_target_pairs={{0,2},{2,4},{4,6},{6,8},{8,10},{10,12},{12,14},{14,16},{16,18},{18... | collective-permute-start | bytes 602120 | tf_op jit(solution)/shard_map/ppermute | solution.py:26
  114.0 13.3 %collective-permute-start.23 = (bf16[196,512]{1,0:T(8,128)(2,1)S(1)}, bf16[196,512]{1,0:T(8,128)(2,1)S(1)}, u32[]{:S(2)}, u32[]{:S(2)}) collective-permute-start(bf16[196,512]{1,0:T(8,128)(2,1)S(1)} %get-tuple-element.76), channel_id=1, source_target_pairs={{0,2},{2,4},{4,6},{6,8},{8,10},{10,12},{12,14},{14,16},{16,18},{18... | collective-permute-start | bytes 602120 | tf_op jit(solution)/shard_map/ppermute | solution.py:26
  115.7 25.6 %collective-permute-start.24 = (bf16[196,512]{1,0:T(8,128)(2,1)S(1)}, bf16[196,512]{1,0:T(8,128)(2,1)S(1)}, u32[]{:S(2)}, u32[]{:S(2)}) collective-permute-start(bf16[196,512]{1,0:T(8,128)(2,1)S(1)} %add_convert_fusion), channel_id=1, source_target_pairs={{0,4},{2,6},{4,8},{6,10},{8,12},{10,14},{12,16},{14,18},{16,20},{1... | collective-permute-start | bytes 602120 | tf_op jit(solution)/shard_map/ppermute | solution.py:26
  (13 other events, 116.4 us)

commit v12 on v11

--- a/solution.py
+++ b/solution.py
@@ -446,9 +446,8 @@
     (furthest,) = window_call((3,), scalars, keep, got)
     third = shifted(furthest, 1)
     base, piece1, piece2 = window_call((0, 1, 2), scalars, keep, got)
-    third, piece1 = tied(third, piece1)
+    nearest = shifted(piece1, 1)
     further = shifted((piece2.astype(F32) + third.astype(F32)).astype(BF16), 2)
-    nearest = shifted(piece1, 1)
     return merge_call(base, nearest, further)
 
 

time: 142 us -> 139 us (0.979)
  the two profiles are of different devices: /device:TPU:32 before, /device:TPU:1 now
where the time goes in v12:
time: 139 us
  starting transfers between devices  53.4 us (38%)
  Pallas kernels  43.8 us (32%)
  waiting for transfers between devices  36.5 us (26%)
  local copies, waits for them, and re-layouts  3.24 us (2%)
    pallas_call x9, Pallas kernels, call(): pl.pallas_call(kernel, in_specs=[SMEM] * len(scalars) + [VMEM] * len(arra...  42.2 us
    ppermute x9, waiting for transfers between devices, shifted(): lax.ppermute(array, 'pairs', [(i, (i + by) % count) for i in range(count)])  28.3 us
    ppermute x9, starting transfers between devices, shifted(): lax.ppermute(array, 'pairs', [(i, (i + by) % count) for i in range(count)])  24.5 us
    ppermute x14, starting transfers between devices, along(): return lax.ppermute(array, 'pairs', [(p, target(p)) for p in range(count)])  19.7 us
    ppermute x2, starting transfers between devices, other_core(): return lax.ppermute(array, 'side', [(0, 1), (1, 0)])  9.16 us
    ppermute x14, waiting for transfers between devices, along(): return lax.ppermute(array, 'pairs', [(p, target(p)) for p in range(count)])  7.25 us
  transfers between devices with their start and end apart: 25, of which 12 were waited for; matrix products, arithmetic and copies ran while one was open for 2% of the time, Pallas kernels for 26%

profile of v12, /device:TPU:1, one launch (start us, length us, event | category | flops | bytes accessed | tf_op | source)
XLA Modules:
  0.0 138.9 jit_solution(15622419824749593119)
XLA Ops:
  1.7 3.9 %collective-permute-start.1 = (bf16[48,768]{1,0:T(8,128)(2,1)}, bf16[48,768]{1,0:T(8,128)(2,1)S(1)}, u32[]{:S(2)}, u32[]{:S(2)}) collective-permute-start(bf16[48,768]{1,0:T(8,128)(2,1)} %get-tuple-element.40), channel_id=1, source_target_pairs={{0,4},{2,6},{4,8},{6,10},{8,12},{10,14},{12,16},{14,18},{16,20},{1... | collective-permute-start | bytes 221192 | tf_op jit(solution)/shard_map/ppermute | solution.py:26
  7.2 6.9 %collective-permute-start.2 = (bf16[152,768]{1,0:T(8,128)(2,1)}, bf16[152,768]{1,0:T(8,128)(2,1)S(1)}, u32[]{:S(2)}, u32[]{:S(2)}) collective-permute-start(bf16[152,768]{1,0:T(8,128)(2,1)} %get-tuple-element.43), channel_id=1, source_target_pairs={{0,252},{2,254},{4,0},{6,2},{8,4},{10,6},{12,8},{14,10},{16,12},{1... | collective-permute-start | bytes 700424 | tf_op jit(solution)/shard_map/ppermute | solution.py:26
  16.6 1.8 %collective-permute-done = bf16[48,768]{1,0:T(8,128)(2,1)S(1)} collective-permute-done((bf16[48,768]{1,0:T(8,128)(2,1)}, bf16[48,768]{1,0:T(8,128)(2,1)S(1)}, u32[]{:S(2)}, u32[]{:S(2)}) %collective-permute-start) | collective-permute-done | bytes 73760 | tf_op jit(solution)/shard_map/ppermute | solution.py:26
  18.6 5.8 %collective-permute-start.8 = (bf16[152,768]{1,0:T(8,128)(2,1)}, bf16[152,768]{1,0:T(8,128)(2,1)S(1)}, u32[]{:S(2)}, u32[]{:S(2)}) collective-permute-start(bf16[152,768]{1,0:T(8,128)(2,1)} %get-tuple-element.43), channel_id=1, source_target_pairs={{0,254},{2,0},{4,2},{6,4},{8,6},{10,8},{12,10},{14,12},{16,14},{18... | collective-permute-start | bytes 700424 | tf_op jit(solution)/shard_map/ppermute | solution.py:26
  24.5 4.6 %collective-permute-start.6 = (bf16[152,768]{1,0:T(8,128)(2,1)S(1)}, bf16[152,768]{1,0:T(8,128)(2,1)S(1)}, u32[]{:S(2)}, u32[]{:S(2)}) collective-permute-start(bf16[152,768]{1,0:T(8,128)(2,1)S(1)} %collective-permute-done.2), channel_id=1, source_target_pairs={{0,254},{2,0},{4,2},{6,4},{8,6},{10,8},{12,10},{14,12},{16,14},{18... | collective-permute-start | bytes 700424 | tf_op jit(solution)/shard_map/ppermute | solution.py:26
  29.2 2.7 %collective-permute-start.4 = (bf16[2,96,768]{2,1,0:T(8,128)(2,1)S(1)}, bf16[2,96,768]{2,1,0:T(8,128)(2,1)S(1)}, u32[]{:S(2)}, u32[]{:S(2)}) collective-permute-start(bf16[2,96,768]{2,1,0:T(8,128)(2,1)S(1)} %get-tuple-element.76), channel_id=1, source_target_pairs={{0,48},{2,50},{4,52},{6,54},{8,56},{10,58},{12,60},{14,62},{16,0},... | collective-permute-start | bytes 884744 | tf_op jit(solution)/shard_map/ppermute | solution.py:369
  32.9 3.0 %collective-permute-start.12 = (bf16[4,104,768]{2,1,0:T(8,128)(2,1)S(1)}, bf16[4,104,768]{2,1,0:T(8,128)(2,1)S(1)}, u32[]{:S(2)}, u32[]{:S(2)}) collective-permute-start(bf16[4,104,768]{2,1,0:T(8,128)(2,1)S(1)} %pad_maximum_fusion.3.mine), channel_id=1, source_target_pairs={{0,1},{1,0},{2,3},{3,2},{4,5},{5,4},{6,7},{7,6},{8,9},{9,8},{10,11... | collective-permute-start | bytes 1916936 | tf_op jit(solution)/shard_map/ppermute | solution.py:30
  36.1 2.7 %collective-permute-start.10 = (bf16[2,96,768]{2,1,0:T(8,128)(2,1)S(1)}, bf16[2,96,768]{2,1,0:T(8,128)(2,1)S(1)}, u32[]{:S(2)}, u32[]{:S(2)}) collective-permute-start(bf16[2,96,768]{2,1,0:T(8,128)(2,1)S(1)} %pad_maximum_fusion.5), channel_id=1, source_target_pairs={{0,192},{2,194},{4,196},{6,198},{8,200},{10,202},{12,204},{14,206}... | collective-permute-start | bytes 884744 | tf_op jit(solution)/shard_map/ppermute | solution.py:369
  38.8 5.0 %triple_part.1 = (f32[624,768]{1,0:T(8,128)S(1)}, bf16[624,2304]{1,0:T(8,128)(2,1)S(1)}) custom-call(s32[128]{0:T(128)S(1)} %copy-done, s32[6]{0:T(128)S(1)} %reshape.4.slot_images, s32[2]{0:T(128)S(1)} %pad_add_fusion.place, bf16[4,104,768]{2,1,0:T(8,128)(2,1)S(1)} %pad_maximum_fusion.3.mine, bf16[4,104,768]{2,1,0:T(8,128)(2,1)S(1)} %collective-permute-done.12.theirs, ...), custom_call_target="tpu_custom_call" | custom-call | flops 4000000000 | bytes 8388608 | tf_op jit(solution)/shard_map/triple_part/pallas_call | solution.py:272
  43.8 3.7 %memory_part.1.key_value = bf16[624,1536]{1,0:T(8,128)(2,1)S(1)} custom-call(s32[128]{0:T(128)S(1)} %copy-done, s32[6]{0:T(128)S(1)} %reshape.4.slot_images, s32[2]{0:T(128)S(1)} %pad_add_fusion.place, bf16[4,104,768]{2,1,0:T(8,128)(2,1)S(1)} %pad_maximum_fusion.3.mine, bf16[4,104,768]{2,1,0:T(8,128)(2,1)S(1)} %collective-permute-done.12.theirs, ...), custom_call_target="tpu_custom_call" | custom-call | flops 3000000000 | bytes 8388608 | tf_op jit(solution)/shard_map/memory_part/pallas_call | solution.py:272
  49.4 2.7 %collective-permute-start.14 = (bf16[2,384,768]{2,1,0:T(8,128)(2,1)S(1)}, bf16[2,384,768]{2,1,0:T(8,128)(2,1)S(1)}, u32[]{:S(2)}, u32[]{:S(2)}) collective-permute-start(bf16[2,384,768]{2,1,0:T(8,128)(2,1)S(1)} %pad_maximum_fusion.1), channel_id=1, source_target_pairs={{0,192},{2,194},{4,196},{6,198},{8,200},{10,202},{12,204},{14,206}... | collective-permute-start | bytes 3538952 | tf_op jit(solution)/shard_map/ppermute | solution.py:369
  52.2 3.6 %collective-permute-start.15 = (bf16[2,384,768]{2,1,0:T(8,128)(2,1)S(1)}, bf16[2,384,768]{2,1,0:T(8,128)(2,1)S(1)}, u32[]{:S(2)}, u32[]{:S(2)}) collective-permute-start(bf16[2,384,768]{2,1,0:T(8,128)(2,1)S(1)} %pad_maximum_fusion.2), channel_id=1, source_target_pairs={{0,16},{2,18},{4,20},{6,22},{8,24},{10,26},{12,28},{14,30},{16,32}... | collective-permute-start | bytes 3538952 | tf_op jit(solution)/shard_map/ppermute | solution.py:369
  55.9 10.5 %self_part.1 = (f32[624,768]{1,0:T(8,128)S(1)}, bf16[624,768]{1,0:T(8,128)(2,1)S(1)}) custom-call(f32[624,768]{1,0:T(8,128)S(1)} %get-tuple-element.55.rows, bf16[624,2304]{1,0:T(8,128)(2,1)S(1)} %get-tuple-element.56.triple, f32[1,768]{1,0:T(1,128)S(1)} %copy-done.9, bf16[768,768]{1,0:T(8,128)(2,1)S(1)} %bitcast.28, bf16[768,768]{1,0:T(8,128)(2,1)S(1)} %bitcast.29), custom_call_target="tpu_custom_call" | custom-call | flops 12000000000 | bytes 8388608 | tf_op jit(solution)/shard_map/self_part/pallas_call | solution.py:272
  66.5 9.2 %cross_part.1 = (f32[624,768]{1,0:T(8,128)S(1)}, bf16[624,768]{1,0:T(8,128)(2,1)S(1)}) custom-call(f32[624,768]{1,0:T(8,128)S(1)} %get-tuple-element.57.first, bf16[624,768]{1,0:T(8,128)(2,1)S(1)} %get-tuple-element.58.query, bf16[624,1536]{1,0:T(8,128)(2,1)S(1)} %memory_part.1.key_value, f32[1,768]{1,0:T(1,128)S(1)} %copy-done.10, bf16[768,768]{1,0:T(8,128)(2,1)S(1)} %bitcast.30), custom_call_target="tpu_custom_call" | custom-call | flops 12000000000 | bytes 8388608 | tf_op jit(solution)/shard_map/cross_part/pallas_call | solution.py:272
  75.7 2.2 %collective-permute-done.16 = bf16[2,384,768]{2,1,0:T(8,128)(2,1)S(1)} collective-permute-done((bf16[2,384,768]{2,1,0:T(8,128)(2,1)S(1)}, bf16[2,384,768]{2,1,0:T(8,128)(2,1)S(1)}, u32[]{:S(2)}, u32[]{:S(2)}) %collective-permute-start.16) | collective-permute-done | bytes 1179680 | tf_op jit(solution)/shard_map/ppermute | solution.py:369
  78.6 3.9 %collective-permute-start.20 = (bf16[2,192,768]{2,1,0:T(8,128)(2,1)S(1)}, bf16[2,192,768]{2,1,0:T(8,128)(2,1)S(1)}, u32[]{:S(2)}, u32[]{:S(2)}) collective-permute-start(bf16[2,192,768]{2,1,0:T(8,128)(2,1)S(1)} %slice.101), channel_id=1, source_target_pairs={{0,48},{2,50},{4,52},{6,54},{8,56},{10,58},{12,60},{14,62},{16,0},... | collective-permute-start | bytes 1769480 | tf_op jit(solution)/shard_map/ppermute | solution.py:369
  82.6 2.2 %collective-permute-start.19 = (bf16[2,192,768]{2,1,0:T(8,128)(2,1)S(1)}, bf16[2,192,768]{2,1,0:T(8,128)(2,1)S(1)}, u32[]{:S(2)}, u32[]{:S(2)}) collective-permute-start(bf16[2,192,768]{2,1,0:T(8,128)(2,1)S(1)} %slice.100), channel_id=1, source_target_pairs={{0,16},{2,18},{4,20},{6,22},{8,24},{10,26},{12,28},{14,30},{16,32}... | collective-permute-start | bytes 1769480 | tf_op jit(solution)/shard_map/ppermute | solution.py:369
  86.3 6.5 %early_part.1.early = f32[624,768]{1,0:T(8,128)S(1)} custom-call(f32[624,768]{1,0:T(8,128)S(1)} %get-tuple-element.64.second, bf16[624,768]{1,0:T(8,128)(2,1)S(1)} %get-tuple-element.65.mlp_in, bf16[2,2304,768]{2,1,0:T(8,128)(2,1)S(1)} %constant_dynamic-update-slice_fusion.fc), custom_call_target="tpu_custom_call" | custom-call | flops 10000000000 | bytes 8388608 | tf_op jit(solution)/shard_map/early_part/pallas_call | solution.py:272
  92.8 1.8 %collective-permute-done.20 = bf16[2,192,768]{2,1,0:T(8,128)(2,1)S(1)} collective-permute-done((bf16[2,192,768]{2,1,0:T(8,128)(2,1)S(1)}, bf16[2,192,768]{2,1,0:T(8,128)(2,1)S(1)}, u32[]{:S(2)}, u32[]{:S(2)}) %collective-permute-start.20) | collective-permute-done | bytes 589856 | tf_op jit(solution)/shard_map/ppermute | solution.py:369
  96.5 4.4 %late_part.1 = (f32[3,196,512]{2,1,0:T(8,128)S(1)}, bf16[3,196,512]{2,1,0:T(8,128)(2,1)S(1)}) custom-call(s32[2]{0:T(128)S(1)} %pad_add_fusion.place, f32[624,768]{1,0:T(8,128)S(1)} %early_part.1.early, bf16[624,768]{1,0:T(8,128)(2,1)S(1)} %get-tuple-element.65.mlp_in, bf16[2,768,768]{2,1,0:T(8,128)(2,1)S(1)} %pad_maximum_fusion.fc, ...), custom_call_target="tpu_custom_call" | custom-call | flops 5000000000 | bytes 8388608 | tf_op jit(solution)/shard_map/late_part/pallas_call | solution.py:272
  101.0 6.2 %collective-permute-start.21 = (bf16[3,196,512]{2,1,0:T(8,128)(2,1)S(1)}, bf16[3,196,512]{2,1,0:T(8,128)(2,1)S(1)}, u32[]{:S(2)}, u32[]{:S(2)}) collective-permute-start(bf16[3,196,512]{2,1,0:T(8,128)(2,1)S(1)} %get-tuple-element.71), channel_id=1, source_target_pairs={{0,1},{1,0},{2,3},{3,2},{4,5},{5,4},{6,7},{7,6},{8,9},{9,8},{10,11... | collective-permute-start | bytes 1806344 | tf_op jit(solution)/shard_map/ppermute | solution.py:30
  112.2 9.3 %collective-permute-done.23 = bf16[196,512]{1,0:T(8,128)(2,1)S(1)} collective-permute-done((bf16[196,512]{1,0:T(8,128)(2,1)S(1)}, bf16[196,512]{1,0:T(8,128)(2,1)S(1)}, u32[]{:S(2)}, u32[]{:S(2)}) %collective-permute-start.23) | collective-permute-done | bytes 200736 | tf_op jit(solution)/shard_map/ppermute | solution.py:26
  121.7 4.2 %collective-permute-done.22.nearest = bf16[196,512]{1,0:T(8,128)(2,1)S(1)} collective-permute-done((bf16[196,512]{1,0:T(8,128)(2,1)S(1)}, bf16[196,512]{1,0:T(8,128)(2,1)S(1)}, u32[]{:S(2)}, u32[]{:S(2)}) %collective-permute-start.22) | collective-permute-done | bytes 200736 | tf_op jit(solution)/shard_map/ppermute | solution.py:26
  125.9 12.2 %collective-permute-done.24.further = bf16[196,512]{1,0:T(8,128)(2,1)S(1)} collective-permute-done((bf16[196,512]{1,0:T(8,128)(2,1)S(1)}, bf16[196,512]{1,0:T(8,128)(2,1)S(1)}, u32[]{:S(2)}, u32[]{:S(2)}) %collective-permute-start.24) | collective-permute-done | bytes 200736 | tf_op jit(solution)/shard_map/ppermute | solution.py:26
  (97 shorter events, 18.5 us)
Async XLA Ops:
  1.7 16.8 %collective-permute-start.1 = (bf16[48,768]{1,0:T(8,128)(2,1)}, bf16[48,768]{1,0:T(8,128)(2,1)S(1)}, u32[]{:S(2)}, u32[]{:S(2)}) collective-permute-start(bf16[48,768]{1,0:T(8,128)(2,1)} %get-tuple-element.40), channel_id=1, source_target_pairs={{0,4},{2,6},{4,8},{6,10},{8,12},{10,14},{12,16},{14,18},{16,20},{1... | collective-permute-start | bytes 221192 | tf_op jit(solution)/shard_map/ppermute | solution.py:26
  5.6 12.9 %collective-permute-start = (bf16[48,768]{1,0:T(8,128)(2,1)}, bf16[48,768]{1,0:T(8,128)(2,1)S(1)}, u32[]{:S(2)}, u32[]{:S(2)}) collective-permute-start(bf16[48,768]{1,0:T(8,128)(2,1)} %get-tuple-element.40), channel_id=1, source_target_pairs={{0,2},{2,4},{4,6},{6,8},{8,10},{10,12},{12,14},{14,16},{16,18},{18... | collective-permute-start | bytes 221192 | tf_op jit(solution)/shard_map/ppermute | solution.py:26
  7.2 17.2 %collective-permute-start.2 = (bf16[152,768]{1,0:T(8,128)(2,1)}, bf16[152,768]{1,0:T(8,128)(2,1)S(1)}, u32[]{:S(2)}, u32[]{:S(2)}) collective-permute-start(bf16[152,768]{1,0:T(8,128)(2,1)} %get-tuple-element.43), channel_id=1, source_target_pairs={{0,252},{2,254},{4,0},{6,2},{8,4},{10,6},{12,8},{14,10},{16,12},{1... | collective-permute-start | bytes 700424 | tf_op jit(solution)/shard_map/ppermute | solution.py:26
  18.5 13.4 %collective-permute-start.7 = (bf16[96,768]{1,0:T(8,128)(2,1)S(1)}, bf16[96,768]{1,0:T(8,128)(2,1)S(1)}, u32[]{:S(2)}, u32[]{:S(2)}) collective-permute-start(bf16[96,768]{1,0:T(8,128)(2,1)S(1)} %pad_maximum_fusion.6), channel_id=1, source_target_pairs={{0,4},{2,6},{4,8},{6,10},{8,12},{10,14},{12,16},{14,18},{16,20},{1... | collective-permute-start | bytes 442376 | tf_op jit(solution)/shard_map/ppermute | solution.py:26
  18.6 13.4 %collective-permute-start.8 = (bf16[152,768]{1,0:T(8,128)(2,1)}, bf16[152,768]{1,0:T(8,128)(2,1)S(1)}, u32[]{:S(2)}, u32[]{:S(2)}) collective-permute-start(bf16[152,768]{1,0:T(8,128)(2,1)} %get-tuple-element.43), channel_id=1, source_target_pairs={{0,254},{2,0},{4,2},{6,4},{8,6},{10,8},{12,10},{14,12},{16,14},{18... | collective-permute-start | bytes 700424 | tf_op jit(solution)/shard_map/ppermute | solution.py:26
  24.5 8.2 %collective-permute-start.6 = (bf16[152,768]{1,0:T(8,128)(2,1)S(1)}, bf16[152,768]{1,0:T(8,128)(2,1)S(1)}, u32[]{:S(2)}, u32[]{:S(2)}) collective-permute-start(bf16[152,768]{1,0:T(8,128)(2,1)S(1)} %collective-permute-done.2), channel_id=1, source_target_pairs={{0,254},{2,0},{4,2},{6,4},{8,6},{10,8},{12,10},{14,12},{16,14},{18... | collective-permute-start | bytes 700424 | tf_op jit(solution)/shard_map/ppermute | solution.py:26
  29.1 6.9 %collective-permute-start.3 = (bf16[2,96,768]{2,1,0:T(8,128)(2,1)S(1)}, bf16[2,96,768]{2,1,0:T(8,128)(2,1)S(1)}, u32[]{:S(2)}, u32[]{:S(2)}) collective-permute-start(bf16[2,96,768]{2,1,0:T(8,128)(2,1)S(1)} %get-tuple-element.76), channel_id=1, source_target_pairs={{0,16},{2,18},{4,20},{6,22},{8,24},{10,26},{12,28},{14,30},{16,32}... | collective-permute-start | bytes 884744 | tf_op jit(solution)/shard_map/ppermute | solution.py:369
  29.2 18.3 %collective-permute-start.4 = (bf16[2,96,768]{2,1,0:T(8,128)(2,1)S(1)}, bf16[2,96,768]{2,1,0:T(8,128)(2,1)S(1)}, u32[]{:S(2)}, u32[]{:S(2)}) collective-permute-start(bf16[2,96,768]{2,1,0:T(8,128)(2,1)S(1)} %get-tuple-element.76), channel_id=1, source_target_pairs={{0,48},{2,50},{4,52},{6,54},{8,56},{10,58},{12,60},{14,62},{16,0},... | collective-permute-start | bytes 884744 | tf_op jit(solution)/shard_map/ppermute | solution.py:369
  31.9 15.6 %collective-permute-start.5 = (bf16[2,96,768]{2,1,0:T(8,128)(2,1)S(1)}, bf16[2,96,768]{2,1,0:T(8,128)(2,1)S(1)}, u32[]{:S(2)}, u32[]{:S(2)}) collective-permute-start(bf16[2,96,768]{2,1,0:T(8,128)(2,1)S(1)} %get-tuple-element.76), channel_id=1, source_target_pairs={{0,32},{2,34},{4,36},{6,38},{8,40},{10,42},{12,44},{14,46},{16,48}... | collective-permute-start | bytes 884744 | tf_op jit(solution)/shard_map/ppermute | solution.py:369
  36.0 13.1 %collective-permute-start.9 = (bf16[2,96,768]{2,1,0:T(8,128)(2,1)S(1)}, bf16[2,96,768]{2,1,0:T(8,128)(2,1)S(1)}, u32[]{:S(2)}, u32[]{:S(2)}) collective-permute-start(bf16[2,96,768]{2,1,0:T(8,128)(2,1)S(1)} %pad_maximum_fusion.5), channel_id=1, source_target_pairs={{0,64},{2,66},{4,68},{6,70},{8,72},{10,74},{12,76},{14,78},{16,80}... | collective-permute-start | bytes 884744 | tf_op jit(solution)/shard_map/ppermute | solution.py:369
  36.1 13.0 %collective-permute-start.10 = (bf16[2,96,768]{2,1,0:T(8,128)(2,1)S(1)}, bf16[2,96,768]{2,1,0:T(8,128)(2,1)S(1)}, u32[]{:S(2)}, u32[]{:S(2)}) collective-permute-start(bf16[2,96,768]{2,1,0:T(8,128)(2,1)S(1)} %pad_maximum_fusion.5), channel_id=1, source_target_pairs={{0,192},{2,194},{4,196},{6,198},{8,200},{10,202},{12,204},{14,206}... | collective-permute-start | bytes 884744 | tf_op jit(solution)/shard_map/ppermute | solution.py:369
  38.7 10.3 %collective-permute-start.11 = (bf16[2,96,768]{2,1,0:T(8,128)(2,1)S(1)}, bf16[2,96,768]{2,1,0:T(8,128)(2,1)S(1)}, u32[]{:S(2)}, u32[]{:S(2)}) collective-permute-start(bf16[2,96,768]{2,1,0:T(8,128)(2,1)S(1)} %pad_maximum_fusion.5), channel_id=1, source_target_pairs={{0,128},{2,130},{4,132},{6,134},{8,136},{10,138},{12,140},{14,142}... | collective-permute-start | bytes 884744 | tf_op jit(solution)/shard_map/ppermute | solution.py:369
  49.1 28.8 %collective-permute-start.13 = (bf16[2,384,768]{2,1,0:T(8,128)(2,1)S(1)}, bf16[2,384,768]{2,1,0:T(8,128)(2,1)S(1)}, u32[]{:S(2)}, u32[]{:S(2)}) collective-permute-start(bf16[2,384,768]{2,1,0:T(8,128)(2,1)S(1)} %pad_maximum_fusion.1), channel_id=1, source_target_pairs={{0,64},{2,66},{4,68},{6,70},{8,72},{10,74},{12,76},{14,78},{16,80}... | collective-permute-start | bytes 3538952 | tf_op jit(solution)/shard_map/ppermute | solution.py:369
  49.4 28.6 %collective-permute-start.14 = (bf16[2,384,768]{2,1,0:T(8,128)(2,1)S(1)}, bf16[2,384,768]{2,1,0:T(8,128)(2,1)S(1)}, u32[]{:S(2)}, u32[]{:S(2)}) collective-permute-start(bf16[2,384,768]{2,1,0:T(8,128)(2,1)S(1)} %pad_maximum_fusion.1), channel_id=1, source_target_pairs={{0,192},{2,194},{4,196},{6,198},{8,200},{10,202},{12,204},{14,206}... | collective-permute-start | bytes 3538952 | tf_op jit(solution)/shard_map/ppermute | solution.py:369
  52.2 23.6 %collective-permute-start.15 = (bf16[2,384,768]{2,1,0:T(8,128)(2,1)S(1)}, bf16[2,384,768]{2,1,0:T(8,128)(2,1)S(1)}, u32[]{:S(2)}, u32[]{:S(2)}) collective-permute-start(bf16[2,384,768]{2,1,0:T(8,128)(2,1)S(1)} %pad_maximum_fusion.2), channel_id=1, source_target_pairs={{0,16},{2,18},{4,20},{6,22},{8,24},{10,26},{12,28},{14,30},{16,32}... | collective-permute-start | bytes 3538952 | tf_op jit(solution)/shard_map/ppermute | solution.py:369
  55.8 22.2 %collective-permute-start.16 = (bf16[2,384,768]{2,1,0:T(8,128)(2,1)S(1)}, bf16[2,384,768]{2,1,0:T(8,128)(2,1)S(1)}, u32[]{:S(2)}, u32[]{:S(2)}) collective-permute-start(bf16[2,384,768]{2,1,0:T(8,128)(2,1)S(1)} %pad_maximum_fusion.2), channel_id=1, source_target_pairs={{0,48},{2,50},{4,52},{6,54},{8,56},{10,58},{12,60},{14,62},{16,0},... | collective-permute-start | bytes 3538952 | tf_op jit(solution)/shard_map/ppermute | solution.py:369
  78.6 16.0 %collective-permute-start.20 = (bf16[2,192,768]{2,1,0:T(8,128)(2,1)S(1)}, bf16[2,192,768]{2,1,0:T(8,128)(2,1)S(1)}, u32[]{:S(2)}, u32[]{:S(2)}) collective-permute-start(bf16[2,192,768]{2,1,0:T(8,128)(2,1)S(1)} %slice.101), channel_id=1, source_target_pairs={{0,48},{2,50},{4,52},{6,54},{8,56},{10,58},{12,60},{14,62},{16,0},... | collective-permute-start | bytes 1769480 | tf_op jit(solution)/shard_map/ppermute | solution.py:369
  82.6 12.5 %collective-permute-start.19 = (bf16[2,192,768]{2,1,0:T(8,128)(2,1)S(1)}, bf16[2,192,768]{2,1,0:T(8,128)(2,1)S(1)}, u32[]{:S(2)}, u32[]{:S(2)}) collective-permute-start(bf16[2,192,768]{2,1,0:T(8,128)(2,1)S(1)} %slice.100), channel_id=1, source_target_pairs={{0,16},{2,18},{4,20},{6,22},{8,24},{10,26},{12,28},{14,30},{16,32}... | collective-permute-start | bytes 1769480 | tf_op jit(solution)/shard_map/ppermute | solution.py:369
  84.8 10.9 %collective-permute-start.18 = (bf16[2,192,768]{2,1,0:T(8,128)(2,1)S(1)}, bf16[2,192,768]{2,1,0:T(8,128)(2,1)S(1)}, u32[]{:S(2)}, u32[]{:S(2)}) collective-permute-start(bf16[2,192,768]{2,1,0:T(8,128)(2,1)S(1)} %slice.99), channel_id=1, source_target_pairs={{0,192},{2,194},{4,196},{6,198},{8,200},{10,202},{12,204},{14,206}... | collective-permute-start | bytes 1769480 | tf_op jit(solution)/shard_map/ppermute | solution.py:369
  85.5 10.9 %collective-permute-start.17 = (bf16[2,192,768]{2,1,0:T(8,128)(2,1)S(1)}, bf16[2,192,768]{2,1,0:T(8,128)(2,1)S(1)}, u32[]{:S(2)}, u32[]{:S(2)}) collective-permute-start(bf16[2,192,768]{2,1,0:T(8,128)(2,1)S(1)} %slice.98), channel_id=1, source_target_pairs={{0,64},{2,66},{4,68},{6,70},{8,72},{10,74},{12,76},{14,78},{16,80}... | collective-permute-start | bytes 1769480 | tf_op jit(solution)/shard_map/ppermute | solution.py:369
  101.0 7.8 %collective-permute-start.21 = (bf16[3,196,512]{2,1,0:T(8,128)(2,1)S(1)}, bf16[3,196,512]{2,1,0:T(8,128)(2,1)S(1)}, u32[]{:S(2)}, u32[]{:S(2)}) collective-permute-start(bf16[3,196,512]{2,1,0:T(8,128)(2,1)S(1)} %get-tuple-element.71), channel_id=1, source_target_pairs={{0,1},{1,0},{2,3},{3,2},{4,5},{5,4},{6,7},{7,6},{8,9},{9,8},{10,11... | collective-permute-start | bytes 1806344 | tf_op jit(solution)/shard_map/ppermute | solution.py:30
  109.6 11.9 %collective-permute-start.23 = (bf16[196,512]{1,0:T(8,128)(2,1)S(1)}, bf16[196,512]{1,0:T(8,128)(2,1)S(1)}, u32[]{:S(2)}, u32[]{:S(2)}) collective-permute-start(bf16[196,512]{1,0:T(8,128)(2,1)S(1)} %furthest_part.1), channel_id=1, source_target_pairs={{0,2},{2,4},{4,6},{6,8},{8,10},{10,12},{12,14},{14,16},{16,18},{18... | collective-permute-start | bytes 602120 | tf_op jit(solution)/shard_map/ppermute | solution.py:26
  110.8 15.1 %collective-permute-start.22 = (bf16[196,512]{1,0:T(8,128)(2,1)S(1)}, bf16[196,512]{1,0:T(8,128)(2,1)S(1)}, u32[]{:S(2)}, u32[]{:S(2)}) collective-permute-start(bf16[196,512]{1,0:T(8,128)(2,1)S(1)} %get-tuple-element.73), channel_id=1, source_target_pairs={{0,2},{2,4},{4,6},{6,8},{8,10},{10,12},{12,14},{14,16},{16,18},{18... | collective-permute-start | bytes 602120 | tf_op jit(solution)/shard_map/ppermute | solution.py:26
  121.6 16.5 %collective-permute-start.24 = (bf16[196,512]{1,0:T(8,128)(2,1)S(1)}, bf16[196,512]{1,0:T(8,128)(2,1)S(1)}, u32[]{:S(2)}, u32[]{:S(2)}) collective-permute-start(bf16[196,512]{1,0:T(8,128)(2,1)S(1)} %add_convert_fusion), channel_id=1, source_target_pairs={{0,4},{2,6},{4,8},{6,10},{8,12},{10,14},{12,16},{14,18},{16,20},{1... | collective-permute-start | bytes 602120 | tf_op jit(solution)/shard_map/ppermute | solution.py:26
  (13 other events, 93.6 us)
